TPU v7x, 256 devices: a whole 4x4x8 slice. The times are simulated.
256 devices in a mesh: outer: 8 (over y, core), inner: 32 (over z, x).
Axes of the slice: x: 4, y: 4, z: 8, core: 2. Of those that a mesh axis runs over, the one named last changes fastest.
Arguments:
- tokens: bfloat16 [98304, 4096], P(('outer', 'inner')), may hold values from -6 to 6
- out_grad: bfloat16 [98304, 1024], P(('outer', 'inner')), may hold values from -0.25 to 0.25
- master_weights: float32 [1024, 4096], P(('outer', 'inner')), may hold values from -0.0421 to 0.0421
- base_weights: bfloat16 [1024, 4096], replicated, may hold values from -0.030029297 to 0.030029297
- adam_m: float32 [1024, 4096], P(('outer', 'inner')), may hold values from -8 to 8
- adam_v: float32 [1024, 4096], P(('outer', 'inner')), may hold values from 0.1 to 10
- grad_exps: int32 [256, 8, 32], P(('outer', 'inner')), may hold values from -13 to -8
- diff_exps: int32 [1024, 32], P(('outer', 'inner')), may hold values from -20 to -15
- hadamard_signs: int32 [32, 128], replicated, may hold values 0 or 1
Outputs:
- projected: bfloat16 [98304, 1024], P(('outer', 'inner'))
- new_master: float32 [1024, 4096], P(('outer', 'inner'))
- new_first: float32 [1024, 4096], P(('outer', 'inner'))
- new_second: float32 [1024, 4096], P(('outer', 'inner'))
All inputs are finite; a program needn't handle non-finite values.
Results may differ from a plain program's by a relative error of at most 0.005.
Values may be sent and summed in bfloat16 or wider, within the bound.
No kernel may reach another device: no remote copies, remote signals or barrier semaphores. Data moves between devices by JAX's collectives and lax.ppermute only.
A program may use at most 128 MiB of HBM per device.

v0:
```python
import math

import jax
import jax.numpy as jnp
from jax import lax
from jax.sharding import Mesh
from jax.sharding import PartitionSpec as P

ADAM_STEP = 10
INNER = ("inner_0", "inner_1")
OUTER_INNER = ("outer", "inner_0", "inner_1")


clip_level = 448.0
beta_one = 0.9
beta_two = 0.95
learn_rate = 0.002
decay_rate = 0.1
adam_eps = 1e-08
highest = lax.Precision.HIGHEST


def summed_rows(terms, axes):
    running = terms.astype(jnp.bfloat16)
    for axis in axes:
        running = lax.psum_scatter(running, axis, scatter_dimension=0, tiled=True)
    return running.astype(jnp.float32)


def in_blocks(value, dim, count):
    before, after = (value.shape[:dim], value.shape[dim + 1 :])
    return jnp.moveaxis(value.reshape(*before, count, -1, *after), dim, 0)


def sum_at_owner(value, axis, dim):
    count = lax.axis_size(axis)
    blocks = lax.all_to_all(in_blocks(value, dim, count), axis, 0, 0, tiled=True)
    return jnp.sum(blocks.astype(jnp.float32), axis=0)


def sent_to_all(value, axis):
    count = lax.axis_size(axis)
    return lax.all_to_all(
        jnp.broadcast_to(value[None], (count, *value.shape)), axis, 0, 0, tiled=True
    )


def joined_along(blocks, dim):
    blocks = jnp.moveaxis(blocks, 0, dim)
    dims = blocks.shape
    return blocks.reshape(*dims[:dim], dims[dim] * dims[dim + 1], *dims[dim + 2 :])


def gathered_copies(value, axis, dim):
    blocks = sent_to_all(value, axis)
    return joined_along(blocks, dim)


def hadamard(matrix_size):
    positions = jnp.arange(matrix_size, dtype=jnp.int32)
    common = positions[:, None] & positions[None, :]
    parity = jnp.zeros((matrix_size, matrix_size), jnp.int32)
    for bit_level in range(matrix_size.bit_length() - 1):
        parity = parity + (common >> bit_level & 1)
    return (1 - 2 * (parity % 2)).astype(jnp.float32)


def rotate_rows(row_block, sign_rows, matrix):
    row_count = row_block.shape[0]
    blocks = row_block.reshape(row_count, sign_rows.shape[0], sign_rows.shape[1]) * sign_rows
    turned = jnp.dot(blocks.reshape(-1, sign_rows.shape[1]), matrix, precision=highest)
    return turned.reshape(row_block.shape) / math.sqrt(sign_rows.shape[1])


def unrotate_rows(row_block, sign_rows, matrix):
    row_count = row_block.shape[0]
    turned = jnp.dot(
        row_block.reshape(-1, sign_rows.shape[1]), matrix, precision=highest
    ) / math.sqrt(sign_rows.shape[1])
    return (turned.reshape(row_count, sign_rows.shape[0], sign_rows.shape[1]) * sign_rows).reshape(
        row_block.shape
    )


def clip_rows(row_block, bound_rows):
    row_count = row_block.shape[0]
    shaped = row_block.reshape(row_count, bound_rows.shape[1], -1)
    limits = bound_rows[:, :, None]
    return jnp.clip(shaped, -limits, limits).reshape(row_block.shape)


def adam_update(gradient, master, first, second):
    new_first = beta_one * first + (1.0 - beta_one) * gradient
    new_second = beta_two * second + (1.0 - beta_two) * gradient * gradient
    fix_one = 1.0 - beta_one**ADAM_STEP
    fix_two = 1.0 - beta_two**ADAM_STEP
    step_dir = new_first / fix_one / (jnp.sqrt(new_second / fix_two) + adam_eps)
    new_master = master - learn_rate * (step_dir + decay_rate * master)
    return (new_master, new_first, new_second)


def shards(
    tokens,
    out_grad,
    master_weights,
    base_weights,
    adam_m,
    adam_v,
    grad_exps,
    diff_exps,
    hadamard_signs,
):
    outer_count = lax.axis_size("outer")
    inner_count = lax.axis_size(INNER)
    token_rows = tokens.shape[0]
    model_width = tokens.shape[1]
    rows_dev = master_weights.shape[0]
    sign_rows = (2 * hadamard_signs - 1).astype(jnp.float32)
    block_len = sign_rows.shape[1]
    col_blocks = sign_rows.shape[0]
    matrix = hadamard(block_len)
    bound_all = jnp.repeat(
        clip_level * jnp.exp2(grad_exps[0].astype(jnp.float32)), block_len, axis=0
    )
    grad_grid = out_grad.reshape(token_rows, outer_count, inner_count, rows_dev).transpose(
        0, 2, 1, 3
    )
    bound_grid = bound_all.reshape(outer_count, inner_count, rows_dev, col_blocks).transpose(
        1, 0, 2, 3
    )
    coded_bound_sel = bound_grid.reshape(-1, col_blocks)
    term_rows = lax.dot_general(
        grad_grid.reshape(token_rows, -1),
        tokens,
        (((0,), (0,)), ((), ())),
        preferred_element_type=jnp.float32,
    )
    turned = rotate_rows(term_rows, sign_rows, matrix)
    coded_rows = lax.optimization_barrier(clip_rows(turned, coded_bound_sel).astype(jnp.bfloat16))
    coded_rows = coded_rows.astype(jnp.float32)
    group_sum = summed_rows(
        coded_rows.reshape(1 * lax.axis_size(INNER), outer_count, rows_dev, model_width), INNER
    )
    summed = sum_at_owner(group_sum.astype(jnp.bfloat16), "outer", 1).reshape(rows_dev, model_width)
    gradient = unrotate_rows(summed, sign_rows, matrix)
    new_master, new_first, new_second = adam_update(gradient, master_weights, adam_m, adam_v)
    owner = lax.axis_index("outer") * inner_count + lax.axis_index(INNER)
    base_own = lax.dynamic_slice_in_dim(base_weights, owner * rows_dev, rows_dev, 0).astype(
        jnp.float32
    )
    diff_bound = clip_level * jnp.exp2(diff_exps.astype(jnp.float32))
    diff_coded = clip_rows(new_master - base_own, diff_bound).astype(jnp.bfloat16)
    outer_part = gathered_copies(diff_coded.reshape(1, 1, rows_dev, model_width), "outer", 0)
    base_grid = base_weights.reshape(outer_count, inner_count, rows_dev, model_width)
    effective = (
        base_grid.astype(jnp.float32)
        + lax.all_gather(outer_part, INNER, axis=1, tiled=True).astype(jnp.float32)
    ).astype(jnp.bfloat16)
    result = lax.dot_general(
        tokens, effective, (((1,), (3,)), ((), ())), preferred_element_type=jnp.float32
    )
    projected = (
        result.reshape(token_rows, outer_count, -1).astype(jnp.bfloat16).reshape(token_rows, -1)
    )
    return (projected, new_master, new_first, new_second)


def solution(mesh):
    split = Mesh(mesh.devices.reshape(mesh.shape["outer"], 8, 4), ("outer", "inner_0", "inner_1"))
    return jax.shard_map(
        shards,
        mesh=split,
        in_specs=(
            P(OUTER_INNER, None),
            P(OUTER_INNER, None),
            P(OUTER_INNER, None),
            P(),
            P(OUTER_INNER, None),
            P(OUTER_INNER, None),
            P(OUTER_INNER, None, None),
            P(OUTER_INNER, None),
            P(),
        ),
        out_specs=(
            P(OUTER_INNER, None),
            P(OUTER_INNER, None),
            P(OUTER_INNER, None),
            P(OUTER_INNER, None),
        ),
        check_vma=False,
    )
```

profile of v0, /device:TPU:1, one launch (start us, length us, event | category | flops | bytes accessed | tf_op | source)
XLA Modules:
  0.0 408.4 jit_solution(3144663483152369432)
XLA Ops:
  7.2 0.0 reduce-scatter.3.cloned.1.call-start
  7.2 0.7 fusion.40
  7.9 3.4 copy.50
  11.4 2.3 copy.38
  13.7 2.4 reshape.73
  16.0 2.3 copy.39
  18.3 2.3 reshape.81
  20.6 5.7 %convolution_multiply_fusion.1 = f32[1024,32,128]{2,0,1:T(8,128)S(1)} fusion(bf16[384,1024,1]{0,1,2:T(8,128)(2,1)} %reshape.81, bf16[32,128,384]{2,1,0:T(8,128)(2,1)S(1)} %bitcast.61, f32[32,128]{1,0:T(8,128)S(1)} %get-tuple-element.25), kind=kOutput, calls=%fused_computation.6 | convolution fusion | flops 3225419776 | bytes 20725760 | tf_op jit(solution)/shard_map/dot_general | solution.py:132
  26.3 20.2 %copy.41 = f32[1024,32,128]{2,1,0:T(8,128)S(1)} copy(f32[1024,32,128]{2,0,1:T(8,128)S(1)} %convolution_multiply_fusion.1) | data formatting | bytes 33554432 | tf_op jit(solution)/shard_map/mul | solution.py:70
  46.4 15.3 %convolution_multiply_fusion = bf16[32768,128]{1,0:T(8,128)(2,1)} fusion(f32[32768,128]{1,0:T(8,128)S(1)} %bitcast.56), kind=kOutput, calls=%fused_computation | convolution fusion | flops 6451412992 | bytes 25165824 | tf_op jit(solution)/shard_map/dot_general | solution.py:71
  61.8 13.4 %div.31 = bf16[1024,4096]{1,0:T(8,128)(2,1)} reshape(bf16[32768,128]{1,0:T(8,128)(2,1)} %convolution_multiply_fusion) | data formatting | bytes 16777216 | tf_op jit(solution)/shard_map/div | solution.py:72
  75.2 0.0 copy-done.4
  75.2 0.1 transpose.19
  75.3 0.0 slice-start
  75.3 11.7 %max.32 = bf16[1024,32,128]{2,1,0:T(8,128)(2,1)S(1)} broadcast(bf16[1024,32]{1,0:T(8,128)(2,1)S(1)} %neg.13), dimensions={0,1} | broadcast | bytes 8454144 | tf_op jit(solution)/shard_map/jit(clip)/max | solution.py:89
  87.1 0.0 slice-start.1
  87.1 10.2 %min.35 = bf16[1024,32,128]{2,1,0:T(8,128)(2,1)S(1)} broadcast(f32[1024,32]{1,0:T(8,128)S(1)} %bitcast.63), dimensions={0,1} | broadcast | bytes 8519680 | tf_op jit(solution)/shard_map/jit(clip)/min | solution.py:89
  97.3 0.0 slice-done
  97.3 0.0 slice-done.1
  97.3 6.5 %fusion.1 = bf16[1024,4096]{1,0:T(8,128)(2,1)} fusion(bf16[1024,4096]{1,0:T(8,128)(2,1)S(1)} %bitcast.58, bf16[128,8,32,128]{3,2,1,0:T(8,128)(2,1)S(1)} %bitcast.59, bf16[128,8,32,128]{3,2,1,0:T(8,128)(2,1)S(1)} %bitcast.60), kind=kLoop, calls=%fused_computation.3 | loop fusion | flops 8388608 | bytes 33554432 | tf_op jit(solution)/shard_map/convert_element_type | solution.py:139
  103.8 13.1 %convert_element_type.63 = bf16[32,8,4,4096]{3,2,1,0:T(4,128)(2,1)} reshape(bf16[1024,4096]{1,0:T(8,128)(2,1)} %fusion.1) | data formatting | bytes 16777216 | tf_op jit(solution)/shard_map/convert_element_type | solution.py:24
  117.0 15.5 %copy.42 = bf16[32,8,4,4096]{3,1,2,0:T(8,128)(2,1)} copy(bf16[32,8,4,4096]{3,2,1,0:T(4,128)(2,1)} %convert_element_type.63) | data formatting | bytes 16777216 | tf_op jit(solution)/shard_map/convert_element_type | solution.py:24
  132.5 0.0 reduce-scatter.3.cloned.1.call-update
  132.5 0.3 reduce-scatter.5.cloned.1.call-start
  132.7 98.6 %reduce-scatter.3.cloned.1.call-done = bf16[4,8,4,4096]{3,1,2,0:T(8,128)(2,1)} async-done(((bf16[32,8,4,4096]{3,1,2,0:T(8,128)(2,1)}), bf16[4,8,4,4096]{3,1,2,0:T(8,128)(2,1)}) %reduce-scatter.3.cloned.1.call-update) | async-done | bytes 1048592 | tf_op jit(solution)/shard_map/reduce_scatter | solution.py:26
  231.4 0.0 reduce-scatter.5.cloned.1.call-update
  231.4 25.8 %reduce-scatter.5.cloned.1.call-done = bf16[1,8,4,4096]{3,1,2,0:T(8,128)(2,1)} async-done(((bf16[4,8,4,4096]{3,1,2,0:T(8,128)(2,1)}), bf16[1,8,4,4096]{3,1,2,0:T(8,128)(2,1)}) %reduce-scatter.5.cloned.1.call-update) | async-done | bytes 262160 | tf_op jit(solution)/shard_map/reduce_scatter | solution.py:26
  257.3 1.9 copy.43
  259.1 6.3 %all-to-all-start = ((bf16[8,1,1,4,4096]{4,3,2,1,0:T(4,128)(2,1)}), bf16[8,1,1,4,4096]{4,3,2,1,0:T(4,128)(2,1)S(1)}, u32[]{:S(2)}, u32[]{:S(2)}) async-start(bf16[8,1,1,4,4096]{4,3,2,1,0:T(4,128)(2,1)} %copy.43), calls=%async_computation.2 | async-start | bytes 524288 | tf_op jit(solution)/shard_map/all_to_all | solution.py:37
  265.4 0.0 all-gather.3.cloned.1.call-start
  265.4 0.0 copy-done.5
  265.4 0.1 broadcast_bitcast_fusion
  265.5 6.4 %all-to-all-done = bf16[8,1,1,4,4096]{4,3,2,1,0:T(4,128)(2,1)S(1)} async-done(((bf16[8,1,1,4,4096]{4,3,2,1,0:T(4,128)(2,1)}), bf16[8,1,1,4,4096]{4,3,2,1,0:T(4,128)(2,1)S(1)}, u32[]{:S(2)}, u32[]{:S(2)}) %all-to-all-start) | async-done | bytes 262176 | tf_op jit(solution)/shard_map/all_to_all | solution.py:37
  271.9 0.1 convert_reduce_fusion
  272.0 0.1 reshape_reshape.4
  272.1 0.3 convolution_multiply_fusion.2
  272.4 1.7 fusion.22
  274.1 0.1 broadcast_in_dim.2
  274.2 9.9 %all_to_all.10 = bf16[8,1,1,4,4096]{4,3,2,1,0:T(4,128)(2,1)S(1)} all-to-all(bf16[8,1,1,4,4096]{4,3,2,1,0:T(4,128)(2,1)S(1)} %broadcast_in_dim.2), channel_id=1, replica_groups=mesh['outer'=8,'inner_0'=8,'inner_1'=4] {'outer'}, dimensions={0} | all-to-all | bytes 524288 | tf_op jit(solution)/shard_map/all_to_all | solution.py:43
  284.1 0.9 copy.44
  285.0 0.0 all-gather.3.cloned.1.call-update
  285.0 15.5 %reshape.78 = f32[8,32,4,4096]{3,2,1,0:T(4,128)} reshape(bf16[1024,4096]{1,0:T(8,128)(2,1)} %param.12) | data formatting | bytes 25165824 | tf_op jit(solution)/shard_map/convert_element_type | solution.py:156
  300.5 80.9 %all-gather.3.cloned.1.call-done = bf16[8,32,1,4,4096]{4,0,3,2,1:T(8,128)(2,1)} async-done(((bf16[8,1,1,4,4096]{4,0,3,2,1:T(8,128)(2,1)}), bf16[8,32,1,4,4096]{4,0,3,2,1:T(8,128)(2,1)}) %all-gather.3.cloned.1.call-update) | async-done | bytes 8388624 | tf_op jit(solution)/shard_map/all_gather | solution.py:157
  381.4 13.8 %fusion.2 = bf16[8,32,4,4096]{3,2,1,0:T(4,128)(2,1)S(1)} fusion(f32[8,32,4,4096]{3,2,1,0:T(4,128)} %reshape.78, bf16[8,32,1,4,4096]{4,0,3,2,1:T(8,128)(2,1)} %all-gather.3.cloned.1.call-done), kind=kLoop, calls=%fused_computation.5 | loop fusion | flops 12582912 | bytes 33554432 | tf_op jit(solution)/shard_map/convert_element_type | solution.py:158
  395.2 5.0 %fusion.11 = bf16[384,8,32,4]{0,1,3,2:T(8,128)(2,1)S(1)} fusion(bf16[384,4096]{1,0:T(8,128)(2,1)S(1)} %copy-done, bf16[8,32,4,4096]{3,2,1,0:T(4,128)(2,1)S(1)} %fusion.2), kind=kOutput, calls=%fused_computation.11 | convolution fusion | flops 3221618688 | bytes 12320768 | tf_op jit(solution)/shard_map/dot_general | solution.py:159
  400.2 0.3 copy.47
  400.5 0.2 convert_element_type.71
  400.7 1.2 copy.48
  (15 shorter events, 0.1 us)
Async XLA Ops:
  7.2 224.2 %reduce-scatter.3.cloned.1.call-start = ((), (), s32[]{:S(2)}) async-start(), calls=%async_computation.4 | async-start | bytes 9437184 | tf_op jit(solution)/shard_map/reduce_scatter | solution.py:26
  61.8 13.4 %copy-start.4 = (s32[1,8,32]{2,1,0:T(8,128)S(1)}, s32[1,8,32]{2,1,0:T(8,128)}, u32[]{:S(2)}) copy-start(s32[1,8,32]{2,1,0:T(8,128)} %param.15) | copy-start | bytes 3076
  75.3 22.0 %slice-start = ((s8[8388608]{0:T(1024)(128)(4,1)}), s8[4194304]{0:T(1024)(128)(4,1)S(1)}, s32[]{:S(2)}) async-start(s8[8388608]{0:T(1024)(128)(4,1)} %bitcast.57), calls=%async_computation.7 | async-start | bytes 8388608
  87.1 10.3 %slice-start.1 = ((s8[8388608]{0:T(1024)(128)(4,1)}), s8[4194304]{0:T(1024)(128)(4,1)S(1)}, s32[]{:S(2)}) async-start(s8[8388608]{0:T(1024)(128)(4,1)} %bitcast.57), calls=%async_computation.8 | async-start | bytes 8388608
  132.4 133.0 %copy-start.5 = (s32[4,32]{1,0:T(4,128)S(1)}, s32[4,32]{1,0:T(4,128)}, u32[]{:S(2)}) copy-start(s32[4,32]{1,0:T(4,128)} %param.16) | copy-start | bytes 1540
  132.4 140.0 %copy-start.1 = (f32[4,4096]{1,0:T(4,128)S(1)}, f32[4,4096]{1,0:T(4,128)}, u32[]{:S(2)}) copy-start(f32[4,4096]{1,0:T(4,128)} %param.11) | copy-start | bytes 196612
  132.4 140.0 %copy-start.2 = (f32[4,4096]{1,0:T(4,128)S(1)}, f32[4,4096]{1,0:T(4,128)}, u32[]{:S(2)}) copy-start(f32[4,4096]{1,0:T(4,128)} %param.13) | copy-start | bytes 196612
  132.4 140.0 %copy-start.3 = (f32[4,4096]{1,0:T(4,128)S(1)}, f32[4,4096]{1,0:T(4,128)}, u32[]{:S(2)}) copy-start(f32[4,4096]{1,0:T(4,128)} %param.14) | copy-start | bytes 196612
  132.5 124.8 %reduce-scatter.5.cloned.1.call-start = ((), (), s32[]{:S(2)}) async-start(), calls=%async_computation.5 | async-start | bytes 1310720 | tf_op jit(solution)/shard_map/reduce_scatter | solution.py:26
  259.1 12.8 %all-to-all-start = ((bf16[8,1,1,4,4096]{4,3,2,1,0:T(4,128)(2,1)}), bf16[8,1,1,4,4096]{4,3,2,1,0:T(4,128)(2,1)S(1)}, u32[]{:S(2)}, u32[]{:S(2)}) async-start(bf16[8,1,1,4,4096]{4,3,2,1,0:T(4,128)(2,1)} %copy.43), calls=%async_computation.2 | async-start | bytes 524288 | tf_op jit(solution)/shard_map/all_to_all | solution.py:37
  265.4 115.9 %all-gather.3.cloned.1.call-start = ((), (), s32[]{:S(2)}) async-start(), calls=%async_computation.6 | async-start | bytes 8650752 | tf_op jit(solution)/shard_map/all_gather | solution.py:157
  300.5 94.7 %copy-start = (bf16[384,4096]{1,0:T(8,128)(2,1)S(1)}, bf16[384,4096]{1,0:T(8,128)(2,1)}, u32[]{:S(2)}) copy-start(bf16[384,4096]{1,0:T(8,128)(2,1)} %param.9) | copy-start | bytes 9437188
Sparse Core Ops, SparseCore 0:
  132.6 98.7 reduce-scatter.2
  233.9 23.2 reduce-scatter.4
  285.1 96.2 all-gather.2
where the time goes:
time: 410 us; the launch traced here: 408 us
  waiting for transfers between devices  212 us (52%)
  local copies, waits for them, and re-layouts  117 us (29%)
  matrix products  26.3 us (6%)
  other arithmetic  22.9 us (6%)
  between operations  13.9 us (3%)
  blocking collectives  9.94 us (2%)
  starting transfers between devices  6.6 us (2%)
    reduce_scatter x2, waiting for transfers between devices, summed_rows(): running = lax.psum_scatter(running, axis, scatter_dimension=0, tiled=True)  124 us
    all_gather x1, waiting for transfers between devices, shards(): lax.all_gather(outer_part, INNER, axis=1, tiled=True).astype(jnp.float32)  80.9 us
    convert_element_type x2, local copies, waits for them, and re-layouts, summed_rows(): running = terms.astype(jnp.bfloat16)  28.6 us
    mul x1, local copies, waits for them, and re-layouts, rotate_rows(): row_block.reshape(row_count, sign_rows.shape[0], sign_rows.shape[1])  20.2 us
    convert_element_type x1, local copies, waits for them, and re-layouts, shards(): base_grid.astype(jnp.float32)  15.5 us
    dot_general x1, matrix products, rotate_rows(): jnp.dot(blocks.reshape(-1, sign_rows.shape[1]), matrix, precision=highest)  15.3 us
    convert_element_type x1, other arithmetic, shards(): effective = (base_grid.astype(jnp.float32) + lax.all_gather(outer_part, I...  13.8 us
    div x1, local copies, waits for them, and re-layouts, rotate_rows(): return turned.reshape(row_block.shape) / math.sqrt(sign_rows.shape[1])  13.4 us
  transfers between devices with their start and end apart: 4, of which 4 were waited for; matrix products, arithmetic and copies ran while one was open for 4% of the time, Pallas kernels for 0%

commit v1 on v0

v1 whole, which is shorter than its diff:
```python
import math

import jax
import jax.numpy as jnp
from jax import lax
from jax.experimental import pallas as pl
from jax.experimental.pallas import tpu as pltpu
from jax.sharding import Mesh
from jax.sharding import PartitionSpec as P

ADAM_STEP = 10
OUTER_INNER = ("outer", "inner_0", "inner_1")

clip_level = 448.0
beta_one = 0.9
beta_two = 0.95
learn_rate = 0.002
decay_rate = 0.1
adam_eps = 1e-08
highest = lax.Precision.HIGHEST


def hadamard(matrix_size):
    positions = jnp.arange(matrix_size, dtype=jnp.int32)
    common = positions[:, None] & positions[None, :]
    parity = jnp.zeros((matrix_size, matrix_size), jnp.int32)
    for bit_level in range(matrix_size.bit_length() - 1):
        parity = parity + (common >> bit_level & 1)
    return (1 - 2 * (parity % 2)).astype(jnp.float32)


def unrotate_rows(row_block, sign_rows, matrix):
    row_count = row_block.shape[0]
    turned = jnp.dot(
        row_block.reshape(-1, sign_rows.shape[1]), matrix, precision=highest
    ) / math.sqrt(sign_rows.shape[1])
    return (turned.reshape(row_count, sign_rows.shape[0], sign_rows.shape[1]) * sign_rows).reshape(
        row_block.shape
    )


def clip_rows(row_block, bound_rows):
    row_count = row_block.shape[0]
    shaped = row_block.reshape(row_count, bound_rows.shape[1], -1)
    limits = bound_rows[:, :, None]
    return jnp.clip(shaped, -limits, limits).reshape(row_block.shape)


def adam_update(gradient, master, first, second):
    new_first = beta_one * first + (1.0 - beta_one) * gradient
    new_second = beta_two * second + (1.0 - beta_two) * gradient * gradient
    fix_one = 1.0 - beta_one**ADAM_STEP
    fix_two = 1.0 - beta_two**ADAM_STEP
    step_dir = new_first / fix_one / (jnp.sqrt(new_second / fix_two) + adam_eps)
    new_master = master - learn_rate * (step_dir + decay_rate * master)
    return (new_master, new_first, new_second)


def coded_kernel(block_len, row_tile, tok_ref, grad_ref, sign_ref, bound_ref, mat_ref, out_ref, turned_ref, grad_t_ref):
    token_rows = tok_ref.shape[0]
    width = tok_ref.shape[1]

    @pl.when(pl.program_id(0) == 0)
    def _():
        grad_t = grad_ref[...].T
        grad_t_ref[:, :token_rows] = grad_t
        grad_t_ref[:, token_rows:] = grad_t

    scale = 1.0 / math.sqrt(block_len)
    for start in range(0, width, block_len):
        cols = slice(start, start + block_len)
        signed = tok_ref[:, cols] * sign_ref[:, cols]
        turned = jnp.dot(signed, mat_ref[...], preferred_element_type=jnp.float32) * scale
        upper = turned.astype(jnp.bfloat16)
        turned_ref[:token_rows, cols] = upper
        turned_ref[token_rows:, cols] = (turned - upper.astype(jnp.float32)).astype(jnp.bfloat16)
    terms = jnp.dot(grad_t_ref[...], turned_ref[...], preferred_element_type=jnp.float32)
    for tile in range(out_ref.shape[0] // row_tile):
        rows = slice(tile * row_tile, (tile + 1) * row_tile)
        limit = bound_ref[tile : tile + 1, :]
        out_ref[rows, :] = jnp.clip(terms[rows, :], -limit, limit).astype(jnp.bfloat16)


def coded_gradient(tokens, out_grad, signs, bounds, matrix):
    token_rows, model_width = tokens.shape
    feature_rows = out_grad.shape[1]
    block_len = matrix.shape[0]
    width = 512
    row_tile = feature_rows // bounds.shape[0]
    body = lambda *refs: coded_kernel(block_len, row_tile, *refs)
    return pl.pallas_call(
        body,
        grid=(model_width // width,),
        in_specs=[
            pl.BlockSpec((token_rows, width), lambda n: (0, n)),
            pl.BlockSpec((token_rows, feature_rows), lambda n: (0, 0)),
            pl.BlockSpec((1, width), lambda n: (0, n)),
            pl.BlockSpec((bounds.shape[0], width), lambda n: (0, n)),
            pl.BlockSpec((block_len, block_len), lambda n: (0, 0)),
        ],
        out_specs=pl.BlockSpec((feature_rows, width), lambda n: (0, n)),
        out_shape=jax.ShapeDtypeStruct((feature_rows, model_width), jnp.bfloat16),
        scratch_shapes=[
            pltpu.VMEM((2 * token_rows, width), jnp.bfloat16),
            pltpu.VMEM((feature_rows, 2 * token_rows), jnp.bfloat16),
        ],
        compiler_params=pltpu.CompilerParams(vmem_limit_bytes=48 << 20),
    )(tokens, out_grad, signs, bounds, matrix)


def shards(
    tokens,
    out_grad,
    master_weights,
    base_weights,
    adam_m,
    adam_v,
    grad_exps,
    diff_exps,
    hadamard_signs,
):
    rows_dev = master_weights.shape[0]
    sign_rows = (2 * hadamard_signs - 1).astype(jnp.float32)
    block_len = sign_rows.shape[1]
    matrix = hadamard(block_len)
    bounds = jnp.repeat(clip_level * jnp.exp2(grad_exps[0].astype(jnp.float32)), block_len, axis=1)
    coded = coded_gradient(
        tokens,
        out_grad,
        sign_rows.reshape(1, -1).astype(jnp.bfloat16),
        bounds,
        matrix.astype(jnp.bfloat16),
    )
    for axis in OUTER_INNER:
        coded = lax.psum_scatter(coded, axis, scatter_dimension=0, tiled=True)
    gradient = unrotate_rows(coded.astype(jnp.float32), sign_rows, matrix)
    new_master, new_first, new_second = adam_update(gradient, master_weights, adam_m, adam_v)
    owner = lax.axis_index(OUTER_INNER)
    base_own = lax.dynamic_slice_in_dim(base_weights, owner * rows_dev, rows_dev, 0).astype(
        jnp.float32
    )
    diff_bound = clip_level * jnp.exp2(diff_exps.astype(jnp.float32))
    diff_coded = clip_rows(new_master - base_own, diff_bound).astype(jnp.bfloat16)
    effective = (base_own + diff_coded.astype(jnp.float32)).astype(jnp.bfloat16)
    for axis in reversed(OUTER_INNER):
        effective = lax.all_gather(effective, axis, axis=0, tiled=True)
    projected = lax.dot_general(
        tokens, effective, (((1,), (1,)), ((), ())), preferred_element_type=jnp.float32
    ).astype(jnp.bfloat16)
    return (projected, new_master, new_first, new_second)


def solution(mesh):
    split = Mesh(mesh.devices.reshape(mesh.shape["outer"], 8, 4), OUTER_INNER)
    rows = P(OUTER_INNER, None)
    return jax.shard_map(
        shards,
        mesh=split,
        in_specs=(rows, rows, rows, P(), rows, rows, P(OUTER_INNER, None, None), rows, P()),
        out_specs=(rows, rows, rows, rows),
        check_vma=False,
    )
```

time: 410 us -> 295 us (0.72)
  local copies, waits for them, and re-layouts: 117 us -> 7.81 us
  waiting for transfers between devices: 212 us -> 240 us
  other arithmetic: 22.9 us -> 3.18 us
  matrix products: 26.3 us -> 8.21 us
  Pallas kernels: 0 us -> 11.6 us
  starting transfers between devices: 6.6 us -> 0.2 us
    unnamed x3 -> x6, waiting for transfers between devices: 0.05 us -> 50.1 us
    convert_element_type x5 -> x0, local copies, waits for them, and re-layouts: 44.6 us -> none  [the longest x2 28.6 us: summed_rows(): running = terms.astype(jnp.bfloat16)]
    reduce_scatter x2, waiting for transfers between devices: 124 us -> 93.4 us  [shards(): coded = lax.psum_scatter(coded, axis, scatter_dimension=0, tiled=True)]
    convert_element_type x3 -> x1, other arithmetic: 22 us -> 0.09 us  [shards(): matrix.astype(jnp.bfloat16)]
    mul x1, local copies, waits for them, and re-layouts: 20.2 us -> 0.08 us  [shards(): clip_level * jnp.exp2(grad_exps[0].astype(jnp.float32))]
    dot_general x3 -> x1, matrix products: 26 us -> 7.95 us  [shards(): lax.dot_general(tokens, effective, (((1,), (1,)), ((), ())), preferred_el...]
    all_gather x1 -> x2, waiting for transfers between devices: 80.9 us -> 96.7 us  [shards(): effective = lax.all_gather(effective, axis, axis=0, tiled=True)]
    div x1 -> x0, local copies, waits for them, and re-layouts: 13.4 us -> none  [rotate_rows(): return turned.reshape(row_block.shape) / math.sqrt(sign_rows.shape[1])]
  transfers between devices with their start and end apart: 4 -> 5, of which waited for: 4 -> 5; matrix products, arithmetic and copies ran while one was open for 4% -> 0% of each run, Pallas kernels for 0% -> 0%
where the time goes in v1:
time: 295 us
  waiting for transfers between devices  240 us (81%)
  between operations  14.5 us (5%)
  Pallas kernels  11.6 us (4%)
  blocking collectives  9.09 us (3%)
  matrix products  8.21 us (3%)
  local copies, waits for them, and re-layouts  7.81 us (3%)
  other arithmetic  3.18 us (1%)
    all_gather x2, waiting for transfers between devices, shards(): effective = lax.all_gather(effective, axis, axis=0, tiled=True)  96.7 us
    reduce_scatter x2, waiting for transfers between devices, shards(): coded = lax.psum_scatter(coded, axis, scatter_dimension=0, tiled=True)  93.4 us
    unnamed x6, waiting for transfers between devices  50.1 us
    pallas_call x1, Pallas kernels, coded_gradient(): pl.pallas_call(body, grid=(model_width // width,), in_specs=[pl.BlockSpec...  11.6 us
    all_gather x1, blocking collectives, shards(): effective = lax.all_gather(effective, axis, axis=0, tiled=True)  9.09 us
    dot_general x1, matrix products, shards(): lax.dot_general(tokens, effective, (((1,), (1,)), ((), ())), preferred_el...  7.95 us
    unnamed x22, local copies, waits for them, and re-layouts  7.57 us
  transfers between devices with their start and end apart: 5, of which 5 were waited for; matrix products, arithmetic and copies ran while one was open for 0% of the time, Pallas kernels for 0%

profile of v1, /device:TPU:1, one launch (start us, length us, event | category | flops | bytes accessed | tf_op | source)
XLA Modules:
  0.0 294.9 jit_solution(12123425448525297674)
XLA Ops:
  7.2 0.0 reduce-scatter.3.cloned.1.call-start
  7.2 0.1 fusion.12.refs_4_
  7.3 0.7 multiply_bitcast_fusion
  8.0 0.1 copy.15
  8.1 0.7 convert_bitcast_fusion
  8.8 0.1 broadcast_bitcast_fusion.refs_3_
  8.9 0.0 copy-start
  8.9 1.9 copy-done
  10.8 0.0 copy-start.2
  10.8 1.1 copy-done.2
  12.0 0.0 copy-start.7
  12.0 0.0 copy-start.6
  12.0 11.6 %shard_map.120 = bf16[1024,4096]{1,0:T(8,128)(2,1)} custom-call(bf16[384,4096]{1,0:T(8,128)(2,1)S(1)} %copy-done, bf16[384,1024]{1,0:T(8,128)(2,1)S(1)} %copy-done.2, bf16[1,4096]{1,0:T(2,128)(2,1)S(1)} %bitcast.32, f32[8,4096]{1,0:T(8,128)S(1)} %broadcast_bitcast_fusion.refs_3_, bf16[128,128]{1,0:T(8,128)(2,1)S(1)} %fusion.12.refs_4_), custom_call_target="tpu_custom_call" | custom-call | tf_op jit(solution)/shard_map/pallas_call | solution.py:91
  23.5 0.0 copy-start.3
  23.5 0.0 copy-start.4
  23.5 0.0 copy-start.5
  23.5 0.0 copy-start.1
  23.5 0.0 reduce-scatter.3.cloned.1.call-update
  23.6 0.0 reduce-scatter.5.cloned.1.call-start
  23.6 58.3 %reduce-scatter.3.cloned.1.call-done = bf16[128,4096]{1,0:T(8,128)(2,1)} async-done(((bf16[1024,4096]{1,0:T(8,128)(2,1)}), bf16[128,4096]{1,0:T(8,128)(2,1)}) %reduce-scatter.3.cloned.1.call-update) | async-done | bytes 1048592 | tf_op jit(solution)/shard_map/reduce_scatter | solution.py:135
  81.9 0.0 reduce-scatter.5.cloned.1.call-update
  82.0 0.0 all-reduce.3.cloned.1.call-start
  82.0 0.0 copy-done.7
  82.0 0.6 dynamic-slice
  83.3 0.0 copy-done.6
  83.3 35.1 %reduce-scatter.5.cloned.1.call-done = bf16[16,4096]{1,0:T(8,128)(2,1)} async-done(((bf16[128,4096]{1,0:T(8,128)(2,1)}), bf16[16,4096]{1,0:T(8,128)(2,1)}) %reduce-scatter.5.cloned.1.call-update) | async-done | bytes 131088 | tf_op jit(solution)/shard_map/reduce_scatter | solution.py:135
  118.4 0.0 all-reduce.3.cloned.1.call-update
  118.4 0.0 all-gather.4.cloned.1.call-start
  118.5 0.1 broadcast_bitcast_fusion.1
  118.6 50.0 %all-reduce.3.cloned.1.call-done = bf16[16,4096]{1,0:T(8,128)(2,1)} async-done(((bf16[16,4096]{1,0:T(8,128)(2,1)}), bf16[16,4096]{1,0:T(8,128)(2,1)}) %all-reduce.3.cloned.1.call-update) | async-done | bytes 131088
  168.6 0.9 constant_dynamic-slice_fusion
  169.5 0.3 convolution_multiply_fusion
  169.8 0.0 copy-done.3
  169.8 0.0 copy-done.4
  169.8 0.0 copy-done.5
  169.9 1.7 fusion.10
  171.5 9.1 %all-gather = bf16[4,4,4096]{2,1,0:T(4,128)(2,1)S(1)} all-gather(bf16[1,4,4096]{2,1,0:T(4,128)(2,1)S(1)} %get-tuple-element.12), channel_id=1, replica_groups=mesh['outer'=8,'inner_0'=8,'inner_1'=4] {'inner_1'}, dimensions={0}, use_global_device_ids=true | all-gather | bytes 163840 | tf_op jit(solution)/shard_map/all_gather | solution.py:146
  180.6 0.7 reshape.53
  181.3 0.0 all-gather.4.cloned.1.call-update
  181.3 0.0 all-gather.6.cloned.1.call-start
  181.4 38.6 %all-gather.4.cloned.1.call-done = bf16[128,4096]{1,0:T(8,128)(2,1)} async-done(((bf16[16,4096]{1,0:T(8,128)(2,1)}), bf16[128,4096]{1,0:T(8,128)(2,1)}) %all-gather.4.cloned.1.call-update) | async-done | bytes 1048592 | tf_op jit(solution)/shard_map/all_gather | solution.py:146
  220.0 0.0 all-gather.6.cloned.1.call-update
  220.0 58.2 %all-gather.6.cloned.1.call-done = bf16[1024,4096]{1,0:T(8,128)(2,1)} async-done(((bf16[128,4096]{1,0:T(8,128)(2,1)}), bf16[1024,4096]{1,0:T(8,128)(2,1)}) %all-gather.6.cloned.1.call-update) | async-done | bytes 8388624 | tf_op jit(solution)/shard_map/all_gather | solution.py:146
  278.1 0.0 copy-done.1
  278.1 7.9 %fusion = bf16[384,1024]{0,1:T(8,128)(2,1)} fusion(bf16[1024,4096]{1,0:T(8,128)(2,1)} %all-gather.6.cloned.1.call-done, bf16[384,4096]{1,0:T(8,128)(2,1)S(1)} %copy-done.1), kind=kOutput, calls=%fused_computation.1 | convolution fusion | flops 3221618688 | bytes 12320768 | tf_op jit(solution)/shard_map/dot_general | solution.py:147
  286.1 2.3 copy.16
  (4 shorter events, 0.1 us)
Async XLA Ops:
  7.2 74.8 %reduce-scatter.3.cloned.1.call-start = ((), (), s32[]{:S(2)}) async-start(), calls=%async_computation.2 | async-start | bytes 9437184 | tf_op jit(solution)/shard_map/reduce_scatter | solution.py:135
  8.9 1.9 copy-start
  10.8 1.1 copy-start.2
  12.0 70.1 %copy-start.7 = (u32[256]{0:T(256)S(1)}, u32[256]{0:T(256)}, u32[]{:S(2)}) copy-start(u32[256]{0:T(256)} %constant.85) | copy-start | bytes 3076
  12.0 71.3 %copy-start.6 = (s32[4,32]{1,0:T(4,128)S(1)}, s32[4,32]{1,0:T(4,128)}, u32[]{:S(2)}) copy-start(s32[4,32]{1,0:T(4,128)} %param.16) | copy-start | bytes 1540
  23.5 146.3 %copy-start.3 = (f32[4,4096]{1,0:T(4,128)S(1)}, f32[4,4096]{1,0:T(4,128)}, u32[]{:S(2)}) copy-start(f32[4,4096]{1,0:T(4,128)} %param.11) | copy-start | bytes 196612
  23.5 146.3 %copy-start.4 = (f32[4,4096]{1,0:T(4,128)S(1)}, f32[4,4096]{1,0:T(4,128)}, u32[]{:S(2)}) copy-start(f32[4,4096]{1,0:T(4,128)} %param.13) | copy-start | bytes 196612
  23.5 146.3 %copy-start.5 = (f32[4,4096]{1,0:T(4,128)S(1)}, f32[4,4096]{1,0:T(4,128)}, u32[]{:S(2)}) copy-start(f32[4,4096]{1,0:T(4,128)} %param.14) | copy-start | bytes 196612
  23.5 254.6 %copy-start.1 = (bf16[384,4096]{1,0:T(8,128)(2,1)S(1)}, bf16[384,4096]{1,0:T(8,128)(2,1)}, u32[]{:S(2)}) copy-start(bf16[384,4096]{1,0:T(8,128)(2,1)} %refs_0_.1) | copy-start | bytes 9437188
  23.6 94.8 %reduce-scatter.5.cloned.1.call-start = ((), (), s32[]{:S(2)}) async-start(), calls=%async_computation.3 | async-start | bytes 1179648 | tf_op jit(solution)/shard_map/reduce_scatter | solution.py:135
  82.0 86.7 %all-reduce.3.cloned.1.call-start = ((), (), s32[]{:S(2)}) async-start(), calls=%async_computation.6 | async-start | bytes 262144
  118.4 101.5 %all-gather.4.cloned.1.call-start = ((), (), s32[]{:S(2)}) async-start(), calls=%async_computation.4 | async-start | bytes 1179648 | tf_op jit(solution)/shard_map/all_gather | solution.py:146
  181.3 96.8 %all-gather.6.cloned.1.call-start = ((), (), s32[]{:S(2)}) async-start(), calls=%async_computation.5 | async-start | bytes 9437184 | tf_op jit(solution)/shard_map/all_gather | solution.py:146
Sparse Core Ops, SparseCore 0:
  23.7 58.2 reduce-scatter.2
  84.5 33.8 reduce-scatter.4
  120.7 47.8 all-reduce.2
  181.4 38.4 all-gather.3
  221.8 56.2 all-gather.5

commit v2 on v1

v2 whole, which is shorter than its diff:
```python
import math

import jax
import jax.numpy as jnp
from jax import lax
from jax.experimental import pallas as pl
from jax.experimental.pallas import tpu as pltpu
from jax.sharding import Mesh
from jax.sharding import PartitionSpec as P

ADAM_STEP = 10
AXES = ("y", "c", "z", "x")
FACE = ("y", "c", "x")

clip_level = 448.0
beta_one = 0.9
beta_two = 0.95
learn_rate = 0.002
decay_rate = 0.1
adam_eps = 1e-08
highest = lax.Precision.HIGHEST


def hadamard(matrix_size):
    positions = jnp.arange(matrix_size, dtype=jnp.int32)
    common = positions[:, None] & positions[None, :]
    parity = jnp.zeros((matrix_size, matrix_size), jnp.int32)
    for bit_level in range(matrix_size.bit_length() - 1):
        parity = parity + (common >> bit_level & 1)
    return (1 - 2 * (parity % 2)).astype(jnp.float32)


def unrotate_rows(row_block, sign_rows, matrix):
    row_count = row_block.shape[0]
    turned = jnp.dot(
        row_block.reshape(-1, sign_rows.shape[1]), matrix, precision=highest
    ) / math.sqrt(sign_rows.shape[1])
    return (turned.reshape(row_count, sign_rows.shape[0], sign_rows.shape[1]) * sign_rows).reshape(
        row_block.shape
    )


def clip_rows(row_block, bound_rows):
    row_count = row_block.shape[0]
    shaped = row_block.reshape(row_count, bound_rows.shape[1], -1)
    limits = bound_rows[:, :, None]
    return jnp.clip(shaped, -limits, limits).reshape(row_block.shape)


def adam_update(gradient, master, first, second):
    new_first = beta_one * first + (1.0 - beta_one) * gradient
    new_second = beta_two * second + (1.0 - beta_two) * gradient * gradient
    fix_one = 1.0 - beta_one**ADAM_STEP
    fix_two = 1.0 - beta_two**ADAM_STEP
    step_dir = new_first / fix_one / (jnp.sqrt(new_second / fix_two) + adam_eps)
    new_master = master - learn_rate * (step_dir + decay_rate * master)
    return (new_master, new_first, new_second)


def row_order(count_z, count_x, rows_dev):
    size = count_z * count_x * rows_dev
    spots = jnp.arange(size, dtype=jnp.int32)
    at_x, at_z, at_j = spots // (count_z * rows_dev), spots // rows_dev % count_z, spots % rows_dev
    natural = (at_z * count_x + at_x) * rows_dev + at_j
    return (natural[:, None] == spots[None, :]).astype(jnp.bfloat16)


def coded_kernel(groups, added, core_ref, tok_ref, *refs):
    grad_refs = refs[:groups]
    sign_ref, bound_ref, mat_ref, order_ref = refs[groups : groups + 4]
    if added:
        own_ref, out_ref, turned_ref, grad_t_ref = refs[groups + 4 :]
    else:
        out_ref, turned_ref, grad_t_ref = refs[groups + 4 :]
    token_rows, width = tok_ref.shape
    block_len = mat_ref.shape[0]
    tile = order_ref.shape[0]
    core = core_ref[0]

    @pl.when(pl.program_id(0) == 0)
    def _():
        for group in range(groups):
            grad_t = lax.dot_general(
                order_ref[...],
                grad_refs[group][...],
                (((1,), (1,)), ((), ())),
                preferred_element_type=jnp.float32,
            ).astype(jnp.bfloat16)
            rows = slice(group * tile, (group + 1) * tile)
            grad_t_ref[rows, :token_rows] = grad_t
            grad_t_ref[rows, token_rows:] = grad_t

    scale = 1.0 / math.sqrt(block_len)
    for start in range(0, width, block_len):
        cols = slice(start, start + block_len)
        signed = tok_ref[:, cols] * sign_ref[:, cols]
        turned = jnp.dot(signed, mat_ref[...], preferred_element_type=jnp.float32) * scale
        upper = turned.astype(jnp.bfloat16)
        turned_ref[:token_rows, cols] = upper
        turned_ref[token_rows:, cols] = (turned - upper.astype(jnp.float32)).astype(jnp.bfloat16)
    terms = jnp.dot(grad_t_ref[...], turned_ref[...], preferred_element_type=jnp.float32)
    for group in range(groups):
        rows = slice(group * tile, (group + 1) * tile)
        limit = bound_ref[pl.ds(2 * group + core, 1), :]
        coded = jnp.clip(terms[rows, :], -limit, limit).astype(jnp.bfloat16)
        if not added:
            out_ref[rows, :] = coded
            continue
        total = (coded.astype(jnp.float32) + own_ref[rows, :].astype(jnp.float32)).astype(
            jnp.bfloat16
        )
        part = out_ref.shape[2]
        for spot in range(tile // part):
            first = jnp.where(core == 0, spot, group)
            second = jnp.where(core == 0, group, spot)
            out_ref[first, second] = total[spot * part : (spot + 1) * part]


def coded_gradient(core, tokens, out_grad, signs, bounds, matrix, order, own=None, count=1):
    token_rows, model_width = tokens.shape
    feature_rows = out_grad.shape[1]
    tile = order.shape[0]
    groups = feature_rows // tile // 2
    width = 512
    added = own is not None
    if added:
        part = tile // count
        out_shape = (count, groups, part, model_width)
        out_spec = pl.BlockSpec((count, groups, part, width), lambda n, core: (0, 0, 0, n))
    else:
        out_shape = (groups * tile, model_width)
        out_spec = pl.BlockSpec((groups * tile, width), lambda n, core: (0, n))
    whole = lambda n, core: (0, 0)
    column = lambda n, core: (0, n)
    grad_spec = lambda group: pl.BlockSpec(
        (token_rows, tile), lambda n, core: (0, 2 * group + core[0])
    )
    in_specs = [
        pl.BlockSpec((token_rows, width), column),
        *[grad_spec(group) for group in range(groups)],
        pl.BlockSpec((1, width), column),
        pl.BlockSpec((bounds.shape[0], width), column),
        pl.BlockSpec(matrix.shape, whole),
        pl.BlockSpec(order.shape, whole),
    ]
    operands = [tokens, *[out_grad] * groups, signs, bounds, matrix, order]
    if added:
        in_specs.append(pl.BlockSpec((groups * tile, width), column))
        operands.append(own)
    body = lambda *refs: coded_kernel(groups, added, *refs)
    return pl.pallas_call(
        body,
        grid_spec=pltpu.PrefetchScalarGridSpec(
            num_scalar_prefetch=1,
            grid=(model_width // width,),
            in_specs=in_specs,
            out_specs=out_spec,
            scratch_shapes=[
                pltpu.VMEM((2 * token_rows, width), jnp.bfloat16),
                pltpu.VMEM((groups * tile, 2 * token_rows), jnp.bfloat16),
            ],
        ),
        out_shape=jax.ShapeDtypeStruct(out_shape, jnp.bfloat16),
        compiler_params=pltpu.CompilerParams(vmem_limit_bytes=24 << 20),
    )(core, *operands)


def project_kernel(pair, core_ref, tok_ref, weight_ref, order_ref, out_ref):
    tile = order_ref.shape[0]
    core = core_ref[0]
    rows = []
    for at in range(pair):
        group = pl.program_id(0) * pair + at
        for spot in range(tile // weight_ref.shape[2]):
            first = jnp.where(core == 0, spot, group)
            second = jnp.where(core == 0, group, spot)
            rows.append(weight_ref[first, second])
    total = lax.dot_general(
        tok_ref[...],
        jnp.concatenate(rows, axis=0),
        (((1,), (1,)), ((), ())),
        preferred_element_type=jnp.float32,
    )
    rounded = total.astype(jnp.bfloat16)
    for at in range(pair):
        cols = slice(at * tile, (at + 1) * tile)
        out_ref[:, cols] = jnp.dot(
            rounded[:, cols], order_ref[...], preferred_element_type=jnp.float32
        ).astype(jnp.bfloat16)


def project(core, tokens, weights, order, groups):
    token_rows = tokens.shape[0]
    tile = order.shape[0]
    pair = 2
    body = lambda *refs: project_kernel(pair, *refs)
    return pl.pallas_call(
        body,
        grid_spec=pltpu.PrefetchScalarGridSpec(
            num_scalar_prefetch=1,
            grid=(groups // pair,),
            in_specs=[
                pl.BlockSpec(tokens.shape, lambda n, core: (0, 0)),
                pl.BlockSpec(weights.shape, lambda n, core: (0, 0, 0, 0)),
                pl.BlockSpec(order.shape, lambda n, core: (0, 0)),
            ],
            out_specs=pl.BlockSpec((token_rows, pair * tile), lambda n, core: (0, n)),
        ),
        out_shape=jax.ShapeDtypeStruct((token_rows, groups * tile), jnp.bfloat16),
        compiler_params=pltpu.CompilerParams(vmem_limit_bytes=32 << 20),
    )(core, tokens, weights, order)


def interleave_kernel(core_ref, own_ref, peer_ref, out_ref):
    tile = own_ref.shape[1]
    first = core_ref[0] == 0
    out_ref[:, :tile] = jnp.where(first, own_ref[...], peer_ref[...])
    out_ref[:, tile:] = jnp.where(first, peer_ref[...], own_ref[...])


def interleaved(core, own_part, peer_part, tile):
    rows, width = own_part.shape
    spec = pl.BlockSpec((rows, tile), lambda n, core: (0, n))
    return pl.pallas_call(
        interleave_kernel,
        grid_spec=pltpu.PrefetchScalarGridSpec(
            num_scalar_prefetch=1,
            grid=(width // tile,),
            in_specs=[spec, spec],
            out_specs=pl.BlockSpec((rows, 2 * tile), lambda n, core: (0, n)),
        ),
        out_shape=jax.ShapeDtypeStruct((rows, 2 * width), jnp.bfloat16),
    )(core, own_part, peer_part)


def swapped(value):
    return lax.ppermute(value, "c", [(0, 1), (1, 0)])


def face_groups(first):
    at = lambda y, c, x: (y * 2 + c) * 4 + x
    groups = []
    for core in (0, 1):
        for line in range(4):
            if (core == 0) == first:
                groups.append([at(line, core, spot) for spot in range(4)])
            else:
                groups.append([at(spot, core, line) for spot in range(4)])
    return groups


def exchanged(value, step):
    if step == "z":
        return lax.all_to_all(value, "z", 0, 0, tiled=True)
    return lax.all_to_all(
        value, FACE, 0, 0, tiled=True, axis_index_groups=face_groups(step == "first")
    )


def reduced(value, step):
    return jnp.sum(exchanged(value, step).astype(jnp.float32), axis=0)


def gathered(value, count, step):
    return exchanged(jnp.broadcast_to(value[None], (count, *value.shape)), step)


def shards(
    tokens,
    out_grad,
    master_weights,
    base_weights,
    adam_m,
    adam_v,
    grad_exps,
    diff_exps,
    hadamard_signs,
):
    count_y, count_z, count_x = (lax.axis_size(axis) for axis in ("y", "z", "x"))
    rows_dev, model_width = master_weights.shape
    sign_rows = (2 * hadamard_signs - 1).astype(jnp.float32)
    block_len = sign_rows.shape[1]
    matrix = hadamard(block_len)
    order = row_order(count_z, count_x, rows_dev)
    core = lax.axis_index("c")
    core_at = core.reshape(1).astype(jnp.int32)
    limits = clip_level * jnp.exp2(grad_exps[0].astype(jnp.float32))
    peer_tokens, peer_grad, peer_limits = swapped(tokens), swapped(out_grad), swapped(limits)
    signs = sign_rows.reshape(1, -1).astype(jnp.bfloat16)
    half_matrix = matrix.astype(jnp.bfloat16)
    own = coded_gradient(
        core_at, tokens, out_grad, signs, jnp.repeat(limits, block_len, axis=1), half_matrix, order
    )
    pair_sum = coded_gradient(
        core_at,
        peer_tokens,
        peer_grad,
        signs,
        jnp.repeat(peer_limits, block_len, axis=1),
        half_matrix,
        order,
        own=own,
        count=count_x,
    )
    line_sum = reduced(pair_sum, "first").astype(jnp.bfloat16)
    face_sum = reduced(line_sum, "second").astype(jnp.bfloat16)
    summed = reduced(face_sum.reshape(count_z, rows_dev, model_width), "z")
    gradient = unrotate_rows(summed, sign_rows, matrix)
    new_master, new_first, new_second = adam_update(gradient, master_weights, adam_m, adam_v)
    owner = lax.axis_index(AXES)
    base_own = lax.dynamic_slice_in_dim(base_weights, owner * rows_dev, rows_dev, 0).astype(
        jnp.float32
    )
    diff_bound = clip_level * jnp.exp2(diff_exps.astype(jnp.float32))
    diff_coded = clip_rows(new_master - base_own, diff_bound).astype(jnp.bfloat16)
    effective = (base_own + diff_coded.astype(jnp.float32)).astype(jnp.bfloat16)
    stacked = gathered(effective, count_z, "z").reshape(count_z * rows_dev, model_width)
    weights = gathered(gathered(stacked, count_y, "second"), count_x, "first")
    peer_part = swapped(project(core_at, peer_tokens, weights, order, count_y))
    own_part = project(core_at, tokens, weights, order, count_y)
    projected = interleaved(core_at, own_part, peer_part, order.shape[0])
    return (projected, new_master, new_first, new_second)


def solution(mesh):
    split = Mesh(mesh.devices.reshape(4, 2, 8, 4), AXES)
    rows = P(AXES, None)
    return jax.shard_map(
        shards,
        mesh=split,
        in_specs=(rows, rows, rows, P(), rows, rows, P(AXES, None, None), rows, P()),
        out_specs=(rows, rows, rows, rows),
        check_vma=False,
    )
```

time: 295 us -> 174 us (0.59)
  waiting for transfers between devices: 240 us -> 8.7 us
  blocking collectives: 9.09 us -> 98.6 us
  starting transfers between devices: 0.2 us -> 17.7 us
  Pallas kernels: 11.6 us -> 25.6 us
  between operations: 14.5 us -> 0.82 us
  matrix products: 8.21 us -> 0.28 us
  other arithmetic: 3.18 us -> 9.34 us
  local copies, waits for them, and re-layouts: 7.81 us -> 12.2 us
    all_to_all x0 -> x5, blocking collectives: none -> 98.6 us  [the longest x4 86.1 us: exchanged(): lax.all_to_all(value, FACE, 0, 0, tiled=True, axis_index_groups=face_grou...]
    all_gather x2 -> x0, waiting for transfers between devices: 96.7 us -> none  [shards(): effective = lax.all_gather(effective, axis, axis=0, tiled=True)]
    reduce_scatter x2 -> x0, waiting for transfers between devices: 93.4 us -> none  [shards(): coded = lax.psum_scatter(coded, axis, scatter_dimension=0, tiled=True)]
    unnamed x6 -> x0, waiting for transfers between devices: 50.1 us -> none
    pallas_call x1 -> x5, Pallas kernels: 11.6 us -> 25.6 us  [the longest x2 17.2 us: coded_gradient(): pl.pallas_call(body, grid_spec=pltpu.PrefetchScalarGridSpec(num_scalar_pr...]
    ppermute x0 -> x4, starting transfers between devices: none -> 10.7 us  [swapped(): return lax.ppermute(value, 'c', [(0, 1), (1, 0)])]
    all_gather x1 -> x0, blocking collectives: 9.09 us -> none  [shards(): effective = lax.all_gather(effective, axis, axis=0, tiled=True)]
    all_to_all x0 -> x1, waiting for transfers between devices: none -> 8.69 us  [exchanged(): return lax.all_to_all(value, 'z', 0, 0, tiled=True)]
  transfers between devices with their start and end apart: 5 -> 5, of which waited for: 5 -> 1; matrix products, arithmetic and copies ran while one was open for 0% -> 2% of each run, Pallas kernels for 0% -> 6%
where the time goes in v2:
time: 174 us; the launch traced here: 173 us
  blocking collectives  98.6 us (57%)
  Pallas kernels  25.6 us (15%)
  starting transfers between devices  17.7 us (10%)
  local copies, waits for them, and re-layouts  12.2 us (7%)
  other arithmetic  9.34 us (5%)
  waiting for transfers between devices  8.7 us (5%)
    all_to_all x4, blocking collectives, exchanged(): lax.all_to_all(value, FACE, 0, 0, tiled=True, axis_index_groups=face_grou...  86.1 us
    pallas_call x2, Pallas kernels, coded_gradient(): pl.pallas_call(body, grid_spec=pltpu.PrefetchScalarGridSpec(num_scalar_pr...  17.2 us
    all_to_all x1, blocking collectives, exchanged(): return lax.all_to_all(value, 'z', 0, 0, tiled=True)  12.5 us
    ppermute x4, starting transfers between devices, swapped(): return lax.ppermute(value, 'c', [(0, 1), (1, 0)])  10.7 us
    unnamed x18, local copies, waits for them, and re-layouts  9.33 us
    all_to_all x1, waiting for transfers between devices, exchanged(): return lax.all_to_all(value, 'z', 0, 0, tiled=True)  8.69 us
    all_to_all x1, starting transfers between devices, exchanged(): return lax.all_to_all(value, 'z', 0, 0, tiled=True)  6.96 us
    reduce_sum x3, other arithmetic, reduced(): return jnp.sum(exchanged(value, step).astype(jnp.float32), axis=0)  5.96 us
  transfers between devices with their start and end apart: 5, of which 1 were waited for; matrix products, arithmetic and copies ran while one was open for 2% of the time, Pallas kernels for 6%

profile of v2, /device:TPU:1, one launch (start us, length us, event | category | flops | bytes accessed | tf_op | source)
XLA Modules:
  0.0 173.3 jit_solution(13889023537722896247)
XLA Ops:
  0.6 3.3 %collective-permute-start = (bf16[384,4096]{1,0:T(8,128)(2,1)}, bf16[384,4096]{1,0:T(8,128)(2,1)S(1)}, u32[]{:S(2)}, u32[]{:S(2)}) collective-permute-start(bf16[384,4096]{1,0:T(8,128)(2,1)} %refs_1_.3), channel_id=1, source_target_pairs={{0,32},{32,0},{1,33},{33,1},{2,34},{34,2},{3,35},{35,3},{4,36},{36... | collective-permute-start | bytes 9437192 | tf_op jit(solution)/shard_map/ppermute | solution.py:237
  4.0 0.7 multiply_bitcast_fusion
  4.7 0.0 collective-permute-start.2
  4.7 0.5 collective-permute-start.1
  5.2 0.1 copy.22
  5.3 0.7 convert_bitcast_fusion
  6.0 0.1 fusion.9.refs_9_.refs_3_
  6.1 0.1 broadcast_bitcast_fusion.refs_7_
  6.2 0.1 fusion.11.refs_8_
  6.3 0.0 copy-start.2
  6.3 1.9 %copy-done.2 = bf16[384,4096]{1,0:T(8,128)(2,1)S(1)} copy-done((bf16[384,4096]{1,0:T(8,128)(2,1)S(1)}, bf16[384,4096]{1,0:T(8,128)(2,1)}, u32[]{:S(2)}) %copy-start.2) | copy-done | bytes 3145752
  8.2 1.1 copy-done.4
  9.3 7.9 %shard_map.120.refs_10_ = bf16[512,4096]{1,0:T(8,128)(2,1)S(1)} custom-call(s32[1]{0:T(128)} %bitcast.refs_0_.core_ref, bf16[384,4096]{1,0:T(8,128)(2,1)S(1)} %copy-done.2, bf16[384,1024]{1,0:T(8,128)(2,1)S(1)} %copy-done.4, bf16[384,1024]{1,0:T(8,128)(2,1)S(1)} %copy-done.4, bf16[384,1024]{1,0:T(8,128)(2,1)S(1)} %copy-done.4, ...), custom_call_target="tpu_custom_call" | custom-call | tf_op jit(solution)/shard_map/pallas_call | solution.py:151
  17.2 1.9 %copy-done = bf16[512,4096]{1,0:T(8,128)(2,1)} copy-done((bf16[512,4096]{1,0:T(8,128)(2,1)}, bf16[512,4096]{1,0:T(8,128)(2,1)S(1)}, u32[]{:S(2)}) %copy-start) | copy-done | bytes 4194328
  19.1 0.0 collective-permute-done.2
  19.1 0.1 copy.21
  19.2 0.1 broadcast_bitcast_fusion.1.refs_7_
  19.3 0.0 collective-permute-done.1.refs_2_.refs_3_.refs_4_.refs_5_
  19.3 0.0 collective-permute-done.refs_1_
  19.3 0.0 copy-start.1
  19.3 2.2 %copy-done.1 = bf16[512,4096]{1,0:T(8,128)(2,1)S(1)} copy-done((bf16[512,4096]{1,0:T(8,128)(2,1)S(1)}, bf16[512,4096]{1,0:T(8,128)(2,1)}, u32[]{:S(2)}) %copy-start.1) | copy-done | bytes 4194328
  21.5 9.3 %shard_map.121 = bf16[4,4,32,4096]{3,2,1,0:T(8,128)(2,1)S(1)} custom-call(s32[1]{0:T(128)} %bitcast.refs_0_.core_ref, bf16[384,4096]{1,0:T(8,128)(2,1)S(1)} %collective-permute-done.refs_1_, bf16[384,1024]{1,0:T(8,128)(2,1)} %collective-permute-done.1.refs_2_.refs_3_.refs_4_.refs_5_, ...), custom_call_target="tpu_custom_call" | custom-call | tf_op jit(solution)/shard_map/pallas_call | solution.py:151
  30.8 30.1 %all_to_all.30 = bf16[4,4,32,4096]{3,2,1,0:T(8,128)(2,1)} all-to-all(bf16[4,4,32,4096]{3,2,1,0:T(8,128)(2,1)S(1)} %shard_map.121), channel_id=1, replica_groups={{0,1,2,3},{64,65,66,67},{128,129,130,131},{192,193,194,195},{32,96,160,..., dimensions={0} | all-to-all | bytes 8388608 | tf_op jit(solution)/shard_map/all_to_all | solution.py:255
  60.9 4.2 %reduce_sum.33 = bf16[4,32,4096]{2,1,0:T(8,128)(2,1)} reduce(bf16[4,4,32,4096]{3,2,1,0:T(8,128)(2,1)} %all_to_all.30, bf16[]{:T(256)} %constant.126.clone.1), dimensions={0}, to_apply=%region_0.1 | reduce | flops 1572864 | bytes 5242882 | tf_op jit(solution)/shard_map/reduce_sum | solution.py:261
  65.1 14.3 %all_to_all.31 = bf16[4,32,4096]{2,1,0:T(8,128)(2,1)} all-to-all(bf16[4,32,4096]{2,1,0:T(8,128)(2,1)} %reduce_sum.33), channel_id=1, replica_groups={{0,64,128,192},{1,65,129,193},{2,66,130,194},{3,67,131,195},{32,33,34,3..., dimensions={0} | all-to-all | bytes 2097152 | tf_op jit(solution)/shard_map/all_to_all | solution.py:255
  79.4 1.4 reduce_sum.34
  80.9 0.8 reshape.107
  81.7 7.0 %all-to-all-start.2 = ((bf16[8,4,4096]{2,1,0:T(4,128)(2,1)}), bf16[8,4,4096]{2,1,0:T(4,128)(2,1)S(1)}, u32[]{:S(2)}, u32[]{:S(2)}) async-start(bf16[8,4,4096]{2,1,0:T(4,128)(2,1)} %reshape.107), calls=%async_computation.2 | async-start | bytes 524288 | tf_op jit(solution)/shard_map/all_to_all | solution.py:254
  88.7 0.7 broadcast_bitcast_fusion.2
  89.4 8.7 %all-to-all-done.2 = bf16[8,4,4096]{2,1,0:T(4,128)(2,1)S(1)} async-done(((bf16[8,4,4096]{2,1,0:T(4,128)(2,1)}), bf16[8,4,4096]{2,1,0:T(4,128)(2,1)S(1)}, u32[]{:S(2)}, u32[]{:S(2)}) %all-to-all-start.2) | async-done | bytes 262176 | tf_op jit(solution)/shard_map/all_to_all | solution.py:254
  98.0 0.3 convert_reduce_fusion
  98.4 0.1 reshape.108
  98.4 0.3 convolution_multiply_fusion
  98.7 1.8 %fusion.3 = (bf16[4,4096]{1,0:T(4,128)(2,1)S(1)}, f32[4,4096]{1,0:T(4,128)}, f32[4,4096]{1,0:T(4,128)}, f32[4,4096]{1,0:T(4,128)}) fusion(bf16[1,4,32,128]{3,2,1,0:T(8,128)(2,1)S(1)} %get-tuple-element.12, bf16[1,4,32,128]{3,2,1,0:T(8,128)(2,1)} %get-tuple-element.13, bf16[1024,4096]{1,0:T(8,128)(2,1)} %param.12, s32[]{:T(128)S(6)} %select_n.72, ...), kind=kLoop, calls=%fused_computation.11 | loop fusion | flops 409600 | bytes 606212 | tf_op jit(solution)/shard_map/convert_element_type | solution.py:316
  100.5 0.1 broadcast_in_dim.14
  100.6 12.5 %all_to_all.32 = bf16[8,4,4096]{2,1,0:T(4,128)(2,1)} all-to-all(bf16[8,4,4096]{2,1,0:T(4,128)(2,1)S(1)} %broadcast_in_dim.14), channel_id=1, replica_groups=mesh['y'=4,'c'=2,'z'=8,'x'=4] {'z'}, dimensions={0} | all-to-all | bytes 524288 | tf_op jit(solution)/shard_map/all_to_all | solution.py:254
  113.1 1.0 broadcast_in_dim.15
  114.1 0.1 broadcast_in_dim.16
  114.2 12.2 %all_to_all.33 = bf16[4,32,4096]{2,1,0:T(8,128)(2,1)S(1)} all-to-all(bf16[4,32,4096]{2,1,0:T(8,128)(2,1)S(1)} %broadcast_in_dim.16), channel_id=1, replica_groups={{0,64,128,192},{1,65,129,193},{2,66,130,194},{3,67,131,195},{32,33,34,3..., dimensions={0} | all-to-all | bytes 2097152 | tf_op jit(solution)/shard_map/all_to_all | solution.py:255
  126.4 0.5 broadcast_in_dim.17
  126.9 29.5 %all_to_all.34.refs_2_ = bf16[4,4,32,4096]{3,2,1,0:T(8,128)(2,1)S(1)} all-to-all(bf16[4,4,32,4096]{3,2,1,0:T(8,128)(2,1)S(1)} %broadcast_in_dim.17), channel_id=1, replica_groups={{0,1,2,3},{64,65,66,67},{128,129,130,131},{192,193,194,195},{32,96,160,..., dimensions={0} | all-to-all | bytes 8388608 | tf_op jit(solution)/shard_map/all_to_all | solution.py:255
  156.5 2.6 %shard_map.123 = bf16[384,512]{1,0:T(8,128)(2,1)S(1)} custom-call(s32[1]{0:T(128)} %bitcast.refs_0_.core_ref, bf16[384,4096]{1,0:T(8,128)(2,1)S(1)} %collective-permute-done.refs_1_, bf16[4,4,32,4096]{3,2,1,0:T(8,128)(2,1)S(1)} %all_to_all.34.refs_2_, bf16[128,128]{1,0:T(8,128)(2,1)S(1)} %fusion.9.refs_9_.refs_3_), custom_call_target="tpu_custom_call" | custom-call | tf_op jit(solution)/shard_map/pallas_call | solution.py:197
  159.0 6.9 %collective-permute-start.3 = (bf16[384,512]{1,0:T(8,128)(2,1)S(1)}, bf16[384,512]{1,0:T(8,128)(2,1)S(1)}, u32[]{:S(2)}, u32[]{:S(2)}) collective-permute-start(bf16[384,512]{1,0:T(8,128)(2,1)S(1)} %shard_map.123), channel_id=1, source_target_pairs={{0,32},{32,0},{1,33},{33,1},{2,34},{34,2},{3,35},{35,3},{4,36},{36... | collective-permute-start | bytes 1179656 | tf_op jit(solution)/shard_map/ppermute | solution.py:237
  165.9 2.6 %shard_map.122.own_ref = bf16[384,512]{1,0:T(8,128)(2,1)S(1)} custom-call(s32[1]{0:T(128)} %bitcast.refs_0_.core_ref, bf16[384,4096]{1,0:T(8,128)(2,1)S(1)} %copy-done.3, bf16[4,4,32,4096]{3,2,1,0:T(8,128)(2,1)S(1)} %all_to_all.34.refs_2_, bf16[128,128]{1,0:T(8,128)(2,1)S(1)} %fusion.9.refs_9_.refs_3_), custom_call_target="tpu_custom_call" | custom-call | tf_op jit(solution)/shard_map/pallas_call | solution.py:197
  168.5 0.7 copy-done.5
  169.2 0.0 collective-permute-done.3.peer_ref
  169.2 0.7 copy-done.6
  170.0 3.3 %shard_map.124 = bf16[384,1024]{1,0:T(8,128)(2,1)} custom-call(s32[1]{0:T(128)} %bitcast.refs_0_.core_ref, bf16[384,512]{1,0:T(8,128)(2,1)} %copy-done.5, bf16[384,512]{1,0:T(8,128)(2,1)} %copy-done.6), custom_call_target="tpu_custom_call" | custom-call | tf_op jit(solution)/shard_map/pallas_call | solution.py:224
  (12 shorter events, 0.1 us)
Async XLA Ops:
  0.6 18.7 %collective-permute-start = (bf16[384,4096]{1,0:T(8,128)(2,1)}, bf16[384,4096]{1,0:T(8,128)(2,1)S(1)}, u32[]{:S(2)}, u32[]{:S(2)}) collective-permute-start(bf16[384,4096]{1,0:T(8,128)(2,1)} %refs_1_.3), channel_id=1, source_target_pairs={{0,32},{32,0},{1,33},{33,1},{2,34},{34,2},{3,35},{35,3},{4,36},{36... | collective-permute-start | bytes 9437192 | tf_op jit(solution)/shard_map/ppermute | solution.py:237
  4.7 14.5 %collective-permute-start.2 = (f32[8,32]{1,0:T(8,128)S(1)}, f32[8,32]{1,0:T(8,128)S(1)}, u32[]{:S(2)}, u32[]{:S(2)}) collective-permute-start(f32[8,32]{1,0:T(8,128)S(1)} %multiply_bitcast_fusion), channel_id=1, source_target_pairs={{0,32},{32,0},{1,33},{33,1},{2,34},{34,2},{3,35},{35,3},{4,36},{36... | collective-permute-start | bytes 3080 | tf_op jit(solution)/shard_map/ppermute | solution.py:237
  4.7 14.6 %collective-permute-start.1 = (bf16[384,1024]{1,0:T(8,128)(2,1)}, bf16[384,1024]{1,0:T(8,128)(2,1)}, u32[]{:S(2)}, u32[]{:S(2)}) collective-permute-start(bf16[384,1024]{1,0:T(8,128)(2,1)} %refs_5_.1), channel_id=1, source_target_pairs={{0,32},{32,0},{1,33},{33,1},{2,34},{34,2},{3,35},{35,3},{4,36},{36... | collective-permute-start | bytes 2359304 | tf_op jit(solution)/shard_map/ppermute | solution.py:237
  6.3 1.9 %copy-start.2 = (bf16[384,4096]{1,0:T(8,128)(2,1)S(1)}, bf16[384,4096]{1,0:T(8,128)(2,1)}, u32[]{:S(2)}) copy-start(bf16[384,4096]{1,0:T(8,128)(2,1)} %refs_1_.3) | copy-start | bytes 9437188
  8.2 1.1 copy-start.4
  17.2 1.9 %copy-start = (bf16[512,4096]{1,0:T(8,128)(2,1)}, bf16[512,4096]{1,0:T(8,128)(2,1)S(1)}, u32[]{:S(2)}) copy-start(bf16[512,4096]{1,0:T(8,128)(2,1)S(1)} %shard_map.120.refs_10_) | copy-start | bytes 12582916
  19.3 2.2 %copy-start.1 = (bf16[512,4096]{1,0:T(8,128)(2,1)S(1)}, bf16[512,4096]{1,0:T(8,128)(2,1)}, u32[]{:S(2)}) copy-start(bf16[512,4096]{1,0:T(8,128)(2,1)} %copy-done) | copy-start | bytes 12582916
  60.9 27.8 %copy-start.7 = (s32[4,32]{1,0:T(4,128)S(1)}, s32[4,32]{1,0:T(4,128)}, u32[]{:S(2)}) copy-start(s32[4,32]{1,0:T(4,128)} %param.16) | copy-start | bytes 1540
  81.7 16.4 %all-to-all-start.2 = ((bf16[8,4,4096]{2,1,0:T(4,128)(2,1)}), bf16[8,4,4096]{2,1,0:T(4,128)(2,1)S(1)}, u32[]{:S(2)}, u32[]{:S(2)}) async-start(bf16[8,4,4096]{2,1,0:T(4,128)(2,1)} %reshape.107), calls=%async_computation.2 | async-start | bytes 524288 | tf_op jit(solution)/shard_map/all_to_all | solution.py:254
  156.5 9.5 %copy-start.3 = (bf16[384,4096]{1,0:T(8,128)(2,1)S(1)}, bf16[384,4096]{1,0:T(8,128)(2,1)}, u32[]{:S(2)}) copy-start(bf16[384,4096]{1,0:T(8,128)(2,1)} %refs_1_.3) | copy-start | bytes 9437188
  159.0 10.2 %collective-permute-start.3 = (bf16[384,512]{1,0:T(8,128)(2,1)S(1)}, bf16[384,512]{1,0:T(8,128)(2,1)S(1)}, u32[]{:S(2)}, u32[]{:S(2)}) collective-permute-start(bf16[384,512]{1,0:T(8,128)(2,1)S(1)} %shard_map.123), channel_id=1, source_target_pairs={{0,32},{32,0},{1,33},{33,1},{2,34},{34,2},{3,35},{35,3},{4,36},{36... | collective-permute-start | bytes 1179656 | tf_op jit(solution)/shard_map/ppermute | solution.py:237
  168.5 0.7 copy-start.5
  169.2 0.7 copy-start.6

commit v3 on v2

--- a/solution.py
+++ b/solution.py
@@ -2,6 +2,7 @@
 
 import jax
 import jax.numpy as jnp
+import numpy as np
 from jax import lax
 from jax.experimental import pallas as pl
 from jax.experimental.pallas import tpu as pltpu
@@ -22,12 +23,12 @@
 
 
 def hadamard(matrix_size):
-    positions = jnp.arange(matrix_size, dtype=jnp.int32)
+    positions = np.arange(matrix_size)
     common = positions[:, None] & positions[None, :]
-    parity = jnp.zeros((matrix_size, matrix_size), jnp.int32)
+    parity = np.zeros((matrix_size, matrix_size), np.int32)
     for bit_level in range(matrix_size.bit_length() - 1):
         parity = parity + (common >> bit_level & 1)
-    return (1 - 2 * (parity % 2)).astype(jnp.float32)
+    return (1 - 2 * (parity % 2)).astype(np.float32)
 
 
 def unrotate_rows(row_block, sign_rows, matrix):
@@ -59,23 +60,24 @@
 
 def row_order(count_z, count_x, rows_dev):
     size = count_z * count_x * rows_dev
-    spots = jnp.arange(size, dtype=jnp.int32)
+    spots = np.arange(size)
     at_x, at_z, at_j = spots // (count_z * rows_dev), spots // rows_dev % count_z, spots % rows_dev
     natural = (at_z * count_x + at_x) * rows_dev + at_j
-    return (natural[:, None] == spots[None, :]).astype(jnp.bfloat16)
+    return (natural[:, None] == spots[None, :]).astype(np.float32)
 
 
 def coded_kernel(groups, added, core_ref, tok_ref, *refs):
     grad_refs = refs[:groups]
-    sign_ref, bound_ref, mat_ref, order_ref = refs[groups : groups + 4]
+    sign_ref, exps_ref, mat_ref, order_ref = refs[groups : groups + 4]
     if added:
-        own_ref, out_ref, turned_ref, grad_t_ref = refs[groups + 4 :]
+        own_ref, out_ref, turned_ref, grad_t_ref, limit_ref = refs[groups + 4 :]
     else:
-        out_ref, turned_ref, grad_t_ref = refs[groups + 4 :]
+        out_ref, turned_ref, grad_t_ref, limit_ref = refs[groups + 4 :]
     token_rows, width = tok_ref.shape
     block_len = mat_ref.shape[0]
     tile = order_ref.shape[0]
     core = core_ref[0]
+    first_block = pl.program_id(0) * (width // block_len)
 
     @pl.when(pl.program_id(0) == 0)
     def _():
@@ -90,10 +92,20 @@
             grad_t_ref[rows, :token_rows] = grad_t
             grad_t_ref[rows, token_rows:] = grad_t
 
+    levels = (clip_level * jnp.exp2(exps_ref[...].astype(jnp.float32))).astype(jnp.bfloat16)
+    spread_shape = (exps_ref.shape[1], width)
+    block_at = lax.broadcasted_iota(jnp.int32, spread_shape, 0) - first_block
+    lane_at = lax.broadcasted_iota(jnp.int32, spread_shape, 1)
+    start_at = block_at * block_len
+    inside = (lane_at >= start_at) & (lane_at < start_at + block_len)
+    spread = jnp.where(inside, 1.0, 0.0).astype(jnp.bfloat16)
+    limit_ref[...] = jnp.dot(levels, spread, preferred_element_type=jnp.float32)
+
     scale = 1.0 / math.sqrt(block_len)
-    for start in range(0, width, block_len):
-        cols = slice(start, start + block_len)
-        signed = tok_ref[:, cols] * sign_ref[:, cols]
+    for block in range(width // block_len):
+        cols = slice(block * block_len, (block + 1) * block_len)
+        signs = 2 * sign_ref[pl.ds(first_block + block, 1), :] - 1
+        signed = tok_ref[:, cols] * signs.astype(jnp.float32).astype(jnp.bfloat16)
         turned = jnp.dot(signed, mat_ref[...], preferred_element_type=jnp.float32) * scale
         upper = turned.astype(jnp.bfloat16)
         turned_ref[:token_rows, cols] = upper
@@ -101,7 +113,7 @@
     terms = jnp.dot(grad_t_ref[...], turned_ref[...], preferred_element_type=jnp.float32)
     for group in range(groups):
         rows = slice(group * tile, (group + 1) * tile)
-        limit = bound_ref[pl.ds(2 * group + core, 1), :]
+        limit = limit_ref[pl.ds(2 * group + core, 1), :]
         coded = jnp.clip(terms[rows, :], -limit, limit).astype(jnp.bfloat16)
         if not added:
             out_ref[rows, :] = coded
@@ -116,12 +128,12 @@
             out_ref[first, second] = total[spot * part : (spot + 1) * part]
 
 
-def coded_gradient(core, tokens, out_grad, signs, bounds, matrix, order, own=None, count=1):
+def coded_gradient(core, tokens, out_grad, signs, exps, matrix, order, own=None, count=1):
     token_rows, model_width = tokens.shape
     feature_rows = out_grad.shape[1]
     tile = order.shape[0]
     groups = feature_rows // tile // 2
-    width = 512
+    width = 1024
     added = own is not None
     if added:
         part = tile // count
@@ -138,12 +150,12 @@
     in_specs = [
         pl.BlockSpec((token_rows, width), column),
         *[grad_spec(group) for group in range(groups)],
-        pl.BlockSpec((1, width), column),
-        pl.BlockSpec((bounds.shape[0], width), column),
+        pl.BlockSpec(signs.shape, whole),
+        pl.BlockSpec(exps.shape, whole),
         pl.BlockSpec(matrix.shape, whole),
         pl.BlockSpec(order.shape, whole),
     ]
-    operands = [tokens, *[out_grad] * groups, signs, bounds, matrix, order]
+    operands = [tokens, *[out_grad] * groups, signs, exps, matrix, order]
     if added:
         in_specs.append(pl.BlockSpec((groups * tile, width), column))
         operands.append(own)
@@ -158,11 +170,32 @@
             scratch_shapes=[
                 pltpu.VMEM((2 * token_rows, width), jnp.bfloat16),
                 pltpu.VMEM((groups * tile, 2 * token_rows), jnp.bfloat16),
+                pltpu.VMEM((exps.shape[0], width), jnp.float32),
             ],
         ),
         out_shape=jax.ShapeDtypeStruct(out_shape, jnp.bfloat16),
-        compiler_params=pltpu.CompilerParams(vmem_limit_bytes=24 << 20),
+        compiler_params=pltpu.CompilerParams(vmem_limit_bytes=(44 if added else 60) << 20),
     )(core, *operands)
+
+
+def sum_kernel(parts_ref, out_ref):
+    total = parts_ref[0].astype(jnp.float32)
+    for at in range(1, parts_ref.shape[0]):
+        total = total + parts_ref[at].astype(jnp.float32)
+    out_ref[...] = total.astype(jnp.bfloat16)
+
+
+def summed_parts(parts):
+    count, groups, part, model_width = parts.shape
+    width = 1024
+    return pl.pallas_call(
+        sum_kernel,
+        grid=(model_width // width,),
+        in_specs=[pl.BlockSpec((count, groups, part, width), lambda n: (0, 0, 0, n))],
+        out_specs=pl.BlockSpec((groups, part, width), lambda n: (0, 0, n)),
+        out_shape=jax.ShapeDtypeStruct((groups, part, model_width), jnp.bfloat16),
+        compiler_params=pltpu.CompilerParams(vmem_limit_bytes=16 << 20),
+    )(parts)
 
 
 def project_kernel(pair, core_ref, tok_ref, weight_ref, order_ref, out_ref):
@@ -212,24 +245,25 @@
 
 
 def interleave_kernel(core_ref, own_ref, peer_ref, out_ref):
-    tile = own_ref.shape[1]
+    tile = 128
     first = core_ref[0] == 0
-    out_ref[:, :tile] = jnp.where(first, own_ref[...], peer_ref[...])
-    out_ref[:, tile:] = jnp.where(first, peer_ref[...], own_ref[...])
-
-
-def interleaved(core, own_part, peer_part, tile):
+    for group in range(own_ref.shape[1] // tile):
+        cols = slice(group * tile, (group + 1) * tile)
+        own, peer = own_ref[:, cols], peer_ref[:, cols]
+        start = 2 * group * tile
+        out_ref[:, start : start + tile] = jnp.where(first, own, peer)
+        out_ref[:, start + tile : start + 2 * tile] = jnp.where(first, peer, own)
+
+
+def interleaved(core, own_part, peer_part):
     rows, width = own_part.shape
-    spec = pl.BlockSpec((rows, tile), lambda n, core: (0, n))
+    whole = pl.BlockSpec(memory_space=pltpu.VMEM)
     return pl.pallas_call(
         interleave_kernel,
-        grid_spec=pltpu.PrefetchScalarGridSpec(
-            num_scalar_prefetch=1,
-            grid=(width // tile,),
-            in_specs=[spec, spec],
-            out_specs=pl.BlockSpec((rows, 2 * tile), lambda n, core: (0, n)),
-        ),
+        in_specs=[pl.BlockSpec(memory_space=pltpu.SMEM), whole, whole],
+        out_specs=whole,
         out_shape=jax.ShapeDtypeStruct((rows, 2 * width), jnp.bfloat16),
+        compiler_params=pltpu.CompilerParams(vmem_limit_bytes=8 << 20),
     )(core, own_part, peer_part)
 
 
@@ -280,29 +314,26 @@
     rows_dev, model_width = master_weights.shape
     sign_rows = (2 * hadamard_signs - 1).astype(jnp.float32)
     block_len = sign_rows.shape[1]
-    matrix = hadamard(block_len)
-    order = row_order(count_z, count_x, rows_dev)
+    matrix = jnp.asarray(hadamard(block_len))
+    order = jnp.asarray(row_order(count_z, count_x, rows_dev))
     core = lax.axis_index("c")
     core_at = core.reshape(1).astype(jnp.int32)
-    limits = clip_level * jnp.exp2(grad_exps[0].astype(jnp.float32))
-    peer_tokens, peer_grad, peer_limits = swapped(tokens), swapped(out_grad), swapped(limits)
-    signs = sign_rows.reshape(1, -1).astype(jnp.bfloat16)
-    half_matrix = matrix.astype(jnp.bfloat16)
-    own = coded_gradient(
-        core_at, tokens, out_grad, signs, jnp.repeat(limits, block_len, axis=1), half_matrix, order
-    )
+    exps = grad_exps[0]
+    peer_tokens, peer_grad, peer_exps = swapped(tokens), swapped(out_grad), swapped(exps)
+    half_matrix, order = matrix.astype(jnp.bfloat16), order.astype(jnp.bfloat16)
+    own = coded_gradient(core_at, tokens, out_grad, hadamard_signs, exps, half_matrix, order)
     pair_sum = coded_gradient(
         core_at,
         peer_tokens,
         peer_grad,
-        signs,
-        jnp.repeat(peer_limits, block_len, axis=1),
+        hadamard_signs,
+        peer_exps,
         half_matrix,
         order,
         own=own,
         count=count_x,
     )
-    line_sum = reduced(pair_sum, "first").astype(jnp.bfloat16)
+    line_sum = summed_parts(exchanged(pair_sum, "first"))
     face_sum = reduced(line_sum, "second").astype(jnp.bfloat16)
     summed = reduced(face_sum.reshape(count_z, rows_dev, model_width), "z")
     gradient = unrotate_rows(summed, sign_rows, matrix)
@@ -318,7 +349,7 @@
     weights = gathered(gathered(stacked, count_y, "second"), count_x, "first")
     peer_part = swapped(project(core_at, peer_tokens, weights, order, count_y))
     own_part = project(core_at, tokens, weights, order, count_y)
-    projected = interleaved(core_at, own_part, peer_part, order.shape[0])
+    projected = interleaved(core_at, own_part, peer_part)
     return (projected, new_master, new_first, new_second)
 
 

time: 174 us -> 158 us (0.908)
  local copies, waits for them, and re-layouts: 12.2 us -> 3.27 us
  other arithmetic: 9.34 us -> 4.16 us
  blocking collectives: 98.6 us -> 96.5 us
  Pallas kernels: 25.6 us -> 23.7 us
  starting transfers between devices: 17.7 us -> 19.5 us
    unnamed x18 -> x11, local copies, waits for them, and re-layouts: 9.33 us -> 0.71 us
    reduce_sum x3 -> x2, other arithmetic: 5.96 us -> 1.74 us  [reduced(): return jnp.sum(exchanged(value, step).astype(jnp.float32), axis=0)]
    all_to_all x4, blocking collectives: 86.1 us -> 84.1 us  [exchanged(): lax.all_to_all(value, FACE, 0, 0, tiled=True, axis_index_groups=face_grou...]
  transfers between devices with their start and end apart: 5 -> 5, of which waited for: 1 -> 1; matrix products, arithmetic and copies ran while one was open for 2% -> 1% of each run, Pallas kernels for 6% -> 7%
where the time goes in v3:
time: 158 us; the launch traced here: 157 us
  blocking collectives  96.5 us (61%)
  Pallas kernels  23.7 us (15%)
  starting transfers between devices  19.5 us (12%)
  waiting for transfers between devices  8.07 us (5%)
  other arithmetic  4.16 us (3%)
  local copies, waits for them, and re-layouts  3.27 us (2%)
    all_to_all x4, blocking collectives, exchanged(): lax.all_to_all(value, FACE, 0, 0, tiled=True, axis_index_groups=face_grou...  84.1 us
    pallas_call x2, Pallas kernels, coded_gradient(): pl.pallas_call(body, grid_spec=pltpu.PrefetchScalarGridSpec(num_scalar_pr...  16.6 us
    all_to_all x1, blocking collectives, exchanged(): return lax.all_to_all(value, 'z', 0, 0, tiled=True)  12.4 us
    ppermute x4, starting transfers between devices, swapped(): return lax.ppermute(value, 'c', [(0, 1), (1, 0)])  11.3 us
    all_to_all x1, starting transfers between devices, exchanged(): return lax.all_to_all(value, 'z', 0, 0, tiled=True)  8.19 us
    all_to_all x1, waiting for transfers between devices, exchanged(): return lax.all_to_all(value, 'z', 0, 0, tiled=True)  8.06 us
    pallas_call x2, Pallas kernels, project(): pl.pallas_call(body, grid_spec=pltpu.PrefetchScalarGridSpec(num_scalar_pr...  5.16 us
  transfers between devices with their start and end apart: 5, of which 1 were waited for; matrix products, arithmetic and copies ran while one was open for 1% of the time, Pallas kernels for 7%

profile of v3, /device:TPU:1, one launch (start us, length us, event | category | flops | bytes accessed | tf_op | source)
XLA Modules:
  0.0 157.0 jit_solution(8085519188581054834)
XLA Ops:
  0.6 3.3 %collective-permute-start = (bf16[384,4096]{1,0:T(8,128)(2,1)}, bf16[384,4096]{1,0:T(8,128)(2,1)S(1)}, u32[]{:S(2)}, u32[]{:S(2)}) collective-permute-start(bf16[384,4096]{1,0:T(8,128)(2,1)} %refs_1_.3), channel_id=1, source_target_pairs={{0,32},{32,0},{1,33},{33,1},{2,34},{34,2},{3,35},{35,3},{4,36},{36... | collective-permute-start | bytes 9437192 | tf_op jit(solution)/shard_map/ppermute | solution.py:271
  4.0 0.1 collective-permute-start.1
  4.1 0.4 collective-permute-start.2
  4.5 0.0 copy-start.1
  4.5 0.0 copy-start.2
  4.5 0.0 copy-start.3
  4.5 8.5 %shard_map.138.refs_10_ = bf16[512,4096]{1,0:T(8,128)(2,1)} custom-call(s32[1]{0:T(128)} %bitcast.refs_0_.core_ref, bf16[384,4096]{1,0:T(8,128)(2,1)} %refs_1_.3, bf16[384,1024]{1,0:T(8,128)(2,1)} %refs_5_.1, bf16[384,1024]{1,0:T(8,128)(2,1)} %refs_5_.1, bf16[384,1024]{1,0:T(8,128)(2,1)} %refs_5_.1, bf16[384,1024]{1,0:T(8,128)(2,1)} %refs_5_.1, ...), custom_call_target="tpu_custom_call" | custom-call | tf_op jit(solution)/shard_map/pallas_call | solution.py:163
  13.0 0.0 collective-permute-done.2.refs_7_
  13.0 0.0 collective-permute-done.1.refs_2_.refs_3_.refs_4_.refs_5_
  13.0 0.0 collective-permute-done.refs_1_
  13.0 0.0 copy-done.1
  13.0 0.0 copy-done.2
  13.0 0.0 copy-done.3
  13.0 8.1 %shard_map.139 = bf16[4,4,32,4096]{3,2,1,0:T(8,128)(2,1)S(1)} custom-call(s32[1]{0:T(128)} %bitcast.refs_0_.core_ref, bf16[384,4096]{1,0:T(8,128)(2,1)S(1)} %collective-permute-done.refs_1_, bf16[384,1024]{1,0:T(8,128)(2,1)} %collective-permute-done.1.refs_2_.refs_3_.refs_4_.refs_5_, ...), custom_call_target="tpu_custom_call" | custom-call | tf_op jit(solution)/shard_map/pallas_call | solution.py:163
  21.1 29.3 %all_to_all.30.parts_ref = bf16[4,4,32,4096]{3,2,1,0:T(8,128)(2,1)S(1)} all-to-all(bf16[4,4,32,4096]{3,2,1,0:T(8,128)(2,1)S(1)} %shard_map.139), channel_id=1, replica_groups={{0,1,2,3},{64,65,66,67},{128,129,130,131},{192,193,194,195},{32,96,160,..., dimensions={0} | all-to-all | bytes 8388608 | tf_op jit(solution)/shard_map/all_to_all | solution.py:289
  50.4 0.0 copy-start.4
  50.4 0.9 shard_map.140
  51.3 13.5 %all_to_all.31 = bf16[4,32,4096]{2,1,0:T(8,128)(2,1)} all-to-all(bf16[4,32,4096]{2,1,0:T(8,128)(2,1)S(1)} %shard_map.140), channel_id=1, replica_groups={{0,64,128,192},{1,65,129,193},{2,66,130,194},{3,67,131,195},{32,33,34,3..., dimensions={0} | all-to-all | bytes 2097152 | tf_op jit(solution)/shard_map/all_to_all | solution.py:289
  64.8 1.4 reduce_sum.21
  66.2 0.8 reshape.36
  67.0 8.2 %all-to-all-start.2 = ((bf16[8,4,4096]{2,1,0:T(4,128)(2,1)}), bf16[8,4,4096]{2,1,0:T(4,128)(2,1)S(1)}, u32[]{:S(2)}, u32[]{:S(2)}) async-start(bf16[8,4,4096]{2,1,0:T(4,128)(2,1)} %reshape.36), calls=%async_computation.2 | async-start | bytes 524288 | tf_op jit(solution)/shard_map/all_to_all | solution.py:288
  75.2 0.0 copy-done.4
  75.3 0.6 convert_bitcast_fusion
  75.9 0.7 broadcast_bitcast_fusion
  76.6 8.1 %all-to-all-done.2 = bf16[8,4,4096]{2,1,0:T(4,128)(2,1)S(1)} async-done(((bf16[8,4,4096]{2,1,0:T(4,128)(2,1)}), bf16[8,4,4096]{2,1,0:T(4,128)(2,1)S(1)}, u32[]{:S(2)}, u32[]{:S(2)}) %all-to-all-start.2) | async-done | bytes 262176 | tf_op jit(solution)/shard_map/all_to_all | solution.py:288
  84.6 0.3 convert_reduce_fusion
  85.0 0.1 reshape.37
  85.0 1.0 convolution_multiply_fusion
  86.1 1.8 %fusion.3 = (bf16[4,4096]{1,0:T(4,128)(2,1)S(1)}, f32[4,4096]{1,0:T(4,128)}, f32[4,4096]{1,0:T(4,128)}, f32[4,4096]{1,0:T(4,128)}) fusion(bf16[1,4,32,128]{3,2,1,0:T(8,128)(2,1)S(1)} %get-tuple-element.10, bf16[1,4,32,128]{3,2,1,0:T(8,128)(2,1)} %get-tuple-element.11, bf16[1024,4096]{1,0:T(8,128)(2,1)} %param.14, s32[]{:T(128)S(6)} %select_n.3, ...), kind=kLoop, calls=%fused_computation.8 | loop fusion | flops 409600 | bytes 606212 | tf_op jit(solution)/shard_map/convert_element_type | solution.py:347
  87.9 0.1 broadcast_in_dim.8
  88.0 12.4 %all_to_all.32 = bf16[8,4,4096]{2,1,0:T(4,128)(2,1)} all-to-all(bf16[8,4,4096]{2,1,0:T(4,128)(2,1)S(1)} %broadcast_in_dim.8), channel_id=1, replica_groups=mesh['y'=4,'c'=2,'z'=8,'x'=4] {'z'}, dimensions={0} | all-to-all | bytes 524288 | tf_op jit(solution)/shard_map/all_to_all | solution.py:288
  100.4 1.0 broadcast_in_dim.9
  101.4 0.1 broadcast_in_dim.10
  101.5 12.2 %all_to_all.33 = bf16[4,32,4096]{2,1,0:T(8,128)(2,1)S(1)} all-to-all(bf16[4,32,4096]{2,1,0:T(8,128)(2,1)S(1)} %broadcast_in_dim.10), channel_id=1, replica_groups={{0,64,128,192},{1,65,129,193},{2,66,130,194},{3,67,131,195},{32,33,34,3..., dimensions={0} | all-to-all | bytes 2097152 | tf_op jit(solution)/shard_map/all_to_all | solution.py:289
  113.7 0.5 broadcast_in_dim.11
  114.2 29.2 %all_to_all.34.refs_2_ = bf16[4,4,32,4096]{3,2,1,0:T(8,128)(2,1)S(1)} all-to-all(bf16[4,4,32,4096]{3,2,1,0:T(8,128)(2,1)S(1)} %broadcast_in_dim.11), channel_id=1, replica_groups={{0,1,2,3},{64,65,66,67},{128,129,130,131},{192,193,194,195},{32,96,160,..., dimensions={0} | all-to-all | bytes 8388608 | tf_op jit(solution)/shard_map/all_to_all | solution.py:289
  143.3 0.0 copy-start
  143.3 2.6 %shard_map.142 = bf16[384,512]{1,0:T(8,128)(2,1)S(1)} custom-call(s32[1]{0:T(128)} %bitcast.refs_0_.core_ref, bf16[384,4096]{1,0:T(8,128)(2,1)S(1)} %collective-permute-done.refs_1_, bf16[4,4,32,4096]{3,2,1,0:T(8,128)(2,1)S(1)} %all_to_all.34.refs_2_, bf16[128,128]{1,0:T(8,128)(2,1)S(1)} %copy-done.1), custom_call_target="tpu_custom_call" | custom-call | tf_op jit(solution)/shard_map/pallas_call | solution.py:230
  145.9 7.5 %collective-permute-start.3 = (bf16[384,512]{1,0:T(8,128)(2,1)S(1)}, bf16[384,512]{1,0:T(8,128)(2,1)S(1)}, u32[]{:S(2)}, u32[]{:S(2)}) collective-permute-start(bf16[384,512]{1,0:T(8,128)(2,1)S(1)} %shard_map.142), channel_id=1, source_target_pairs={{0,32},{32,0},{1,33},{33,1},{2,34},{34,2},{3,35},{35,3},{4,36},{36... | collective-permute-start | bytes 1179656 | tf_op jit(solution)/shard_map/ppermute | solution.py:271
  153.4 0.0 copy-done
  153.4 2.6 %shard_map.141.own_ref = bf16[384,512]{1,0:T(8,128)(2,1)S(1)} custom-call(s32[1]{0:T(128)} %bitcast.refs_0_.core_ref, bf16[384,4096]{1,0:T(8,128)(2,1)S(1)} %copy-done, bf16[4,4,32,4096]{3,2,1,0:T(8,128)(2,1)S(1)} %all_to_all.34.refs_2_, bf16[128,128]{1,0:T(8,128)(2,1)S(1)} %copy-done.1), custom_call_target="tpu_custom_call" | custom-call | tf_op jit(solution)/shard_map/pallas_call | solution.py:230
  156.0 0.0 collective-permute-done.3.peer_ref
  156.0 1.0 shard_map.143
  (2 shorter events, 0.0 us)
Async XLA Ops:
  0.6 12.3 %collective-permute-start = (bf16[384,4096]{1,0:T(8,128)(2,1)}, bf16[384,4096]{1,0:T(8,128)(2,1)S(1)}, u32[]{:S(2)}, u32[]{:S(2)}) collective-permute-start(bf16[384,4096]{1,0:T(8,128)(2,1)} %refs_1_.3), channel_id=1, source_target_pairs={{0,32},{32,0},{1,33},{33,1},{2,34},{34,2},{3,35},{35,3},{4,36},{36... | collective-permute-start | bytes 9437192 | tf_op jit(solution)/shard_map/ppermute | solution.py:271
  4.0 9.0 %collective-permute-start.1 = (bf16[384,1024]{1,0:T(8,128)(2,1)}, bf16[384,1024]{1,0:T(8,128)(2,1)}, u32[]{:S(2)}, u32[]{:S(2)}) collective-permute-start(bf16[384,1024]{1,0:T(8,128)(2,1)} %refs_5_.1), channel_id=1, source_target_pairs={{0,32},{32,0},{1,33},{33,1},{2,34},{34,2},{3,35},{35,3},{4,36},{36... | collective-permute-start | bytes 2359304 | tf_op jit(solution)/shard_map/ppermute | solution.py:271
  4.1 8.9 %collective-permute-start.2 = (s32[8,32]{1,0:T(8,128)}, s32[8,32]{1,0:T(8,128)S(1)}, u32[]{:S(2)}, u32[]{:S(2)}) collective-permute-start(s32[8,32]{1,0:T(8,128)} %bitcast.18), channel_id=1, source_target_pairs={{0,32},{32,0},{1,33},{33,1},{2,34},{34,2},{3,35},{35,3},{4,36},{36... | collective-permute-start | bytes 3080 | tf_op jit(solution)/shard_map/ppermute | solution.py:271
  4.5 8.5 %copy-start.1 = (bf16[128,128]{1,0:T(8,128)(2,1)S(1)}, bf16[128,128]{1,0:T(8,128)(2,1)}, u32[]{:S(2)}) copy-start(bf16[128,128]{1,0:T(8,128)(2,1)} %constant.77.refs_9_.refs_3_) | copy-start | bytes 98308
  4.5 8.5 %copy-start.2 = (s32[32,128]{1,0:T(8,128)S(1)}, s32[32,128]{1,0:T(8,128)}, u32[]{:S(2)}) copy-start(s32[32,128]{1,0:T(8,128)} %refs_6_.3) | copy-start | bytes 49156
  4.5 8.5 %copy-start.3 = (bf16[128,128]{1,0:T(8,128)(2,1)S(1)}, bf16[128,128]{1,0:T(8,128)(2,1)}, u32[]{:S(2)}) copy-start(bf16[128,128]{1,0:T(8,128)(2,1)} %constant.76.refs_8_) | copy-start | bytes 98308
  50.4 24.9 %copy-start.4 = (s32[4,32]{1,0:T(4,128)S(1)}, s32[4,32]{1,0:T(4,128)}, u32[]{:S(2)}) copy-start(s32[4,32]{1,0:T(4,128)} %param.18) | copy-start | bytes 1540
  67.0 17.6 %all-to-all-start.2 = ((bf16[8,4,4096]{2,1,0:T(4,128)(2,1)}), bf16[8,4,4096]{2,1,0:T(4,128)(2,1)S(1)}, u32[]{:S(2)}, u32[]{:S(2)}) async-start(bf16[8,4,4096]{2,1,0:T(4,128)(2,1)} %reshape.36), calls=%async_computation.2 | async-start | bytes 524288 | tf_op jit(solution)/shard_map/all_to_all | solution.py:288
  143.3 10.1 %copy-start = (bf16[384,4096]{1,0:T(8,128)(2,1)S(1)}, bf16[384,4096]{1,0:T(8,128)(2,1)}, u32[]{:S(2)}) copy-start(bf16[384,4096]{1,0:T(8,128)(2,1)} %refs_1_.3) | copy-start | bytes 9437188
  145.9 10.1 %collective-permute-start.3 = (bf16[384,512]{1,0:T(8,128)(2,1)S(1)}, bf16[384,512]{1,0:T(8,128)(2,1)S(1)}, u32[]{:S(2)}, u32[]{:S(2)}) collective-permute-start(bf16[384,512]{1,0:T(8,128)(2,1)S(1)} %shard_map.142), channel_id=1, source_target_pairs={{0,32},{32,0},{1,33},{33,1},{2,34},{34,2},{3,35},{35,3},{4,36},{36... | collective-permute-start | bytes 1179656 | tf_op jit(solution)/shard_map/ppermute | solution.py:271

commit v4 on v3

v4 whole, which is shorter than its diff:
```python
import math

import jax
import jax.numpy as jnp
import numpy as np
from jax import lax
from jax.experimental import pallas as pl
from jax.experimental.pallas import tpu as pltpu
from jax.sharding import Mesh
from jax.sharding import PartitionSpec as P

ADAM_STEP = 10
AXES = ("y", "c", "z", "x")
FACE = ("y", "c", "x")

clip_level = 448.0
beta_one = 0.9
beta_two = 0.95
learn_rate = 0.002
decay_rate = 0.1
adam_eps = 1e-08
highest = lax.Precision.HIGHEST


def hadamard(matrix_size):
    positions = np.arange(matrix_size)
    common = positions[:, None] & positions[None, :]
    parity = np.zeros((matrix_size, matrix_size), np.int32)
    for bit_level in range(matrix_size.bit_length() - 1):
        parity = parity + (common >> bit_level & 1)
    return (1 - 2 * (parity % 2)).astype(np.float32)


def unrotate_rows(row_block, sign_rows, matrix):
    row_count = row_block.shape[0]
    turned = jnp.dot(
        row_block.reshape(-1, sign_rows.shape[1]), matrix, precision=highest
    ) / math.sqrt(sign_rows.shape[1])
    return (turned.reshape(row_count, sign_rows.shape[0], sign_rows.shape[1]) * sign_rows).reshape(
        row_block.shape
    )


def clip_rows(row_block, bound_rows):
    row_count = row_block.shape[0]
    shaped = row_block.reshape(row_count, bound_rows.shape[1], -1)
    limits = bound_rows[:, :, None]
    return jnp.clip(shaped, -limits, limits).reshape(row_block.shape)


def adam_update(gradient, master, first, second):
    new_first = beta_one * first + (1.0 - beta_one) * gradient
    new_second = beta_two * second + (1.0 - beta_two) * gradient * gradient
    fix_one = 1.0 - beta_one**ADAM_STEP
    fix_two = 1.0 - beta_two**ADAM_STEP
    step_dir = new_first / fix_one / (jnp.sqrt(new_second / fix_two) + adam_eps)
    new_master = master - learn_rate * (step_dir + decay_rate * master)
    return (new_master, new_first, new_second)


def row_order(count_z, count_x, rows_dev):
    size = count_z * count_x * rows_dev
    spots = np.arange(size)
    at_x, at_z, at_j = spots // (count_z * rows_dev), spots // rows_dev % count_z, spots % rows_dev
    natural = (at_z * count_x + at_x) * rows_dev + at_j
    return (natural[:, None] == spots[None, :]).astype(np.float32)


def coded_kernel(groups, spots, added, place_ref, tok_ref, *refs):
    grad_refs = refs[:groups]
    sign_ref, exps_ref, mat_ref, order_ref = refs[groups : groups + 4]
    refs = refs[groups + 4 :]
    own_ref = refs[0] if added else None
    out_refs = refs[added:-3]
    turned_ref, grad_t_ref, limit_ref = refs[-3:]
    token_rows, width = tok_ref.shape
    block_len = mat_ref.shape[0]
    tile = order_ref.shape[0]
    part = tile // spots
    core, at_x, at_y = place_ref[0], place_ref[1], place_ref[2]
    first_block = pl.program_id(0) * (width // block_len)

    @pl.when(pl.program_id(0) == 0)
    def _():
        for group in range(groups):
            grad_t = lax.dot_general(
                order_ref[...],
                grad_refs[group][...],
                (((1,), (1,)), ((), ())),
                preferred_element_type=jnp.float32,
            ).astype(jnp.bfloat16)
            from_y = lax.rem(group - at_y + groups, groups)
            for spot in range(spots):
                from_x = lax.rem(spot - at_x + spots, spots)
                piece = jnp.where(core == 0, from_x * groups + from_y, from_y * spots + from_x)
                rows = pl.ds(pl.multiple_of(piece * part, part), part)
                values = grad_t[spot * part : (spot + 1) * part]
                grad_t_ref[rows, :token_rows] = values
                grad_t_ref[rows, token_rows:] = values

    levels = (clip_level * jnp.exp2(exps_ref[...].astype(jnp.float32))).astype(jnp.bfloat16)
    spread_shape = (exps_ref.shape[1], width)
    block_at = lax.broadcasted_iota(jnp.int32, spread_shape, 0) - first_block
    lane_at = lax.broadcasted_iota(jnp.int32, spread_shape, 1)
    start_at = block_at * block_len
    inside = (lane_at >= start_at) & (lane_at < start_at + block_len)
    spread = jnp.where(inside, 1.0, 0.0).astype(jnp.bfloat16)
    limit_ref[...] = jnp.dot(levels, spread, preferred_element_type=jnp.float32)

    scale = 1.0 / math.sqrt(block_len)
    for block in range(width // block_len):
        cols = slice(block * block_len, (block + 1) * block_len)
        signs = 2 * sign_ref[pl.ds(first_block + block, 1), :] - 1
        signed = tok_ref[:, cols] * signs.astype(jnp.float32).astype(jnp.bfloat16)
        turned = jnp.dot(signed, mat_ref[...], preferred_element_type=jnp.float32) * scale
        upper = turned.astype(jnp.bfloat16)
        turned_ref[:token_rows, cols] = upper
        turned_ref[token_rows:, cols] = (turned - upper.astype(jnp.float32)).astype(jnp.bfloat16)
    terms = jnp.dot(grad_t_ref[...], turned_ref[...], preferred_element_type=jnp.float32)
    for first in range(4):
        for second in range(4):
            group = lax.rem(at_y + jnp.where(core == 0, second, first), groups)
            start = (first * 4 + second) * part
            rows = slice(start, start + part)
            limit = limit_ref[pl.ds(2 * group + core, 1), :]
            coded = jnp.clip(terms[rows, :], -limit, limit).astype(jnp.bfloat16)
            if not added:
                out_refs[0][rows, :] = coded
                continue
            total = (coded.astype(jnp.float32) + own_ref[rows, :].astype(jnp.float32)).astype(
                jnp.bfloat16
            )
            if second == 0:
                out_refs[2 * first][...] = total
            else:
                out_refs[2 * first + 1][(second - 1) * part : second * part, :] = total


def coded_gradient(place, tokens, out_grad, signs, exps, matrix, order, own=None):
    token_rows, model_width = tokens.shape
    feature_rows = out_grad.shape[1]
    tile = order.shape[0]
    groups = feature_rows // tile // 2
    spots = 4
    part = tile // spots
    width = 1024
    added = own is not None
    heights = [part, tile - part] * 4 if added else [groups * tile]
    whole = lambda n, place: (0, 0)
    column = lambda n, place: (0, n)
    grad_spec = lambda group: pl.BlockSpec(
        (token_rows, tile), lambda n, place: (0, 2 * group + place[0])
    )
    in_specs = [
        pl.BlockSpec((token_rows, width), column),
        *[grad_spec(group) for group in range(groups)],
        pl.BlockSpec(signs.shape, whole),
        pl.BlockSpec(exps.shape, whole),
        pl.BlockSpec(matrix.shape, whole),
        pl.BlockSpec(order.shape, whole),
    ]
    operands = [tokens, *[out_grad] * groups, signs, exps, matrix, order]
    if added:
        in_specs.append(pl.BlockSpec((groups * tile, width), column))
        operands.append(own)
    body = lambda *refs: coded_kernel(groups, spots, added, *refs)
    return pl.pallas_call(
        body,
        grid_spec=pltpu.PrefetchScalarGridSpec(
            num_scalar_prefetch=1,
            grid=(model_width // width,),
            in_specs=in_specs,
            out_specs=[pl.BlockSpec((height, width), column) for height in heights],
            scratch_shapes=[
                pltpu.VMEM((2 * token_rows, width), jnp.bfloat16),
                pltpu.VMEM((groups * tile, 2 * token_rows), jnp.bfloat16),
                pltpu.VMEM((exps.shape[0], width), jnp.float32),
            ],
        ),
        out_shape=[jax.ShapeDtypeStruct((height, model_width), jnp.bfloat16) for height in heights],
        compiler_params=pltpu.CompilerParams(vmem_limit_bytes=(44 if added else 60) << 20),
    )(place, *operands)


def added_up(refs):
    total = refs[0][...].astype(jnp.float32)
    for ref in refs[1:]:
        total = total + ref[...].astype(jnp.float32)
    return total.astype(jnp.bfloat16)


def line_kernel(count, *refs):
    total = added_up(refs[:count])
    part = refs[count].shape[0]
    for at, out_ref in enumerate(refs[count:]):
        out_ref[...] = total[at * part : (at + 1) * part]


def line_sums(terms, outputs):
    rows, model_width = terms[0].shape
    width = 1024
    spec = lambda height: pl.BlockSpec((height, width), lambda n: (0, n))
    body = lambda *refs: line_kernel(len(terms), *refs)
    return pl.pallas_call(
        body,
        grid=(model_width // width,),
        in_specs=[spec(rows)] * len(terms),
        out_specs=[spec(rows // outputs)] * outputs,
        out_shape=[jax.ShapeDtypeStruct((rows // outputs, model_width), jnp.bfloat16)] * outputs,
        compiler_params=pltpu.CompilerParams(vmem_limit_bytes=16 << 20),
    )(*terms)


def face_kernel(*refs):
    total = added_up(refs[:-1])
    out_ref = refs[-1]
    rows = out_ref.shape[1]
    for at in range(out_ref.shape[0]):
        out_ref[at] = total[at * rows : (at + 1) * rows]


def face_sum(terms, count_z):
    rows, model_width = terms[0].shape
    width = 1024
    return pl.pallas_call(
        face_kernel,
        grid=(model_width // width,),
        in_specs=[pl.BlockSpec((rows, width), lambda n: (0, n))] * len(terms),
        out_specs=pl.BlockSpec((count_z, rows // count_z, width), lambda n: (0, 0, n)),
        out_shape=jax.ShapeDtypeStruct((count_z, rows // count_z, model_width), jnp.bfloat16),
        compiler_params=pltpu.CompilerParams(vmem_limit_bytes=16 << 20),
    )(*terms)


def product(tok_ref, weight_refs):
    weights = jnp.concatenate([ref[...] for ref in weight_refs], axis=0)
    return lax.dot_general(
        weights, tok_ref[...], (((1,), (1,)), ((), ())), preferred_element_type=jnp.float32
    ).astype(jnp.bfloat16)


def early_kernel(tok_ref, *refs):
    refs[-1][...] = product(tok_ref, refs[:-1])


def early_product(tokens, weights):
    whole = pl.BlockSpec(memory_space=pltpu.VMEM)
    rows = sum(value.shape[0] for value in weights)
    return pl.pallas_call(
        early_kernel,
        in_specs=[whole] * (1 + len(weights)),
        out_specs=whole,
        out_shape=jax.ShapeDtypeStruct((rows, tokens.shape[0]), jnp.bfloat16),
        compiler_params=pltpu.CompilerParams(vmem_limit_bytes=24 << 20),
    )(tokens, *weights)


def late_kernel(tok_ref, early_ref, spread_ref, *refs):
    late = product(tok_ref, refs[:-1])
    early_rows = early_ref.shape[0]
    down = (((0,), (0,)), ((), ()))
    out = lax.dot_general(
        early_ref[...], spread_ref[:early_rows, :], down, preferred_element_type=jnp.float32
    )
    out = out + lax.dot_general(
        late, spread_ref[early_rows:, :], down, preferred_element_type=jnp.float32
    )
    refs[-1][...] = out.astype(jnp.bfloat16)


def late_product(tokens, early, spread, weights):
    whole = pl.BlockSpec(memory_space=pltpu.VMEM)
    return pl.pallas_call(
        late_kernel,
        in_specs=[whole] * (3 + len(weights)),
        out_specs=whole,
        out_shape=jax.ShapeDtypeStruct((tokens.shape[0], spread.shape[1]), jnp.bfloat16),
        compiler_params=pltpu.CompilerParams(vmem_limit_bytes=24 << 20),
    )(tokens, early, spread, *weights)


def interleave_kernel(place_ref, own_ref, peer_ref, out_ref):
    tile = 128
    first = place_ref[0] == 0
    for group in range(own_ref.shape[1] // tile):
        cols = slice(group * tile, (group + 1) * tile)
        own, peer = own_ref[:, cols], peer_ref[:, cols]
        start = 2 * group * tile
        out_ref[:, start : start + tile] = jnp.where(first, own, peer)
        out_ref[:, start + tile : start + 2 * tile] = jnp.where(first, peer, own)


def interleaved(place, own_part, peer_part):
    rows, width = own_part.shape
    whole = pl.BlockSpec(memory_space=pltpu.VMEM)
    return pl.pallas_call(
        interleave_kernel,
        in_specs=[pl.BlockSpec(memory_space=pltpu.SMEM), whole, whole],
        out_specs=whole,
        out_shape=jax.ShapeDtypeStruct((rows, 2 * width), jnp.bfloat16),
        compiler_params=pltpu.CompilerParams(vmem_limit_bytes=8 << 20),
    )(place, own_part, peer_part)


def swapped(value):
    return lax.ppermute(value, "c", [(0, 1), (1, 0)])


def shifted(value, axis_at, shift):
    pairs = []
    for y in range(4):
        for core in range(2):
            for x in range(4):
                along_x = core == axis_at
                to_y, to_x = (y, (x + shift) % 4) if along_x else ((y + shift) % 4, x)
                pairs.append(((y * 2 + core) * 4 + x, (to_y * 2 + core) * 4 + to_x))
    return lax.ppermute(value, FACE, pairs)


def column_spread(place, offsets, count_z, rows_dev):
    core, at_x, at_y = place[0], place[1], place[2]
    first = jnp.asarray([offset[0] for offset in offsets], jnp.int32)
    second = jnp.asarray([offset[1] for offset in offsets], jnp.int32)
    from_x = (at_x - jnp.where(core == 0, first, second)) % 4
    from_y = (at_y - jnp.where(core == 0, second, first)) % 4
    at_z = jnp.arange(count_z, dtype=jnp.int32)[None, :, None]
    at_j = jnp.arange(rows_dev, dtype=jnp.int32)[None, None, :]
    column = (
        (from_y[:, None, None] * count_z + at_z) * 4 + from_x[:, None, None]
    ) * rows_dev + at_j
    size = len(offsets) * count_z * rows_dev
    return (column.reshape(size, 1) == jnp.arange(size, dtype=jnp.int32)[None, :]).astype(
        jnp.bfloat16
    )


def shards(
    tokens,
    out_grad,
    master_weights,
    base_weights,
    adam_m,
    adam_v,
    grad_exps,
    diff_exps,
    hadamard_signs,
):
    count_z = lax.axis_size("z")
    rows_dev, model_width = master_weights.shape
    sign_rows = (2 * hadamard_signs - 1).astype(jnp.float32)
    block_len = sign_rows.shape[1]
    matrix = jnp.asarray(hadamard(block_len))
    order = jnp.asarray(row_order(count_z, 4, rows_dev)).astype(jnp.bfloat16)
    half_matrix = matrix.astype(jnp.bfloat16)
    place = jnp.stack([lax.axis_index(axis) for axis in ("c", "x", "y")]).astype(jnp.int32)
    exps = grad_exps[0]
    peer_tokens, peer_grad, peer_exps = swapped(tokens), swapped(out_grad), swapped(exps)
    (own,) = coded_gradient(place, tokens, out_grad, hadamard_signs, exps, half_matrix, order)
    pair_sums = coded_gradient(
        place, peer_tokens, peer_grad, hadamard_signs, peer_exps, half_matrix, order, own=own
    )
    here, far = pair_sums[0::2], pair_sums[1::2]
    arrived = [shifted(far[shift], 0, shift) for shift in (1, 2, 3)]
    lines = line_sums([far[0], *arrived], 3)
    lines, nears = lax.optimization_barrier((list(lines), list(here[1:])))
    crossed = [shifted(lines[shift - 1], 1, shift) for shift in (1, 2, 3)]
    nears = [shifted(nears[shift - 1], 0, shift) for shift in (1, 2, 3)]
    parts = face_sum([here[0], *nears, *crossed], count_z)
    parts = lax.all_to_all(parts, "z", 0, 0, tiled=True)
    summed = jnp.sum(parts.astype(jnp.float32), axis=0)
    gradient = unrotate_rows(summed, sign_rows, matrix)
    new_master, new_first, new_second = adam_update(gradient, master_weights, adam_m, adam_v)
    owner = lax.axis_index(AXES)
    base_own = lax.dynamic_slice_in_dim(base_weights, owner * rows_dev, rows_dev, 0).astype(
        jnp.float32
    )
    diff_bound = clip_level * jnp.exp2(diff_exps.astype(jnp.float32))
    diff_coded = clip_rows(new_master - base_own, diff_bound).astype(jnp.bfloat16)
    effective = (base_own + diff_coded.astype(jnp.float32)).astype(jnp.bfloat16)
    stacked = lax.all_to_all(
        jnp.broadcast_to(effective[None], (count_z, *effective.shape)), "z", 0, 0, tiled=True
    ).reshape(count_z * rows_dev, model_width)
    crossed = [shifted(stacked, 1, shift) for shift in (1, 2, 3)]
    nears = [shifted(stacked, 0, shift) for shift in (1, 2, 3)]
    crossed_rows = jnp.concatenate(crossed, axis=0)
    fars = [shifted(crossed_rows, 0, shift) for shift in (1, 2, 3)]
    offsets = [(0, 0), (1, 0), (2, 0), (3, 0), (0, 1), (0, 2), (0, 3)]
    offsets += [(first, second) for first in (1, 2, 3) for second in (1, 2, 3)]
    spread = column_spread(place, offsets, count_z, rows_dev)
    close = [stacked, *nears, crossed_rows]
    early_own, early_peer = early_product(tokens, close), early_product(peer_tokens, close)
    peer_part = swapped(late_product(peer_tokens, early_peer, spread, fars))
    own_part = late_product(tokens, early_own, spread, fars)
    projected = interleaved(place, own_part, peer_part)
    return (projected, new_master, new_first, new_second)


def solution(mesh):
    split = Mesh(mesh.devices.reshape(4, 2, 8, 4), AXES)
    rows = P(AXES, None)
    return jax.shard_map(
        shards,
        mesh=split,
        in_specs=(rows, rows, rows, P(), rows, rows, P(AXES, None, None), rows, P()),
        out_specs=(rows, rows, rows, rows),
        check_vma=False,
    )
```

time: 158 us -> 163 us (1.032)
  blocking collectives: 96.5 us -> 12.5 us
  waiting for transfers between devices: 8.07 us -> 56.1 us
  starting transfers between devices: 19.5 us -> 48.7 us
  Pallas kernels: 23.7 us -> 34 us
  local copies, waits for them, and re-layouts: 3.27 us -> 6.16 us
    all_to_all x5 -> x1, blocking collectives: 96.5 us -> 12.5 us  [shards(): lax.all_to_all(jnp.broadcast_to(effective[None], (count_z, *effective.sha...]
    ppermute x0 -> x18, waiting for transfers between devices: none -> 46.7 us  [shifted(): return lax.ppermute(value, FACE, pairs)]
    ppermute x0 -> x18, starting transfers between devices: none -> 25.5 us  [shifted(): return lax.ppermute(value, FACE, pairs)]
    pallas_call x3 -> x6, Pallas kernels: 6.07 us -> 14.5 us  [the longest x2 7.16 us: late_product(): pl.pallas_call(late_kernel, in_specs=[whole] * (3 + len(weights)), out_sp...]
    ppermute x4, starting transfers between devices: 11.3 us -> 15 us  [swapped(): return lax.ppermute(value, 'c', [(0, 1), (1, 0)])]
    unnamed x11 -> x27, local copies, waits for them, and re-layouts: 0.71 us -> 4.18 us
  transfers between devices with their start and end apart: 5 -> 23, of which waited for: 1 -> 11; matrix products, arithmetic and copies ran while one was open for 1% -> 3% of each run, Pallas kernels for 7% -> 11%
where the time goes in v4:
time: 163 us; the launch traced here: 162 us
  waiting for transfers between devices  56.1 us (34%)
  starting transfers between devices  48.7 us (30%)
  Pallas kernels  34 us (21%)
  blocking collectives  12.5 us (8%)
  local copies, waits for them, and re-layouts  6.16 us (4%)
  other arithmetic  3.73 us (2%)
    ppermute x18, waiting for transfers between devices, shifted(): return lax.ppermute(value, FACE, pairs)  46.7 us
    ppermute x18, starting transfers between devices, shifted(): return lax.ppermute(value, FACE, pairs)  25.5 us
    pallas_call x2, Pallas kernels, coded_gradient(): pl.pallas_call(body, grid_spec=pltpu.PrefetchScalarGridSpec(num_scalar_pr...  17.9 us
    ppermute x4, starting transfers between devices, swapped(): return lax.ppermute(value, 'c', [(0, 1), (1, 0)])  15 us
    all_to_all x1, blocking collectives, shards(): lax.all_to_all(jnp.broadcast_to(effective[None], (count_z, *effective.sha...  12.5 us
    all_to_all x1, waiting for transfers between devices, shards(): parts = lax.all_to_all(parts, 'z', 0, 0, tiled=True)  9.43 us
    all_to_all x1, starting transfers between devices, shards(): parts = lax.all_to_all(parts, 'z', 0, 0, tiled=True)  8.19 us
    pallas_call x2, Pallas kernels, late_product(): pl.pallas_call(late_kernel, in_specs=[whole] * (3 + len(weights)), out_sp...  7.16 us
  transfers between devices with their start and end apart: 23, of which 11 were waited for; matrix products, arithmetic and copies ran while one was open for 3% of the time, Pallas kernels for 11%

profile of v4, /device:TPU:1, one launch (start us, length us, event | category | flops | bytes accessed | tf_op | source)
XLA Modules:
  0.0 162.4 jit_solution(2956695431013772355)
XLA Ops:
  0.6 3.3 %collective-permute-start = (bf16[384,4096]{1,0:T(8,128)(2,1)}, bf16[384,4096]{1,0:T(8,128)(2,1)S(1)}, u32[]{:S(2)}, u32[]{:S(2)}) collective-permute-start(bf16[384,4096]{1,0:T(8,128)(2,1)} %tok_ref.3), channel_id=1, source_target_pairs={{0,32},{32,0},{1,33},{33,1},{2,34},{34,2},{3,35},{35,3},{4,36},{36... | collective-permute-start | bytes 9437192 | tf_op jit(solution)/shard_map/ppermute | solution.py:306
  4.5 0.6 pad_add_fusion.refs_0_.place_ref
  5.1 9.1 %shard_map.156.refs_10_ = bf16[512,4096]{1,0:T(8,128)(2,1)} custom-call(s32[3]{0:T(128)} %pad_add_fusion.refs_0_.place_ref, bf16[384,4096]{1,0:T(8,128)(2,1)} %tok_ref.3, bf16[384,1024]{1,0:T(8,128)(2,1)} %refs_5_.1, bf16[384,1024]{1,0:T(8,128)(2,1)} %refs_5_.1, bf16[384,1024]{1,0:T(8,128)(2,1)} %refs_5_.1, bf16[384,1024]{1,0:T(8,128)(2,1)} %refs_5_.1, ...), custom_call_target="tpu_custom_call" | custom-call | tf_op jit(solution)/shard_map/pallas_call | solution.py:167
  14.2 8.9 %shard_map.157 = (bf16[32,4096]{1,0:T(8,128)(2,1)S(1)}, bf16[96,4096]{1,0:T(8,128)(2,1)S(1)}, bf16[32,4096]{1,0:T(8,128)(2,1)S(1)}, bf16[96,4096]{1,0:T(8,128)(2...) custom-call(s32[3]{0:T(128)S(1)} %copy-done.6, ...), custom_call_target="tpu_custom_call" | custom-call | tf_op jit(solution)/shard_map/pallas_call | solution.py:167
  23.2 2.2 %collective-permute-start.4 = (bf16[96,4096]{1,0:T(8,128)(2,1)S(1)}, bf16[96,4096]{1,0:T(8,128)(2,1)S(1)}, u32[]{:S(2)}, u32[]{:S(2)}) collective-permute-start(bf16[96,4096]{1,0:T(8,128)(2,1)S(1)} %get-tuple-element.24), channel_id=1, source_target_pairs={{0,2},{1,3},{2,0},{3,1},{32,160},{33,161},{34,162},{35,163},{64,66... | collective-permute-start | bytes 2359304 | tf_op jit(solution)/shard_map/ppermute | solution.py:317
  25.4 1.1 collective-permute-start.5
  26.4 17.5 %collective-permute-done.3.refs_1_ = bf16[96,4096]{1,0:T(8,128)(2,1)S(1)} collective-permute-done((bf16[96,4096]{1,0:T(8,128)(2,1)S(1)}, bf16[96,4096]{1,0:T(8,128)(2,1)S(1)}, u32[]{:S(2)}, u32[]{:S(2)}) %collective-permute-start.3) | collective-permute-done | bytes 786464 | tf_op jit(solution)/shard_map/ppermute | solution.py:317
  44.0 0.6 collective-permute-done.5.refs_3_
  44.6 0.8 shard_map.158
  45.4 1.4 collective-permute-start.10
  46.8 0.9 collective-permute-start.11
  47.7 1.3 collective-permute-start.6
  48.9 1.8 %collective-permute-start.7 = (bf16[32,4096]{1,0:T(8,128)(2,1)S(1)}, bf16[32,4096]{1,0:T(8,128)(2,1)S(1)}, u32[]{:S(2)}, u32[]{:S(2)}) collective-permute-start(bf16[32,4096]{1,0:T(8,128)(2,1)S(1)} %get-tuple-element.33), channel_id=1, source_target_pairs={{0,2},{1,3},{2,0},{3,1},{32,160},{33,161},{34,162},{35,163},{64,66... | collective-permute-start | bytes 786440 | tf_op jit(solution)/shard_map/ppermute | solution.py:317
  50.7 1.6 collective-permute-start.8
  52.5 0.5 collective-permute-start.9
  52.9 1.1 collective-permute-done.11.refs_6_
  54.0 2.7 %collective-permute-done.6.refs_1_ = bf16[32,4096]{1,0:T(8,128)(2,1)S(1)} collective-permute-done((bf16[32,4096]{1,0:T(8,128)(2,1)S(1)}, bf16[32,4096]{1,0:T(8,128)(2,1)S(1)}, u32[]{:S(2)}, u32[]{:S(2)}) %collective-permute-start.6) | collective-permute-done | bytes 262176 | tf_op jit(solution)/shard_map/ppermute | solution.py:317
  56.7 3.2 %collective-permute-done.7.refs_2_ = bf16[32,4096]{1,0:T(8,128)(2,1)S(1)} collective-permute-done((bf16[32,4096]{1,0:T(8,128)(2,1)S(1)}, bf16[32,4096]{1,0:T(8,128)(2,1)S(1)}, u32[]{:S(2)}, u32[]{:S(2)}) %collective-permute-start.7) | collective-permute-done | bytes 262176 | tf_op jit(solution)/shard_map/ppermute | solution.py:317
  59.9 1.5 collective-permute-done.8.refs_3_
  61.3 1.6 shard_map.159
  63.0 8.2 %all-to-all-start = ((bf16[8,4,4096]{2,1,0:T(4,128)(2,1)}), bf16[8,4,4096]{2,1,0:T(4,128)(2,1)}, u32[]{:S(2)}, u32[]{:S(2)}) async-start(bf16[8,4,4096]{2,1,0:T(4,128)(2,1)} %shard_map.159), calls=%async_computation | async-start | bytes 524288 | tf_op jit(solution)/shard_map/all_to_all | solution.py:369
  71.3 9.4 %all-to-all-done = bf16[8,4,4096]{2,1,0:T(4,128)(2,1)} async-done(((bf16[8,4,4096]{2,1,0:T(4,128)(2,1)}), bf16[8,4,4096]{2,1,0:T(4,128)(2,1)}, u32[]{:S(2)}, u32[]{:S(2)}) %all-to-all-start) | async-done | bytes 262176 | tf_op jit(solution)/shard_map/all_to_all | solution.py:369
  80.7 1.1 convert_reduce_fusion
  82.1 1.7 %fusion.4 = (bf16[4,4096]{1,0:T(4,128)(2,1)S(1)}, f32[4,4096]{1,0:T(4,128)}, f32[4,4096]{1,0:T(4,128)}, f32[4,4096]{1,0:T(4,128)}) fusion(bf16[1,4,32,128]{3,2,1,0:T(8,128)(2,1)S(1)} %get-tuple-element.46, bf16[1,4,32,128]{3,2,1,0:T(8,128)(2,1)S(1)} %get-tuple-element.47, bf16[1024,4096]{1,0:T(8,128)(2,1)} %param.16, s32[]{:T(128)S(6)} %select_n.26, ...), kind=kLoop, calls=%fused_computation.10 | loop fusion | flops 409600 | bytes 606212 | tf_op jit(solution)/shard_map/convert_element_type | solution.py:379
  83.9 12.5 %all_to_all.10 = bf16[8,4,4096]{2,1,0:T(4,128)(2,1)} all-to-all(bf16[8,4,4096]{2,1,0:T(4,128)(2,1)S(1)} %broadcast_in_dim.2), channel_id=1, replica_groups=mesh['y'=4,'c'=2,'z'=8,'x'=4] {'z'}, dimensions={0} | all-to-all | bytes 524288 | tf_op jit(solution)/shard_map/all_to_all | solution.py:380
  96.4 1.0 reshape.96.refs_0_
  97.5 2.3 %collective-permute-start.15 = (bf16[32,4096]{1,0:T(8,128)(2,1)S(1)}, bf16[32,4096]{1,0:T(8,128)(2,1)}, u32[]{:S(2)}, u32[]{:S(2)}) collective-permute-start(bf16[32,4096]{1,0:T(8,128)(2,1)S(1)} %reshape.96.refs_0_), channel_id=1, source_target_pairs={{0,64},{1,65},{2,66},{3,67},{32,33},{33,34},{34,35},{35,32},{64,12... | collective-permute-start | bytes 786440 | tf_op jit(solution)/shard_map/ppermute | solution.py:317
  99.7 1.2 collective-permute-start.16
  100.9 2.0 %collective-permute-start.17 = (bf16[32,4096]{1,0:T(8,128)(2,1)S(1)}, bf16[32,4096]{1,0:T(8,128)(2,1)S(1)}, u32[]{:S(2)}, u32[]{:S(2)}) collective-permute-start(bf16[32,4096]{1,0:T(8,128)(2,1)S(1)} %reshape.96.refs_0_), channel_id=1, source_target_pairs={{0,192},{1,193},{2,194},{3,195},{32,35},{33,32},{34,33},{35,34},{6... | collective-permute-start | bytes 786440 | tf_op jit(solution)/shard_map/ppermute | solution.py:317
  102.9 1.3 collective-permute-start.12
  104.2 1.7 %constant_dynamic-update-slice_fusion.2 = bf16[96,4096]{1,0:T(8,128)(2,1)} fusion(bf16[32,4096]{1,0:T(8,128)(2,1)} %collective-permute-done.15), kind=kLoop, calls=%fused_computation.20 | loop fusion | bytes 524288
  105.9 1.5 collective-permute-done.16
  107.4 0.7 constant_dynamic-update-slice_fusion.1
  108.1 0.7 constant_dynamic-update-slice_fusion.refs_4_
  108.8 2.1 %collective-permute-start.18 = (bf16[96,4096]{1,0:T(8,128)(2,1)}, bf16[96,4096]{1,0:T(8,128)(2,1)}, u32[]{:S(2)}, u32[]{:S(2)}) collective-permute-start(bf16[96,4096]{1,0:T(8,128)(2,1)} %constant_dynamic-update-slice_fusion.refs_4_), channel_id=1, source_target_pairs={{0,1},{1,2},{2,3},{3,0},{32,96},{33,97},{34,98},{35,99},{64,65},{6... | collective-permute-start | bytes 2359304 | tf_op jit(solution)/shard_map/ppermute | solution.py:317
  110.9 2.0 %collective-permute-start.19 = (bf16[96,4096]{1,0:T(8,128)(2,1)}, bf16[96,4096]{1,0:T(8,128)(2,1)}, u32[]{:S(2)}, u32[]{:S(2)}) collective-permute-start(bf16[96,4096]{1,0:T(8,128)(2,1)} %constant_dynamic-update-slice_fusion.refs_4_), channel_id=1, source_target_pairs={{0,2},{1,3},{2,0},{3,1},{32,160},{33,161},{34,162},{35,163},{64,66... | collective-permute-start | bytes 2359304 | tf_op jit(solution)/shard_map/ppermute | solution.py:317
  113.4 0.8 collective-permute-start.13
  114.2 0.7 copy-done.1
  114.9 2.7 %collective-permute-start.14 = (bf16[32,4096]{1,0:T(8,128)(2,1)S(1)}, bf16[32,4096]{1,0:T(8,128)(2,1)}, u32[]{:S(2)}, u32[]{:S(2)}) collective-permute-start(bf16[32,4096]{1,0:T(8,128)(2,1)S(1)} %reshape.96.refs_0_), channel_id=1, source_target_pairs={{0,3},{1,0},{2,1},{3,2},{32,224},{33,225},{34,226},{35,227},{64,67... | collective-permute-start | bytes 786440 | tf_op jit(solution)/shard_map/ppermute | solution.py:317
  117.9 17.6 %collective-permute-done.13.refs_2_ = bf16[32,4096]{1,0:T(8,128)(2,1)} collective-permute-done((bf16[32,4096]{1,0:T(8,128)(2,1)S(1)}, bf16[32,4096]{1,0:T(8,128)(2,1)}, u32[]{:S(2)}, u32[]{:S(2)}) %collective-permute-start.13) | collective-permute-done | bytes 262176 | tf_op jit(solution)/shard_map/ppermute | solution.py:317
  135.6 0.9 collective-permute-done.14.refs_3_
  136.4 0.9 copy-done.2
  137.4 2.5 %shard_map.162.early_ref = bf16[224,384]{1,0:T(8,128)(2,1)S(1)} custom-call(bf16[384,4096]{1,0:T(8,128)(2,1)S(1)} %collective-permute-done.refs_1_.tok_ref, bf16[32,4096]{1,0:T(8,128)(2,1)S(1)} %reshape.96.refs_0_, bf16[32,4096]{1,0:T(8,128)(2,1)S(1)} %copy-done.2, bf16[32,4096]{1,0:T(8,128)(2,1)} %collective-permute-done.13.refs_2_, ...), custom_call_target="tpu_custom_call" | custom-call | tf_op jit(solution)/shard_map/pallas_call | solution.py:249
  139.9 3.6 %shard_map.163 = bf16[384,512]{1,0:T(8,128)(2,1)S(1)} custom-call(bf16[384,4096]{1,0:T(8,128)(2,1)S(1)} %collective-permute-done.refs_1_.tok_ref, bf16[224,384]{1,0:T(8,128)(2,1)S(1)} %shard_map.162.early_ref, bf16[512,512]{1,0:T(8,128)(2,1)S(1)} %fusion.spread_ref, bf16[96,4096]{1,0:T(8,128)(2,1)} %collective-permute-done.18.refs_0_, ...), custom_call_target="tpu_custom_call" | custom-call | tf_op jit(solution)/shard_map/pallas_call | solution.py:273
  143.6 11.2 %collective-permute-start.21 = (bf16[384,512]{1,0:T(8,128)(2,1)S(1)}, bf16[384,512]{1,0:T(8,128)(2,1)S(1)}, u32[]{:S(2)}, u32[]{:S(2)}) collective-permute-start(bf16[384,512]{1,0:T(8,128)(2,1)S(1)} %shard_map.163), channel_id=1, source_target_pairs={{0,32},{32,0},{1,33},{33,1},{2,34},{34,2},{3,35},{35,3},{4,36},{36... | collective-permute-start | bytes 1179656 | tf_op jit(solution)/shard_map/ppermute | solution.py:306
  154.8 2.5 %shard_map.160.early_ref = bf16[224,384]{1,0:T(8,128)(2,1)S(1)} custom-call(bf16[384,4096]{1,0:T(8,128)(2,1)S(1)} %copy-done, bf16[32,4096]{1,0:T(8,128)(2,1)S(1)} %reshape.96.refs_0_, bf16[32,4096]{1,0:T(8,128)(2,1)S(1)} %copy-done.2, bf16[32,4096]{1,0:T(8,128)(2,1)} %collective-permute-done.13.refs_2_, bf16[32,4096]{1,0:T(8,128)(2,1)} %collective-permute-done.14.refs_3_, ...), custom_call_target="tpu_custom_call" | custom-call | tf_op jit(solution)/shard_map/pallas_call | solution.py:249
  157.3 3.5 %shard_map.161.own_ref = bf16[384,512]{1,0:T(8,128)(2,1)S(1)} custom-call(bf16[384,4096]{1,0:T(8,128)(2,1)S(1)} %copy-done, bf16[224,384]{1,0:T(8,128)(2,1)S(1)} %shard_map.160.early_ref, bf16[512,512]{1,0:T(8,128)(2,1)S(1)} %fusion.spread_ref, bf16[96,4096]{1,0:T(8,128)(2,1)} %collective-permute-done.18.refs_0_, ...), custom_call_target="tpu_custom_call" | custom-call | tf_op jit(solution)/shard_map/pallas_call | solution.py:273
  160.8 1.6 shard_map.164
  (51 shorter events, 2.1 us)
Async XLA Ops:
  0.6 13.5 %collective-permute-start = (bf16[384,4096]{1,0:T(8,128)(2,1)}, bf16[384,4096]{1,0:T(8,128)(2,1)S(1)}, u32[]{:S(2)}, u32[]{:S(2)}) collective-permute-start(bf16[384,4096]{1,0:T(8,128)(2,1)} %tok_ref.3), channel_id=1, source_target_pairs={{0,32},{32,0},{1,33},{33,1},{2,34},{34,2},{3,35},{35,3},{4,36},{36... | collective-permute-start | bytes 9437192 | tf_op jit(solution)/shard_map/ppermute | solution.py:306
  4.0 10.2 %collective-permute-start.1 = (bf16[384,1024]{1,0:T(8,128)(2,1)}, bf16[384,1024]{1,0:T(8,128)(2,1)}, u32[]{:S(2)}, u32[]{:S(2)}) collective-permute-start(bf16[384,1024]{1,0:T(8,128)(2,1)} %refs_5_.1), channel_id=1, source_target_pairs={{0,32},{32,0},{1,33},{33,1},{2,34},{34,2},{3,35},{35,3},{4,36},{36... | collective-permute-start | bytes 2359304 | tf_op jit(solution)/shard_map/ppermute | solution.py:306
  4.1 10.1 %collective-permute-start.2 = (s32[8,32]{1,0:T(8,128)}, s32[8,32]{1,0:T(8,128)S(1)}, u32[]{:S(2)}, u32[]{:S(2)}) collective-permute-start(s32[8,32]{1,0:T(8,128)} %bitcast.20), channel_id=1, source_target_pairs={{0,32},{32,0},{1,33},{33,1},{2,34},{34,2},{3,35},{35,3},{4,36},{36... | collective-permute-start | bytes 3080 | tf_op jit(solution)/shard_map/ppermute | solution.py:306
  5.1 9.1 %copy-start.3 = (s32[32,128]{1,0:T(8,128)S(1)}, s32[32,128]{1,0:T(8,128)}, u32[]{:S(2)}) copy-start(s32[32,128]{1,0:T(8,128)} %refs_6_.3) | copy-start | bytes 49156
  5.1 9.1 %copy-start.4 = (bf16[128,128]{1,0:T(8,128)(2,1)S(1)}, bf16[128,128]{1,0:T(8,128)(2,1)}, u32[]{:S(2)}) copy-start(bf16[128,128]{1,0:T(8,128)(2,1)} %constant.100.refs_8_) | copy-start | bytes 98308
  5.1 9.1 %copy-start.5 = (bf16[128,128]{1,0:T(8,128)(2,1)S(1)}, bf16[128,128]{1,0:T(8,128)(2,1)}, u32[]{:S(2)}) copy-start(bf16[128,128]{1,0:T(8,128)(2,1)} %constant.101.refs_9_) | copy-start | bytes 98308
  5.1 9.1 %copy-start.6 = (s32[3]{0:T(128)S(1)}, s32[3]{0:T(128)}, u32[]{:S(2)}) copy-start(s32[3]{0:T(128)} %pad_add_fusion.refs_0_.place_ref) | copy-start | bytes 40
  23.1 48.1 %copy-start.9 = (s32[4,32]{1,0:T(4,128)S(1)}, s32[4,32]{1,0:T(4,128)}, u32[]{:S(2)}) copy-start(s32[4,32]{1,0:T(4,128)} %param.20) | copy-start | bytes 1540
  23.1 58.8 %copy-start.7 = (f32[128,128]{1,0:T(8,128)S(1)}, f32[128,128]{1,0:T(8,128)}, u32[]{:S(2)}) copy-start(f32[128,128]{1,0:T(8,128)} %constant.89.clone) | copy-start | bytes 196612
  23.1 59.0 %copy-start.8 = (f32[4,4096]{1,0:T(4,128)S(1)}, f32[4,4096]{1,0:T(4,128)}, u32[]{:S(2)}) copy-start(f32[4,4096]{1,0:T(4,128)} %param.15) | copy-start | bytes 196612
  23.1 20.8 %collective-permute-start.3 = (bf16[96,4096]{1,0:T(8,128)(2,1)S(1)}, bf16[96,4096]{1,0:T(8,128)(2,1)S(1)}, u32[]{:S(2)}, u32[]{:S(2)}) collective-permute-start(bf16[96,4096]{1,0:T(8,128)(2,1)S(1)} %get-tuple-element.23), channel_id=1, source_target_pairs={{0,1},{1,2},{2,3},{3,0},{32,96},{33,97},{34,98},{35,99},{64,65},{6... | collective-permute-start | bytes 2359304 | tf_op jit(solution)/shard_map/ppermute | solution.py:317
  23.2 20.8 %collective-permute-start.4 = (bf16[96,4096]{1,0:T(8,128)(2,1)S(1)}, bf16[96,4096]{1,0:T(8,128)(2,1)S(1)}, u32[]{:S(2)}, u32[]{:S(2)}) collective-permute-start(bf16[96,4096]{1,0:T(8,128)(2,1)S(1)} %get-tuple-element.24), channel_id=1, source_target_pairs={{0,2},{1,3},{2,0},{3,1},{32,160},{33,161},{34,162},{35,163},{64,66... | collective-permute-start | bytes 2359304 | tf_op jit(solution)/shard_map/ppermute | solution.py:317
  25.4 19.2 %collective-permute-start.5 = (bf16[96,4096]{1,0:T(8,128)(2,1)S(1)}, bf16[96,4096]{1,0:T(8,128)(2,1)S(1)}, u32[]{:S(2)}, u32[]{:S(2)}) collective-permute-start(bf16[96,4096]{1,0:T(8,128)(2,1)S(1)} %get-tuple-element.25), channel_id=1, source_target_pairs={{0,3},{1,0},{2,1},{3,2},{32,224},{33,225},{34,226},{35,227},{64,67... | collective-permute-start | bytes 2359304 | tf_op jit(solution)/shard_map/ppermute | solution.py:317
  45.3 68.0 %copy-start.10 = (s32[16]{0:T(128)S(1)}, s32[16]{0:T(128)}, u32[]{:S(2)}) copy-start(s32[16]{0:T(128)} %constant.91.clone) | copy-start | bytes 196
  45.4 68.0 %copy-start.11 = (s32[16]{0:T(128)S(1)}, s32[16]{0:T(128)}, u32[]{:S(2)}) copy-start(s32[16]{0:T(128)} %constant.92.clone) | copy-start | bytes 196
  45.4 7.1 %collective-permute-start.10 = (bf16[32,4096]{1,0:T(8,128)(2,1)S(1)}, bf16[32,4096]{1,0:T(8,128)(2,1)S(1)}, u32[]{:S(2)}, u32[]{:S(2)}) collective-permute-start(bf16[32,4096]{1,0:T(8,128)(2,1)S(1)} %get-tuple-element.36), channel_id=1, source_target_pairs={{0,128},{1,129},{2,130},{3,131},{32,34},{33,35},{34,32},{35,33},{6... | collective-permute-start | bytes 786440 | tf_op jit(solution)/shard_map/ppermute | solution.py:317
  46.8 7.2 %collective-permute-start.11 = (bf16[32,4096]{1,0:T(8,128)(2,1)S(1)}, bf16[32,4096]{1,0:T(8,128)(2,1)S(1)}, u32[]{:S(2)}, u32[]{:S(2)}) collective-permute-start(bf16[32,4096]{1,0:T(8,128)(2,1)S(1)} %get-tuple-element.37), channel_id=1, source_target_pairs={{0,192},{1,193},{2,194},{3,195},{32,35},{33,32},{34,33},{35,34},{6... | collective-permute-start | bytes 786440 | tf_op jit(solution)/shard_map/ppermute | solution.py:317
  47.7 9.0 %collective-permute-start.6 = (bf16[32,4096]{1,0:T(8,128)(2,1)S(1)}, bf16[32,4096]{1,0:T(8,128)(2,1)S(1)}, u32[]{:S(2)}, u32[]{:S(2)}) collective-permute-start(bf16[32,4096]{1,0:T(8,128)(2,1)S(1)} %get-tuple-element.32), channel_id=1, source_target_pairs={{0,1},{1,2},{2,3},{3,0},{32,96},{33,97},{34,98},{35,99},{64,65},{6... | collective-permute-start | bytes 786440 | tf_op jit(solution)/shard_map/ppermute | solution.py:317
  48.9 10.9 %collective-permute-start.7 = (bf16[32,4096]{1,0:T(8,128)(2,1)S(1)}, bf16[32,4096]{1,0:T(8,128)(2,1)S(1)}, u32[]{:S(2)}, u32[]{:S(2)}) collective-permute-start(bf16[32,4096]{1,0:T(8,128)(2,1)S(1)} %get-tuple-element.33), channel_id=1, source_target_pairs={{0,2},{1,3},{2,0},{3,1},{32,160},{33,161},{34,162},{35,163},{64,66... | collective-permute-start | bytes 786440 | tf_op jit(solution)/shard_map/ppermute | solution.py:317
  50.7 10.6 %collective-permute-start.8 = (bf16[32,4096]{1,0:T(8,128)(2,1)S(1)}, bf16[32,4096]{1,0:T(8,128)(2,1)S(1)}, u32[]{:S(2)}, u32[]{:S(2)}) collective-permute-start(bf16[32,4096]{1,0:T(8,128)(2,1)S(1)} %get-tuple-element.34), channel_id=1, source_target_pairs={{0,3},{1,0},{2,1},{3,2},{32,224},{33,225},{34,226},{35,227},{64,67... | collective-permute-start | bytes 786440 | tf_op jit(solution)/shard_map/ppermute | solution.py:317
  52.5 8.9 %collective-permute-start.9 = (bf16[32,4096]{1,0:T(8,128)(2,1)S(1)}, bf16[32,4096]{1,0:T(8,128)(2,1)S(1)}, u32[]{:S(2)}, u32[]{:S(2)}) collective-permute-start(bf16[32,4096]{1,0:T(8,128)(2,1)S(1)} %get-tuple-element.35), channel_id=1, source_target_pairs={{0,64},{1,65},{2,66},{3,67},{32,33},{33,34},{34,35},{35,32},{64,12... | collective-permute-start | bytes 786440 | tf_op jit(solution)/shard_map/ppermute | solution.py:317
  63.0 17.8 %all-to-all-start = ((bf16[8,4,4096]{2,1,0:T(4,128)(2,1)}), bf16[8,4,4096]{2,1,0:T(4,128)(2,1)}, u32[]{:S(2)}, u32[]{:S(2)}) async-start(bf16[8,4,4096]{2,1,0:T(4,128)(2,1)} %shard_map.159), calls=%async_computation | async-start | bytes 524288 | tf_op jit(solution)/shard_map/all_to_all | solution.py:369
  97.5 6.8 %collective-permute-start.15 = (bf16[32,4096]{1,0:T(8,128)(2,1)S(1)}, bf16[32,4096]{1,0:T(8,128)(2,1)}, u32[]{:S(2)}, u32[]{:S(2)}) collective-permute-start(bf16[32,4096]{1,0:T(8,128)(2,1)S(1)} %reshape.96.refs_0_), channel_id=1, source_target_pairs={{0,64},{1,65},{2,66},{3,67},{32,33},{33,34},{34,35},{35,32},{64,12... | collective-permute-start | bytes 786440 | tf_op jit(solution)/shard_map/ppermute | solution.py:317
  99.7 7.7 %collective-permute-start.16 = (bf16[32,4096]{1,0:T(8,128)(2,1)S(1)}, bf16[32,4096]{1,0:T(8,128)(2,1)S(1)}, u32[]{:S(2)}, u32[]{:S(2)}) collective-permute-start(bf16[32,4096]{1,0:T(8,128)(2,1)S(1)} %reshape.96.refs_0_), channel_id=1, source_target_pairs={{0,128},{1,129},{2,130},{3,131},{32,34},{33,35},{34,32},{35,33},{6... | collective-permute-start | bytes 786440 | tf_op jit(solution)/shard_map/ppermute | solution.py:317
  100.9 7.2 %collective-permute-start.17 = (bf16[32,4096]{1,0:T(8,128)(2,1)S(1)}, bf16[32,4096]{1,0:T(8,128)(2,1)S(1)}, u32[]{:S(2)}, u32[]{:S(2)}) collective-permute-start(bf16[32,4096]{1,0:T(8,128)(2,1)S(1)} %reshape.96.refs_0_), channel_id=1, source_target_pairs={{0,192},{1,193},{2,194},{3,195},{32,35},{33,32},{34,33},{35,34},{6... | collective-permute-start | bytes 786440 | tf_op jit(solution)/shard_map/ppermute | solution.py:317
  102.9 11.3 %collective-permute-start.12 = (bf16[32,4096]{1,0:T(8,128)(2,1)S(1)}, bf16[32,4096]{1,0:T(8,128)(2,1)S(1)}, u32[]{:S(2)}, u32[]{:S(2)}) collective-permute-start(bf16[32,4096]{1,0:T(8,128)(2,1)S(1)} %reshape.96.refs_0_), channel_id=1, source_target_pairs={{0,1},{1,2},{2,3},{3,0},{32,96},{33,97},{34,98},{35,99},{64,65},{6... | collective-permute-start | bytes 786440 | tf_op jit(solution)/shard_map/ppermute | solution.py:317
  108.8 31.1 %collective-permute-start.18 = (bf16[96,4096]{1,0:T(8,128)(2,1)}, bf16[96,4096]{1,0:T(8,128)(2,1)}, u32[]{:S(2)}, u32[]{:S(2)}) collective-permute-start(bf16[96,4096]{1,0:T(8,128)(2,1)} %constant_dynamic-update-slice_fusion.refs_4_), channel_id=1, source_target_pairs={{0,1},{1,2},{2,3},{3,0},{32,96},{33,97},{34,98},{35,99},{64,65},{6... | collective-permute-start | bytes 2359304 | tf_op jit(solution)/shard_map/ppermute | solution.py:317
  110.9 29.0 %collective-permute-start.19 = (bf16[96,4096]{1,0:T(8,128)(2,1)}, bf16[96,4096]{1,0:T(8,128)(2,1)}, u32[]{:S(2)}, u32[]{:S(2)}) collective-permute-start(bf16[96,4096]{1,0:T(8,128)(2,1)} %constant_dynamic-update-slice_fusion.refs_4_), channel_id=1, source_target_pairs={{0,2},{1,3},{2,0},{3,1},{32,160},{33,161},{34,162},{35,163},{64,66... | collective-permute-start | bytes 2359304 | tf_op jit(solution)/shard_map/ppermute | solution.py:317
  112.9 27.0 %collective-permute-start.20 = (bf16[96,4096]{1,0:T(8,128)(2,1)}, bf16[96,4096]{1,0:T(8,128)(2,1)}, u32[]{:S(2)}, u32[]{:S(2)}) collective-permute-start(bf16[96,4096]{1,0:T(8,128)(2,1)} %constant_dynamic-update-slice_fusion.refs_4_), channel_id=1, source_target_pairs={{0,3},{1,0},{2,1},{3,2},{32,224},{33,225},{34,226},{35,227},{64,67... | collective-permute-start | bytes 2359304 | tf_op jit(solution)/shard_map/ppermute | solution.py:317
  113.4 22.1 %collective-permute-start.13 = (bf16[32,4096]{1,0:T(8,128)(2,1)S(1)}, bf16[32,4096]{1,0:T(8,128)(2,1)}, u32[]{:S(2)}, u32[]{:S(2)}) collective-permute-start(bf16[32,4096]{1,0:T(8,128)(2,1)S(1)} %reshape.96.refs_0_), channel_id=1, source_target_pairs={{0,2},{1,3},{2,0},{3,1},{32,160},{33,161},{34,162},{35,163},{64,66... | collective-permute-start | bytes 786440 | tf_op jit(solution)/shard_map/ppermute | solution.py:317
  114.2 0.7 copy-start.1
  114.9 21.5 %collective-permute-start.14 = (bf16[32,4096]{1,0:T(8,128)(2,1)S(1)}, bf16[32,4096]{1,0:T(8,128)(2,1)}, u32[]{:S(2)}, u32[]{:S(2)}) collective-permute-start(bf16[32,4096]{1,0:T(8,128)(2,1)S(1)} %reshape.96.refs_0_), channel_id=1, source_target_pairs={{0,3},{1,0},{2,1},{3,2},{32,224},{33,225},{34,226},{35,227},{64,67... | collective-permute-start | bytes 786440 | tf_op jit(solution)/shard_map/ppermute | solution.py:317
  136.4 1.0 copy-start.2
  139.9 14.9 %copy-start = (bf16[384,4096]{1,0:T(8,128)(2,1)S(1)}, bf16[384,4096]{1,0:T(8,128)(2,1)}, u32[]{:S(2)}) copy-start(bf16[384,4096]{1,0:T(8,128)(2,1)} %tok_ref.3) | copy-start | bytes 9437188
  143.6 17.2 %collective-permute-start.21 = (bf16[384,512]{1,0:T(8,128)(2,1)S(1)}, bf16[384,512]{1,0:T(8,128)(2,1)S(1)}, u32[]{:S(2)}, u32[]{:S(2)}) collective-permute-start(bf16[384,512]{1,0:T(8,128)(2,1)S(1)} %shard_map.163), channel_id=1, source_target_pairs={{0,32},{32,0},{1,33},{33,1},{2,34},{34,2},{3,35},{35,3},{4,36},{36... | collective-permute-start | bytes 1179656 | tf_op jit(solution)/shard_map/ppermute | solution.py:306

commit v5 on v3

--- a/solution.py
+++ b/solution.py
@@ -66,18 +66,19 @@
     return (natural[:, None] == spots[None, :]).astype(np.float32)
 
 
-def coded_kernel(groups, added, core_ref, tok_ref, *refs):
+def coded_kernel(groups, spots, added, offset, core_ref, x_ref, y_ref, tok_ref, *refs):
     grad_refs = refs[:groups]
     sign_ref, exps_ref, mat_ref, order_ref = refs[groups : groups + 4]
-    if added:
-        own_ref, out_ref, turned_ref, grad_t_ref, limit_ref = refs[groups + 4 :]
-    else:
-        out_ref, turned_ref, grad_t_ref, limit_ref = refs[groups + 4 :]
+    refs = refs[groups + 4 :]
+    own_ref = refs[0] if added else None
+    out_refs = refs[added:-3]
+    turned_ref, grad_t_ref, limit_ref = refs[-3:]
     token_rows, width = tok_ref.shape
     block_len = mat_ref.shape[0]
     tile = order_ref.shape[0]
-    core = core_ref[0]
-    first_block = pl.program_id(0) * (width // block_len)
+    part = tile // spots
+    core, at_x, at_y = core_ref[0], x_ref[0], y_ref[0]
+    first_block = (pl.program_id(0) + offset) * (width // block_len)
 
     @pl.when(pl.program_id(0) == 0)
     def _():
@@ -88,9 +89,14 @@
                 (((1,), (1,)), ((), ())),
                 preferred_element_type=jnp.float32,
             ).astype(jnp.bfloat16)
-            rows = slice(group * tile, (group + 1) * tile)
-            grad_t_ref[rows, :token_rows] = grad_t
-            grad_t_ref[rows, token_rows:] = grad_t
+            from_y = lax.rem(group - at_y + groups, groups)
+            for spot in range(spots):
+                from_x = lax.rem(spot - at_x + spots, spots)
+                piece = jnp.where(core == 0, from_x * groups + group, from_y * spots + spot)
+                rows = pl.ds(pl.multiple_of(piece * part, part), part)
+                values = grad_t[spot * part : (spot + 1) * part]
+                grad_t_ref[rows, :token_rows] = values
+                grad_t_ref[rows, token_rows:] = values
 
     levels = (clip_level * jnp.exp2(exps_ref[...].astype(jnp.float32))).astype(jnp.bfloat16)
     spread_shape = (exps_ref.shape[1], width)
@@ -111,41 +117,38 @@
         turned_ref[:token_rows, cols] = upper
         turned_ref[token_rows:, cols] = (turned - upper.astype(jnp.float32)).astype(jnp.bfloat16)
     terms = jnp.dot(grad_t_ref[...], turned_ref[...], preferred_element_type=jnp.float32)
-    for group in range(groups):
-        rows = slice(group * tile, (group + 1) * tile)
-        limit = limit_ref[pl.ds(2 * group + core, 1), :]
-        coded = jnp.clip(terms[rows, :], -limit, limit).astype(jnp.bfloat16)
-        if not added:
-            out_ref[rows, :] = coded
-            continue
-        total = (coded.astype(jnp.float32) + own_ref[rows, :].astype(jnp.float32)).astype(
-            jnp.bfloat16
-        )
-        part = out_ref.shape[2]
-        for spot in range(tile // part):
-            first = jnp.where(core == 0, spot, group)
-            second = jnp.where(core == 0, group, spot)
-            out_ref[first, second] = total[spot * part : (spot + 1) * part]
-
-
-def coded_gradient(core, tokens, out_grad, signs, exps, matrix, order, own=None, count=1):
+    for first in range(4):
+        for second in range(4):
+            group = jnp.where(core == 0, second, lax.rem(at_y + first, groups))
+            start = (first * 4 + second) * part
+            rows = slice(start, start + part)
+            limit = limit_ref[pl.ds(2 * group + core, 1), :]
+            coded = jnp.clip(terms[rows, :], -limit, limit).astype(jnp.bfloat16)
+            if not added:
+                out_refs[0][rows, :] = coded
+                continue
+            total = (coded.astype(jnp.float32) + own_ref[rows, :].astype(jnp.float32)).astype(
+                jnp.bfloat16
+            )
+            out_refs[first][second * part : (second + 1) * part, :] = total
+
+
+def coded_gradient(place, tokens, out_grad, signs, exps, matrix, order, own=None, half=0):
     token_rows, model_width = tokens.shape
     feature_rows = out_grad.shape[1]
     tile = order.shape[0]
     groups = feature_rows // tile // 2
+    spots = 4
     width = 1024
     added = own is not None
-    if added:
-        part = tile // count
-        out_shape = (count, groups, part, model_width)
-        out_spec = pl.BlockSpec((count, groups, part, width), lambda n, core: (0, 0, 0, n))
-    else:
-        out_shape = (groups * tile, model_width)
-        out_spec = pl.BlockSpec((groups * tile, width), lambda n, core: (0, n))
-    whole = lambda n, core: (0, 0)
-    column = lambda n, core: (0, n)
+    heights = [tile] * spots if added else [groups * tile]
+    steps = model_width // width // (2 if added else 1)
+    offset = half * steps
+    whole = lambda n, *place: (0, 0)
+    column = lambda n, *place: (0, n + offset)
+    placed = lambda n, *place: (0, n)
     grad_spec = lambda group: pl.BlockSpec(
-        (token_rows, tile), lambda n, core: (0, 2 * group + core[0])
+        (token_rows, tile), lambda n, *place: (0, 2 * group + place[0][0])
     )
     in_specs = [
         pl.BlockSpec((token_rows, width), column),
@@ -159,43 +162,58 @@
     if added:
         in_specs.append(pl.BlockSpec((groups * tile, width), column))
         operands.append(own)
-    body = lambda *refs: coded_kernel(groups, added, *refs)
+    body = lambda *refs: coded_kernel(groups, spots, added, offset, *refs)
     return pl.pallas_call(
         body,
         grid_spec=pltpu.PrefetchScalarGridSpec(
-            num_scalar_prefetch=1,
-            grid=(model_width // width,),
+            num_scalar_prefetch=3,
+            grid=(steps,),
             in_specs=in_specs,
-            out_specs=out_spec,
+            out_specs=[pl.BlockSpec((height, width), placed) for height in heights],
             scratch_shapes=[
                 pltpu.VMEM((2 * token_rows, width), jnp.bfloat16),
                 pltpu.VMEM((groups * tile, 2 * token_rows), jnp.bfloat16),
                 pltpu.VMEM((exps.shape[0], width), jnp.float32),
             ],
         ),
-        out_shape=jax.ShapeDtypeStruct(out_shape, jnp.bfloat16),
-        compiler_params=pltpu.CompilerParams(vmem_limit_bytes=(44 if added else 60) << 20),
-    )(core, *operands)
-
-
-def sum_kernel(parts_ref, out_ref):
-    total = parts_ref[0].astype(jnp.float32)
-    for at in range(1, parts_ref.shape[0]):
-        total = total + parts_ref[at].astype(jnp.float32)
-    out_ref[...] = total.astype(jnp.bfloat16)
-
-
-def summed_parts(parts):
-    count, groups, part, model_width = parts.shape
+        out_shape=[
+            jax.ShapeDtypeStruct((height, steps * width), jnp.bfloat16) for height in heights
+        ],
+        compiler_params=pltpu.CompilerParams(vmem_limit_bytes=(46 if added else 60) << 20),
+    )(*place, *operands)
+
+
+def line_kernel(count, *refs):
+    out_ref = refs[-1]
+    sums = []
+    for terms in (refs[:count], refs[count:-1]):
+        total = terms[0][...].astype(jnp.float32)
+        for ref in terms[1:]:
+            total = total + ref[...].astype(jnp.float32)
+        sums.append(total)
+    rows = 8
+    for at in range(sums[0].shape[0] // rows):
+        left, right = (total[at * rows : (at + 1) * rows] for total in sums)
+        upper = lax.broadcasted_iota(jnp.int32, left.shape, 0) < rows // 2
+        even = jnp.where(upper, left, pltpu.roll(right, rows // 2, 0))
+        odd = jnp.where(upper, pltpu.roll(left, rows // 2, 0), right)
+        out_ref[2 * at] = even.astype(jnp.bfloat16)
+        out_ref[2 * at + 1] = odd.astype(jnp.bfloat16)
+
+
+def line_sums(left_terms, right_terms):
+    rows, half = left_terms[0].shape
     width = 1024
+    count = len(left_terms)
+    body = lambda *refs: line_kernel(count, *refs)
     return pl.pallas_call(
-        sum_kernel,
-        grid=(model_width // width,),
-        in_specs=[pl.BlockSpec((count, groups, part, width), lambda n: (0, 0, 0, n))],
-        out_specs=pl.BlockSpec((groups, part, width), lambda n: (0, 0, n)),
-        out_shape=jax.ShapeDtypeStruct((groups, part, model_width), jnp.bfloat16),
+        body,
+        grid=(half // width,),
+        in_specs=[pl.BlockSpec((rows, width), lambda n: (0, n))] * (2 * count),
+        out_specs=pl.BlockSpec((rows // 4, 8, width), lambda n: (0, 0, n)),
+        out_shape=jax.ShapeDtypeStruct((rows // 4, 8, half), jnp.bfloat16),
         compiler_params=pltpu.CompilerParams(vmem_limit_bytes=16 << 20),
-    )(parts)
+    )(*left_terms, *right_terms)
 
 
 def project_kernel(pair, core_ref, tok_ref, weight_ref, order_ref, out_ref):
@@ -283,16 +301,29 @@
     return groups
 
 
+def shifted(value, axis_at, shift):
+    pairs = []
+    for y in range(4):
+        for core in range(2):
+            for x in range(4):
+                along_x = core == axis_at
+                to_y, to_x = (y, (x + shift) % 4) if along_x else ((y + shift) % 4, x)
+                pairs.append(((y * 2 + core) * 4 + x, (to_y * 2 + core) * 4 + to_x))
+    return lax.ppermute(value, FACE, pairs)
+
+
+def slab_groups():
+    at = lambda y, c, z, x: ((y * 2 + c) * 8 + z) * 4 + x
+    groups = [[at(y, 0, z, x) for y in range(4) for z in range(8)] for x in range(4)]
+    return groups + [[at(y, 1, z, x) for x in range(4) for z in range(8)] for y in range(4)]
+
+
 def exchanged(value, step):
     if step == "z":
         return lax.all_to_all(value, "z", 0, 0, tiled=True)
     return lax.all_to_all(
         value, FACE, 0, 0, tiled=True, axis_index_groups=face_groups(step == "first")
     )
-
-
-def reduced(value, step):
-    return jnp.sum(exchanged(value, step).astype(jnp.float32), axis=0)
 
 
 def gathered(value, count, step):
@@ -316,26 +347,29 @@
     block_len = sign_rows.shape[1]
     matrix = jnp.asarray(hadamard(block_len))
     order = jnp.asarray(row_order(count_z, count_x, rows_dev))
-    core = lax.axis_index("c")
-    core_at = core.reshape(1).astype(jnp.int32)
+    place = [lax.axis_index(axis).reshape(1).astype(jnp.int32) for axis in ("c", "x", "y")]
     exps = grad_exps[0]
     peer_tokens, peer_grad, peer_exps = swapped(tokens), swapped(out_grad), swapped(exps)
     half_matrix, order = matrix.astype(jnp.bfloat16), order.astype(jnp.bfloat16)
-    own = coded_gradient(core_at, tokens, out_grad, hadamard_signs, exps, half_matrix, order)
-    pair_sum = coded_gradient(
-        core_at,
-        peer_tokens,
-        peer_grad,
-        hadamard_signs,
-        peer_exps,
-        half_matrix,
-        order,
-        own=own,
-        count=count_x,
-    )
-    line_sum = summed_parts(exchanged(pair_sum, "first"))
-    face_sum = reduced(line_sum, "second").astype(jnp.bfloat16)
-    summed = reduced(face_sum.reshape(count_z, rows_dev, model_width), "z")
+    (own,) = coded_gradient(place, tokens, out_grad, hadamard_signs, exps, half_matrix, order)
+    halves = []
+    for half in (0, 1):
+        pair_sums = coded_gradient(
+            place,
+            peer_tokens,
+            peer_grad,
+            hadamard_signs,
+            peer_exps,
+            half_matrix,
+            order,
+            own=own,
+            half=half,
+        )
+        halves.append([pair_sums[0], *(shifted(pair_sums[far], 0, far) for far in (2, 1, 3))])
+    lines = line_sums(*halves)
+    parts = lax.all_to_all(lines, AXES, 0, 0, tiled=True, axis_index_groups=slab_groups())
+    summed = jnp.sum(parts.astype(jnp.float32), axis=0)
+    summed = jnp.swapaxes(summed.reshape(2, rows_dev, -1), 0, 1).reshape(rows_dev, model_width)
     gradient = unrotate_rows(summed, sign_rows, matrix)
     new_master, new_first, new_second = adam_update(gradient, master_weights, adam_m, adam_v)
     owner = lax.axis_index(AXES)
@@ -347,9 +381,9 @@
     effective = (base_own + diff_coded.astype(jnp.float32)).astype(jnp.bfloat16)
     stacked = gathered(effective, count_z, "z").reshape(count_z * rows_dev, model_width)
     weights = gathered(gathered(stacked, count_y, "second"), count_x, "first")
-    peer_part = swapped(project(core_at, peer_tokens, weights, order, count_y))
-    own_part = project(core_at, tokens, weights, order, count_y)
-    projected = interleaved(core_at, own_part, peer_part)
+    peer_part = swapped(project(place[0], peer_tokens, weights, order, count_y))
+    own_part = project(place[0], tokens, weights, order, count_y)
+    projected = interleaved(place[0], own_part, peer_part)
     return (projected, new_master, new_first, new_second)
 
 

time: 158 us -> 157 us (level)
  blocking collectives: 96.5 us -> 59 us
  waiting for transfers between devices: 8.07 us -> 39.4 us
  starting transfers between devices: 19.5 us -> 25.8 us
  Pallas kernels: 23.7 us -> 28.3 us
  other arithmetic: 4.16 us -> 1.83 us
  local copies, waits for them, and re-layouts: 3.27 us -> 1.02 us
    all_to_all x4 -> x2, blocking collectives: 84.1 us -> 42.9 us  [exchanged(): lax.all_to_all(value, FACE, 0, 0, tiled=True, axis_index_groups=face_grou...]
    all_to_all x1, waiting for transfers between devices: 8.06 us -> 24.5 us  [shards(): lax.all_to_all(lines, AXES, 0, 0, tiled=True, axis_index_groups=slab_grou...]
    ppermute x0 -> x6, waiting for transfers between devices: none -> 14.9 us  [shifted(): return lax.ppermute(value, FACE, pairs)]
    ppermute x0 -> x6, starting transfers between devices: none -> 6.9 us  [shifted(): return lax.ppermute(value, FACE, pairs)]
    all_to_all x1, blocking collectives: 12.4 us -> 16.2 us  [exchanged(): return lax.all_to_all(value, 'z', 0, 0, tiled=True)]
    ppermute x4, starting transfers between devices: 11.3 us -> 9.25 us  [swapped(): return lax.ppermute(value, 'c', [(0, 1), (1, 0)])]
    pallas_call x2, Pallas kernels: 5.16 us -> 7.18 us  [project(): pl.pallas_call(body, grid_spec=pltpu.PrefetchScalarGridSpec(num_scalar_pr...]
    pallas_call x2 -> x3, Pallas kernels: 16.6 us -> 18.3 us  [coded_gradient(): pl.pallas_call(body, grid_spec=pltpu.PrefetchScalarGridSpec(num_scalar_pr...]
  transfers between devices with their start and end apart: 5 -> 11, of which waited for: 1 -> 5; matrix products, arithmetic and copies ran while one was open for 1% -> 0% of each run, Pallas kernels for 7% -> 10%
where the time goes in v5:
time: 157 us; the launch traced here: 156 us
  blocking collectives  59 us (38%)
  waiting for transfers between devices  39.4 us (25%)
  Pallas kernels  28.3 us (18%)
  starting transfers between devices  25.8 us (16%)
  other arithmetic  1.83 us (1%)
    all_to_all x2, blocking collectives, exchanged(): lax.all_to_all(value, FACE, 0, 0, tiled=True, axis_index_groups=face_grou...  42.9 us
    all_to_all x1, waiting for transfers between devices, shards(): lax.all_to_all(lines, AXES, 0, 0, tiled=True, axis_index_groups=slab_grou...  24.5 us
    pallas_call x3, Pallas kernels, coded_gradient(): pl.pallas_call(body, grid_spec=pltpu.PrefetchScalarGridSpec(num_scalar_pr...  18.3 us
    all_to_all x1, blocking collectives, exchanged(): return lax.all_to_all(value, 'z', 0, 0, tiled=True)  16.2 us
    ppermute x6, waiting for transfers between devices, shifted(): return lax.ppermute(value, FACE, pairs)  14.9 us
    all_to_all x1, starting transfers between devices, shards(): lax.all_to_all(lines, AXES, 0, 0, tiled=True, axis_index_groups=slab_grou...  9.63 us
    ppermute x4, starting transfers between devices, swapped(): return lax.ppermute(value, 'c', [(0, 1), (1, 0)])  9.25 us
    pallas_call x2, Pallas kernels, project(): pl.pallas_call(body, grid_spec=pltpu.PrefetchScalarGridSpec(num_scalar_pr...  7.18 us
  transfers between devices with their start and end apart: 11, of which 5 were waited for; matrix products, arithmetic and copies ran while one was open for 0% of the time, Pallas kernels for 10%

profile of v5, /device:TPU:1, one launch (start us, length us, event | category | flops | bytes accessed | tf_op | source)
XLA Modules:
  0.0 156.5 jit_solution(16083986890087915290)
XLA Ops:
  0.6 3.3 %collective-permute-start = (bf16[384,4096]{1,0:T(8,128)(2,1)}, bf16[384,4096]{1,0:T(8,128)(2,1)}, u32[]{:S(2)}, u32[]{:S(2)}) collective-permute-start(bf16[384,4096]{1,0:T(8,128)(2,1)} %refs_1_.1), channel_id=1, source_target_pairs={{0,32},{32,0},{1,33},{33,1},{2,34},{34,2},{3,35},{35,3},{4,36},{36... | collective-permute-start | bytes 9437192 | tf_op jit(solution)/shard_map/ppermute | solution.py:289
  4.0 0.1 collective-permute-start.1
  4.1 0.4 collective-permute-start.2
  4.5 8.4 %shard_map.138.refs_12_ = bf16[512,4096]{1,0:T(8,128)(2,1)} custom-call(s32[1]{0:T(128)} %bitcast.refs_0_.core_ref, s32[1]{0:T(128)} %bitcast.1.refs_1_, s32[1]{0:T(128)} %bitcast.2.refs_2_, bf16[384,4096]{1,0:T(8,128)(2,1)} %refs_1_.1, bf16[384,1024]{1,0:T(8,128)(2,1)} %refs_7_.1, bf16[384,1024]{1,0:T(8,128)(2,1)} %refs_7_.1, bf16[384,1024]{1,0:T(8,128)(2,1)} %refs_7_.1, ...), custom_call_target="tpu_custom_call" | custom-call | tf_op jit(solution)/shard_map/pallas_call | solution.py:166
  12.9 0.0 collective-permute-done.2.refs_9_
  12.9 0.0 collective-permute-done.1.refs_4_.refs_5_.refs_6_.refs_7_
  12.9 0.0 collective-permute-done.refs_3_.refs_1_
  12.9 0.0 copy-done.1
  12.9 0.0 copy-done.2
  12.9 0.0 copy-done.3
  12.9 5.0 %shard_map.139 = (bf16[128,2048]{1,0:T(8,128)(2,1)S(1)}, bf16[128,2048]{1,0:T(8,128)(2,1)S(1)}, bf16[128,2048]{1,0:T(8,128)(2,1)S(1)}, bf16[128,2048]{1,0:T(8,128)(2,1)S(1)}) custom-call(s32[1]{0:T(128)} %bitcast.refs_0_.core_ref, s32[1]{0:T(128)} %bitcast.1.refs_1_, s32[1]{0:T(128)} %bitcast.2.refs_2_, ...), custom_call_target="tpu_custom_call" | custom-call | tf_op jit(solution)/shard_map/pallas_call | solution.py:166
  17.9 1.3 collective-permute-start.3
  19.2 0.4 collective-permute-start.4
  19.6 2.3 %collective-permute-start.5 = (bf16[128,2048]{1,0:T(8,128)(2,1)S(1)}, bf16[128,2048]{1,0:T(8,128)(2,1)S(1)}, u32[]{:S(2)}, u32[]{:S(2)}) collective-permute-start(bf16[128,2048]{1,0:T(8,128)(2,1)S(1)} %get-tuple-element.15), channel_id=1, source_target_pairs={{0,3},{1,0},{2,1},{3,2},{32,224},{33,225},{34,226},{35,227},{64,67... | collective-permute-start | bytes 1572872 | tf_op jit(solution)/shard_map/ppermute | solution.py:312
  21.9 4.9 %shard_map.140 = (bf16[128,2048]{1,0:T(8,128)(2,1)S(1)}, bf16[128,2048]{1,0:T(8,128)(2,1)S(1)}, bf16[128,2048]{1,0:T(8,128)(2,1)S(1)}, bf16[128,2048]{1,0:T(8,128)(2,1)S(1)}) custom-call(s32[1]{0:T(128)} %bitcast.refs_0_.core_ref, s32[1]{0:T(128)} %bitcast.1.refs_1_, s32[1]{0:T(128)} %bitcast.2.refs_2_, ...), custom_call_target="tpu_custom_call" | custom-call | tf_op jit(solution)/shard_map/pallas_call | solution.py:166
  26.8 0.0 copy-start.8
  26.8 0.7 collective-permute-start.6
  27.5 0.0 collective-permute-start.7
  27.5 0.4 collective-permute-done.3.refs_1_
  27.9 2.3 %collective-permute-start.8 = (bf16[128,2048]{1,0:T(8,128)(2,1)S(1)}, bf16[128,2048]{1,0:T(8,128)(2,1)S(1)}, u32[]{:S(2)}, u32[]{:S(2)}) collective-permute-start(bf16[128,2048]{1,0:T(8,128)(2,1)S(1)} %get-tuple-element.19), channel_id=1, source_target_pairs={{0,3},{1,0},{2,1},{3,2},{32,224},{33,225},{34,226},{35,227},{64,67... | collective-permute-start | bytes 1572872 | tf_op jit(solution)/shard_map/ppermute | solution.py:312
  30.2 3.3 %collective-permute-done.4.refs_2_ = bf16[128,2048]{1,0:T(8,128)(2,1)S(1)} collective-permute-done((bf16[128,2048]{1,0:T(8,128)(2,1)S(1)}, bf16[128,2048]{1,0:T(8,128)(2,1)S(1)}, u32[]{:S(2)}, u32[]{:S(2)}) %collective-permute-start.4) | collective-permute-done | bytes 524320 | tf_op jit(solution)/shard_map/ppermute | solution.py:312
  33.4 0.0 collective-permute-done.5.refs_3_
  33.4 5.7 %collective-permute-done.6.refs_5_ = bf16[128,2048]{1,0:T(8,128)(2,1)S(1)} collective-permute-done((bf16[128,2048]{1,0:T(8,128)(2,1)S(1)}, bf16[128,2048]{1,0:T(8,128)(2,1)S(1)}, u32[]{:S(2)}, u32[]{:S(2)}) %collective-permute-start.6) | collective-permute-done | bytes 524320 | tf_op jit(solution)/shard_map/ppermute | solution.py:312
  39.1 5.5 %collective-permute-done.7.refs_6_ = bf16[128,2048]{1,0:T(8,128)(2,1)S(1)} collective-permute-done((bf16[128,2048]{1,0:T(8,128)(2,1)S(1)}, bf16[128,2048]{1,0:T(8,128)(2,1)S(1)}, u32[]{:S(2)}, u32[]{:S(2)}) %collective-permute-start.7) | collective-permute-done | bytes 524320 | tf_op jit(solution)/shard_map/ppermute | solution.py:312
  44.7 0.0 collective-permute-done.8.refs_7_
  44.7 0.0 copy-start.7
  44.7 1.8 %shard_map.141 = bf16[32,8,2048]{2,1,0:T(8,128)(2,1)} custom-call(bf16[128,2048]{1,0:T(8,128)(2,1)S(1)} %get-tuple-element.12.refs_0_, bf16[128,2048]{1,0:T(8,128)(2,1)S(1)} %collective-permute-done.3.refs_1_, bf16[128,2048]{1,0:T(8,128)(2,1)S(1)} %collective-permute-done.4.refs_2_, bf16[128,2048]{1,0:T(8,128)(2,1)S(1)} %collective-permute-done.5.refs_3_, ...), custom_call_target="tpu_custom_call" | custom-call | tf_op jit(solution)/shard_map/pallas_call | solution.py:209
  46.5 9.6 %all-to-all-start = ((bf16[32,8,2048]{2,1,0:T(8,128)(2,1)}), bf16[32,8,2048]{2,1,0:T(8,128)(2,1)S(1)}, u32[]{:S(2)}, u32[]{:S(2)}) async-start(bf16[32,8,2048]{2,1,0:T(8,128)(2,1)} %shard_map.141), calls=%async_computation | async-start | bytes 2097152 | tf_op jit(solution)/shard_map/all_to_all | solution.py:370
  56.1 0.0 copy-done.8
  56.2 0.1 broadcast_bitcast_fusion
  56.3 24.5 %all-to-all-done = bf16[32,8,2048]{2,1,0:T(8,128)(2,1)S(1)} async-done(((bf16[32,8,2048]{2,1,0:T(8,128)(2,1)}), bf16[32,8,2048]{2,1,0:T(8,128)(2,1)S(1)}, u32[]{:S(2)}, u32[]{:S(2)}) %all-to-all-start) | async-done | bytes 1048608 | tf_op jit(solution)/shard_map/all_to_all | solution.py:370
  80.8 0.2 convert_reduce_fusion
  81.0 0.1 copy.15
  81.0 0.1 reshape_reshape.3
  81.1 0.2 convolution_multiply_fusion
  81.4 1.7 %fusion.3 = (bf16[4,4096]{1,0:T(4,128)(2,1)S(1)}, f32[4,4096]{1,0:T(4,128)}, f32[4,4096]{1,0:T(4,128)}, f32[4,4096]{1,0:T(4,128)}) fusion(bf16[1,4,32,128]{3,2,1,0:T(8,128)(2,1)S(1)} %get-tuple-element.26, bf16[1,4,32,128]{3,2,1,0:T(8,128)(2,1)S(1)} %get-tuple-element.27, bf16[1024,4096]{1,0:T(8,128)(2,1)} %param.14, s32[]{:T(128)S(6)} %select_n.3, ...), kind=kLoop, calls=%fused_computation.8 | loop fusion | flops 409600 | bytes 606212 | tf_op jit(solution)/shard_map/convert_element_type | solution.py:381
  83.0 0.1 broadcast_in_dim.8
  83.1 16.2 %all_to_all.20 = bf16[8,4,4096]{2,1,0:T(4,128)(2,1)S(1)} all-to-all(bf16[8,4,4096]{2,1,0:T(4,128)(2,1)S(1)} %broadcast_in_dim.8), channel_id=1, replica_groups=mesh['y'=4,'c'=2,'z'=8,'x'=4] {'z'}, dimensions={0} | all-to-all | bytes 524288 | tf_op jit(solution)/shard_map/all_to_all | solution.py:323
  99.3 0.1 broadcast_in_dim.9
  99.3 0.1 broadcast_in_dim.10
  99.4 12.2 %all_to_all.21 = bf16[4,32,4096]{2,1,0:T(8,128)(2,1)S(1)} all-to-all(bf16[4,32,4096]{2,1,0:T(8,128)(2,1)S(1)} %broadcast_in_dim.10), channel_id=1, replica_groups={{0,64,128,192},{1,65,129,193},{2,66,130,194},{3,67,131,195},{32,33,34,3..., dimensions={0} | all-to-all | bytes 2097152 | tf_op jit(solution)/shard_map/all_to_all | solution.py:324
  111.6 0.5 broadcast_in_dim.11
  112.1 30.7 %all_to_all.22.refs_2_ = bf16[4,4,32,4096]{3,2,1,0:T(8,128)(2,1)S(1)} all-to-all(bf16[4,4,32,4096]{3,2,1,0:T(8,128)(2,1)S(1)} %broadcast_in_dim.11), channel_id=1, replica_groups={{0,1,2,3},{64,65,66,67},{128,129,130,131},{192,193,194,195},{32,96,160,..., dimensions={0} | all-to-all | bytes 8388608 | tf_op jit(solution)/shard_map/all_to_all | solution.py:324
  142.8 4.6 %shard_map.143 = bf16[384,512]{1,0:T(8,128)(2,1)S(1)} custom-call(s32[1]{0:T(128)} %bitcast.refs_0_.core_ref, bf16[384,4096]{1,0:T(8,128)(2,1)} %collective-permute-done.refs_3_.refs_1_, bf16[4,4,32,4096]{3,2,1,0:T(8,128)(2,1)S(1)} %all_to_all.22.refs_2_, bf16[128,128]{1,0:T(8,128)(2,1)S(1)} %copy-done.1), custom_call_target="tpu_custom_call" | custom-call | tf_op jit(solution)/shard_map/pallas_call | solution.py:248
  147.4 5.4 %collective-permute-start.9 = (bf16[384,512]{1,0:T(8,128)(2,1)S(1)}, bf16[384,512]{1,0:T(8,128)(2,1)S(1)}, u32[]{:S(2)}, u32[]{:S(2)}) collective-permute-start(bf16[384,512]{1,0:T(8,128)(2,1)S(1)} %shard_map.143), channel_id=1, source_target_pairs={{0,32},{32,0},{1,33},{33,1},{2,34},{34,2},{3,35},{35,3},{4,36},{36... | collective-permute-start | bytes 1179656 | tf_op jit(solution)/shard_map/ppermute | solution.py:289
  152.8 2.6 %shard_map.142.own_ref = bf16[384,512]{1,0:T(8,128)(2,1)S(1)} custom-call(s32[1]{0:T(128)} %bitcast.refs_0_.core_ref, bf16[384,4096]{1,0:T(8,128)(2,1)S(1)} %copy-done, bf16[4,4,32,4096]{3,2,1,0:T(8,128)(2,1)S(1)} %all_to_all.22.refs_2_, bf16[128,128]{1,0:T(8,128)(2,1)S(1)} %copy-done.1), custom_call_target="tpu_custom_call" | custom-call | tf_op jit(solution)/shard_map/pallas_call | solution.py:248
  155.4 0.0 collective-permute-done.9.peer_ref
  155.4 1.0 shard_map.144
  (16 shorter events, 0.1 us)
Async XLA Ops:
  0.6 12.3 %collective-permute-start = (bf16[384,4096]{1,0:T(8,128)(2,1)}, bf16[384,4096]{1,0:T(8,128)(2,1)}, u32[]{:S(2)}, u32[]{:S(2)}) collective-permute-start(bf16[384,4096]{1,0:T(8,128)(2,1)} %refs_1_.1), channel_id=1, source_target_pairs={{0,32},{32,0},{1,33},{33,1},{2,34},{34,2},{3,35},{35,3},{4,36},{36... | collective-permute-start | bytes 9437192 | tf_op jit(solution)/shard_map/ppermute | solution.py:289
  4.0 8.9 %collective-permute-start.1 = (bf16[384,1024]{1,0:T(8,128)(2,1)}, bf16[384,1024]{1,0:T(8,128)(2,1)S(1)}, u32[]{:S(2)}, u32[]{:S(2)}) collective-permute-start(bf16[384,1024]{1,0:T(8,128)(2,1)} %refs_7_.1), channel_id=1, source_target_pairs={{0,32},{32,0},{1,33},{33,1},{2,34},{34,2},{3,35},{35,3},{4,36},{36... | collective-permute-start | bytes 2359304 | tf_op jit(solution)/shard_map/ppermute | solution.py:289
  4.1 8.8 %collective-permute-start.2 = (s32[8,32]{1,0:T(8,128)}, s32[8,32]{1,0:T(8,128)S(1)}, u32[]{:S(2)}, u32[]{:S(2)}) collective-permute-start(s32[8,32]{1,0:T(8,128)} %bitcast.22), channel_id=1, source_target_pairs={{0,32},{32,0},{1,33},{33,1},{2,34},{34,2},{3,35},{35,3},{4,36},{36... | collective-permute-start | bytes 3080 | tf_op jit(solution)/shard_map/ppermute | solution.py:289
  4.5 8.4 %copy-start.1 = (bf16[128,128]{1,0:T(8,128)(2,1)S(1)}, bf16[128,128]{1,0:T(8,128)(2,1)}, u32[]{:S(2)}) copy-start(bf16[128,128]{1,0:T(8,128)(2,1)} %constant.75.refs_11_.refs_3_) | copy-start | bytes 98308
  4.5 8.4 %copy-start.2 = (bf16[128,128]{1,0:T(8,128)(2,1)S(1)}, bf16[128,128]{1,0:T(8,128)(2,1)}, u32[]{:S(2)}) copy-start(bf16[128,128]{1,0:T(8,128)(2,1)} %constant.74.refs_10_) | copy-start | bytes 98308
  4.5 8.4 %copy-start.3 = (s32[32,128]{1,0:T(8,128)S(1)}, s32[32,128]{1,0:T(8,128)}, u32[]{:S(2)}) copy-start(s32[32,128]{1,0:T(8,128)} %refs_8_.5) | copy-start | bytes 49156
  17.9 10.0 %collective-permute-start.3 = (bf16[128,2048]{1,0:T(8,128)(2,1)S(1)}, bf16[128,2048]{1,0:T(8,128)(2,1)S(1)}, u32[]{:S(2)}, u32[]{:S(2)}) collective-permute-start(bf16[128,2048]{1,0:T(8,128)(2,1)S(1)} %get-tuple-element.13), channel_id=1, source_target_pairs={{0,2},{1,3},{2,0},{3,1},{32,160},{33,161},{34,162},{35,163},{64,66... | collective-permute-start | bytes 1572872 | tf_op jit(solution)/shard_map/ppermute | solution.py:312
  19.2 14.3 %collective-permute-start.4 = (bf16[128,2048]{1,0:T(8,128)(2,1)S(1)}, bf16[128,2048]{1,0:T(8,128)(2,1)S(1)}, u32[]{:S(2)}, u32[]{:S(2)}) collective-permute-start(bf16[128,2048]{1,0:T(8,128)(2,1)S(1)} %get-tuple-element.14), channel_id=1, source_target_pairs={{0,1},{1,2},{2,3},{3,0},{32,96},{33,97},{34,98},{35,99},{64,65},{6... | collective-permute-start | bytes 1572872 | tf_op jit(solution)/shard_map/ppermute | solution.py:312
  19.6 13.9 %collective-permute-start.5 = (bf16[128,2048]{1,0:T(8,128)(2,1)S(1)}, bf16[128,2048]{1,0:T(8,128)(2,1)S(1)}, u32[]{:S(2)}, u32[]{:S(2)}) collective-permute-start(bf16[128,2048]{1,0:T(8,128)(2,1)S(1)} %get-tuple-element.15), channel_id=1, source_target_pairs={{0,3},{1,0},{2,1},{3,2},{32,224},{33,225},{34,226},{35,227},{64,67... | collective-permute-start | bytes 1572872 | tf_op jit(solution)/shard_map/ppermute | solution.py:312
  26.8 29.4 %copy-start.8 = (s32[4,32]{1,0:T(4,128)S(1)}, s32[4,32]{1,0:T(4,128)}, u32[]{:S(2)}) copy-start(s32[4,32]{1,0:T(4,128)} %param.18) | copy-start | bytes 1540
  26.8 12.3 %collective-permute-start.6 = (bf16[128,2048]{1,0:T(8,128)(2,1)S(1)}, bf16[128,2048]{1,0:T(8,128)(2,1)S(1)}, u32[]{:S(2)}, u32[]{:S(2)}) collective-permute-start(bf16[128,2048]{1,0:T(8,128)(2,1)S(1)} %get-tuple-element.17), channel_id=1, source_target_pairs={{0,2},{1,3},{2,0},{3,1},{32,160},{33,161},{34,162},{35,163},{64,66... | collective-permute-start | bytes 1572872 | tf_op jit(solution)/shard_map/ppermute | solution.py:312
  27.5 17.2 %collective-permute-start.7 = (bf16[128,2048]{1,0:T(8,128)(2,1)S(1)}, bf16[128,2048]{1,0:T(8,128)(2,1)S(1)}, u32[]{:S(2)}, u32[]{:S(2)}) collective-permute-start(bf16[128,2048]{1,0:T(8,128)(2,1)S(1)} %get-tuple-element.18), channel_id=1, source_target_pairs={{0,1},{1,2},{2,3},{3,0},{32,96},{33,97},{34,98},{35,99},{64,65},{6... | collective-permute-start | bytes 1572872 | tf_op jit(solution)/shard_map/ppermute | solution.py:312
  27.9 16.8 %collective-permute-start.8 = (bf16[128,2048]{1,0:T(8,128)(2,1)S(1)}, bf16[128,2048]{1,0:T(8,128)(2,1)S(1)}, u32[]{:S(2)}, u32[]{:S(2)}) collective-permute-start(bf16[128,2048]{1,0:T(8,128)(2,1)S(1)} %get-tuple-element.19), channel_id=1, source_target_pairs={{0,3},{1,0},{2,1},{3,2},{32,224},{33,225},{34,226},{35,227},{64,67... | collective-permute-start | bytes 1572872 | tf_op jit(solution)/shard_map/ppermute | solution.py:312
  44.7 36.4 %copy-start.4 = (f32[128,128]{1,0:T(8,128)S(1)}, f32[128,128]{1,0:T(8,128)}, u32[]{:S(2)}) copy-start(f32[128,128]{1,0:T(8,128)} %constant.65.clone) | copy-start | bytes 196612
  44.7 36.6 %copy-start.5 = (f32[4,4096]{1,0:T(4,128)S(1)}, f32[4,4096]{1,0:T(4,128)}, u32[]{:S(2)}) copy-start(f32[4,4096]{1,0:T(4,128)} %param.13) | copy-start | bytes 196612
  44.7 36.7 %copy-start.6 = (f32[4,4096]{1,0:T(4,128)S(1)}, f32[4,4096]{1,0:T(4,128)}, u32[]{:S(2)}) copy-start(f32[4,4096]{1,0:T(4,128)} %param.15) | copy-start | bytes 196612
  44.7 36.7 %copy-start.7 = (f32[4,4096]{1,0:T(4,128)S(1)}, f32[4,4096]{1,0:T(4,128)}, u32[]{:S(2)}) copy-start(f32[4,4096]{1,0:T(4,128)} %param.16) | copy-start | bytes 196612
  46.5 34.3 %all-to-all-start = ((bf16[32,8,2048]{2,1,0:T(8,128)(2,1)}), bf16[32,8,2048]{2,1,0:T(8,128)(2,1)S(1)}, u32[]{:S(2)}, u32[]{:S(2)}) async-start(bf16[32,8,2048]{2,1,0:T(8,128)(2,1)} %shard_map.141), calls=%async_computation | async-start | bytes 2097152 | tf_op jit(solution)/shard_map/all_to_all | solution.py:370
  142.8 10.0 %copy-start = (bf16[384,4096]{1,0:T(8,128)(2,1)S(1)}, bf16[384,4096]{1,0:T(8,128)(2,1)}, u32[]{:S(2)}) copy-start(bf16[384,4096]{1,0:T(8,128)(2,1)} %refs_1_.1) | copy-start | bytes 9437188
  147.4 8.0 %collective-permute-start.9 = (bf16[384,512]{1,0:T(8,128)(2,1)S(1)}, bf16[384,512]{1,0:T(8,128)(2,1)S(1)}, u32[]{:S(2)}, u32[]{:S(2)}) collective-permute-start(bf16[384,512]{1,0:T(8,128)(2,1)S(1)} %shard_map.143), channel_id=1, source_target_pairs={{0,32},{32,0},{1,33},{33,1},{2,34},{34,2},{3,35},{35,3},{4,36},{36... | collective-permute-start | bytes 1179656 | tf_op jit(solution)/shard_map/ppermute | solution.py:289

commit v6 on v5

--- a/solution.py
+++ b/solution.py
@@ -216,50 +216,71 @@
     )(*left_terms, *right_terms)
 
 
-def project_kernel(pair, core_ref, tok_ref, weight_ref, order_ref, out_ref):
-    tile = order_ref.shape[0]
-    core = core_ref[0]
-    rows = []
-    for at in range(pair):
-        group = pl.program_id(0) * pair + at
-        for spot in range(tile // weight_ref.shape[2]):
-            first = jnp.where(core == 0, spot, group)
-            second = jnp.where(core == 0, group, spot)
-            rows.append(weight_ref[first, second])
-    total = lax.dot_general(
-        tok_ref[...],
-        jnp.concatenate(rows, axis=0),
-        (((1,), (1,)), ((), ())),
-        preferred_element_type=jnp.float32,
-    )
-    rounded = total.astype(jnp.bfloat16)
-    for at in range(pair):
-        cols = slice(at * tile, (at + 1) * tile)
-        out_ref[:, cols] = jnp.dot(
-            rounded[:, cols], order_ref[...], preferred_element_type=jnp.float32
-        ).astype(jnp.bfloat16)
-
-
-def project(core, tokens, weights, order, groups):
-    token_rows = tokens.shape[0]
-    tile = order.shape[0]
-    pair = 2
-    body = lambda *refs: project_kernel(pair, *refs)
+def face_kernel(parts_ref, out_ref):
+    total = parts_ref[0].astype(jnp.float32)
+    for at in range(1, parts_ref.shape[0]):
+        total = total + parts_ref[at].astype(jnp.float32)
+    out_ref[...] = total.astype(jnp.bfloat16)
+
+
+def face_sum(parts):
+    count, count_z, rows, half = parts.shape
+    width = 1024
+    return pl.pallas_call(
+        face_kernel,
+        grid=(half // width,),
+        in_specs=[pl.BlockSpec((count, count_z, rows, width), lambda n: (0, 0, 0, n))],
+        out_specs=pl.BlockSpec((count_z, rows, width), lambda n: (0, 0, n)),
+        out_shape=jax.ShapeDtypeStruct((count_z, rows, half), jnp.bfloat16),
+        compiler_params=pltpu.CompilerParams(vmem_limit_bytes=16 << 20),
+    )(parts)
+
+
+def product(tok_ref, weight_refs):
+    weights = jnp.concatenate([ref[...] for ref in weight_refs], axis=0)
+    return lax.dot_general(
+        tok_ref[...], weights, (((1,), (1,)), ((), ())), preferred_element_type=jnp.float32
+    ).astype(jnp.bfloat16)
+
+
+def early_kernel(tok_ref, *refs):
+    refs[-1][...] = product(tok_ref, refs[:-1])
+
+
+def early_product(tokens, weights):
+    whole = pl.BlockSpec(memory_space=pltpu.VMEM)
+    columns = sum(value.shape[0] for value in weights)
+    return pl.pallas_call(
+        early_kernel,
+        in_specs=[whole] * (1 + len(weights)),
+        out_specs=whole,
+        out_shape=jax.ShapeDtypeStruct((tokens.shape[0], columns), jnp.bfloat16),
+        compiler_params=pltpu.CompilerParams(vmem_limit_bytes=20 << 20),
+    )(tokens, *weights)
+
+
+def late_kernel(count, tok_ref, spread_ref, *refs):
+    pieces = [ref[...] for ref in refs[:count]]
+    pieces.append(product(tok_ref, refs[count:-1]))
+    start, out = 0, None
+    for piece in pieces:
+        stop = start + piece.shape[1]
+        part = jnp.dot(piece, spread_ref[start:stop, :], preferred_element_type=jnp.float32)
+        out = part if out is None else out + part
+        start = stop
+    refs[-1][...] = out.astype(jnp.bfloat16)
+
+
+def late_product(tokens, spread, done, weights):
+    whole = pl.BlockSpec(memory_space=pltpu.VMEM)
+    body = lambda *refs: late_kernel(len(done), *refs)
     return pl.pallas_call(
         body,
-        grid_spec=pltpu.PrefetchScalarGridSpec(
-            num_scalar_prefetch=1,
-            grid=(groups // pair,),
-            in_specs=[
-                pl.BlockSpec(tokens.shape, lambda n, core: (0, 0)),
-                pl.BlockSpec(weights.shape, lambda n, core: (0, 0, 0, 0)),
-                pl.BlockSpec(order.shape, lambda n, core: (0, 0)),
-            ],
-            out_specs=pl.BlockSpec((token_rows, pair * tile), lambda n, core: (0, n)),
-        ),
-        out_shape=jax.ShapeDtypeStruct((token_rows, groups * tile), jnp.bfloat16),
-        compiler_params=pltpu.CompilerParams(vmem_limit_bytes=32 << 20),
-    )(core, tokens, weights, order)
+        in_specs=[whole] * (2 + len(done) + len(weights)),
+        out_specs=whole,
+        out_shape=jax.ShapeDtypeStruct((tokens.shape[0], spread.shape[1]), jnp.bfloat16),
+        compiler_params=pltpu.CompilerParams(vmem_limit_bytes=20 << 20),
+    )(tokens, spread, *done, *weights)
 
 
 def interleave_kernel(core_ref, own_ref, peer_ref, out_ref):
@@ -312,10 +333,21 @@
     return lax.ppermute(value, FACE, pairs)
 
 
-def slab_groups():
-    at = lambda y, c, z, x: ((y * 2 + c) * 8 + z) * 4 + x
-    groups = [[at(y, 0, z, x) for y in range(4) for z in range(8)] for x in range(4)]
-    return groups + [[at(y, 1, z, x) for x in range(4) for z in range(8)] for y in range(4)]
+def column_spread(place, offsets, count_z, rows_dev):
+    core, at_x, at_y = place
+    shift = jnp.asarray([offset[0] for offset in offsets], jnp.int32)
+    second = jnp.asarray([offset[1] for offset in offsets], jnp.int32)
+    from_x = jnp.where(core == 0, (at_x - shift) % 4, second)
+    from_y = jnp.where(core == 0, second, (at_y - shift) % 4)
+    at_z = jnp.arange(count_z, dtype=jnp.int32)[None, :, None]
+    at_j = jnp.arange(rows_dev, dtype=jnp.int32)[None, None, :]
+    column = (
+        (from_y[:, None, None] * count_z + at_z) * 4 + from_x[:, None, None]
+    ) * rows_dev + at_j
+    size = len(offsets) * count_z * rows_dev
+    return (column.reshape(size, 1) == jnp.arange(size, dtype=jnp.int32)[None, :]).astype(
+        jnp.bfloat16
+    )
 
 
 def exchanged(value, step):
@@ -341,12 +373,12 @@
     diff_exps,
     hadamard_signs,
 ):
-    count_y, count_z, count_x = (lax.axis_size(axis) for axis in ("y", "z", "x"))
+    count_z = lax.axis_size("z")
     rows_dev, model_width = master_weights.shape
     sign_rows = (2 * hadamard_signs - 1).astype(jnp.float32)
     block_len = sign_rows.shape[1]
     matrix = jnp.asarray(hadamard(block_len))
-    order = jnp.asarray(row_order(count_z, count_x, rows_dev))
+    order = jnp.asarray(row_order(count_z, 4, rows_dev))
     place = [lax.axis_index(axis).reshape(1).astype(jnp.int32) for axis in ("c", "x", "y")]
     exps = grad_exps[0]
     peer_tokens, peer_grad, peer_exps = swapped(tokens), swapped(out_grad), swapped(exps)
@@ -367,7 +399,8 @@
         )
         halves.append([pair_sums[0], *(shifted(pair_sums[far], 0, far) for far in (2, 1, 3))])
     lines = line_sums(*halves)
-    parts = lax.all_to_all(lines, AXES, 0, 0, tiled=True, axis_index_groups=slab_groups())
+    lines = exchanged(lines.reshape(4, count_z, 2 * rows_dev, -1), "second")
+    parts = exchanged(face_sum(lines), "z")
     summed = jnp.sum(parts.astype(jnp.float32), axis=0)
     summed = jnp.swapaxes(summed.reshape(2, rows_dev, -1), 0, 1).reshape(rows_dev, model_width)
     gradient = unrotate_rows(summed, sign_rows, matrix)
@@ -380,9 +413,20 @@
     diff_coded = clip_rows(new_master - base_own, diff_bound).astype(jnp.bfloat16)
     effective = (base_own + diff_coded.astype(jnp.float32)).astype(jnp.bfloat16)
     stacked = gathered(effective, count_z, "z").reshape(count_z * rows_dev, model_width)
-    weights = gathered(gathered(stacked, count_y, "second"), count_x, "first")
-    peer_part = swapped(project(place[0], peer_tokens, weights, order, count_y))
-    own_part = project(place[0], tokens, weights, order, count_y)
+    face = gathered(stacked, 4, "second").reshape(-1, model_width)
+    middle = face.shape[0] // 2
+    sent = [face[:middle], face[middle:]]
+    arrived = [[shifted(rows, 0, far) for far in (2, 1, 3)] for rows in sent]
+    offsets = [(0, at) for at in range(4)]
+    offsets += [(far, at) for start in (0, 2) for far in (2, 1, 3) for at in (start, start + 1)]
+    spread = column_spread(place, offsets, count_z, rows_dev)
+    done = [
+        [early_product(rows, [face]), early_product(rows, arrived[0])]
+        for rows in (tokens, peer_tokens)
+    ]
+    done, last = lax.optimization_barrier((done, arrived[1]))
+    peer_part = swapped(late_product(peer_tokens, spread, done[1], last))
+    own_part = late_product(tokens, spread, done[0], last)
     projected = interleaved(place[0], own_part, peer_part)
     return (projected, new_master, new_first, new_second)
 

time: 157 us -> 151 us (0.962); the launches traced: 156 us -> 149 us
  blocking collectives: 59 us -> 37.2 us
  starting transfers between devices: 25.8 us -> 32.8 us
  waiting for transfers between devices: 39.4 us -> 32.7 us
  local copies, waits for them, and re-layouts: 1.02 us -> 7.52 us
  Pallas kernels: 28.3 us -> 33.2 us
  other arithmetic: 1.83 us -> 3.42 us
    all_to_all x2, blocking collectives: 42.9 us -> 24.7 us  [exchanged(): lax.all_to_all(value, FACE, 0, 0, tiled=True, axis_index_groups=face_grou...]
    all_to_all x1, waiting for transfers between devices: 24.5 us -> 8.66 us  [exchanged(): return lax.all_to_all(value, 'z', 0, 0, tiled=True)]
    ppermute x6 -> x12, waiting for transfers between devices: 14.9 us -> 24 us  [shifted(): return lax.ppermute(value, FACE, pairs)]
    ppermute x6 -> x12, starting transfers between devices: 6.9 us -> 14.4 us  [shifted(): return lax.ppermute(value, FACE, pairs)]
    pallas_call x2 -> x7, Pallas kernels: 7.18 us -> 13 us  [the longest x4 6.33 us: early_product(): pl.pallas_call(early_kernel, in_specs=[whole] * (1 + len(weights)), out_s...]
    unnamed x19, local copies, waits for them, and re-layouts: 0.14 us -> 5.02 us
    all_to_all x1, blocking collectives: 16.2 us -> 12.5 us  [exchanged(): return lax.all_to_all(value, 'z', 0, 0, tiled=True)]
    all_to_all x1, starting transfers between devices: 9.63 us -> 7.64 us  [exchanged(): return lax.all_to_all(value, 'z', 0, 0, tiled=True)]
  transfers between devices with their start and end apart: 11 -> 17, of which waited for: 5 -> 8; matrix products, arithmetic and copies ran while one was open for 0% -> 1% of each run, Pallas kernels for 10% -> 15%
where the time goes in v6:
time: 151 us; the launch traced here: 149 us
  blocking collectives  37.2 us (25%)
  Pallas kernels  33.2 us (22%)
  starting transfers between devices  32.8 us (22%)
  waiting for transfers between devices  32.7 us (22%)
  local copies, waits for them, and re-layouts  7.52 us (5%)
  other arithmetic  3.42 us (2%)
    all_to_all x2, blocking collectives, exchanged(): lax.all_to_all(value, FACE, 0, 0, tiled=True, axis_index_groups=face_grou...  24.7 us
    ppermute x12, waiting for transfers between devices, shifted(): return lax.ppermute(value, FACE, pairs)  24 us
    pallas_call x3, Pallas kernels, coded_gradient(): pl.pallas_call(body, grid_spec=pltpu.PrefetchScalarGridSpec(num_scalar_pr...  18.1 us
    ppermute x12, starting transfers between devices, shifted(): return lax.ppermute(value, FACE, pairs)  14.4 us
    all_to_all x1, blocking collectives, exchanged(): return lax.all_to_all(value, 'z', 0, 0, tiled=True)  12.5 us
    ppermute x4, starting transfers between devices, swapped(): return lax.ppermute(value, 'c', [(0, 1), (1, 0)])  10.8 us
    all_to_all x1, waiting for transfers between devices, exchanged(): return lax.all_to_all(value, 'z', 0, 0, tiled=True)  8.66 us
    all_to_all x1, starting transfers between devices, exchanged(): return lax.all_to_all(value, 'z', 0, 0, tiled=True)  7.64 us
  transfers between devices with their start and end apart: 17, of which 8 were waited for; matrix products, arithmetic and copies ran while one was open for 1% of the time, Pallas kernels for 15%

profile of v6, /device:TPU:1, one launch (start us, length us, event | category | flops | bytes accessed | tf_op | source)
XLA Modules:
  0.0 148.8 jit_solution(17301639554880690626)
XLA Ops:
  0.6 3.3 %collective-permute-start = (bf16[384,4096]{1,0:T(8,128)(2,1)}, bf16[384,4096]{1,0:T(8,128)(2,1)S(1)}, u32[]{:S(2)}, u32[]{:S(2)}) collective-permute-start(bf16[384,4096]{1,0:T(8,128)(2,1)} %refs_0_.1), channel_id=1, source_target_pairs={{0,32},{32,0},{1,33},{33,1},{2,34},{34,2},{3,35},{35,3},{4,36},{36... | collective-permute-start | bytes 9437192 | tf_op jit(solution)/shard_map/ppermute | solution.py:310
  4.1 0.4 collective-permute-start.2
  4.5 8.4 %shard_map.156.refs_12_ = bf16[512,4096]{1,0:T(8,128)(2,1)} custom-call(s32[1]{0:T(128)} %bitcast.refs_0_.core_ref, s32[1]{0:T(128)} %bitcast.2.refs_1_, s32[1]{0:T(128)} %bitcast.3.refs_2_, bf16[384,4096]{1,0:T(8,128)(2,1)} %refs_0_.1, bf16[384,1024]{1,0:T(8,128)(2,1)} %refs_7_.1, bf16[384,1024]{1,0:T(8,128)(2,1)} %refs_7_.1, bf16[384,1024]{1,0:T(8,128)(2,1)} %refs_7_.1, ...), custom_call_target="tpu_custom_call" | custom-call | tf_op jit(solution)/shard_map/pallas_call | solution.py:166
  12.9 4.9 %shard_map.157 = (bf16[128,2048]{1,0:T(8,128)(2,1)S(1)}, bf16[128,2048]{1,0:T(8,128)(2,1)S(1)}, bf16[128,2048]{1,0:T(8,128)(2,1)S(1)}, bf16[128,2048]{1,0:T(8,128)(2,1)S(1)}) custom-call(s32[1]{0:T(128)} %bitcast.refs_0_.core_ref, s32[1]{0:T(128)} %bitcast.2.refs_1_, s32[1]{0:T(128)} %bitcast.3.refs_2_, ...), custom_call_target="tpu_custom_call" | custom-call | tf_op jit(solution)/shard_map/pallas_call | solution.py:166
  17.8 1.3 collective-permute-start.3
  19.1 0.4 collective-permute-start.4
  19.5 2.3 %collective-permute-start.5 = (bf16[128,2048]{1,0:T(8,128)(2,1)S(1)}, bf16[128,2048]{1,0:T(8,128)(2,1)S(1)}, u32[]{:S(2)}, u32[]{:S(2)}) collective-permute-start(bf16[128,2048]{1,0:T(8,128)(2,1)S(1)} %get-tuple-element.22), channel_id=1, source_target_pairs={{0,3},{1,0},{2,1},{3,2},{32,224},{33,225},{34,226},{35,227},{64,67... | collective-permute-start | bytes 1572872 | tf_op jit(solution)/shard_map/ppermute | solution.py:333
  21.8 4.8 %shard_map.158 = (bf16[128,2048]{1,0:T(8,128)(2,1)S(1)}, bf16[128,2048]{1,0:T(8,128)(2,1)S(1)}, bf16[128,2048]{1,0:T(8,128)(2,1)S(1)}, bf16[128,2048]{1,0:T(8,128)(2,1)S(1)}) custom-call(s32[1]{0:T(128)} %bitcast.refs_0_.core_ref, s32[1]{0:T(128)} %bitcast.2.refs_1_, s32[1]{0:T(128)} %bitcast.3.refs_2_, ...), custom_call_target="tpu_custom_call" | custom-call | tf_op jit(solution)/shard_map/pallas_call | solution.py:166
  26.6 0.7 collective-permute-start.6
  27.3 0.5 collective-permute-done.3.refs_1_
  27.8 2.2 %collective-permute-start.8 = (bf16[128,2048]{1,0:T(8,128)(2,1)S(1)}, bf16[128,2048]{1,0:T(8,128)(2,1)S(1)}, u32[]{:S(2)}, u32[]{:S(2)}) collective-permute-start(bf16[128,2048]{1,0:T(8,128)(2,1)S(1)} %get-tuple-element.26), channel_id=1, source_target_pairs={{0,3},{1,0},{2,1},{3,2},{32,224},{33,225},{34,226},{35,227},{64,67... | collective-permute-start | bytes 1572872 | tf_op jit(solution)/shard_map/ppermute | solution.py:333
  30.0 3.4 %collective-permute-done.4.refs_2_ = bf16[128,2048]{1,0:T(8,128)(2,1)S(1)} collective-permute-done((bf16[128,2048]{1,0:T(8,128)(2,1)S(1)}, bf16[128,2048]{1,0:T(8,128)(2,1)S(1)}, u32[]{:S(2)}, u32[]{:S(2)}) %collective-permute-start.4) | collective-permute-done | bytes 524320 | tf_op jit(solution)/shard_map/ppermute | solution.py:333
  33.4 5.7 %collective-permute-done.6.refs_5_ = bf16[128,2048]{1,0:T(8,128)(2,1)S(1)} collective-permute-done((bf16[128,2048]{1,0:T(8,128)(2,1)S(1)}, bf16[128,2048]{1,0:T(8,128)(2,1)S(1)}, u32[]{:S(2)}, u32[]{:S(2)}) %collective-permute-start.6) | collective-permute-done | bytes 524320 | tf_op jit(solution)/shard_map/ppermute | solution.py:333
  39.1 5.5 %collective-permute-done.7.refs_6_ = bf16[128,2048]{1,0:T(8,128)(2,1)S(1)} collective-permute-done((bf16[128,2048]{1,0:T(8,128)(2,1)S(1)}, bf16[128,2048]{1,0:T(8,128)(2,1)S(1)}, u32[]{:S(2)}, u32[]{:S(2)}) %collective-permute-start.7) | collective-permute-done | bytes 524320 | tf_op jit(solution)/shard_map/ppermute | solution.py:333
  44.6 1.1 shard_map.159
  45.7 12.5 %all_to_all.20.parts_ref = bf16[4,8,8,2048]{3,2,1,0:T(8,128)(2,1)S(1)} all-to-all(bf16[4,8,8,2048]{3,2,1,0:T(8,128)(2,1)S(1)} %bitcast.28), channel_id=1, replica_groups={{0,64,128,192},{1,65,129,193},{2,66,130,194},{3,67,131,195},{32,33,34,3..., dimensions={0} | all-to-all | bytes 2097152 | tf_op jit(solution)/shard_map/all_to_all | solution.py:356
  58.2 0.9 shard_map.160
  59.1 7.6 %all-to-all-start.1 = ((bf16[8,8,2048]{2,1,0:T(8,128)(2,1)}), bf16[8,8,2048]{2,1,0:T(8,128)(2,1)S(1)}, u32[]{:S(2)}, u32[]{:S(2)}) async-start(bf16[8,8,2048]{2,1,0:T(8,128)(2,1)} %shard_map.160), calls=%async_computation.1 | async-start | bytes 524288 | tf_op jit(solution)/shard_map/all_to_all | solution.py:355
  66.8 0.6 convert_bitcast_fusion
  67.5 8.7 %all-to-all-done.1 = bf16[8,8,2048]{2,1,0:T(8,128)(2,1)S(1)} async-done(((bf16[8,8,2048]{2,1,0:T(8,128)(2,1)}), bf16[8,8,2048]{2,1,0:T(8,128)(2,1)S(1)}, u32[]{:S(2)}, u32[]{:S(2)}) %all-to-all-start.1) | async-done | bytes 262176 | tf_op jit(solution)/shard_map/all_to_all | solution.py:355
  76.3 1.0 convolution_multiply_fusion
  77.4 1.8 %fusion.4 = (bf16[4,4096]{1,0:T(4,128)(2,1)S(1)}, f32[4,4096]{1,0:T(4,128)}, f32[4,4096]{1,0:T(4,128)}, f32[4,4096]{1,0:T(4,128)}) fusion(bf16[1,4,32,128]{3,2,1,0:T(8,128)(2,1)S(1)} %get-tuple-element.44, bf16[1,4,32,128]{3,2,1,0:T(8,128)(2,1)S(1)} %get-tuple-element.45, bf16[1024,4096]{1,0:T(8,128)(2,1)} %param.16, s32[]{:T(128)S(6)} %select_n.26, ...), kind=kLoop, calls=%fused_computation.10 | loop fusion | flops 409600 | bytes 606212 | tf_op jit(solution)/shard_map/convert_element_type | solution.py:414
  79.3 12.5 %all_to_all.21 = bf16[8,4,4096]{2,1,0:T(4,128)(2,1)} all-to-all(bf16[8,4,4096]{2,1,0:T(4,128)(2,1)S(1)} %broadcast_in_dim.24), channel_id=1, replica_groups=mesh['y'=4,'c'=2,'z'=8,'x'=4] {'z'}, dimensions={0} | all-to-all | bytes 524288 | tf_op jit(solution)/shard_map/all_to_all | solution.py:355
  91.8 1.0 broadcast_in_dim.25
  92.9 12.2 %all_to_all.22 = bf16[4,32,4096]{2,1,0:T(8,128)(2,1)S(1)} all-to-all(bf16[4,32,4096]{2,1,0:T(8,128)(2,1)S(1)} %broadcast_in_dim.40), channel_id=1, replica_groups={{0,64,128,192},{1,65,129,193},{2,66,130,194},{3,67,131,195},{32,33,34,3..., dimensions={0} | all-to-all | bytes 2097152 | tf_op jit(solution)/shard_map/all_to_all | solution.py:356
  105.1 1.1 fusion.11
  106.2 1.0 copy-done.1
  107.1 0.9 collective-permute-start.10
  108.0 0.7 fusion.8
  108.7 2.3 %collective-permute-start.11 = (bf16[64,4096]{1,0:T(8,128)(2,1)}, bf16[64,4096]{1,0:T(8,128)(2,1)}, u32[]{:S(2)}, u32[]{:S(2)}) collective-permute-start(bf16[64,4096]{1,0:T(8,128)(2,1)} %bitcast.9), channel_id=1, source_target_pairs={{0,3},{1,0},{2,1},{3,2},{32,224},{33,225},{34,226},{35,227},{64,67... | collective-permute-start | bytes 1572872 | tf_op jit(solution)/shard_map/ppermute | solution.py:333
  111.0 1.3 collective-permute-start.9
  112.3 1.7 %collective-permute-start.12 = (bf16[64,4096]{1,0:T(8,128)(2,1)}, bf16[64,4096]{1,0:T(8,128)(2,1)}, u32[]{:S(2)}, u32[]{:S(2)}) collective-permute-start(bf16[64,4096]{1,0:T(8,128)(2,1)} %bitcast.10), channel_id=1, source_target_pairs={{0,2},{1,3},{2,0},{3,1},{32,160},{33,161},{34,162},{35,163},{64,66... | collective-permute-start | bytes 1572872 | tf_op jit(solution)/shard_map/ppermute | solution.py:333
  114.0 3.0 %collective-permute-done.10.refs_1_ = bf16[64,4096]{1,0:T(8,128)(2,1)S(1)} collective-permute-done((bf16[64,4096]{1,0:T(8,128)(2,1)}, bf16[64,4096]{1,0:T(8,128)(2,1)S(1)}, u32[]{:S(2)}, u32[]{:S(2)}) %collective-permute-start.10) | collective-permute-done | bytes 524320 | tf_op jit(solution)/shard_map/ppermute | solution.py:333
  117.0 0.8 copy-done.3
  117.8 1.5 collective-permute-start.14
  119.6 0.2 fusion.refs_1_
  119.7 1.9 %copy-done = bf16[384,4096]{1,0:T(8,128)(2,1)S(1)} copy-done((bf16[384,4096]{1,0:T(8,128)(2,1)S(1)}, bf16[384,4096]{1,0:T(8,128)(2,1)}, u32[]{:S(2)}) %copy-start) | copy-done | bytes 3145752
  121.6 1.2 copy-done.2
  122.8 1.0 shard_map.161.refs_2_
  123.8 1.0 shard_map.163.refs_2_
  124.8 3.9 %collective-permute-done.11.refs_2_ = bf16[64,4096]{1,0:T(8,128)(2,1)} collective-permute-done((bf16[64,4096]{1,0:T(8,128)(2,1)}, bf16[64,4096]{1,0:T(8,128)(2,1)}, u32[]{:S(2)}, u32[]{:S(2)}) %collective-permute-start.11) | collective-permute-done | bytes 524320 | tf_op jit(solution)/shard_map/ppermute | solution.py:333
  128.7 2.2 %shard_map.164.refs_3_ = bf16[384,192]{1,0:T(8,128)(2,1)S(1)} custom-call(bf16[384,4096]{1,0:T(8,128)(2,1)S(1)} %collective-permute-done.refs_3_.tok_ref.refs_0_, bf16[64,4096]{1,0:T(8,128)(2,1)} %collective-permute-done.9.refs_0_, bf16[64,4096]{1,0:T(8,128)(2,1)S(1)} %copy-done.4, bf16[64,4096]{1,0:T(8,128)(2,1)} %collective-permute-done.11.refs_2_), custom_call_target="tpu_custom_call" | custom-call | tf_op jit(solution)/shard_map/pallas_call | solution.py:253
  130.9 2.2 %shard_map.162.refs_3_ = bf16[384,192]{1,0:T(8,128)(2,1)S(1)} custom-call(bf16[384,4096]{1,0:T(8,128)(2,1)S(1)} %copy-done, bf16[64,4096]{1,0:T(8,128)(2,1)} %collective-permute-done.9.refs_0_, bf16[64,4096]{1,0:T(8,128)(2,1)S(1)} %copy-done.4, bf16[64,4096]{1,0:T(8,128)(2,1)} %collective-permute-done.11.refs_2_), custom_call_target="tpu_custom_call" | custom-call | tf_op jit(solution)/shard_map/pallas_call | solution.py:253
  133.1 1.9 %collective-permute-done.13.refs_5_ = bf16[64,4096]{1,0:T(8,128)(2,1)} collective-permute-done((bf16[64,4096]{1,0:T(8,128)(2,1)}, bf16[64,4096]{1,0:T(8,128)(2,1)}, u32[]{:S(2)}, u32[]{:S(2)}) %collective-permute-start.13) | collective-permute-done | bytes 524320 | tf_op jit(solution)/shard_map/ppermute | solution.py:333
  135.0 2.9 %shard_map.166 = bf16[384,512]{1,0:T(8,128)(2,1)S(1)} custom-call(bf16[384,4096]{1,0:T(8,128)(2,1)S(1)} %collective-permute-done.refs_3_.tok_ref.refs_0_, bf16[512,512]{1,0:T(8,128)(2,1)S(1)} %fusion.refs_1_, bf16[384,128]{1,0:T(8,128)(2,1)S(1)} %shard_map.163.refs_2_, bf16[384,192]{1,0:T(8,128)(2,1)S(1)} %shard_map.164.refs_3_, ...), custom_call_target="tpu_custom_call" | custom-call | tf_op jit(solution)/shard_map/pallas_call | solution.py:277
  137.9 7.0 %collective-permute-start.15 = (bf16[384,512]{1,0:T(8,128)(2,1)S(1)}, bf16[384,512]{1,0:T(8,128)(2,1)S(1)}, u32[]{:S(2)}, u32[]{:S(2)}) collective-permute-start(bf16[384,512]{1,0:T(8,128)(2,1)S(1)} %shard_map.166), channel_id=1, source_target_pairs={{0,32},{32,0},{1,33},{33,1},{2,34},{34,2},{3,35},{35,3},{4,36},{36... | collective-permute-start | bytes 1179656 | tf_op jit(solution)/shard_map/ppermute | solution.py:310
  144.9 2.9 %shard_map.165.own_ref = bf16[384,512]{1,0:T(8,128)(2,1)S(1)} custom-call(bf16[384,4096]{1,0:T(8,128)(2,1)S(1)} %copy-done, bf16[512,512]{1,0:T(8,128)(2,1)S(1)} %fusion.refs_1_, bf16[384,128]{1,0:T(8,128)(2,1)S(1)} %shard_map.161.refs_2_, bf16[384,192]{1,0:T(8,128)(2,1)S(1)} %shard_map.162.refs_3_, bf16[64,4096]{1,0:T(8,128)(2,1)} %collective-permute-done.12.refs_4_, ...), custom_call_target="tpu_custom_call" | custom-call | tf_op jit(solution)/shard_map/pallas_call | solution.py:277
  147.8 1.0 shard_map.167
  (38 shorter events, 0.9 us)
Async XLA Ops:
  0.6 12.3 %collective-permute-start = (bf16[384,4096]{1,0:T(8,128)(2,1)}, bf16[384,4096]{1,0:T(8,128)(2,1)S(1)}, u32[]{:S(2)}, u32[]{:S(2)}) collective-permute-start(bf16[384,4096]{1,0:T(8,128)(2,1)} %refs_0_.1), channel_id=1, source_target_pairs={{0,32},{32,0},{1,33},{33,1},{2,34},{34,2},{3,35},{35,3},{4,36},{36... | collective-permute-start | bytes 9437192 | tf_op jit(solution)/shard_map/ppermute | solution.py:310
  4.0 8.9 %collective-permute-start.1 = (bf16[384,1024]{1,0:T(8,128)(2,1)}, bf16[384,1024]{1,0:T(8,128)(2,1)}, u32[]{:S(2)}, u32[]{:S(2)}) collective-permute-start(bf16[384,1024]{1,0:T(8,128)(2,1)} %refs_7_.1), channel_id=1, source_target_pairs={{0,32},{32,0},{1,33},{33,1},{2,34},{34,2},{3,35},{35,3},{4,36},{36... | collective-permute-start | bytes 2359304 | tf_op jit(solution)/shard_map/ppermute | solution.py:310
  4.1 8.8 %collective-permute-start.2 = (s32[8,32]{1,0:T(8,128)}, s32[8,32]{1,0:T(8,128)S(1)}, u32[]{:S(2)}, u32[]{:S(2)}) collective-permute-start(s32[8,32]{1,0:T(8,128)} %bitcast.30), channel_id=1, source_target_pairs={{0,32},{32,0},{1,33},{33,1},{2,34},{34,2},{3,35},{35,3},{4,36},{36... | collective-permute-start | bytes 3080 | tf_op jit(solution)/shard_map/ppermute | solution.py:310
  4.5 8.5 %copy-start.5 = (bf16[128,128]{1,0:T(8,128)(2,1)S(1)}, bf16[128,128]{1,0:T(8,128)(2,1)}, u32[]{:S(2)}) copy-start(bf16[128,128]{1,0:T(8,128)(2,1)} %constant.103.refs_10_) | copy-start | bytes 98308
  4.5 8.5 %copy-start.6 = (bf16[128,128]{1,0:T(8,128)(2,1)S(1)}, bf16[128,128]{1,0:T(8,128)(2,1)}, u32[]{:S(2)}) copy-start(bf16[128,128]{1,0:T(8,128)(2,1)} %constant.104.refs_11_) | copy-start | bytes 98308
  4.5 8.5 %copy-start.7 = (s32[32,128]{1,0:T(8,128)S(1)}, s32[32,128]{1,0:T(8,128)}, u32[]{:S(2)}) copy-start(s32[32,128]{1,0:T(8,128)} %refs_8_.5) | copy-start | bytes 49156
  17.8 10.0 %collective-permute-start.3 = (bf16[128,2048]{1,0:T(8,128)(2,1)S(1)}, bf16[128,2048]{1,0:T(8,128)(2,1)S(1)}, u32[]{:S(2)}, u32[]{:S(2)}) collective-permute-start(bf16[128,2048]{1,0:T(8,128)(2,1)S(1)} %get-tuple-element.20), channel_id=1, source_target_pairs={{0,2},{1,3},{2,0},{3,1},{32,160},{33,161},{34,162},{35,163},{64,66... | collective-permute-start | bytes 1572872 | tf_op jit(solution)/shard_map/ppermute | solution.py:333
  19.1 14.3 %collective-permute-start.4 = (bf16[128,2048]{1,0:T(8,128)(2,1)S(1)}, bf16[128,2048]{1,0:T(8,128)(2,1)S(1)}, u32[]{:S(2)}, u32[]{:S(2)}) collective-permute-start(bf16[128,2048]{1,0:T(8,128)(2,1)S(1)} %get-tuple-element.21), channel_id=1, source_target_pairs={{0,1},{1,2},{2,3},{3,0},{32,96},{33,97},{34,98},{35,99},{64,65},{6... | collective-permute-start | bytes 1572872 | tf_op jit(solution)/shard_map/ppermute | solution.py:333
  19.5 13.9 %collective-permute-start.5 = (bf16[128,2048]{1,0:T(8,128)(2,1)S(1)}, bf16[128,2048]{1,0:T(8,128)(2,1)S(1)}, u32[]{:S(2)}, u32[]{:S(2)}) collective-permute-start(bf16[128,2048]{1,0:T(8,128)(2,1)S(1)} %get-tuple-element.22), channel_id=1, source_target_pairs={{0,3},{1,0},{2,1},{3,2},{32,224},{33,225},{34,226},{35,227},{64,67... | collective-permute-start | bytes 1572872 | tf_op jit(solution)/shard_map/ppermute | solution.py:333
  26.6 12.5 %collective-permute-start.6 = (bf16[128,2048]{1,0:T(8,128)(2,1)S(1)}, bf16[128,2048]{1,0:T(8,128)(2,1)S(1)}, u32[]{:S(2)}, u32[]{:S(2)}) collective-permute-start(bf16[128,2048]{1,0:T(8,128)(2,1)S(1)} %get-tuple-element.24), channel_id=1, source_target_pairs={{0,2},{1,3},{2,0},{3,1},{32,160},{33,161},{34,162},{35,163},{64,66... | collective-permute-start | bytes 1572872 | tf_op jit(solution)/shard_map/ppermute | solution.py:333
  27.3 17.3 %collective-permute-start.7 = (bf16[128,2048]{1,0:T(8,128)(2,1)S(1)}, bf16[128,2048]{1,0:T(8,128)(2,1)S(1)}, u32[]{:S(2)}, u32[]{:S(2)}) collective-permute-start(bf16[128,2048]{1,0:T(8,128)(2,1)S(1)} %get-tuple-element.25), channel_id=1, source_target_pairs={{0,1},{1,2},{2,3},{3,0},{32,96},{33,97},{34,98},{35,99},{64,65},{6... | collective-permute-start | bytes 1572872 | tf_op jit(solution)/shard_map/ppermute | solution.py:333
  27.8 16.8 %collective-permute-start.8 = (bf16[128,2048]{1,0:T(8,128)(2,1)S(1)}, bf16[128,2048]{1,0:T(8,128)(2,1)S(1)}, u32[]{:S(2)}, u32[]{:S(2)}) collective-permute-start(bf16[128,2048]{1,0:T(8,128)(2,1)S(1)} %get-tuple-element.26), channel_id=1, source_target_pairs={{0,3},{1,0},{2,1},{3,2},{32,224},{33,225},{34,226},{35,227},{64,67... | collective-permute-start | bytes 1572872 | tf_op jit(solution)/shard_map/ppermute | solution.py:333
  44.6 22.1 %copy-start.8 = (s32[4,32]{1,0:T(4,128)S(1)}, s32[4,32]{1,0:T(4,128)}, u32[]{:S(2)}) copy-start(s32[4,32]{1,0:T(4,128)} %param.20) | copy-start | bytes 1540
  59.1 17.0 %all-to-all-start.1 = ((bf16[8,8,2048]{2,1,0:T(8,128)(2,1)}), bf16[8,8,2048]{2,1,0:T(8,128)(2,1)S(1)}, u32[]{:S(2)}, u32[]{:S(2)}) async-start(bf16[8,8,2048]{2,1,0:T(8,128)(2,1)} %shard_map.160), calls=%async_computation.1 | async-start | bytes 524288 | tf_op jit(solution)/shard_map/all_to_all | solution.py:355
  106.1 1.0 copy-start.1
  107.1 9.9 %collective-permute-start.10 = (bf16[64,4096]{1,0:T(8,128)(2,1)}, bf16[64,4096]{1,0:T(8,128)(2,1)S(1)}, u32[]{:S(2)}, u32[]{:S(2)}) collective-permute-start(bf16[64,4096]{1,0:T(8,128)(2,1)} %bitcast.9), channel_id=1, source_target_pairs={{0,1},{1,2},{2,3},{3,0},{32,96},{33,97},{34,98},{35,99},{64,65},{6... | collective-permute-start | bytes 1572872 | tf_op jit(solution)/shard_map/ppermute | solution.py:333
  108.7 20.0 %collective-permute-start.11 = (bf16[64,4096]{1,0:T(8,128)(2,1)}, bf16[64,4096]{1,0:T(8,128)(2,1)}, u32[]{:S(2)}, u32[]{:S(2)}) collective-permute-start(bf16[64,4096]{1,0:T(8,128)(2,1)} %bitcast.9), channel_id=1, source_target_pairs={{0,3},{1,0},{2,1},{3,2},{32,224},{33,225},{34,226},{35,227},{64,67... | collective-permute-start | bytes 1572872 | tf_op jit(solution)/shard_map/ppermute | solution.py:333
  111.0 17.7 %collective-permute-start.9 = (bf16[64,4096]{1,0:T(8,128)(2,1)}, bf16[64,4096]{1,0:T(8,128)(2,1)}, u32[]{:S(2)}, u32[]{:S(2)}) collective-permute-start(bf16[64,4096]{1,0:T(8,128)(2,1)} %bitcast.9), channel_id=1, source_target_pairs={{0,2},{1,3},{2,0},{3,1},{32,160},{33,161},{34,162},{35,163},{64,66... | collective-permute-start | bytes 1572872 | tf_op jit(solution)/shard_map/ppermute | solution.py:333
  112.3 20.8 %collective-permute-start.12 = (bf16[64,4096]{1,0:T(8,128)(2,1)}, bf16[64,4096]{1,0:T(8,128)(2,1)}, u32[]{:S(2)}, u32[]{:S(2)}) collective-permute-start(bf16[64,4096]{1,0:T(8,128)(2,1)} %bitcast.10), channel_id=1, source_target_pairs={{0,2},{1,3},{2,0},{3,1},{32,160},{33,161},{34,162},{35,163},{64,66... | collective-permute-start | bytes 1572872 | tf_op jit(solution)/shard_map/ppermute | solution.py:333
  114.0 21.1 %collective-permute-start.13 = (bf16[64,4096]{1,0:T(8,128)(2,1)}, bf16[64,4096]{1,0:T(8,128)(2,1)}, u32[]{:S(2)}, u32[]{:S(2)}) collective-permute-start(bf16[64,4096]{1,0:T(8,128)(2,1)} %bitcast.10), channel_id=1, source_target_pairs={{0,1},{1,2},{2,3},{3,0},{32,96},{33,97},{34,98},{35,99},{64,65},{6... | collective-permute-start | bytes 1572872 | tf_op jit(solution)/shard_map/ppermute | solution.py:333
  117.0 0.8 copy-start.3
  117.8 17.2 %collective-permute-start.14 = (bf16[64,4096]{1,0:T(8,128)(2,1)}, bf16[64,4096]{1,0:T(8,128)(2,1)}, u32[]{:S(2)}, u32[]{:S(2)}) collective-permute-start(bf16[64,4096]{1,0:T(8,128)(2,1)} %bitcast.10), channel_id=1, source_target_pairs={{0,3},{1,0},{2,1},{3,2},{32,224},{33,225},{34,226},{35,227},{64,67... | collective-permute-start | bytes 1572872 | tf_op jit(solution)/shard_map/ppermute | solution.py:333
  119.7 1.9 %copy-start = (bf16[384,4096]{1,0:T(8,128)(2,1)S(1)}, bf16[384,4096]{1,0:T(8,128)(2,1)}, u32[]{:S(2)}) copy-start(bf16[384,4096]{1,0:T(8,128)(2,1)} %refs_0_.1) | copy-start | bytes 9437188
  121.6 1.2 copy-start.2
  122.8 5.9 %copy-start.4 = (bf16[64,4096]{1,0:T(8,128)(2,1)S(1)}, bf16[64,4096]{1,0:T(8,128)(2,1)}, u32[]{:S(2)}) copy-start(bf16[64,4096]{1,0:T(8,128)(2,1)} %copy-done.3) | copy-start | bytes 1572868
  137.9 9.9 %collective-permute-start.15 = (bf16[384,512]{1,0:T(8,128)(2,1)S(1)}, bf16[384,512]{1,0:T(8,128)(2,1)S(1)}, u32[]{:S(2)}, u32[]{:S(2)}) collective-permute-start(bf16[384,512]{1,0:T(8,128)(2,1)S(1)} %shard_map.166), channel_id=1, source_target_pairs={{0,32},{32,0},{1,33},{33,1},{2,34},{34,2},{3,35},{35,3},{4,36},{36... | collective-permute-start | bytes 1179656 | tf_op jit(solution)/shard_map/ppermute | solution.py:310

commit v7 on v5

--- a/solution.py
+++ b/solution.py
@@ -183,17 +183,38 @@
     )(*place, *operands)
 
 
-def line_kernel(count, *refs):
-    out_ref = refs[-1]
-    sums = []
-    for terms in (refs[:count], refs[count:-1]):
-        total = terms[0][...].astype(jnp.float32)
-        for ref in terms[1:]:
-            total = total + ref[...].astype(jnp.float32)
-        sums.append(total)
+def added_up(refs):
+    total = refs[0][...].astype(jnp.float32)
+    for ref in refs[1:]:
+        total = total + ref[...].astype(jnp.float32)
+    return total
+
+
+def line_kernel(*refs):
+    refs[-1][...] = added_up(refs[:-1]).astype(jnp.bfloat16)
+
+
+def line_sum(terms):
+    rows, half = terms[0].shape
+    width = 1024
+    spec = pl.BlockSpec((rows, width), lambda n: (0, n))
+    return pl.pallas_call(
+        line_kernel,
+        grid=(half // width,),
+        in_specs=[spec] * len(terms),
+        out_specs=spec,
+        out_shape=jax.ShapeDtypeStruct((rows, half), jnp.bfloat16),
+        compiler_params=pltpu.CompilerParams(vmem_limit_bytes=16 << 20),
+    )(*terms)
+
+
+def face_kernel(left_ref, right_ref, out_ref):
+    left_sum, right_sum = (
+        added_up([ref.at[at] for at in range(ref.shape[0])]) for ref in (left_ref, right_ref)
+    )
     rows = 8
-    for at in range(sums[0].shape[0] // rows):
-        left, right = (total[at * rows : (at + 1) * rows] for total in sums)
+    for at in range(left_sum.shape[0] // rows):
+        left, right = (total[at * rows : (at + 1) * rows] for total in (left_sum, right_sum))
         upper = lax.broadcasted_iota(jnp.int32, left.shape, 0) < rows // 2
         even = jnp.where(upper, left, pltpu.roll(right, rows // 2, 0))
         odd = jnp.where(upper, pltpu.roll(left, rows // 2, 0), right)
@@ -201,65 +222,59 @@
         out_ref[2 * at + 1] = odd.astype(jnp.bfloat16)
 
 
-def line_sums(left_terms, right_terms):
-    rows, half = left_terms[0].shape
+def face_sum(left, right):
+    count, rows, half = left.shape
     width = 1024
-    count = len(left_terms)
-    body = lambda *refs: line_kernel(count, *refs)
-    return pl.pallas_call(
-        body,
+    return pl.pallas_call(
+        face_kernel,
         grid=(half // width,),
-        in_specs=[pl.BlockSpec((rows, width), lambda n: (0, n))] * (2 * count),
+        in_specs=[pl.BlockSpec((count, rows, width), lambda n: (0, 0, n))] * 2,
         out_specs=pl.BlockSpec((rows // 4, 8, width), lambda n: (0, 0, n)),
         out_shape=jax.ShapeDtypeStruct((rows // 4, 8, half), jnp.bfloat16),
         compiler_params=pltpu.CompilerParams(vmem_limit_bytes=16 << 20),
-    )(*left_terms, *right_terms)
-
-
-def project_kernel(pair, core_ref, tok_ref, weight_ref, order_ref, out_ref):
-    tile = order_ref.shape[0]
-    core = core_ref[0]
-    rows = []
-    for at in range(pair):
-        group = pl.program_id(0) * pair + at
-        for spot in range(tile // weight_ref.shape[2]):
-            first = jnp.where(core == 0, spot, group)
-            second = jnp.where(core == 0, group, spot)
-            rows.append(weight_ref[first, second])
-    total = lax.dot_general(
-        tok_ref[...],
-        jnp.concatenate(rows, axis=0),
-        (((1,), (1,)), ((), ())),
-        preferred_element_type=jnp.float32,
-    )
-    rounded = total.astype(jnp.bfloat16)
-    for at in range(pair):
-        cols = slice(at * tile, (at + 1) * tile)
-        out_ref[:, cols] = jnp.dot(
-            rounded[:, cols], order_ref[...], preferred_element_type=jnp.float32
-        ).astype(jnp.bfloat16)
-
-
-def project(core, tokens, weights, order, groups):
-    token_rows = tokens.shape[0]
-    tile = order.shape[0]
-    pair = 2
-    body = lambda *refs: project_kernel(pair, *refs)
-    return pl.pallas_call(
-        body,
-        grid_spec=pltpu.PrefetchScalarGridSpec(
-            num_scalar_prefetch=1,
-            grid=(groups // pair,),
-            in_specs=[
-                pl.BlockSpec(tokens.shape, lambda n, core: (0, 0)),
-                pl.BlockSpec(weights.shape, lambda n, core: (0, 0, 0, 0)),
-                pl.BlockSpec(order.shape, lambda n, core: (0, 0)),
-            ],
-            out_specs=pl.BlockSpec((token_rows, pair * tile), lambda n, core: (0, n)),
-        ),
-        out_shape=jax.ShapeDtypeStruct((token_rows, groups * tile), jnp.bfloat16),
-        compiler_params=pltpu.CompilerParams(vmem_limit_bytes=32 << 20),
-    )(core, tokens, weights, order)
+    )(left, right)
+
+
+def product(tok_ref, weight_refs):
+    weights = jnp.concatenate([ref[...] for ref in weight_refs], axis=0)
+    return lax.dot_general(
+        tok_ref[...], weights, (((1,), (1,)), ((), ())), preferred_element_type=jnp.float32
+    ).astype(jnp.bfloat16)
+
+
+def early_kernel(tok_ref, spread_ref, *refs):
+    refs[-1][...] = jnp.dot(
+        product(tok_ref, refs[:-1]), spread_ref[...], preferred_element_type=jnp.float32
+    ).astype(jnp.bfloat16)
+
+
+def early_product(tokens, spread, weights):
+    whole = pl.BlockSpec(memory_space=pltpu.VMEM)
+    return pl.pallas_call(
+        early_kernel,
+        in_specs=[whole] * (2 + len(weights)),
+        out_specs=whole,
+        out_shape=jax.ShapeDtypeStruct((tokens.shape[0], spread.shape[1]), jnp.bfloat16),
+        compiler_params=pltpu.CompilerParams(vmem_limit_bytes=20 << 20),
+    )(tokens, spread, *weights)
+
+
+def late_kernel(tok_ref, spread_ref, early_ref, *refs):
+    late = jnp.dot(
+        product(tok_ref, refs[:-1]), spread_ref[...], preferred_element_type=jnp.float32
+    )
+    refs[-1][...] = (late + early_ref[...].astype(jnp.float32)).astype(jnp.bfloat16)
+
+
+def late_product(tokens, spread, early, weights):
+    whole = pl.BlockSpec(memory_space=pltpu.VMEM)
+    return pl.pallas_call(
+        late_kernel,
+        in_specs=[whole] * (3 + len(weights)),
+        out_specs=whole,
+        out_shape=jax.ShapeDtypeStruct((tokens.shape[0], spread.shape[1]), jnp.bfloat16),
+        compiler_params=pltpu.CompilerParams(vmem_limit_bytes=20 << 20),
+    )(tokens, spread, early, *weights)
 
 
 def interleave_kernel(core_ref, own_ref, peer_ref, out_ref):
@@ -312,10 +327,20 @@
     return lax.ppermute(value, FACE, pairs)
 
 
-def slab_groups():
-    at = lambda y, c, z, x: ((y * 2 + c) * 8 + z) * 4 + x
-    groups = [[at(y, 0, z, x) for y in range(4) for z in range(8)] for x in range(4)]
-    return groups + [[at(y, 1, z, x) for x in range(4) for z in range(8)] for y in range(4)]
+def column_spread(place, pieces, count_z, rows_dev):
+    core, at_x, at_y = place
+    shift = jnp.asarray([piece[0] for piece in pieces], jnp.int32)[:, None, None, None]
+    start = jnp.asarray([piece[1] for piece in pieces], jnp.int32)[:, None, None, None]
+    second = jnp.arange(4, dtype=jnp.int32)[None, :, None, None]
+    at_z = jnp.arange(count_z // 2, dtype=jnp.int32)[None, None, :, None] + start
+    at_j = jnp.arange(rows_dev, dtype=jnp.int32)[None, None, None, :]
+    from_x = jnp.where(core == 0, (at_x - shift) % 4, second)
+    from_y = jnp.where(core == 0, second, (at_y - shift) % 4)
+    column = ((from_y * count_z + at_z) * 4 + from_x) * rows_dev + at_j
+    size = 16 * count_z * rows_dev
+    return (column.reshape(-1, 1) == jnp.arange(size, dtype=jnp.int32)[None, :]).astype(
+        jnp.bfloat16
+    )
 
 
 def exchanged(value, step):
@@ -341,12 +366,12 @@
     diff_exps,
     hadamard_signs,
 ):
-    count_y, count_z, count_x = (lax.axis_size(axis) for axis in ("y", "z", "x"))
+    count_z = lax.axis_size("z")
     rows_dev, model_width = master_weights.shape
     sign_rows = (2 * hadamard_signs - 1).astype(jnp.float32)
     block_len = sign_rows.shape[1]
     matrix = jnp.asarray(hadamard(block_len))
-    order = jnp.asarray(row_order(count_z, count_x, rows_dev))
+    order = jnp.asarray(row_order(count_z, 4, rows_dev))
     place = [lax.axis_index(axis).reshape(1).astype(jnp.int32) for axis in ("c", "x", "y")]
     exps = grad_exps[0]
     peer_tokens, peer_grad, peer_exps = swapped(tokens), swapped(out_grad), swapped(exps)
@@ -366,8 +391,8 @@
             half=half,
         )
         halves.append([pair_sums[0], *(shifted(pair_sums[far], 0, far) for far in (2, 1, 3))])
-    lines = line_sums(*halves)
-    parts = lax.all_to_all(lines, AXES, 0, 0, tiled=True, axis_index_groups=slab_groups())
+    lines = [line_sum(terms).reshape(4, -1, terms[0].shape[1]) for terms in halves]
+    parts = exchanged(face_sum(*(exchanged(rows, "second") for rows in lines)), "z")
     summed = jnp.sum(parts.astype(jnp.float32), axis=0)
     summed = jnp.swapaxes(summed.reshape(2, rows_dev, -1), 0, 1).reshape(rows_dev, model_width)
     gradient = unrotate_rows(summed, sign_rows, matrix)
@@ -380,9 +405,22 @@
     diff_coded = clip_rows(new_master - base_own, diff_bound).astype(jnp.bfloat16)
     effective = (base_own + diff_coded.astype(jnp.float32)).astype(jnp.bfloat16)
     stacked = gathered(effective, count_z, "z").reshape(count_z * rows_dev, model_width)
-    weights = gathered(gathered(stacked, count_y, "second"), count_x, "first")
-    peer_part = swapped(project(place[0], peer_tokens, weights, order, count_y))
-    own_part = project(place[0], tokens, weights, order, count_y)
+    middle = stacked.shape[0] // 2
+    faces, arrived = [], []
+    for rows in (stacked[:middle], stacked[middle:]):
+        faces.append(gathered(rows, 4, "second").reshape(-1, model_width))
+        arrived.append([shifted(faces[-1], 0, far) for far in (2, 1, 3)])
+    first_z = (0, count_z // 2)
+    early_pieces = [(0, first_z[0]), *((far, first_z[0]) for far in (2, 1, 3)), (0, first_z[1])]
+    early_spread = column_spread(place, early_pieces, count_z, rows_dev)
+    late_spread = column_spread(
+        place, [(far, first_z[1]) for far in (2, 1, 3)], count_z, rows_dev
+    )
+    near = [faces[0], *arrived[0], faces[1]]
+    early = [early_product(rows, early_spread, near) for rows in (peer_tokens, tokens)]
+    early, last = lax.optimization_barrier((early, arrived[1]))
+    peer_part = swapped(late_product(peer_tokens, late_spread, early[0], last))
+    own_part = late_product(tokens, late_spread, early[1], last)
     projected = interleaved(place[0], own_part, peer_part)
     return (projected, new_master, new_first, new_second)
 

time: 157 us -> 165 us (1.051)
  blocking collectives: 59 us -> 0 us
  starting transfers between devices: 25.8 us -> 62.2 us
  Pallas kernels: 28.3 us -> 36.8 us
  local copies, waits for them, and re-layouts: 1.02 us -> 9.17 us
  waiting for transfers between devices: 39.4 us -> 47 us
  other arithmetic: 1.83 us -> 5.76 us
    all_to_all x3 -> x0, blocking collectives: 59 us -> none  [the longest x2 42.9 us: exchanged(): lax.all_to_all(value, FACE, 0, 0, tiled=True, axis_index_groups=face_grou...]
    all_to_all x1 -> x6, starting transfers between devices: 9.63 us -> 28.9 us  [the longest x4 16.8 us: exchanged(): lax.all_to_all(value, FACE, 0, 0, tiled=True, axis_index_groups=face_grou...]
    ppermute x6 -> x12, starting transfers between devices: 6.9 us -> 18.3 us  [shifted(): return lax.ppermute(value, FACE, pairs)]
    all_to_all x1 -> x6, waiting for transfers between devices: 24.5 us -> 33.8 us  [the longest x4 17.7 us: exchanged(): lax.all_to_all(value, FACE, 0, 0, tiled=True, axis_index_groups=face_grou...]
    pallas_call x3 -> x7, Pallas kernels: 8.96 us -> 16.8 us  [the longest x2 7.51 us: early_product(): pl.pallas_call(early_kernel, in_specs=[whole] * (2 + len(weights)), out_s...]
    ppermute x4, starting transfers between devices: 9.25 us -> 15 us  [swapped(): return lax.ppermute(value, 'c', [(0, 1), (1, 0)])]
    unnamed x19 -> x21, local copies, waits for them, and re-layouts: 0.14 us -> 4.64 us
    broadcast_in_dim x4 -> x5, local copies, waits for them, and re-layouts: 0.73 us -> 3.4 us  [gathered(): return exchanged(jnp.broadcast_to(value[None], (count, *value.shape)), step)]
  transfers between devices with their start and end apart: 11 -> 22, of which waited for: 5 -> 10; matrix products, arithmetic and copies ran while one was open for 0% -> 3% of each run, Pallas kernels for 10% -> 16%
where the time goes in v7:
time: 165 us; the launch traced here: 163 us
  starting transfers between devices  62.2 us (38%)
  waiting for transfers between devices  47 us (28%)
  Pallas kernels  36.8 us (22%)
  local copies, waits for them, and re-layouts  9.17 us (6%)
  other arithmetic  5.76 us (3%)
    pallas_call x3, Pallas kernels, coded_gradient(): pl.pallas_call(body, grid_spec=pltpu.PrefetchScalarGridSpec(num_scalar_pr...  18.9 us
    ppermute x12, starting transfers between devices, shifted(): return lax.ppermute(value, FACE, pairs)  18.3 us
    all_to_all x4, waiting for transfers between devices, exchanged(): lax.all_to_all(value, FACE, 0, 0, tiled=True, axis_index_groups=face_grou...  17.7 us
    all_to_all x4, starting transfers between devices, exchanged(): lax.all_to_all(value, FACE, 0, 0, tiled=True, axis_index_groups=face_grou...  16.8 us
    all_to_all x2, waiting for transfers between devices, exchanged(): return lax.all_to_all(value, 'z', 0, 0, tiled=True)  16.1 us
    ppermute x4, starting transfers between devices, swapped(): return lax.ppermute(value, 'c', [(0, 1), (1, 0)])  15 us
    ppermute x12, waiting for transfers between devices, shifted(): return lax.ppermute(value, FACE, pairs)  13.2 us
    all_to_all x2, starting transfers between devices, exchanged(): return lax.all_to_all(value, 'z', 0, 0, tiled=True)  12.1 us
  transfers between devices with their start and end apart: 22, of which 10 were waited for; matrix products, arithmetic and copies ran while one was open for 3% of the time, Pallas kernels for 16%

profile of v7, /device:TPU:1, one launch (start us, length us, event | category | flops | bytes accessed | tf_op | source)
XLA Modules:
  0.0 162.8 jit_solution(12873753008272283682)
XLA Ops:
  0.6 3.3 %collective-permute-start = (bf16[384,4096]{1,0:T(8,128)(2,1)}, bf16[384,4096]{1,0:T(8,128)(2,1)S(1)}, u32[]{:S(2)}, u32[]{:S(2)}) collective-permute-start(bf16[384,4096]{1,0:T(8,128)(2,1)} %tok_ref.3), channel_id=1, source_target_pairs={{0,32},{32,0},{1,33},{33,1},{2,34},{34,2},{3,35},{35,3},{4,36},{36... | collective-permute-start | bytes 9437192 | tf_op jit(solution)/shard_map/ppermute | solution.py:304
  4.5 8.5 %shard_map.174.refs_12_ = bf16[512,4096]{1,0:T(8,128)(2,1)} custom-call(s32[1]{0:T(128)} %bitcast.refs_0_.core_ref, s32[1]{0:T(128)} %bitcast.2.refs_1_, s32[1]{0:T(128)} %bitcast.3.refs_2_, bf16[384,4096]{1,0:T(8,128)(2,1)} %tok_ref.3, bf16[384,1024]{1,0:T(8,128)(2,1)} %refs_7_.1, bf16[384,1024]{1,0:T(8,128)(2,1)} %refs_7_.1, bf16[384,1024]{1,0:T(8,128)(2,1)} %refs_7_.1, ...), custom_call_target="tpu_custom_call" | custom-call | tf_op jit(solution)/shard_map/pallas_call | solution.py:166
  13.0 4.9 %shard_map.177 = (bf16[128,2048]{1,0:T(8,128)(2,1)S(1)}, bf16[128,2048]{1,0:T(8,128)(2,1)S(1)}, bf16[128,2048]{1,0:T(8,128)(2,1)S(1)}, bf16[128,2048]{1,0:T(8,128)(2,1)S(1)}) custom-call(s32[1]{0:T(128)} %bitcast.refs_0_.core_ref, s32[1]{0:T(128)} %bitcast.2.refs_1_, s32[1]{0:T(128)} %bitcast.3.refs_2_, ...), custom_call_target="tpu_custom_call" | custom-call | tf_op jit(solution)/shard_map/pallas_call | solution.py:166
  17.9 1.3 collective-permute-start.6
  19.6 2.3 %collective-permute-start.8 = (bf16[128,2048]{1,0:T(8,128)(2,1)S(1)}, bf16[128,2048]{1,0:T(8,128)(2,1)S(1)}, u32[]{:S(2)}, u32[]{:S(2)}) collective-permute-start(bf16[128,2048]{1,0:T(8,128)(2,1)S(1)} %get-tuple-element.24), channel_id=1, source_target_pairs={{0,3},{1,0},{2,1},{3,2},{32,224},{33,225},{34,226},{35,227},{64,67... | collective-permute-start | bytes 1572872 | tf_op jit(solution)/shard_map/ppermute | solution.py:327
  21.9 5.6 %shard_map.175 = (bf16[128,2048]{1,0:T(8,128)(2,1)S(1)}, bf16[128,2048]{1,0:T(8,128)(2,1)}, bf16[128,2048]{1,0:T(8,128)(2,1)}, bf16[128,2048]{1,0:T(8,128)(2,1)}) custom-call(s32[1]{0:T(128)} %bitcast.refs_0_.core_ref, s32[1]{0:T(128)} %bitcast.2.refs_1_, s32[1]{0:T(128)} %bitcast.3.refs_2_, bf16[384,4096]{1,0:T(8,128)(2,1)S(1)} %collective-permute-done.refs_3_.tok_ref, ...), custom_call_target="tpu_custom_call" | custom-call | tf_op jit(solution)/shard_map/pallas_call | solution.py:166
  28.1 2.6 %collective-permute-start.5 = (bf16[128,2048]{1,0:T(8,128)(2,1)}, bf16[128,2048]{1,0:T(8,128)(2,1)}, u32[]{:S(2)}, u32[]{:S(2)}) collective-permute-start(bf16[128,2048]{1,0:T(8,128)(2,1)} %get-tuple-element.20), channel_id=1, source_target_pairs={{0,3},{1,0},{2,1},{3,2},{32,224},{33,225},{34,226},{35,227},{64,67... | collective-permute-start | bytes 1572872 | tf_op jit(solution)/shard_map/ppermute | solution.py:327
  30.8 2.7 %collective-permute-done.7.refs_2_ = bf16[128,2048]{1,0:T(8,128)(2,1)S(1)} collective-permute-done((bf16[128,2048]{1,0:T(8,128)(2,1)S(1)}, bf16[128,2048]{1,0:T(8,128)(2,1)S(1)}, u32[]{:S(2)}, u32[]{:S(2)}) %collective-permute-start.7) | collective-permute-done | bytes 524320 | tf_op jit(solution)/shard_map/ppermute | solution.py:327
  34.0 0.8 copy-done.1
  34.8 4.1 %all-to-all-start.1 = ((bf16[4,32,2048]{2,1,0:T(8,128)(2,1)}), bf16[4,32,2048]{2,1,0:T(8,128)(2,1)}, u32[]{:S(2)}, u32[]{:S(2)}) async-start(bf16[4,32,2048]{2,1,0:T(8,128)(2,1)} %bitcast.26), calls=%async_computation.1 | async-start | bytes 1048576 | tf_op jit(solution)/shard_map/all_to_all | solution.py:349
  39.2 5.7 %collective-permute-done.4.refs_2_ = bf16[128,2048]{1,0:T(8,128)(2,1)} collective-permute-done((bf16[128,2048]{1,0:T(8,128)(2,1)}, bf16[128,2048]{1,0:T(8,128)(2,1)}, u32[]{:S(2)}, u32[]{:S(2)}) %collective-permute-start.4) | collective-permute-done | bytes 524320 | tf_op jit(solution)/shard_map/ppermute | solution.py:327
  45.0 1.0 copy-done.4
  46.0 1.5 shard_map.176
  47.6 0.8 copy-done.2
  48.4 4.4 %all-to-all-start = ((bf16[4,32,2048]{2,1,0:T(8,128)(2,1)}), bf16[4,32,2048]{2,1,0:T(8,128)(2,1)}, u32[]{:S(2)}, u32[]{:S(2)}) async-start(bf16[4,32,2048]{2,1,0:T(8,128)(2,1)} %bitcast.27), calls=%async_computation | async-start | bytes 1048576 | tf_op jit(solution)/shard_map/all_to_all | solution.py:349
  52.8 7.0 %all-to-all-done.left_ref = bf16[4,32,2048]{2,1,0:T(8,128)(2,1)} async-done(((bf16[4,32,2048]{2,1,0:T(8,128)(2,1)}), bf16[4,32,2048]{2,1,0:T(8,128)(2,1)}, u32[]{:S(2)}, u32[]{:S(2)}) %all-to-all-start) | async-done | bytes 524320 | tf_op jit(solution)/shard_map/all_to_all | solution.py:349
  59.8 1.9 %shard_map.179 = bf16[8,8,2048]{2,1,0:T(8,128)(2,1)} custom-call(bf16[4,32,2048]{2,1,0:T(8,128)(2,1)} %all-to-all-done.left_ref, bf16[4,32,2048]{2,1,0:T(8,128)(2,1)} %all-to-all-done.1.right_ref), custom_call_target="tpu_custom_call" | custom-call | tf_op jit(solution)/shard_map/pallas_call | solution.py:228
  61.7 8.7 %all-to-all-start.2 = ((bf16[8,8,2048]{2,1,0:T(8,128)(2,1)}), bf16[8,8,2048]{2,1,0:T(8,128)(2,1)S(1)}, u32[]{:S(2)}, u32[]{:S(2)}) async-start(bf16[8,8,2048]{2,1,0:T(8,128)(2,1)} %shard_map.179), calls=%async_computation.2 | async-start | bytes 524288 | tf_op jit(solution)/shard_map/all_to_all | solution.py:348
  71.7 8.2 %all-to-all-done.2 = bf16[8,8,2048]{2,1,0:T(8,128)(2,1)S(1)} async-done(((bf16[8,8,2048]{2,1,0:T(8,128)(2,1)}), bf16[8,8,2048]{2,1,0:T(8,128)(2,1)S(1)}, u32[]{:S(2)}, u32[]{:S(2)}) %all-to-all-start.2) | async-done | bytes 262176 | tf_op jit(solution)/shard_map/all_to_all | solution.py:348
  80.1 1.0 convolution_multiply_fusion
  81.2 1.8 %fusion.5 = (bf16[4,4096]{1,0:T(4,128)(2,1)S(1)}, f32[4,4096]{1,0:T(4,128)}, f32[4,4096]{1,0:T(4,128)}, f32[4,4096]{1,0:T(4,128)}) fusion(bf16[1,4,32,128]{3,2,1,0:T(8,128)(2,1)S(1)} %get-tuple-element.46, bf16[1,4,32,128]{3,2,1,0:T(8,128)(2,1)S(1)} %get-tuple-element.47, bf16[1024,4096]{1,0:T(8,128)(2,1)} %param.18, s32[]{:T(128)S(6)} %select_n.72, ...), kind=kLoop, calls=%fused_computation.12 | loop fusion | flops 409600 | bytes 606212 | tf_op jit(solution)/shard_map/convert_element_type | solution.py:406
  83.0 0.8 broadcast_in_dim.122
  83.7 3.4 %all-to-all-start.3 = ((bf16[8,4,4096]{2,1,0:T(4,128)(2,1)}), bf16[8,4,4096]{2,1,0:T(4,128)(2,1)S(1)}, u32[]{:S(2)}, u32[]{:S(2)}) async-start(bf16[8,4,4096]{2,1,0:T(4,128)(2,1)} %broadcast_in_dim.122), calls=%async_computation.3 | async-start | bytes 524288 | tf_op jit(solution)/shard_map/all_to_all | solution.py:348
  87.9 0.7 iota_select_fusion
  88.7 7.9 %all-to-all-done.3 = bf16[8,4,4096]{2,1,0:T(4,128)(2,1)S(1)} async-done(((bf16[8,4,4096]{2,1,0:T(4,128)(2,1)}), bf16[8,4,4096]{2,1,0:T(4,128)(2,1)S(1)}, u32[]{:S(2)}, u32[]{:S(2)}) %all-to-all-start.3) | async-done | bytes 262176 | tf_op jit(solution)/shard_map/all_to_all | solution.py:348
  96.5 0.7 fusion.13
  97.3 0.9 broadcast_in_dim.123
  98.2 0.8 broadcast_in_dim.124
  99.0 4.1 %all-to-all-start.4 = ((bf16[4,16,4096]{2,1,0:T(8,128)(2,1)}), bf16[4,16,4096]{2,1,0:T(8,128)(2,1)}, u32[]{:S(2)}, u32[]{:S(2)}) async-start(bf16[4,16,4096]{2,1,0:T(8,128)(2,1)} %broadcast_in_dim.124), calls=%async_computation.4 | async-start | bytes 1048576 | tf_op jit(solution)/shard_map/all_to_all | solution.py:349
  103.2 0.7 iota_add_fusion.2
  104.0 6.2 %all-to-all-done.4 = bf16[4,16,4096]{2,1,0:T(8,128)(2,1)} async-done(((bf16[4,16,4096]{2,1,0:T(8,128)(2,1)}), bf16[4,16,4096]{2,1,0:T(8,128)(2,1)}, u32[]{:S(2)}, u32[]{:S(2)}) %all-to-all-start.4) | async-done | bytes 524320 | tf_op jit(solution)/shard_map/all_to_all | solution.py:349
  110.2 1.5 collective-permute-start.10
  111.7 0.8 broadcast_in_dim.126
  112.5 4.1 %all-to-all-start.5 = ((bf16[4,16,4096]{2,1,0:T(8,128)(2,1)}), bf16[4,16,4096]{2,1,0:T(8,128)(2,1)}, u32[]{:S(2)}, u32[]{:S(2)}) async-start(bf16[4,16,4096]{2,1,0:T(8,128)(2,1)} %broadcast_in_dim.126), calls=%async_computation.5 | async-start | bytes 1048576 | tf_op jit(solution)/shard_map/all_to_all | solution.py:349
  116.8 1.3 collective-permute-start.11
  118.1 1.2 collective-permute-start.9
  119.3 4.5 %all-to-all-done.5 = bf16[4,16,4096]{2,1,0:T(8,128)(2,1)} async-done(((bf16[4,16,4096]{2,1,0:T(8,128)(2,1)}), bf16[4,16,4096]{2,1,0:T(8,128)(2,1)}, u32[]{:S(2)}, u32[]{:S(2)}) %all-to-all-start.5) | async-done | bytes 524320 | tf_op jit(solution)/shard_map/all_to_all | solution.py:349
  123.7 4.4 %collective-permute-start.12 = (bf16[64,4096]{1,0:T(8,128)(2,1)}, bf16[64,4096]{1,0:T(8,128)(2,1)}, u32[]{:S(2)}, u32[]{:S(2)}) collective-permute-start(bf16[64,4096]{1,0:T(8,128)(2,1)} %bitcast.10.refs_4_), channel_id=1, source_target_pairs={{0,2},{1,3},{2,0},{3,1},{32,160},{33,161},{34,162},{35,163},{64,66... | collective-permute-start | bytes 1572872 | tf_op jit(solution)/shard_map/ppermute | solution.py:327
  128.1 2.7 %collective-permute-start.14 = (bf16[64,4096]{1,0:T(8,128)(2,1)}, bf16[64,4096]{1,0:T(8,128)(2,1)}, u32[]{:S(2)}, u32[]{:S(2)}) collective-permute-start(bf16[64,4096]{1,0:T(8,128)(2,1)} %bitcast.10.refs_4_), channel_id=1, source_target_pairs={{0,3},{1,0},{2,1},{3,2},{32,224},{33,225},{34,226},{35,227},{64,67... | collective-permute-start | bytes 1572872 | tf_op jit(solution)/shard_map/ppermute | solution.py:327
  131.4 1.9 %copy-done = bf16[384,4096]{1,0:T(8,128)(2,1)S(1)} copy-done((bf16[384,4096]{1,0:T(8,128)(2,1)S(1)}, bf16[384,4096]{1,0:T(8,128)(2,1)}, u32[]{:S(2)}) %copy-start) | copy-done | bytes 3145752
  133.3 3.8 %shard_map.181.early_ref = bf16[384,512]{1,0:T(8,128)(2,1)S(1)} custom-call(bf16[384,4096]{1,0:T(8,128)(2,1)S(1)} %copy-done, bf16[320,512]{1,0:T(8,128)(2,1)S(1)} %fusion.spread_ref, bf16[64,4096]{1,0:T(8,128)(2,1)} %bitcast.9.refs_0_, bf16[64,4096]{1,0:T(8,128)(2,1)} %collective-permute-done.9.refs_1_, bf16[64,4096]{1,0:T(8,128)(2,1)} %collective-permute-done.10.refs_2_, ...), custom_call_target="tpu_custom_call" | custom-call | tf_op jit(solution)/shard_map/pallas_call | solution.py:253
  137.0 3.8 %shard_map.180.early_ref = bf16[384,512]{1,0:T(8,128)(2,1)S(1)} custom-call(bf16[384,4096]{1,0:T(8,128)(2,1)S(1)} %collective-permute-done.refs_3_.tok_ref, bf16[320,512]{1,0:T(8,128)(2,1)S(1)} %fusion.spread_ref, bf16[64,4096]{1,0:T(8,128)(2,1)} %bitcast.9.refs_0_, bf16[64,4096]{1,0:T(8,128)(2,1)} %collective-permute-done.9.refs_1_, ...), custom_call_target="tpu_custom_call" | custom-call | tf_op jit(solution)/shard_map/pallas_call | solution.py:253
  140.8 2.3 %collective-permute-done.13.refs_1_ = bf16[64,4096]{1,0:T(8,128)(2,1)} collective-permute-done((bf16[64,4096]{1,0:T(8,128)(2,1)}, bf16[64,4096]{1,0:T(8,128)(2,1)}, u32[]{:S(2)}, u32[]{:S(2)}) %collective-permute-start.13) | collective-permute-done | bytes 524320 | tf_op jit(solution)/shard_map/ppermute | solution.py:327
  143.1 2.1 %collective-permute-done.14.refs_2_ = bf16[64,4096]{1,0:T(8,128)(2,1)} collective-permute-done((bf16[64,4096]{1,0:T(8,128)(2,1)}, bf16[64,4096]{1,0:T(8,128)(2,1)}, u32[]{:S(2)}, u32[]{:S(2)}) %collective-permute-start.14) | collective-permute-done | bytes 524320 | tf_op jit(solution)/shard_map/ppermute | solution.py:327
  145.2 2.7 %shard_map.183 = bf16[384,512]{1,0:T(8,128)(2,1)S(1)} custom-call(bf16[384,4096]{1,0:T(8,128)(2,1)S(1)} %collective-permute-done.refs_3_.tok_ref, bf16[192,512]{1,0:T(8,128)(2,1)S(1)} %fusion.1.spread_ref, bf16[384,512]{1,0:T(8,128)(2,1)S(1)} %shard_map.180.early_ref, bf16[64,4096]{1,0:T(8,128)(2,1)} %collective-permute-done.12.refs_0_, ...), custom_call_target="tpu_custom_call" | custom-call | tf_op jit(solution)/shard_map/pallas_call | solution.py:271
  147.9 11.2 %collective-permute-start.15 = (bf16[384,512]{1,0:T(8,128)(2,1)S(1)}, bf16[384,512]{1,0:T(8,128)(2,1)S(1)}, u32[]{:S(2)}, u32[]{:S(2)}) collective-permute-start(bf16[384,512]{1,0:T(8,128)(2,1)S(1)} %shard_map.183), channel_id=1, source_target_pairs={{0,32},{32,0},{1,33},{33,1},{2,34},{34,2},{3,35},{35,3},{4,36},{36... | collective-permute-start | bytes 1179656 | tf_op jit(solution)/shard_map/ppermute | solution.py:304
  159.1 2.7 %shard_map.182.own_ref = bf16[384,512]{1,0:T(8,128)(2,1)S(1)} custom-call(bf16[384,4096]{1,0:T(8,128)(2,1)S(1)} %copy-done, bf16[192,512]{1,0:T(8,128)(2,1)S(1)} %fusion.1.spread_ref, bf16[384,512]{1,0:T(8,128)(2,1)S(1)} %shard_map.181.early_ref, bf16[64,4096]{1,0:T(8,128)(2,1)} %collective-permute-done.12.refs_0_, ...), custom_call_target="tpu_custom_call" | custom-call | tf_op jit(solution)/shard_map/pallas_call | solution.py:271
  161.8 1.0 shard_map.184
  (57 shorter events, 5.5 us)
Async XLA Ops:
  0.6 12.3 %collective-permute-start = (bf16[384,4096]{1,0:T(8,128)(2,1)}, bf16[384,4096]{1,0:T(8,128)(2,1)S(1)}, u32[]{:S(2)}, u32[]{:S(2)}) collective-permute-start(bf16[384,4096]{1,0:T(8,128)(2,1)} %tok_ref.3), channel_id=1, source_target_pairs={{0,32},{32,0},{1,33},{33,1},{2,34},{34,2},{3,35},{35,3},{4,36},{36... | collective-permute-start | bytes 9437192 | tf_op jit(solution)/shard_map/ppermute | solution.py:304
  4.0 9.0 %collective-permute-start.1 = (bf16[384,1024]{1,0:T(8,128)(2,1)}, bf16[384,1024]{1,0:T(8,128)(2,1)}, u32[]{:S(2)}, u32[]{:S(2)}) collective-permute-start(bf16[384,1024]{1,0:T(8,128)(2,1)} %refs_7_.1), channel_id=1, source_target_pairs={{0,32},{32,0},{1,33},{33,1},{2,34},{34,2},{3,35},{35,3},{4,36},{36... | collective-permute-start | bytes 2359304 | tf_op jit(solution)/shard_map/ppermute | solution.py:304
  4.1 8.9 %collective-permute-start.2 = (s32[8,32]{1,0:T(8,128)}, s32[8,32]{1,0:T(8,128)S(1)}, u32[]{:S(2)}, u32[]{:S(2)}) collective-permute-start(s32[8,32]{1,0:T(8,128)} %bitcast.29), channel_id=1, source_target_pairs={{0,32},{32,0},{1,33},{33,1},{2,34},{34,2},{3,35},{35,3},{4,36},{36... | collective-permute-start | bytes 3080 | tf_op jit(solution)/shard_map/ppermute | solution.py:304
  4.5 8.5 %copy-start.5 = (bf16[128,128]{1,0:T(8,128)(2,1)S(1)}, bf16[128,128]{1,0:T(8,128)(2,1)}, u32[]{:S(2)}) copy-start(bf16[128,128]{1,0:T(8,128)(2,1)} %constant.125.refs_10_) | copy-start | bytes 98308
  4.5 8.5 %copy-start.6 = (bf16[128,128]{1,0:T(8,128)(2,1)S(1)}, bf16[128,128]{1,0:T(8,128)(2,1)}, u32[]{:S(2)}) copy-start(bf16[128,128]{1,0:T(8,128)(2,1)} %constant.126.refs_11_) | copy-start | bytes 98308
  4.5 8.5 %copy-start.7 = (s32[32,128]{1,0:T(8,128)S(1)}, s32[32,128]{1,0:T(8,128)}, u32[]{:S(2)}) copy-start(s32[32,128]{1,0:T(8,128)} %refs_8_.5) | copy-start | bytes 49156
  17.9 10.2 %collective-permute-start.6 = (bf16[128,2048]{1,0:T(8,128)(2,1)S(1)}, bf16[128,2048]{1,0:T(8,128)(2,1)S(1)}, u32[]{:S(2)}, u32[]{:S(2)}) collective-permute-start(bf16[128,2048]{1,0:T(8,128)(2,1)S(1)} %get-tuple-element.22), channel_id=1, source_target_pairs={{0,2},{1,3},{2,0},{3,1},{32,160},{33,161},{34,162},{35,163},{64,66... | collective-permute-start | bytes 1572872 | tf_op jit(solution)/shard_map/ppermute | solution.py:327
  19.2 14.3 %collective-permute-start.7 = (bf16[128,2048]{1,0:T(8,128)(2,1)S(1)}, bf16[128,2048]{1,0:T(8,128)(2,1)S(1)}, u32[]{:S(2)}, u32[]{:S(2)}) collective-permute-start(bf16[128,2048]{1,0:T(8,128)(2,1)S(1)} %get-tuple-element.23), channel_id=1, source_target_pairs={{0,1},{1,2},{2,3},{3,0},{32,96},{33,97},{34,98},{35,99},{64,65},{6... | collective-permute-start | bytes 1572872 | tf_op jit(solution)/shard_map/ppermute | solution.py:327
  19.6 13.9 %collective-permute-start.8 = (bf16[128,2048]{1,0:T(8,128)(2,1)S(1)}, bf16[128,2048]{1,0:T(8,128)(2,1)S(1)}, u32[]{:S(2)}, u32[]{:S(2)}) collective-permute-start(bf16[128,2048]{1,0:T(8,128)(2,1)S(1)} %get-tuple-element.24), channel_id=1, source_target_pairs={{0,3},{1,0},{2,1},{3,2},{32,224},{33,225},{34,226},{35,227},{64,67... | collective-permute-start | bytes 1572872 | tf_op jit(solution)/shard_map/ppermute | solution.py:327
  27.4 6.5 %copy-start.3 = (bf16[128,2048]{1,0:T(8,128)(2,1)}, bf16[128,2048]{1,0:T(8,128)(2,1)S(1)}, u32[]{:S(2)}) copy-start(bf16[128,2048]{1,0:T(8,128)(2,1)S(1)} %get-tuple-element.17.refs_0_) | copy-start | bytes 1572868
  27.4 25.3 %copy-start.8 = (s32[4,32]{1,0:T(4,128)S(1)}, s32[4,32]{1,0:T(4,128)}, u32[]{:S(2)}) copy-start(s32[4,32]{1,0:T(4,128)} %param.22) | copy-start | bytes 1540
  27.4 11.8 %collective-permute-start.3 = (bf16[128,2048]{1,0:T(8,128)(2,1)}, bf16[128,2048]{1,0:T(8,128)(2,1)}, u32[]{:S(2)}, u32[]{:S(2)}) collective-permute-start(bf16[128,2048]{1,0:T(8,128)(2,1)} %get-tuple-element.18), channel_id=1, source_target_pairs={{0,2},{1,3},{2,0},{3,1},{32,160},{33,161},{34,162},{35,163},{64,66... | collective-permute-start | bytes 1572872 | tf_op jit(solution)/shard_map/ppermute | solution.py:327
  28.1 16.9 %collective-permute-start.4 = (bf16[128,2048]{1,0:T(8,128)(2,1)}, bf16[128,2048]{1,0:T(8,128)(2,1)}, u32[]{:S(2)}, u32[]{:S(2)}) collective-permute-start(bf16[128,2048]{1,0:T(8,128)(2,1)} %get-tuple-element.19), channel_id=1, source_target_pairs={{0,1},{1,2},{2,3},{3,0},{32,96},{33,97},{34,98},{35,99},{64,65},{6... | collective-permute-start | bytes 1572872 | tf_op jit(solution)/shard_map/ppermute | solution.py:327
  28.1 16.9 %collective-permute-start.5 = (bf16[128,2048]{1,0:T(8,128)(2,1)}, bf16[128,2048]{1,0:T(8,128)(2,1)}, u32[]{:S(2)}, u32[]{:S(2)}) collective-permute-start(bf16[128,2048]{1,0:T(8,128)(2,1)} %get-tuple-element.20), channel_id=1, source_target_pairs={{0,3},{1,0},{2,1},{3,2},{32,224},{33,225},{34,226},{35,227},{64,67... | collective-permute-start | bytes 1572872 | tf_op jit(solution)/shard_map/ppermute | solution.py:327
  33.4 37.0 %copy-start.9 = (s32[5]{0:T(128)S(1)}, s32[5]{0:T(128)}, u32[]{:S(2)}) copy-start(s32[5]{0:T(128)} %constant.124) | copy-start | bytes 64
  33.9 0.8 copy-start.1
  34.8 13.6 %all-to-all-start.1 = ((bf16[4,32,2048]{2,1,0:T(8,128)(2,1)}), bf16[4,32,2048]{2,1,0:T(8,128)(2,1)}, u32[]{:S(2)}, u32[]{:S(2)}) async-start(bf16[4,32,2048]{2,1,0:T(8,128)(2,1)} %bitcast.26), calls=%async_computation.1 | async-start | bytes 1048576 | tf_op jit(solution)/shard_map/all_to_all | solution.py:349
  45.0 1.0 copy-start.4
  47.6 0.8 copy-start.2
  48.4 11.4 %all-to-all-start = ((bf16[4,32,2048]{2,1,0:T(8,128)(2,1)}), bf16[4,32,2048]{2,1,0:T(8,128)(2,1)}, u32[]{:S(2)}, u32[]{:S(2)}) async-start(bf16[4,32,2048]{2,1,0:T(8,128)(2,1)} %bitcast.27), calls=%async_computation | async-start | bytes 1048576 | tf_op jit(solution)/shard_map/all_to_all | solution.py:349
  61.7 18.2 %all-to-all-start.2 = ((bf16[8,8,2048]{2,1,0:T(8,128)(2,1)}), bf16[8,8,2048]{2,1,0:T(8,128)(2,1)S(1)}, u32[]{:S(2)}, u32[]{:S(2)}) async-start(bf16[8,8,2048]{2,1,0:T(8,128)(2,1)} %shard_map.179), calls=%async_computation.2 | async-start | bytes 524288 | tf_op jit(solution)/shard_map/all_to_all | solution.py:348
  83.7 12.8 %all-to-all-start.3 = ((bf16[8,4,4096]{2,1,0:T(4,128)(2,1)}), bf16[8,4,4096]{2,1,0:T(4,128)(2,1)S(1)}, u32[]{:S(2)}, u32[]{:S(2)}) async-start(bf16[8,4,4096]{2,1,0:T(4,128)(2,1)} %broadcast_in_dim.122), calls=%async_computation.3 | async-start | bytes 524288 | tf_op jit(solution)/shard_map/all_to_all | solution.py:348
  99.0 11.1 %all-to-all-start.4 = ((bf16[4,16,4096]{2,1,0:T(8,128)(2,1)}), bf16[4,16,4096]{2,1,0:T(8,128)(2,1)}, u32[]{:S(2)}, u32[]{:S(2)}) async-start(bf16[4,16,4096]{2,1,0:T(8,128)(2,1)} %broadcast_in_dim.124), calls=%async_computation.4 | async-start | bytes 1048576 | tf_op jit(solution)/shard_map/all_to_all | solution.py:349
  110.2 18.0 %collective-permute-start.10 = (bf16[64,4096]{1,0:T(8,128)(2,1)}, bf16[64,4096]{1,0:T(8,128)(2,1)}, u32[]{:S(2)}, u32[]{:S(2)}) collective-permute-start(bf16[64,4096]{1,0:T(8,128)(2,1)} %bitcast.9.refs_0_), channel_id=1, source_target_pairs={{0,1},{1,2},{2,3},{3,0},{32,96},{33,97},{34,98},{35,99},{64,65},{6... | collective-permute-start | bytes 1572872 | tf_op jit(solution)/shard_map/ppermute | solution.py:327
  112.5 11.2 %all-to-all-start.5 = ((bf16[4,16,4096]{2,1,0:T(8,128)(2,1)}), bf16[4,16,4096]{2,1,0:T(8,128)(2,1)}, u32[]{:S(2)}, u32[]{:S(2)}) async-start(bf16[4,16,4096]{2,1,0:T(8,128)(2,1)} %broadcast_in_dim.126), calls=%async_computation.5 | async-start | bytes 1048576 | tf_op jit(solution)/shard_map/all_to_all | solution.py:349
  116.8 14.5 %collective-permute-start.11 = (bf16[64,4096]{1,0:T(8,128)(2,1)}, bf16[64,4096]{1,0:T(8,128)(2,1)}, u32[]{:S(2)}, u32[]{:S(2)}) collective-permute-start(bf16[64,4096]{1,0:T(8,128)(2,1)} %bitcast.9.refs_0_), channel_id=1, source_target_pairs={{0,3},{1,0},{2,1},{3,2},{32,224},{33,225},{34,226},{35,227},{64,67... | collective-permute-start | bytes 1572872 | tf_op jit(solution)/shard_map/ppermute | solution.py:327
  118.1 13.3 %collective-permute-start.9 = (bf16[64,4096]{1,0:T(8,128)(2,1)}, bf16[64,4096]{1,0:T(8,128)(2,1)}, u32[]{:S(2)}, u32[]{:S(2)}) collective-permute-start(bf16[64,4096]{1,0:T(8,128)(2,1)} %bitcast.9.refs_0_), channel_id=1, source_target_pairs={{0,2},{1,3},{2,0},{3,1},{32,160},{33,161},{34,162},{35,163},{64,66... | collective-permute-start | bytes 1572872 | tf_op jit(solution)/shard_map/ppermute | solution.py:327
  123.7 17.1 %collective-permute-start.12 = (bf16[64,4096]{1,0:T(8,128)(2,1)}, bf16[64,4096]{1,0:T(8,128)(2,1)}, u32[]{:S(2)}, u32[]{:S(2)}) collective-permute-start(bf16[64,4096]{1,0:T(8,128)(2,1)} %bitcast.10.refs_4_), channel_id=1, source_target_pairs={{0,2},{1,3},{2,0},{3,1},{32,160},{33,161},{34,162},{35,163},{64,66... | collective-permute-start | bytes 1572872 | tf_op jit(solution)/shard_map/ppermute | solution.py:327
  128.1 15.0 %collective-permute-start.13 = (bf16[64,4096]{1,0:T(8,128)(2,1)}, bf16[64,4096]{1,0:T(8,128)(2,1)}, u32[]{:S(2)}, u32[]{:S(2)}) collective-permute-start(bf16[64,4096]{1,0:T(8,128)(2,1)} %bitcast.10.refs_4_), channel_id=1, source_target_pairs={{0,1},{1,2},{2,3},{3,0},{32,96},{33,97},{34,98},{35,99},{64,65},{6... | collective-permute-start | bytes 1572872 | tf_op jit(solution)/shard_map/ppermute | solution.py:327
  128.1 17.1 %collective-permute-start.14 = (bf16[64,4096]{1,0:T(8,128)(2,1)}, bf16[64,4096]{1,0:T(8,128)(2,1)}, u32[]{:S(2)}, u32[]{:S(2)}) collective-permute-start(bf16[64,4096]{1,0:T(8,128)(2,1)} %bitcast.10.refs_4_), channel_id=1, source_target_pairs={{0,3},{1,0},{2,1},{3,2},{32,224},{33,225},{34,226},{35,227},{64,67... | collective-permute-start | bytes 1572872 | tf_op jit(solution)/shard_map/ppermute | solution.py:327
  131.4 1.9 %copy-start = (bf16[384,4096]{1,0:T(8,128)(2,1)S(1)}, bf16[384,4096]{1,0:T(8,128)(2,1)}, u32[]{:S(2)}) copy-start(bf16[384,4096]{1,0:T(8,128)(2,1)} %tok_ref.3) | copy-start | bytes 9437188
  147.9 13.9 %collective-permute-start.15 = (bf16[384,512]{1,0:T(8,128)(2,1)S(1)}, bf16[384,512]{1,0:T(8,128)(2,1)S(1)}, u32[]{:S(2)}, u32[]{:S(2)}) collective-permute-start(bf16[384,512]{1,0:T(8,128)(2,1)S(1)} %shard_map.183), channel_id=1, source_target_pairs={{0,32},{32,0},{1,33},{33,1},{2,34},{34,2},{3,35},{35,3},{4,36},{36... | collective-permute-start | bytes 1179656 | tf_op jit(solution)/shard_map/ppermute | solution.py:304

commit v8 on v6

--- a/solution.py
+++ b/solution.py
@@ -92,7 +92,7 @@
             from_y = lax.rem(group - at_y + groups, groups)
             for spot in range(spots):
                 from_x = lax.rem(spot - at_x + spots, spots)
-                piece = jnp.where(core == 0, from_x * groups + group, from_y * spots + spot)
+                piece = jnp.where(core == 0, from_x * groups + from_y, from_y * spots + from_x)
                 rows = pl.ds(pl.multiple_of(piece * part, part), part)
                 values = grad_t[spot * part : (spot + 1) * part]
                 grad_t_ref[rows, :token_rows] = values
@@ -119,7 +119,7 @@
     terms = jnp.dot(grad_t_ref[...], turned_ref[...], preferred_element_type=jnp.float32)
     for first in range(4):
         for second in range(4):
-            group = jnp.where(core == 0, second, lax.rem(at_y + first, groups))
+            group = lax.rem(at_y + jnp.where(core == 0, second, first), groups)
             start = (first * 4 + second) * part
             rows = slice(start, start + part)
             limit = limit_ref[pl.ds(2 * group + core, 1), :]
@@ -183,104 +183,128 @@
     )(*place, *operands)
 
 
+def added_up(refs):
+    total = refs[0][...].astype(jnp.float32)
+    for ref in refs[1:]:
+        total = total + ref[...].astype(jnp.float32)
+    return total
+
+
 def line_kernel(count, *refs):
-    out_ref = refs[-1]
-    sums = []
-    for terms in (refs[:count], refs[count:-1]):
-        total = terms[0][...].astype(jnp.float32)
-        for ref in terms[1:]:
-            total = total + ref[...].astype(jnp.float32)
-        sums.append(total)
+    out_refs = refs[2 * count :]
+    sums = added_up(refs[:count]), added_up(refs[count : 2 * count])
     rows = 8
+    pairs = sums[0].shape[0] // rows // len(out_refs)
     for at in range(sums[0].shape[0] // rows):
         left, right = (total[at * rows : (at + 1) * rows] for total in sums)
         upper = lax.broadcasted_iota(jnp.int32, left.shape, 0) < rows // 2
         even = jnp.where(upper, left, pltpu.roll(right, rows // 2, 0))
         odd = jnp.where(upper, pltpu.roll(left, rows // 2, 0), right)
-        out_ref[2 * at] = even.astype(jnp.bfloat16)
-        out_ref[2 * at + 1] = odd.astype(jnp.bfloat16)
+        out_refs[at // pairs][2 * (at % pairs)] = even.astype(jnp.bfloat16)
+        out_refs[at // pairs][2 * (at % pairs) + 1] = odd.astype(jnp.bfloat16)
 
 
 def line_sums(left_terms, right_terms):
     rows, half = left_terms[0].shape
     width = 1024
     count = len(left_terms)
+    shape = (rows // 16, 8, half)
     body = lambda *refs: line_kernel(count, *refs)
     return pl.pallas_call(
         body,
         grid=(half // width,),
         in_specs=[pl.BlockSpec((rows, width), lambda n: (0, n))] * (2 * count),
-        out_specs=pl.BlockSpec((rows // 4, 8, width), lambda n: (0, 0, n)),
-        out_shape=jax.ShapeDtypeStruct((rows // 4, 8, half), jnp.bfloat16),
+        out_specs=[pl.BlockSpec((*shape[:2], width), lambda n: (0, 0, n))] * 4,
+        out_shape=[jax.ShapeDtypeStruct(shape, jnp.bfloat16)] * 4,
         compiler_params=pltpu.CompilerParams(vmem_limit_bytes=16 << 20),
     )(*left_terms, *right_terms)
 
 
-def face_kernel(parts_ref, out_ref):
-    total = parts_ref[0].astype(jnp.float32)
-    for at in range(1, parts_ref.shape[0]):
-        total = total + parts_ref[at].astype(jnp.float32)
-    out_ref[...] = total.astype(jnp.bfloat16)
-
-
-def face_sum(parts):
-    count, count_z, rows, half = parts.shape
+def face_kernel(*refs):
+    refs[-1][...] = added_up(refs[:-1]).astype(jnp.bfloat16)
+
+
+def face_sum(terms):
+    count_z, rows, half = terms[0].shape
     width = 1024
+    spec = pl.BlockSpec((count_z, rows, width), lambda n: (0, 0, n))
     return pl.pallas_call(
         face_kernel,
         grid=(half // width,),
-        in_specs=[pl.BlockSpec((count, count_z, rows, width), lambda n: (0, 0, 0, n))],
-        out_specs=pl.BlockSpec((count_z, rows, width), lambda n: (0, 0, n)),
-        out_shape=jax.ShapeDtypeStruct((count_z, rows, half), jnp.bfloat16),
+        in_specs=[spec] * len(terms),
+        out_specs=spec,
+        out_shape=jax.ShapeDtypeStruct(terms[0].shape, jnp.bfloat16),
         compiler_params=pltpu.CompilerParams(vmem_limit_bytes=16 << 20),
-    )(parts)
-
-
-def product(tok_ref, weight_refs):
+    )(*terms)
+
+
+def pack_kernel(*refs):
+    rows = refs[0].shape[0]
+    for at, ref in enumerate(refs[:-1]):
+        refs[-1][at * rows : (at + 1) * rows, :] = ref[...]
+
+
+def packed(pieces):
+    rows, model_width = pieces[0].shape
+    whole = pl.BlockSpec(memory_space=pltpu.VMEM)
+    return pl.pallas_call(
+        pack_kernel,
+        in_specs=[whole] * len(pieces),
+        out_specs=whole,
+        out_shape=jax.ShapeDtypeStruct((len(pieces) * rows, model_width), jnp.bfloat16),
+        compiler_params=pltpu.CompilerParams(vmem_limit_bytes=8 << 20),
+    )(*pieces)
+
+
+def product_kernel(added, tok_ref, spread_ref, *refs):
+    early_refs, weight_refs, (out_ref, total_ref) = refs[:added], refs[added:-2], refs[-2:]
     weights = jnp.concatenate([ref[...] for ref in weight_refs], axis=0)
-    return lax.dot_general(
+    part = lax.dot_general(
         tok_ref[...], weights, (((1,), (1,)), ((), ())), preferred_element_type=jnp.float32
-    ).astype(jnp.bfloat16)
-
-
-def early_kernel(tok_ref, *refs):
-    refs[-1][...] = product(tok_ref, refs[:-1])
-
-
-def early_product(tokens, weights):
-    whole = pl.BlockSpec(memory_space=pltpu.VMEM)
-    columns = sum(value.shape[0] for value in weights)
-    return pl.pallas_call(
-        early_kernel,
-        in_specs=[whole] * (1 + len(weights)),
-        out_specs=whole,
-        out_shape=jax.ShapeDtypeStruct((tokens.shape[0], columns), jnp.bfloat16),
+    )
+    step = pl.program_id(0)
+
+    @pl.when(step == 0)
+    def _():
+        total_ref[...] = part
+
+    @pl.when(step > 0)
+    def _():
+        total_ref[...] += part
+
+    @pl.when(step == pl.num_programs(0) - 1)
+    def _():
+        out = jnp.dot(
+            total_ref[...].astype(jnp.bfloat16),
+            spread_ref[...],
+            preferred_element_type=jnp.float32,
+        )
+        for early_ref in early_refs:
+            out = out + early_ref[...].astype(jnp.float32)
+        out_ref[...] = out.astype(jnp.bfloat16)
+
+
+def spread_product(tokens, spread, weights, early=()):
+    token_rows, model_width = tokens.shape
+    rows, columns = spread.shape
+    width = 1024
+    whole = lambda n: (0, 0)
+    split = lambda n: (0, n)
+    body = lambda *refs: product_kernel(len(early), *refs)
+    return pl.pallas_call(
+        body,
+        grid=(model_width // width,),
+        in_specs=[
+            pl.BlockSpec((token_rows, width), split),
+            pl.BlockSpec((rows, columns), whole),
+            *[pl.BlockSpec((token_rows, columns), whole) for _ in early],
+            *[pl.BlockSpec((value.shape[0], width), split) for value in weights],
+        ],
+        out_specs=pl.BlockSpec((token_rows, columns), whole),
+        out_shape=jax.ShapeDtypeStruct((token_rows, columns), jnp.bfloat16),
+        scratch_shapes=[pltpu.VMEM((token_rows, rows), jnp.float32)],
         compiler_params=pltpu.CompilerParams(vmem_limit_bytes=20 << 20),
-    )(tokens, *weights)
-
-
-def late_kernel(count, tok_ref, spread_ref, *refs):
-    pieces = [ref[...] for ref in refs[:count]]
-    pieces.append(product(tok_ref, refs[count:-1]))
-    start, out = 0, None
-    for piece in pieces:
-        stop = start + piece.shape[1]
-        part = jnp.dot(piece, spread_ref[start:stop, :], preferred_element_type=jnp.float32)
-        out = part if out is None else out + part
-        start = stop
-    refs[-1][...] = out.astype(jnp.bfloat16)
-
-
-def late_product(tokens, spread, done, weights):
-    whole = pl.BlockSpec(memory_space=pltpu.VMEM)
-    body = lambda *refs: late_kernel(len(done), *refs)
-    return pl.pallas_call(
-        body,
-        in_specs=[whole] * (2 + len(done) + len(weights)),
-        out_specs=whole,
-        out_shape=jax.ShapeDtypeStruct((tokens.shape[0], spread.shape[1]), jnp.bfloat16),
-        compiler_params=pltpu.CompilerParams(vmem_limit_bytes=20 << 20),
-    )(tokens, spread, *done, *weights)
+    )(tokens, spread, *early, *weights)
 
 
 def interleave_kernel(core_ref, own_ref, peer_ref, out_ref):
@@ -310,18 +334,6 @@
     return lax.ppermute(value, "c", [(0, 1), (1, 0)])
 
 
-def face_groups(first):
-    at = lambda y, c, x: (y * 2 + c) * 4 + x
-    groups = []
-    for core in (0, 1):
-        for line in range(4):
-            if (core == 0) == first:
-                groups.append([at(line, core, spot) for spot in range(4)])
-            else:
-                groups.append([at(spot, core, line) for spot in range(4)])
-    return groups
-
-
 def shifted(value, axis_at, shift):
     pairs = []
     for y in range(4):
@@ -335,31 +347,19 @@
 
 def column_spread(place, offsets, count_z, rows_dev):
     core, at_x, at_y = place
-    shift = jnp.asarray([offset[0] for offset in offsets], jnp.int32)
+    first = jnp.asarray([offset[0] for offset in offsets], jnp.int32)
     second = jnp.asarray([offset[1] for offset in offsets], jnp.int32)
-    from_x = jnp.where(core == 0, (at_x - shift) % 4, second)
-    from_y = jnp.where(core == 0, second, (at_y - shift) % 4)
+    from_x = (at_x - jnp.where(core == 0, first, second)) % 4
+    from_y = (at_y - jnp.where(core == 0, second, first)) % 4
     at_z = jnp.arange(count_z, dtype=jnp.int32)[None, :, None]
     at_j = jnp.arange(rows_dev, dtype=jnp.int32)[None, None, :]
     column = (
         (from_y[:, None, None] * count_z + at_z) * 4 + from_x[:, None, None]
     ) * rows_dev + at_j
-    size = len(offsets) * count_z * rows_dev
-    return (column.reshape(size, 1) == jnp.arange(size, dtype=jnp.int32)[None, :]).astype(
+    size = 16 * count_z * rows_dev
+    return (column.reshape(-1, 1) == jnp.arange(size, dtype=jnp.int32)[None, :]).astype(
         jnp.bfloat16
     )
-
-
-def exchanged(value, step):
-    if step == "z":
-        return lax.all_to_all(value, "z", 0, 0, tiled=True)
-    return lax.all_to_all(
-        value, FACE, 0, 0, tiled=True, axis_index_groups=face_groups(step == "first")
-    )
-
-
-def gathered(value, count, step):
-    return exchanged(jnp.broadcast_to(value[None], (count, *value.shape)), step)
 
 
 def shards(
@@ -399,8 +399,8 @@
         )
         halves.append([pair_sums[0], *(shifted(pair_sums[far], 0, far) for far in (2, 1, 3))])
     lines = line_sums(*halves)
-    lines = exchanged(lines.reshape(4, count_z, 2 * rows_dev, -1), "second")
-    parts = exchanged(face_sum(lines), "z")
+    face = face_sum([lines[0], *(shifted(lines[far], 1, far) for far in (2, 1, 3))])
+    parts = lax.all_to_all(face, "z", 0, 0, tiled=True)
     summed = jnp.sum(parts.astype(jnp.float32), axis=0)
     summed = jnp.swapaxes(summed.reshape(2, rows_dev, -1), 0, 1).reshape(rows_dev, model_width)
     gradient = unrotate_rows(summed, sign_rows, matrix)
@@ -412,21 +412,21 @@
     diff_bound = clip_level * jnp.exp2(diff_exps.astype(jnp.float32))
     diff_coded = clip_rows(new_master - base_own, diff_bound).astype(jnp.bfloat16)
     effective = (base_own + diff_coded.astype(jnp.float32)).astype(jnp.bfloat16)
-    stacked = gathered(effective, count_z, "z").reshape(count_z * rows_dev, model_width)
-    face = gathered(stacked, 4, "second").reshape(-1, model_width)
-    middle = face.shape[0] // 2
-    sent = [face[:middle], face[middle:]]
-    arrived = [[shifted(rows, 0, far) for far in (2, 1, 3)] for rows in sent]
-    offsets = [(0, at) for at in range(4)]
-    offsets += [(far, at) for start in (0, 2) for far in (2, 1, 3) for at in (start, start + 1)]
-    spread = column_spread(place, offsets, count_z, rows_dev)
-    done = [
-        [early_product(rows, [face]), early_product(rows, arrived[0])]
-        for rows in (tokens, peer_tokens)
-    ]
-    done, last = lax.optimization_barrier((done, arrived[1]))
-    peer_part = swapped(late_product(peer_tokens, spread, done[1], last))
-    own_part = late_product(tokens, spread, done[0], last)
+    stacked = lax.all_to_all(
+        jnp.broadcast_to(effective[None], (count_z, *effective.shape)), "z", 0, 0, tiled=True
+    ).reshape(count_z * rows_dev, model_width)
+    order_far = (0, 2, 1, 3)
+    face = packed([stacked, *(shifted(stacked, 1, far) for far in order_far[1:])])
+    arrived = [shifted(face, 0, far) for far in order_far[1:]]
+    spread = column_spread(
+        place, [(first, second) for first in order_far for second in order_far], count_z, rows_dev
+    )
+    near_rows = face.shape[0]
+    early = [spread_product(rows, spread[:near_rows], [face]) for rows in (peer_tokens, tokens)]
+    early, arrived = lax.optimization_barrier((early, arrived))
+    late_spread = spread[near_rows:]
+    peer_part = swapped(spread_product(peer_tokens, late_spread, arrived, early[:1]))
+    own_part = spread_product(tokens, late_spread, arrived, early[1:])
     projected = interleaved(place[0], own_part, peer_part)
     return (projected, new_master, new_first, new_second)
 

time: 151 us -> 154 us (1.020)
  the two profiles are of different devices: /device:TPU:1 before, /device:TPU:73 now
where the time goes in v8:
time: 154 us; the launch traced here: 153 us
  starting transfers between devices  46.4 us (30%)
  waiting for transfers between devices  46.3 us (30%)
  Pallas kernels  38.8 us (25%)
  blocking collectives  12.5 us (8%)
  other arithmetic  3.42 us (2%)
  local copies, waits for them, and re-layouts  3.38 us (2%)
    ppermute x15, waiting for transfers between devices, shifted(): return lax.ppermute(value, FACE, pairs)  40.4 us
    ppermute x4, starting transfers between devices, swapped(): return lax.ppermute(value, 'c', [(0, 1), (1, 0)])  19.6 us
    ppermute x15, starting transfers between devices, shifted(): return lax.ppermute(value, FACE, pairs)  19.3 us
    pallas_call x3, Pallas kernels, coded_gradient(): pl.pallas_call(body, grid_spec=pltpu.PrefetchScalarGridSpec(num_scalar_pr...  18.2 us
    pallas_call x4, Pallas kernels, spread_product(): pl.pallas_call(body, grid=(model_width // width,), in_specs=[pl.BlockSpec...  16.6 us
    all_to_all x1, blocking collectives, shards(): lax.all_to_all(jnp.broadcast_to(effective[None], (count_z, *effective.sha...  12.5 us
    all_to_all x1, starting transfers between devices, shards(): parts = lax.all_to_all(face, 'z', 0, 0, tiled=True)  7.56 us
    all_to_all x1, waiting for transfers between devices, shards(): parts = lax.all_to_all(face, 'z', 0, 0, tiled=True)  5.89 us
  transfers between devices with their start and end apart: 20, of which 12 were waited for; matrix products, arithmetic and copies ran while one was open for 1% of the time, Pallas kernels for 16%

profile of v8, /device:TPU:73, one launch (start us, length us, event | category | flops | bytes accessed | tf_op | source)
XLA Modules:
  0.0 152.7 jit_solution(309994214967097595)
XLA Ops:
  0.6 0.8 collective-permute-start
  1.5 0.4 collective-permute-start.2
  1.9 8.5 %shard_map.156.refs_12_ = bf16[512,4096]{1,0:T(8,128)(2,1)} custom-call(s32[1]{0:T(128)} %bitcast.refs_0_.core_ref, s32[1]{0:T(128)} %bitcast.2.refs_1_, s32[1]{0:T(128)} %bitcast.3.refs_2_, bf16[384,4096]{1,0:T(8,128)(2,1)} %refs_0_.3, bf16[384,1024]{1,0:T(8,128)(2,1)} %refs_7_.1, bf16[384,1024]{1,0:T(8,128)(2,1)} %refs_7_.1, bf16[384,1024]{1,0:T(8,128)(2,1)} %refs_7_.1, ...), custom_call_target="tpu_custom_call" | custom-call | tf_op jit(solution)/shard_map/pallas_call | solution.py:166
  10.4 4.9 %shard_map.157 = (bf16[128,2048]{1,0:T(8,128)(2,1)S(1)}, bf16[128,2048]{1,0:T(8,128)(2,1)S(1)}, bf16[128,2048]{1,0:T(8,128)(2,1)S(1)}, bf16[128,2048]{1,0:T(8,128)(2,1)S(1)}) custom-call(s32[1]{0:T(128)} %bitcast.refs_0_.core_ref, s32[1]{0:T(128)} %bitcast.2.refs_1_, s32[1]{0:T(128)} %bitcast.3.refs_2_, ...), custom_call_target="tpu_custom_call" | custom-call | tf_op jit(solution)/shard_map/pallas_call | solution.py:166
  15.3 2.1 %collective-permute-start.3 = (bf16[128,2048]{1,0:T(8,128)(2,1)S(1)}, bf16[128,2048]{1,0:T(8,128)(2,1)S(1)}, u32[]{:S(2)}, u32[]{:S(2)}) collective-permute-start(bf16[128,2048]{1,0:T(8,128)(2,1)S(1)} %get-tuple-element.22), channel_id=1, source_target_pairs={{0,2},{1,3},{2,0},{3,1},{32,160},{33,161},{34,162},{35,163},{64,66... | collective-permute-start | bytes 1572872 | tf_op jit(solution)/shard_map/ppermute | solution.py:345
  17.4 1.5 collective-permute-start.5
  18.9 4.8 %shard_map.158 = (bf16[128,2048]{1,0:T(8,128)(2,1)S(1)}, bf16[128,2048]{1,0:T(8,128)(2,1)S(1)}, bf16[128,2048]{1,0:T(8,128)(2,1)S(1)}, bf16[128,2048]{1,0:T(8,128)(2,1)S(1)}) custom-call(s32[1]{0:T(128)} %bitcast.refs_0_.core_ref, s32[1]{0:T(128)} %bitcast.2.refs_1_, s32[1]{0:T(128)} %bitcast.3.refs_2_, ...), custom_call_target="tpu_custom_call" | custom-call | tf_op jit(solution)/shard_map/pallas_call | solution.py:166
  23.7 1.5 collective-permute-start.6
  25.2 2.1 %collective-permute-start.7 = (bf16[128,2048]{1,0:T(8,128)(2,1)S(1)}, bf16[128,2048]{1,0:T(8,128)(2,1)S(1)}, u32[]{:S(2)}, u32[]{:S(2)}) collective-permute-start(bf16[128,2048]{1,0:T(8,128)(2,1)S(1)} %get-tuple-element.27), channel_id=1, source_target_pairs={{0,1},{1,2},{2,3},{3,0},{32,96},{33,97},{34,98},{35,99},{64,65},{6... | collective-permute-start | bytes 1572872 | tf_op jit(solution)/shard_map/ppermute | solution.py:345
  27.3 3.7 %collective-permute-done.4.refs_2_ = bf16[128,2048]{1,0:T(8,128)(2,1)S(1)} collective-permute-done((bf16[128,2048]{1,0:T(8,128)(2,1)S(1)}, bf16[128,2048]{1,0:T(8,128)(2,1)S(1)}, u32[]{:S(2)}, u32[]{:S(2)}) %collective-permute-start.4) | collective-permute-done | bytes 524320 | tf_op jit(solution)/shard_map/ppermute | solution.py:345
  31.0 5.5 %collective-permute-done.6.refs_5_ = bf16[128,2048]{1,0:T(8,128)(2,1)S(1)} collective-permute-done((bf16[128,2048]{1,0:T(8,128)(2,1)S(1)}, bf16[128,2048]{1,0:T(8,128)(2,1)S(1)}, u32[]{:S(2)}, u32[]{:S(2)}) %collective-permute-start.6) | collective-permute-done | bytes 524320 | tf_op jit(solution)/shard_map/ppermute | solution.py:345
  36.5 5.7 %collective-permute-done.7.refs_6_ = bf16[128,2048]{1,0:T(8,128)(2,1)S(1)} collective-permute-done((bf16[128,2048]{1,0:T(8,128)(2,1)S(1)}, bf16[128,2048]{1,0:T(8,128)(2,1)S(1)}, u32[]{:S(2)}, u32[]{:S(2)}) %collective-permute-start.7) | collective-permute-done | bytes 524320 | tf_op jit(solution)/shard_map/ppermute | solution.py:345
  42.3 1.1 shard_map.159
  43.3 1.5 collective-permute-start.10
  44.8 1.5 collective-permute-start.11
  46.3 1.2 collective-permute-start.9
  47.5 2.5 %collective-permute-done.10.refs_2_ = bf16[8,8,2048]{2,1,0:T(8,128)(2,1)S(1)} collective-permute-done((bf16[8,8,2048]{2,1,0:T(8,128)(2,1)S(1)}, bf16[8,8,2048]{2,1,0:T(8,128)(2,1)S(1)}, u32[]{:S(2)}, u32[]{:S(2)}) %collective-permute-start.10) | collective-permute-done | bytes 262176 | tf_op jit(solution)/shard_map/ppermute | solution.py:345
  50.0 0.3 collective-permute-done.11.refs_3_
  50.3 3.5 %collective-permute-done.9.refs_1_ = bf16[8,8,2048]{2,1,0:T(8,128)(2,1)S(1)} collective-permute-done((bf16[8,8,2048]{2,1,0:T(8,128)(2,1)S(1)}, bf16[8,8,2048]{2,1,0:T(8,128)(2,1)S(1)}, u32[]{:S(2)}, u32[]{:S(2)}) %collective-permute-start.9) | collective-permute-done | bytes 262176 | tf_op jit(solution)/shard_map/ppermute | solution.py:345
  53.8 0.9 shard_map.160
  54.7 7.6 %all-to-all-start = ((bf16[8,8,2048]{2,1,0:T(8,128)(2,1)}), bf16[8,8,2048]{2,1,0:T(8,128)(2,1)S(1)}, u32[]{:S(2)}, u32[]{:S(2)}) async-start(bf16[8,8,2048]{2,1,0:T(8,128)(2,1)} %shard_map.160), calls=%async_computation | async-start | bytes 524288 | tf_op jit(solution)/shard_map/all_to_all | solution.py:403
  62.3 0.6 convert_bitcast_fusion
  63.0 5.9 %all-to-all-done = bf16[8,8,2048]{2,1,0:T(8,128)(2,1)S(1)} async-done(((bf16[8,8,2048]{2,1,0:T(8,128)(2,1)}), bf16[8,8,2048]{2,1,0:T(8,128)(2,1)S(1)}, u32[]{:S(2)}, u32[]{:S(2)}) %all-to-all-start) | async-done | bytes 262176 | tf_op jit(solution)/shard_map/all_to_all | solution.py:403
  69.1 1.0 convolution_multiply_fusion
  70.2 1.8 %fusion.4 = (bf16[4,4096]{1,0:T(4,128)(2,1)S(1)}, f32[4,4096]{1,0:T(4,128)}, f32[4,4096]{1,0:T(4,128)}, f32[4,4096]{1,0:T(4,128)}) fusion(bf16[1,4,32,128]{3,2,1,0:T(8,128)(2,1)S(1)} %get-tuple-element.46, bf16[1,4,32,128]{3,2,1,0:T(8,128)(2,1)S(1)} %get-tuple-element.47, bf16[1024,4096]{1,0:T(8,128)(2,1)} %param.16, s32[]{:T(128)S(6)} %select_n.25, ...), kind=kLoop, calls=%fused_computation.10 | loop fusion | flops 409600 | bytes 606212 | tf_op jit(solution)/shard_map/convert_element_type | solution.py:414
  72.0 12.5 %all_to_all.10 = bf16[8,4,4096]{2,1,0:T(4,128)(2,1)} all-to-all(bf16[8,4,4096]{2,1,0:T(4,128)(2,1)S(1)} %broadcast_in_dim.28), channel_id=1, replica_groups=mesh['y'=4,'c'=2,'z'=8,'x'=4] {'z'}, dimensions={0} | all-to-all | bytes 524288 | tf_op jit(solution)/shard_map/all_to_all | solution.py:415
  84.6 1.0 reshape.110.refs_0_
  85.6 0.9 collective-permute-start.12
  86.5 1.5 collective-permute-start.13
  88.1 1.2 collective-permute-start.14
  89.2 3.3 %collective-permute-done.12.refs_1_ = bf16[32,4096]{1,0:T(8,128)(2,1)S(1)} collective-permute-done((bf16[32,4096]{1,0:T(8,128)(2,1)S(1)}, bf16[32,4096]{1,0:T(8,128)(2,1)S(1)}, u32[]{:S(2)}, u32[]{:S(2)}) %collective-permute-start.12) | collective-permute-done | bytes 262176 | tf_op jit(solution)/shard_map/ppermute | solution.py:345
  92.5 2.7 %collective-permute-done.13.refs_2_ = bf16[32,4096]{1,0:T(8,128)(2,1)S(1)} collective-permute-done((bf16[32,4096]{1,0:T(8,128)(2,1)S(1)}, bf16[32,4096]{1,0:T(8,128)(2,1)S(1)}, u32[]{:S(2)}, u32[]{:S(2)}) %collective-permute-start.13) | collective-permute-done | bytes 262176 | tf_op jit(solution)/shard_map/ppermute | solution.py:345
  95.2 1.1 shard_map.161.refs_2_
  96.3 2.9 %collective-permute-start.15 = (bf16[128,4096]{1,0:T(8,128)(2,1)}, bf16[128,4096]{1,0:T(8,128)(2,1)}, u32[]{:S(2)}, u32[]{:S(2)}) collective-permute-start(bf16[128,4096]{1,0:T(8,128)(2,1)} %shard_map.161.refs_2_), channel_id=1, source_target_pairs={{0,2},{1,3},{2,0},{3,1},{32,160},{33,161},{34,162},{35,163},{64,66... | collective-permute-start | bytes 3145736 | tf_op jit(solution)/shard_map/ppermute | solution.py:345
  99.2 1.5 collective-permute-start.17
  100.6 0.7 fusion.8
  101.5 0.1 add.102
  101.6 0.2 fusion
  101.8 1.9 %copy-done = bf16[384,4096]{1,0:T(8,128)(2,1)S(1)} copy-done((bf16[384,4096]{1,0:T(8,128)(2,1)S(1)}, bf16[384,4096]{1,0:T(8,128)(2,1)}, u32[]{:S(2)}) %copy-start) | copy-done | bytes 3145752
  103.7 3.5 %shard_map.163.refs_2_ = bf16[384,512]{1,0:T(8,128)(2,1)S(1)} custom-call(bf16[384,4096]{1,0:T(8,128)(2,1)S(1)} %copy-done, bf16[128,512]{1,0:T(8,128)(2,1)S(1)} %slice.10.refs_1_, bf16[128,4096]{1,0:T(8,128)(2,1)} %shard_map.161.refs_2_), custom_call_target="tpu_custom_call" | custom-call | tf_op jit(solution)/shard_map/pallas_call | solution.py:294
  107.2 3.5 %shard_map.162.refs_2_ = bf16[384,512]{1,0:T(8,128)(2,1)S(1)} custom-call(bf16[384,4096]{1,0:T(8,128)(2,1)S(1)} %collective-permute-done.refs_3_.refs_0_, bf16[128,512]{1,0:T(8,128)(2,1)S(1)} %slice.10.refs_1_, bf16[128,4096]{1,0:T(8,128)(2,1)} %shard_map.161.refs_2_), custom_call_target="tpu_custom_call" | custom-call | tf_op jit(solution)/shard_map/pallas_call | solution.py:294
  110.7 1.9 %collective-permute-done.15.refs_3_ = bf16[128,4096]{1,0:T(8,128)(2,1)} collective-permute-done((bf16[128,4096]{1,0:T(8,128)(2,1)}, bf16[128,4096]{1,0:T(8,128)(2,1)}, u32[]{:S(2)}, u32[]{:S(2)}) %collective-permute-start.15) | collective-permute-done | bytes 1048608 | tf_op jit(solution)/shard_map/ppermute | solution.py:345
  112.6 10.3 %collective-permute-done.16.refs_4_ = bf16[128,4096]{1,0:T(8,128)(2,1)} collective-permute-done((bf16[128,4096]{1,0:T(8,128)(2,1)}, bf16[128,4096]{1,0:T(8,128)(2,1)}, u32[]{:S(2)}, u32[]{:S(2)}) %collective-permute-start.16) | collective-permute-done | bytes 1048608 | tf_op jit(solution)/shard_map/ppermute | solution.py:345
  123.0 0.9 collective-permute-done.17.refs_5_
  123.8 4.8 %shard_map.165 = bf16[384,512]{1,0:T(8,128)(2,1)S(1)} custom-call(bf16[384,4096]{1,0:T(8,128)(2,1)S(1)} %collective-permute-done.refs_3_.refs_0_, bf16[384,512]{1,0:T(8,128)(2,1)S(1)} %slice.9.refs_1_, bf16[384,512]{1,0:T(8,128)(2,1)S(1)} %shard_map.162.refs_2_, bf16[128,4096]{1,0:T(8,128)(2,1)} %collective-permute-done.15.refs_3_, ...), custom_call_target="tpu_custom_call" | custom-call | tf_op jit(solution)/shard_map/pallas_call | solution.py:294
  128.6 18.3 %collective-permute-start.18 = (bf16[384,512]{1,0:T(8,128)(2,1)S(1)}, bf16[384,512]{1,0:T(8,128)(2,1)S(1)}, u32[]{:S(2)}, u32[]{:S(2)}) collective-permute-start(bf16[384,512]{1,0:T(8,128)(2,1)S(1)} %shard_map.165), channel_id=1, source_target_pairs={{0,32},{32,0},{1,33},{33,1},{2,34},{34,2},{3,35},{35,3},{4,36},{36... | collective-permute-start | bytes 1179656 | tf_op jit(solution)/shard_map/ppermute | solution.py:334
  146.9 4.8 %shard_map.164.own_ref = bf16[384,512]{1,0:T(8,128)(2,1)S(1)} custom-call(bf16[384,4096]{1,0:T(8,128)(2,1)S(1)} %copy-done, bf16[384,512]{1,0:T(8,128)(2,1)S(1)} %slice.9.refs_1_, bf16[384,512]{1,0:T(8,128)(2,1)S(1)} %shard_map.163.refs_2_, bf16[128,4096]{1,0:T(8,128)(2,1)} %collective-permute-done.15.refs_3_, ...), custom_call_target="tpu_custom_call" | custom-call | tf_op jit(solution)/shard_map/pallas_call | solution.py:294
  151.7 1.0 shard_map.166
  (33 shorter events, 0.7 us)
Async XLA Ops:
  0.6 9.8 %collective-permute-start = (bf16[384,4096]{1,0:T(8,128)(2,1)}, bf16[384,4096]{1,0:T(8,128)(2,1)S(1)}, u32[]{:S(2)}, u32[]{:S(2)}) collective-permute-start(bf16[384,4096]{1,0:T(8,128)(2,1)} %refs_0_.3), channel_id=1, source_target_pairs={{0,32},{32,0},{1,33},{33,1},{2,34},{34,2},{3,35},{35,3},{4,36},{36... | collective-permute-start | bytes 9437192 | tf_op jit(solution)/shard_map/ppermute | solution.py:334
  1.4 9.0 %collective-permute-start.1 = (bf16[384,1024]{1,0:T(8,128)(2,1)}, bf16[384,1024]{1,0:T(8,128)(2,1)}, u32[]{:S(2)}, u32[]{:S(2)}) collective-permute-start(bf16[384,1024]{1,0:T(8,128)(2,1)} %refs_7_.1), channel_id=1, source_target_pairs={{0,32},{32,0},{1,33},{33,1},{2,34},{34,2},{3,35},{35,3},{4,36},{36... | collective-permute-start | bytes 2359304 | tf_op jit(solution)/shard_map/ppermute | solution.py:334
  1.5 8.9 %collective-permute-start.2 = (s32[8,32]{1,0:T(8,128)}, s32[8,32]{1,0:T(8,128)S(1)}, u32[]{:S(2)}, u32[]{:S(2)}) collective-permute-start(s32[8,32]{1,0:T(8,128)} %bitcast.23), channel_id=1, source_target_pairs={{0,32},{32,0},{1,33},{33,1},{2,34},{34,2},{3,35},{35,3},{4,36},{36... | collective-permute-start | bytes 3080 | tf_op jit(solution)/shard_map/ppermute | solution.py:334
  1.9 8.5 %copy-start.1 = (bf16[128,128]{1,0:T(8,128)(2,1)S(1)}, bf16[128,128]{1,0:T(8,128)(2,1)}, u32[]{:S(2)}) copy-start(bf16[128,128]{1,0:T(8,128)(2,1)} %constant.102.refs_10_) | copy-start | bytes 98308
  1.9 8.5 %copy-start.2 = (bf16[128,128]{1,0:T(8,128)(2,1)S(1)}, bf16[128,128]{1,0:T(8,128)(2,1)}, u32[]{:S(2)}) copy-start(bf16[128,128]{1,0:T(8,128)(2,1)} %constant.103.refs_11_) | copy-start | bytes 98308
  1.9 8.5 %copy-start.3 = (s32[32,128]{1,0:T(8,128)S(1)}, s32[32,128]{1,0:T(8,128)}, u32[]{:S(2)}) copy-start(s32[32,128]{1,0:T(8,128)} %refs_8_.5) | copy-start | bytes 49156
  15.3 12.0 %collective-permute-start.3 = (bf16[128,2048]{1,0:T(8,128)(2,1)S(1)}, bf16[128,2048]{1,0:T(8,128)(2,1)S(1)}, u32[]{:S(2)}, u32[]{:S(2)}) collective-permute-start(bf16[128,2048]{1,0:T(8,128)(2,1)S(1)} %get-tuple-element.22), channel_id=1, source_target_pairs={{0,2},{1,3},{2,0},{3,1},{32,160},{33,161},{34,162},{35,163},{64,66... | collective-permute-start | bytes 1572872 | tf_op jit(solution)/shard_map/ppermute | solution.py:345
  17.4 13.6 %collective-permute-start.4 = (bf16[128,2048]{1,0:T(8,128)(2,1)S(1)}, bf16[128,2048]{1,0:T(8,128)(2,1)S(1)}, u32[]{:S(2)}, u32[]{:S(2)}) collective-permute-start(bf16[128,2048]{1,0:T(8,128)(2,1)S(1)} %get-tuple-element.23), channel_id=1, source_target_pairs={{0,1},{1,2},{2,3},{3,0},{32,96},{33,97},{34,98},{35,99},{64,65},{6... | collective-permute-start | bytes 1572872 | tf_op jit(solution)/shard_map/ppermute | solution.py:345
  17.4 13.6 %collective-permute-start.5 = (bf16[128,2048]{1,0:T(8,128)(2,1)S(1)}, bf16[128,2048]{1,0:T(8,128)(2,1)S(1)}, u32[]{:S(2)}, u32[]{:S(2)}) collective-permute-start(bf16[128,2048]{1,0:T(8,128)(2,1)S(1)} %get-tuple-element.24), channel_id=1, source_target_pairs={{0,3},{1,0},{2,1},{3,2},{32,224},{33,225},{34,226},{35,227},{64,67... | collective-permute-start | bytes 1572872 | tf_op jit(solution)/shard_map/ppermute | solution.py:345
  23.7 38.6 %copy-start.4 = (s32[4,32]{1,0:T(4,128)S(1)}, s32[4,32]{1,0:T(4,128)}, u32[]{:S(2)}) copy-start(s32[4,32]{1,0:T(4,128)} %param.20) | copy-start | bytes 1540
  23.7 12.8 %collective-permute-start.6 = (bf16[128,2048]{1,0:T(8,128)(2,1)S(1)}, bf16[128,2048]{1,0:T(8,128)(2,1)S(1)}, u32[]{:S(2)}, u32[]{:S(2)}) collective-permute-start(bf16[128,2048]{1,0:T(8,128)(2,1)S(1)} %get-tuple-element.26), channel_id=1, source_target_pairs={{0,2},{1,3},{2,0},{3,1},{32,160},{33,161},{34,162},{35,163},{64,66... | collective-permute-start | bytes 1572872 | tf_op jit(solution)/shard_map/ppermute | solution.py:345
  25.2 17.1 %collective-permute-start.7 = (bf16[128,2048]{1,0:T(8,128)(2,1)S(1)}, bf16[128,2048]{1,0:T(8,128)(2,1)S(1)}, u32[]{:S(2)}, u32[]{:S(2)}) collective-permute-start(bf16[128,2048]{1,0:T(8,128)(2,1)S(1)} %get-tuple-element.27), channel_id=1, source_target_pairs={{0,1},{1,2},{2,3},{3,0},{32,96},{33,97},{34,98},{35,99},{64,65},{6... | collective-permute-start | bytes 1572872 | tf_op jit(solution)/shard_map/ppermute | solution.py:345
  27.3 15.0 %collective-permute-start.8 = (bf16[128,2048]{1,0:T(8,128)(2,1)S(1)}, bf16[128,2048]{1,0:T(8,128)(2,1)S(1)}, u32[]{:S(2)}, u32[]{:S(2)}) collective-permute-start(bf16[128,2048]{1,0:T(8,128)(2,1)S(1)} %get-tuple-element.28), channel_id=1, source_target_pairs={{0,3},{1,0},{2,1},{3,2},{32,224},{33,225},{34,226},{35,227},{64,67... | collective-permute-start | bytes 1572872 | tf_op jit(solution)/shard_map/ppermute | solution.py:345
  43.3 6.7 %collective-permute-start.10 = (bf16[8,8,2048]{2,1,0:T(8,128)(2,1)S(1)}, bf16[8,8,2048]{2,1,0:T(8,128)(2,1)S(1)}, u32[]{:S(2)}, u32[]{:S(2)}) collective-permute-start(bf16[8,8,2048]{2,1,0:T(8,128)(2,1)S(1)} %get-tuple-element.31), channel_id=1, source_target_pairs={{0,64},{1,65},{2,66},{3,67},{32,33},{33,34},{34,35},{35,32},{64,12... | collective-permute-start | bytes 786440 | tf_op jit(solution)/shard_map/ppermute | solution.py:345
  44.8 5.5 %collective-permute-start.11 = (bf16[8,8,2048]{2,1,0:T(8,128)(2,1)S(1)}, bf16[8,8,2048]{2,1,0:T(8,128)(2,1)S(1)}, u32[]{:S(2)}, u32[]{:S(2)}) collective-permute-start(bf16[8,8,2048]{2,1,0:T(8,128)(2,1)S(1)} %get-tuple-element.32), channel_id=1, source_target_pairs={{0,192},{1,193},{2,194},{3,195},{32,35},{33,32},{34,33},{35,34},{6... | collective-permute-start | bytes 786440 | tf_op jit(solution)/shard_map/ppermute | solution.py:345
  46.3 7.6 %collective-permute-start.9 = (bf16[8,8,2048]{2,1,0:T(8,128)(2,1)S(1)}, bf16[8,8,2048]{2,1,0:T(8,128)(2,1)S(1)}, u32[]{:S(2)}, u32[]{:S(2)}) collective-permute-start(bf16[8,8,2048]{2,1,0:T(8,128)(2,1)S(1)} %get-tuple-element.30), channel_id=1, source_target_pairs={{0,128},{1,129},{2,130},{3,131},{32,34},{33,35},{34,32},{35,33},{6... | collective-permute-start | bytes 786440 | tf_op jit(solution)/shard_map/ppermute | solution.py:345
  54.7 14.2 %all-to-all-start = ((bf16[8,8,2048]{2,1,0:T(8,128)(2,1)}), bf16[8,8,2048]{2,1,0:T(8,128)(2,1)S(1)}, u32[]{:S(2)}, u32[]{:S(2)}) async-start(bf16[8,8,2048]{2,1,0:T(8,128)(2,1)} %shard_map.160), calls=%async_computation | async-start | bytes 524288 | tf_op jit(solution)/shard_map/all_to_all | solution.py:403
  85.6 6.9 %collective-permute-start.12 = (bf16[32,4096]{1,0:T(8,128)(2,1)S(1)}, bf16[32,4096]{1,0:T(8,128)(2,1)S(1)}, u32[]{:S(2)}, u32[]{:S(2)}) collective-permute-start(bf16[32,4096]{1,0:T(8,128)(2,1)S(1)} %reshape.110.refs_0_), channel_id=1, source_target_pairs={{0,128},{1,129},{2,130},{3,131},{32,34},{33,35},{34,32},{35,33},{6... | collective-permute-start | bytes 786440 | tf_op jit(solution)/shard_map/ppermute | solution.py:345
  86.5 8.7 %collective-permute-start.13 = (bf16[32,4096]{1,0:T(8,128)(2,1)S(1)}, bf16[32,4096]{1,0:T(8,128)(2,1)S(1)}, u32[]{:S(2)}, u32[]{:S(2)}) collective-permute-start(bf16[32,4096]{1,0:T(8,128)(2,1)S(1)} %reshape.110.refs_0_), channel_id=1, source_target_pairs={{0,64},{1,65},{2,66},{3,67},{32,33},{33,34},{34,35},{35,32},{64,12... | collective-permute-start | bytes 786440 | tf_op jit(solution)/shard_map/ppermute | solution.py:345
  88.1 7.2 %collective-permute-start.14 = (bf16[32,4096]{1,0:T(8,128)(2,1)S(1)}, bf16[32,4096]{1,0:T(8,128)(2,1)S(1)}, u32[]{:S(2)}, u32[]{:S(2)}) collective-permute-start(bf16[32,4096]{1,0:T(8,128)(2,1)S(1)} %reshape.110.refs_0_), channel_id=1, source_target_pairs={{0,192},{1,193},{2,194},{3,195},{32,35},{33,32},{34,33},{35,34},{6... | collective-permute-start | bytes 786440 | tf_op jit(solution)/shard_map/ppermute | solution.py:345
  96.3 16.3 %collective-permute-start.15 = (bf16[128,4096]{1,0:T(8,128)(2,1)}, bf16[128,4096]{1,0:T(8,128)(2,1)}, u32[]{:S(2)}, u32[]{:S(2)}) collective-permute-start(bf16[128,4096]{1,0:T(8,128)(2,1)} %shard_map.161.refs_2_), channel_id=1, source_target_pairs={{0,2},{1,3},{2,0},{3,1},{32,160},{33,161},{34,162},{35,163},{64,66... | collective-permute-start | bytes 3145736 | tf_op jit(solution)/shard_map/ppermute | solution.py:345
  99.2 23.8 %collective-permute-start.16 = (bf16[128,4096]{1,0:T(8,128)(2,1)}, bf16[128,4096]{1,0:T(8,128)(2,1)}, u32[]{:S(2)}, u32[]{:S(2)}) collective-permute-start(bf16[128,4096]{1,0:T(8,128)(2,1)} %shard_map.161.refs_2_), channel_id=1, source_target_pairs={{0,1},{1,2},{2,3},{3,0},{32,96},{33,97},{34,98},{35,99},{64,65},{6... | collective-permute-start | bytes 3145736 | tf_op jit(solution)/shard_map/ppermute | solution.py:345
  99.2 24.6 %collective-permute-start.17 = (bf16[128,4096]{1,0:T(8,128)(2,1)}, bf16[128,4096]{1,0:T(8,128)(2,1)}, u32[]{:S(2)}, u32[]{:S(2)}) collective-permute-start(bf16[128,4096]{1,0:T(8,128)(2,1)} %shard_map.161.refs_2_), channel_id=1, source_target_pairs={{0,3},{1,0},{2,1},{3,2},{32,224},{33,225},{34,226},{35,227},{64,67... | collective-permute-start | bytes 3145736 | tf_op jit(solution)/shard_map/ppermute | solution.py:345
  101.8 1.9 %copy-start = (bf16[384,4096]{1,0:T(8,128)(2,1)S(1)}, bf16[384,4096]{1,0:T(8,128)(2,1)}, u32[]{:S(2)}) copy-start(bf16[384,4096]{1,0:T(8,128)(2,1)} %refs_0_.3) | copy-start | bytes 9437188
  128.6 23.1 %collective-permute-start.18 = (bf16[384,512]{1,0:T(8,128)(2,1)S(1)}, bf16[384,512]{1,0:T(8,128)(2,1)S(1)}, u32[]{:S(2)}, u32[]{:S(2)}) collective-permute-start(bf16[384,512]{1,0:T(8,128)(2,1)S(1)} %shard_map.165), channel_id=1, source_target_pairs={{0,32},{32,0},{1,33},{33,1},{2,34},{34,2},{3,35},{35,3},{4,36},{36... | collective-permute-start | bytes 1179656 | tf_op jit(solution)/shard_map/ppermute | solution.py:334

commit v9 on v8

--- a/solution.py
+++ b/solution.py
@@ -256,55 +256,46 @@
     )(*pieces)
 
 
-def product_kernel(added, tok_ref, spread_ref, *refs):
-    early_refs, weight_refs, (out_ref, total_ref) = refs[:added], refs[added:-2], refs[-2:]
+def product_kernel(offsets, added, core_ref, x_ref, y_ref, tok_ref, *refs):
+    early_refs, weight_refs, (out_ref, spread_ref) = refs[:added], refs[added:-2], refs[-2:]
+    core, at_x, at_y = core_ref[0], x_ref[0], y_ref[0]
+    piece, columns = spread_ref.shape[0] // len(offsets), spread_ref.shape[1]
+    row_at = lax.broadcasted_iota(jnp.int32, (piece, columns), 0)
+    column_at = lax.broadcasted_iota(jnp.int32, (piece, columns), 1)
+    past_start = column_at - ((row_at >> 2) * 16 + (row_at & 3))
+    for at, (first, second) in enumerate(offsets):
+        from_x = lax.rem(at_x - jnp.where(core == 0, first, second) + 4, 4)
+        from_y = lax.rem(at_y - jnp.where(core == 0, second, first) + 4, 4)
+        start = from_y * (4 * piece) + from_x * 4
+        spread_ref[at * piece : (at + 1) * piece, :] = jnp.where(
+            past_start == start, 1.0, 0.0
+        ).astype(jnp.bfloat16)
     weights = jnp.concatenate([ref[...] for ref in weight_refs], axis=0)
-    part = lax.dot_general(
+    total = lax.dot_general(
         tok_ref[...], weights, (((1,), (1,)), ((), ())), preferred_element_type=jnp.float32
     )
-    step = pl.program_id(0)
-
-    @pl.when(step == 0)
-    def _():
-        total_ref[...] = part
-
-    @pl.when(step > 0)
-    def _():
-        total_ref[...] += part
-
-    @pl.when(step == pl.num_programs(0) - 1)
-    def _():
-        out = jnp.dot(
-            total_ref[...].astype(jnp.bfloat16),
-            spread_ref[...],
-            preferred_element_type=jnp.float32,
-        )
-        for early_ref in early_refs:
-            out = out + early_ref[...].astype(jnp.float32)
-        out_ref[...] = out.astype(jnp.bfloat16)
-
-
-def spread_product(tokens, spread, weights, early=()):
-    token_rows, model_width = tokens.shape
-    rows, columns = spread.shape
-    width = 1024
-    whole = lambda n: (0, 0)
-    split = lambda n: (0, n)
-    body = lambda *refs: product_kernel(len(early), *refs)
+    out = jnp.dot(
+        total.astype(jnp.bfloat16), spread_ref[...], preferred_element_type=jnp.float32
+    )
+    for early_ref in early_refs:
+        out = out + early_ref[...].astype(jnp.float32)
+    out_ref[...] = out.astype(jnp.bfloat16)
+
+
+def spread_product(place, offsets, tokens, weights, early=()):
+    whole = pl.BlockSpec(memory_space=pltpu.VMEM)
+    scalar = pl.BlockSpec(memory_space=pltpu.SMEM)
+    rows = sum(value.shape[0] for value in weights)
+    columns = 16 * (rows // len(offsets))
+    body = lambda *refs: product_kernel(offsets, len(early), *refs)
     return pl.pallas_call(
         body,
-        grid=(model_width // width,),
-        in_specs=[
-            pl.BlockSpec((token_rows, width), split),
-            pl.BlockSpec((rows, columns), whole),
-            *[pl.BlockSpec((token_rows, columns), whole) for _ in early],
-            *[pl.BlockSpec((value.shape[0], width), split) for value in weights],
-        ],
-        out_specs=pl.BlockSpec((token_rows, columns), whole),
-        out_shape=jax.ShapeDtypeStruct((token_rows, columns), jnp.bfloat16),
-        scratch_shapes=[pltpu.VMEM((token_rows, rows), jnp.float32)],
-        compiler_params=pltpu.CompilerParams(vmem_limit_bytes=20 << 20),
-    )(tokens, spread, *early, *weights)
+        in_specs=[scalar] * 3 + [whole] * (1 + len(early) + len(weights)),
+        out_specs=whole,
+        out_shape=jax.ShapeDtypeStruct((tokens.shape[0], columns), jnp.bfloat16),
+        scratch_shapes=[pltpu.VMEM((rows, columns), jnp.bfloat16)],
+        compiler_params=pltpu.CompilerParams(vmem_limit_bytes=12 << 20),
+    )(*place, tokens, *early, *weights)
 
 
 def interleave_kernel(core_ref, own_ref, peer_ref, out_ref):
@@ -343,23 +334,6 @@
                 to_y, to_x = (y, (x + shift) % 4) if along_x else ((y + shift) % 4, x)
                 pairs.append(((y * 2 + core) * 4 + x, (to_y * 2 + core) * 4 + to_x))
     return lax.ppermute(value, FACE, pairs)
-
-
-def column_spread(place, offsets, count_z, rows_dev):
-    core, at_x, at_y = place
-    first = jnp.asarray([offset[0] for offset in offsets], jnp.int32)
-    second = jnp.asarray([offset[1] for offset in offsets], jnp.int32)
-    from_x = (at_x - jnp.where(core == 0, first, second)) % 4
-    from_y = (at_y - jnp.where(core == 0, second, first)) % 4
-    at_z = jnp.arange(count_z, dtype=jnp.int32)[None, :, None]
-    at_j = jnp.arange(rows_dev, dtype=jnp.int32)[None, None, :]
-    column = (
-        (from_y[:, None, None] * count_z + at_z) * 4 + from_x[:, None, None]
-    ) * rows_dev + at_j
-    size = 16 * count_z * rows_dev
-    return (column.reshape(-1, 1) == jnp.arange(size, dtype=jnp.int32)[None, :]).astype(
-        jnp.bfloat16
-    )
 
 
 def shards(
@@ -412,21 +386,18 @@
     diff_bound = clip_level * jnp.exp2(diff_exps.astype(jnp.float32))
     diff_coded = clip_rows(new_master - base_own, diff_bound).astype(jnp.bfloat16)
     effective = (base_own + diff_coded.astype(jnp.float32)).astype(jnp.bfloat16)
+    order_far = (0, 2, 1, 3)
     stacked = lax.all_to_all(
         jnp.broadcast_to(effective[None], (count_z, *effective.shape)), "z", 0, 0, tiled=True
     ).reshape(count_z * rows_dev, model_width)
-    order_far = (0, 2, 1, 3)
     face = packed([stacked, *(shifted(stacked, 1, far) for far in order_far[1:])])
     arrived = [shifted(face, 0, far) for far in order_far[1:]]
-    spread = column_spread(
-        place, [(first, second) for first in order_far for second in order_far], count_z, rows_dev
-    )
-    near_rows = face.shape[0]
-    early = [spread_product(rows, spread[:near_rows], [face]) for rows in (peer_tokens, tokens)]
+    near = [(0, second) for second in order_far]
+    beyond = [(first, second) for first in order_far[1:] for second in order_far]
+    early = [spread_product(place, near, rows, [face]) for rows in (peer_tokens, tokens)]
     early, arrived = lax.optimization_barrier((early, arrived))
-    late_spread = spread[near_rows:]
-    peer_part = swapped(spread_product(peer_tokens, late_spread, arrived, early[:1]))
-    own_part = spread_product(tokens, late_spread, arrived, early[1:])
+    peer_part = swapped(spread_product(place, beyond, peer_tokens, arrived, early[:1]))
+    own_part = spread_product(place, beyond, tokens, arrived, early[1:])
     projected = interleaved(place[0], own_part, peer_part)
     return (projected, new_master, new_first, new_second)
 

time: 154 us -> 150 us (0.974)
  the two profiles are of different devices: /device:TPU:73 before, /device:TPU:1 now
where the time goes in v9:
time: 150 us
  waiting for transfers between devices  55.5 us (37%)
  starting transfers between devices  46.1 us (31%)
  Pallas kernels  28 us (19%)
  blocking collectives  12.5 us (8%)
  local copies, waits for them, and re-layouts  3.25 us (2%)
  other arithmetic  2.42 us (2%)
    ppermute x15, waiting for transfers between devices, shifted(): return lax.ppermute(value, FACE, pairs)  47 us
    ppermute x4, starting transfers between devices, swapped(): return lax.ppermute(value, 'c', [(0, 1), (1, 0)])  20.6 us
    pallas_call x3, Pallas kernels, coded_gradient(): pl.pallas_call(body, grid_spec=pltpu.PrefetchScalarGridSpec(num_scalar_pr...  18.2 us
    ppermute x15, starting transfers between devices, shifted(): return lax.ppermute(value, FACE, pairs)  17.8 us
    all_to_all x1, blocking collectives, shards(): lax.all_to_all(jnp.broadcast_to(effective[None], (count_z, *effective.sha...  12.5 us
    all_to_all x1, waiting for transfers between devices, shards(): parts = lax.all_to_all(face, 'z', 0, 0, tiled=True)  8.45 us
    all_to_all x1, starting transfers between devices, shards(): parts = lax.all_to_all(face, 'z', 0, 0, tiled=True)  7.7 us
    pallas_call x4, Pallas kernels, spread_product(): pl.pallas_call(body, in_specs=[scalar] * 3 + [whole] * (1 + len(early) +...  6.74 us
  transfers between devices with their start and end apart: 20, of which 12 were waited for; matrix products, arithmetic and copies ran while one was open for 0% of the time, Pallas kernels for 12%

profile of v9, /device:TPU:1, one launch (start us, length us, event | category | flops | bytes accessed | tf_op | source)
XLA Modules:
  0.0 149.7 jit_solution(6390082779119299187)
XLA Ops:
  0.6 3.3 %collective-permute-start = (bf16[384,4096]{1,0:T(8,128)(2,1)}, bf16[384,4096]{1,0:T(8,128)(2,1)S(1)}, u32[]{:S(2)}, u32[]{:S(2)}) collective-permute-start(bf16[384,4096]{1,0:T(8,128)(2,1)} %refs_3_.5), channel_id=1, source_target_pairs={{0,32},{32,0},{1,33},{33,1},{2,34},{34,2},{3,35},{35,3},{4,36},{36... | collective-permute-start | bytes 9437192 | tf_op jit(solution)/shard_map/ppermute | solution.py:325
  4.0 0.1 collective-permute-start.1
  4.1 0.4 collective-permute-start.2
  4.5 8.5 %shard_map.138.refs_12_ = bf16[512,4096]{1,0:T(8,128)(2,1)} custom-call(s32[1]{0:T(128)} %bitcast.refs_0_.core_ref, s32[1]{0:T(128)} %bitcast.1.refs_1_, s32[1]{0:T(128)} %bitcast.2.refs_2_, bf16[384,4096]{1,0:T(8,128)(2,1)} %refs_3_.5, bf16[384,1024]{1,0:T(8,128)(2,1)} %refs_7_.1, bf16[384,1024]{1,0:T(8,128)(2,1)} %refs_7_.1, bf16[384,1024]{1,0:T(8,128)(2,1)} %refs_7_.1, ...), custom_call_target="tpu_custom_call" | custom-call | tf_op jit(solution)/shard_map/pallas_call | solution.py:166
  13.1 4.9 %shard_map.139 = (bf16[128,2048]{1,0:T(8,128)(2,1)S(1)}, bf16[128,2048]{1,0:T(8,128)(2,1)S(1)}, bf16[128,2048]{1,0:T(8,128)(2,1)S(1)}, bf16[128,2048]{1,0:T(8,128)(2,1)S(1)}) custom-call(s32[1]{0:T(128)} %bitcast.refs_0_.core_ref, s32[1]{0:T(128)} %bitcast.1.refs_1_, s32[1]{0:T(128)} %bitcast.2.refs_2_, bf16[384,4096]{1,0:T(8,128)(2,1)S(1)} %collective-permute-done.refs_3_, ...), custom_call_target="tpu_custom_call" | custom-call | tf_op jit(solution)/shard_map/pallas_call | solution.py:166
  17.9 1.3 collective-permute-start.3
  19.2 0.4 collective-permute-start.4
  19.6 2.3 %collective-permute-start.5 = (bf16[128,2048]{1,0:T(8,128)(2,1)S(1)}, bf16[128,2048]{1,0:T(8,128)(2,1)S(1)}, u32[]{:S(2)}, u32[]{:S(2)}) collective-permute-start(bf16[128,2048]{1,0:T(8,128)(2,1)S(1)} %get-tuple-element.24), channel_id=1, source_target_pairs={{0,3},{1,0},{2,1},{3,2},{32,224},{33,225},{34,226},{35,227},{64,67... | collective-permute-start | bytes 1572872 | tf_op jit(solution)/shard_map/ppermute | solution.py:336
  21.9 4.8 %shard_map.140 = (bf16[128,2048]{1,0:T(8,128)(2,1)S(1)}, bf16[128,2048]{1,0:T(8,128)(2,1)S(1)}, bf16[128,2048]{1,0:T(8,128)(2,1)S(1)}, bf16[128,2048]{1,0:T(8,128)(2,1)S(1)}) custom-call(s32[1]{0:T(128)} %bitcast.refs_0_.core_ref, s32[1]{0:T(128)} %bitcast.1.refs_1_, s32[1]{0:T(128)} %bitcast.2.refs_2_, bf16[384,4096]{1,0:T(8,128)(2,1)S(1)} %collective-permute-done.refs_3_, ...), custom_call_target="tpu_custom_call" | custom-call | tf_op jit(solution)/shard_map/pallas_call | solution.py:166
  26.7 0.7 collective-permute-start.6
  27.4 0.5 collective-permute-done.3.refs_1_
  27.9 2.2 %collective-permute-start.8 = (bf16[128,2048]{1,0:T(8,128)(2,1)S(1)}, bf16[128,2048]{1,0:T(8,128)(2,1)S(1)}, u32[]{:S(2)}, u32[]{:S(2)}) collective-permute-start(bf16[128,2048]{1,0:T(8,128)(2,1)S(1)} %get-tuple-element.28), channel_id=1, source_target_pairs={{0,3},{1,0},{2,1},{3,2},{32,224},{33,225},{34,226},{35,227},{64,67... | collective-permute-start | bytes 1572872 | tf_op jit(solution)/shard_map/ppermute | solution.py:336
  30.1 3.4 %collective-permute-done.4.refs_2_ = bf16[128,2048]{1,0:T(8,128)(2,1)S(1)} collective-permute-done((bf16[128,2048]{1,0:T(8,128)(2,1)S(1)}, bf16[128,2048]{1,0:T(8,128)(2,1)S(1)}, u32[]{:S(2)}, u32[]{:S(2)}) %collective-permute-start.4) | collective-permute-done | bytes 524320 | tf_op jit(solution)/shard_map/ppermute | solution.py:336
  33.5 5.7 %collective-permute-done.6.refs_5_ = bf16[128,2048]{1,0:T(8,128)(2,1)S(1)} collective-permute-done((bf16[128,2048]{1,0:T(8,128)(2,1)S(1)}, bf16[128,2048]{1,0:T(8,128)(2,1)S(1)}, u32[]{:S(2)}, u32[]{:S(2)}) %collective-permute-start.6) | collective-permute-done | bytes 524320 | tf_op jit(solution)/shard_map/ppermute | solution.py:336
  39.2 5.5 %collective-permute-done.7.refs_6_ = bf16[128,2048]{1,0:T(8,128)(2,1)S(1)} collective-permute-done((bf16[128,2048]{1,0:T(8,128)(2,1)S(1)}, bf16[128,2048]{1,0:T(8,128)(2,1)S(1)}, u32[]{:S(2)}, u32[]{:S(2)}) %collective-permute-start.7) | collective-permute-done | bytes 524320 | tf_op jit(solution)/shard_map/ppermute | solution.py:336
  44.7 1.1 shard_map.141
  45.8 0.3 collective-permute-start.10
  46.0 2.7 %collective-permute-start.11 = (bf16[8,8,2048]{2,1,0:T(8,128)(2,1)S(1)}, bf16[8,8,2048]{2,1,0:T(8,128)(2,1)S(1)}, u32[]{:S(2)}, u32[]{:S(2)}) collective-permute-start(bf16[8,8,2048]{2,1,0:T(8,128)(2,1)S(1)} %get-tuple-element.32), channel_id=1, source_target_pairs={{0,192},{1,193},{2,194},{3,195},{32,35},{33,32},{34,33},{35,34},{6... | collective-permute-start | bytes 786440 | tf_op jit(solution)/shard_map/ppermute | solution.py:336
  48.7 0.2 collective-permute-start.9
  48.9 3.8 %collective-permute-done.10.refs_2_ = bf16[8,8,2048]{2,1,0:T(8,128)(2,1)S(1)} collective-permute-done((bf16[8,8,2048]{2,1,0:T(8,128)(2,1)S(1)}, bf16[8,8,2048]{2,1,0:T(8,128)(2,1)S(1)}, u32[]{:S(2)}, u32[]{:S(2)}) %collective-permute-start.10) | collective-permute-done | bytes 262176 | tf_op jit(solution)/shard_map/ppermute | solution.py:336
  52.8 2.1 %collective-permute-done.11.refs_3_ = bf16[8,8,2048]{2,1,0:T(8,128)(2,1)S(1)} collective-permute-done((bf16[8,8,2048]{2,1,0:T(8,128)(2,1)S(1)}, bf16[8,8,2048]{2,1,0:T(8,128)(2,1)S(1)}, u32[]{:S(2)}, u32[]{:S(2)}) %collective-permute-start.11) | collective-permute-done | bytes 262176 | tf_op jit(solution)/shard_map/ppermute | solution.py:336
  54.8 0.9 collective-permute-done.9.refs_1_
  55.7 0.9 shard_map.142
  56.6 7.7 %all-to-all-start = ((bf16[8,8,2048]{2,1,0:T(8,128)(2,1)}), bf16[8,8,2048]{2,1,0:T(8,128)(2,1)S(1)}, u32[]{:S(2)}, u32[]{:S(2)}) async-start(bf16[8,8,2048]{2,1,0:T(8,128)(2,1)} %shard_map.142), calls=%async_computation | async-start | bytes 524288 | tf_op jit(solution)/shard_map/all_to_all | solution.py:377
  64.4 0.6 convert_bitcast_fusion
  65.0 0.1 broadcast_bitcast_fusion
  65.1 8.4 %all-to-all-done = bf16[8,8,2048]{2,1,0:T(8,128)(2,1)S(1)} async-done(((bf16[8,8,2048]{2,1,0:T(8,128)(2,1)}), bf16[8,8,2048]{2,1,0:T(8,128)(2,1)S(1)}, u32[]{:S(2)}, u32[]{:S(2)}) %all-to-all-start) | async-done | bytes 262176 | tf_op jit(solution)/shard_map/all_to_all | solution.py:377
  73.7 1.0 convolution_multiply_fusion
  74.8 1.8 %fusion.3 = (bf16[4,4096]{1,0:T(4,128)(2,1)S(1)}, f32[4,4096]{1,0:T(4,128)}, f32[4,4096]{1,0:T(4,128)}, f32[4,4096]{1,0:T(4,128)}) fusion(bf16[1,4,32,128]{3,2,1,0:T(8,128)(2,1)S(1)} %get-tuple-element.44, bf16[1,4,32,128]{3,2,1,0:T(8,128)(2,1)S(1)} %get-tuple-element.45, bf16[1024,4096]{1,0:T(8,128)(2,1)} %param.14, s32[]{:T(128)S(6)} %select_n.3, ...), kind=kLoop, calls=%fused_computation.8 | loop fusion | flops 409600 | bytes 606212 | tf_op jit(solution)/shard_map/convert_element_type | solution.py:388
  76.7 12.5 %all_to_all.10 = bf16[8,4,4096]{2,1,0:T(4,128)(2,1)} all-to-all(bf16[8,4,4096]{2,1,0:T(4,128)(2,1)S(1)} %broadcast_in_dim.2), channel_id=1, replica_groups=mesh['y'=4,'c'=2,'z'=8,'x'=4] {'z'}, dimensions={0} | all-to-all | bytes 524288 | tf_op jit(solution)/shard_map/all_to_all | solution.py:390
  89.2 1.0 reshape.44.refs_0_
  90.2 0.7 collective-permute-start.12
  90.9 1.9 %collective-permute-start.13 = (bf16[32,4096]{1,0:T(8,128)(2,1)S(1)}, bf16[32,4096]{1,0:T(8,128)(2,1)S(1)}, u32[]{:S(2)}, u32[]{:S(2)}) collective-permute-start(bf16[32,4096]{1,0:T(8,128)(2,1)S(1)} %reshape.44.refs_0_), channel_id=1, source_target_pairs={{0,64},{1,65},{2,66},{3,67},{32,33},{33,34},{34,35},{35,32},{64,12... | collective-permute-start | bytes 786440 | tf_op jit(solution)/shard_map/ppermute | solution.py:336
  92.8 1.0 collective-permute-start.14
  93.8 3.3 %collective-permute-done.12.refs_1_ = bf16[32,4096]{1,0:T(8,128)(2,1)S(1)} collective-permute-done((bf16[32,4096]{1,0:T(8,128)(2,1)S(1)}, bf16[32,4096]{1,0:T(8,128)(2,1)S(1)}, u32[]{:S(2)}, u32[]{:S(2)}) %collective-permute-start.12) | collective-permute-done | bytes 262176 | tf_op jit(solution)/shard_map/ppermute | solution.py:336
  97.1 3.0 %collective-permute-done.13.refs_2_ = bf16[32,4096]{1,0:T(8,128)(2,1)S(1)} collective-permute-done((bf16[32,4096]{1,0:T(8,128)(2,1)S(1)}, bf16[32,4096]{1,0:T(8,128)(2,1)S(1)}, u32[]{:S(2)}, u32[]{:S(2)}) %collective-permute-start.13) | collective-permute-done | bytes 262176 | tf_op jit(solution)/shard_map/ppermute | solution.py:336
  100.2 1.6 %collective-permute-start.15 = (bf16[128,4096]{1,0:T(8,128)(2,1)S(1)}, bf16[128,4096]{1,0:T(8,128)(2,1)S(1)}, u32[]{:S(2)}, u32[]{:S(2)}) collective-permute-start(bf16[128,4096]{1,0:T(8,128)(2,1)S(1)} %shard_map.143.refs_4_), channel_id=1, source_target_pairs={{0,2},{1,3},{2,0},{3,1},{32,160},{33,161},{34,162},{35,163},{64,66... | collective-permute-start | bytes 3145736 | tf_op jit(solution)/shard_map/ppermute | solution.py:336
  101.8 2.1 %collective-permute-start.16 = (bf16[128,4096]{1,0:T(8,128)(2,1)S(1)}, bf16[128,4096]{1,0:T(8,128)(2,1)S(1)}, u32[]{:S(2)}, u32[]{:S(2)}) collective-permute-start(bf16[128,4096]{1,0:T(8,128)(2,1)S(1)} %shard_map.143.refs_4_), channel_id=1, source_target_pairs={{0,1},{1,2},{2,3},{3,0},{32,96},{33,97},{34,98},{35,99},{64,65},{6... | collective-permute-start | bytes 3145736 | tf_op jit(solution)/shard_map/ppermute | solution.py:336
  103.9 0.6 collective-permute-start.17
  104.5 1.9 %copy-done = bf16[384,4096]{1,0:T(8,128)(2,1)S(1)} copy-done((bf16[384,4096]{1,0:T(8,128)(2,1)S(1)}, bf16[384,4096]{1,0:T(8,128)(2,1)}, u32[]{:S(2)}) %copy-start) | copy-done | bytes 3145752
  106.4 1.3 shard_map.145.refs_4_
  107.7 1.3 shard_map.144.refs_4_
  109.0 7.5 %collective-permute-done.15.refs_5_ = bf16[128,4096]{1,0:T(8,128)(2,1)S(1)} collective-permute-done((bf16[128,4096]{1,0:T(8,128)(2,1)S(1)}, bf16[128,4096]{1,0:T(8,128)(2,1)S(1)}, u32[]{:S(2)}, u32[]{:S(2)}) %collective-permute-start.15) | collective-permute-done | bytes 1048608 | tf_op jit(solution)/shard_map/ppermute | solution.py:336
  116.5 11.2 %collective-permute-done.16.refs_6_ = bf16[128,4096]{1,0:T(8,128)(2,1)S(1)} collective-permute-done((bf16[128,4096]{1,0:T(8,128)(2,1)S(1)}, bf16[128,4096]{1,0:T(8,128)(2,1)S(1)}, u32[]{:S(2)}, u32[]{:S(2)}) %collective-permute-start.16) | collective-permute-done | bytes 1048608 | tf_op jit(solution)/shard_map/ppermute | solution.py:336
  127.7 2.1 %shard_map.147 = bf16[384,512]{1,0:T(8,128)(2,1)S(1)} custom-call(s32[1]{0:T(128)} %bitcast.refs_0_.core_ref, s32[1]{0:T(128)} %bitcast.1.refs_1_, s32[1]{0:T(128)} %bitcast.2.refs_2_, bf16[384,4096]{1,0:T(8,128)(2,1)S(1)} %collective-permute-done.refs_3_, bf16[384,512]{1,0:T(8,128)(2,1)S(1)} %shard_map.144.refs_4_, ...), custom_call_target="tpu_custom_call" | custom-call | tf_op jit(solution)/shard_map/pallas_call | solution.py:291
  129.8 16.8 %collective-permute-start.18 = (bf16[384,512]{1,0:T(8,128)(2,1)S(1)}, bf16[384,512]{1,0:T(8,128)(2,1)S(1)}, u32[]{:S(2)}, u32[]{:S(2)}) collective-permute-start(bf16[384,512]{1,0:T(8,128)(2,1)S(1)} %shard_map.147), channel_id=1, source_target_pairs={{0,32},{32,0},{1,33},{33,1},{2,34},{34,2},{3,35},{35,3},{4,36},{36... | collective-permute-start | bytes 1179656 | tf_op jit(solution)/shard_map/ppermute | solution.py:325
  146.6 2.1 %shard_map.146.own_ref = bf16[384,512]{1,0:T(8,128)(2,1)S(1)} custom-call(s32[1]{0:T(128)} %bitcast.refs_0_.core_ref, s32[1]{0:T(128)} %bitcast.1.refs_1_, s32[1]{0:T(128)} %bitcast.2.refs_2_, bf16[384,4096]{1,0:T(8,128)(2,1)S(1)} %copy-done, bf16[384,512]{1,0:T(8,128)(2,1)S(1)} %shard_map.145.refs_4_, ...), custom_call_target="tpu_custom_call" | custom-call | tf_op jit(solution)/shard_map/pallas_call | solution.py:291
  148.6 1.0 shard_map.148
  (26 shorter events, 0.4 us)
Async XLA Ops:
  0.6 12.4 %collective-permute-start = (bf16[384,4096]{1,0:T(8,128)(2,1)}, bf16[384,4096]{1,0:T(8,128)(2,1)S(1)}, u32[]{:S(2)}, u32[]{:S(2)}) collective-permute-start(bf16[384,4096]{1,0:T(8,128)(2,1)} %refs_3_.5), channel_id=1, source_target_pairs={{0,32},{32,0},{1,33},{33,1},{2,34},{34,2},{3,35},{35,3},{4,36},{36... | collective-permute-start | bytes 9437192 | tf_op jit(solution)/shard_map/ppermute | solution.py:325
  4.0 9.1 %collective-permute-start.1 = (bf16[384,1024]{1,0:T(8,128)(2,1)}, bf16[384,1024]{1,0:T(8,128)(2,1)}, u32[]{:S(2)}, u32[]{:S(2)}) collective-permute-start(bf16[384,1024]{1,0:T(8,128)(2,1)} %refs_7_.1), channel_id=1, source_target_pairs={{0,32},{32,0},{1,33},{33,1},{2,34},{34,2},{3,35},{35,3},{4,36},{36... | collective-permute-start | bytes 2359304 | tf_op jit(solution)/shard_map/ppermute | solution.py:325
  4.1 9.0 %collective-permute-start.2 = (s32[8,32]{1,0:T(8,128)}, s32[8,32]{1,0:T(8,128)S(1)}, u32[]{:S(2)}, u32[]{:S(2)}) collective-permute-start(s32[8,32]{1,0:T(8,128)} %bitcast.22), channel_id=1, source_target_pairs={{0,32},{32,0},{1,33},{33,1},{2,34},{34,2},{3,35},{35,3},{4,36},{36... | collective-permute-start | bytes 3080 | tf_op jit(solution)/shard_map/ppermute | solution.py:325
  4.5 8.6 %copy-start.1 = (bf16[128,128]{1,0:T(8,128)(2,1)S(1)}, bf16[128,128]{1,0:T(8,128)(2,1)}, u32[]{:S(2)}) copy-start(bf16[128,128]{1,0:T(8,128)(2,1)} %constant.74.refs_10_) | copy-start | bytes 98308
  4.5 8.6 %copy-start.2 = (bf16[128,128]{1,0:T(8,128)(2,1)S(1)}, bf16[128,128]{1,0:T(8,128)(2,1)}, u32[]{:S(2)}) copy-start(bf16[128,128]{1,0:T(8,128)(2,1)} %constant.75.refs_11_) | copy-start | bytes 98308
  4.5 8.6 %copy-start.3 = (s32[32,128]{1,0:T(8,128)S(1)}, s32[32,128]{1,0:T(8,128)}, u32[]{:S(2)}) copy-start(s32[32,128]{1,0:T(8,128)} %refs_8_.5) | copy-start | bytes 49156
  17.9 10.0 %collective-permute-start.3 = (bf16[128,2048]{1,0:T(8,128)(2,1)S(1)}, bf16[128,2048]{1,0:T(8,128)(2,1)S(1)}, u32[]{:S(2)}, u32[]{:S(2)}) collective-permute-start(bf16[128,2048]{1,0:T(8,128)(2,1)S(1)} %get-tuple-element.22), channel_id=1, source_target_pairs={{0,2},{1,3},{2,0},{3,1},{32,160},{33,161},{34,162},{35,163},{64,66... | collective-permute-start | bytes 1572872 | tf_op jit(solution)/shard_map/ppermute | solution.py:336
  19.2 14.3 %collective-permute-start.4 = (bf16[128,2048]{1,0:T(8,128)(2,1)S(1)}, bf16[128,2048]{1,0:T(8,128)(2,1)S(1)}, u32[]{:S(2)}, u32[]{:S(2)}) collective-permute-start(bf16[128,2048]{1,0:T(8,128)(2,1)S(1)} %get-tuple-element.23), channel_id=1, source_target_pairs={{0,1},{1,2},{2,3},{3,0},{32,96},{33,97},{34,98},{35,99},{64,65},{6... | collective-permute-start | bytes 1572872 | tf_op jit(solution)/shard_map/ppermute | solution.py:336
  19.6 13.9 %collective-permute-start.5 = (bf16[128,2048]{1,0:T(8,128)(2,1)S(1)}, bf16[128,2048]{1,0:T(8,128)(2,1)S(1)}, u32[]{:S(2)}, u32[]{:S(2)}) collective-permute-start(bf16[128,2048]{1,0:T(8,128)(2,1)S(1)} %get-tuple-element.24), channel_id=1, source_target_pairs={{0,3},{1,0},{2,1},{3,2},{32,224},{33,225},{34,226},{35,227},{64,67... | collective-permute-start | bytes 1572872 | tf_op jit(solution)/shard_map/ppermute | solution.py:336
  26.7 37.6 %copy-start.4 = (s32[4,32]{1,0:T(4,128)S(1)}, s32[4,32]{1,0:T(4,128)}, u32[]{:S(2)}) copy-start(s32[4,32]{1,0:T(4,128)} %param.18) | copy-start | bytes 1540
  26.7 12.5 %collective-permute-start.6 = (bf16[128,2048]{1,0:T(8,128)(2,1)S(1)}, bf16[128,2048]{1,0:T(8,128)(2,1)S(1)}, u32[]{:S(2)}, u32[]{:S(2)}) collective-permute-start(bf16[128,2048]{1,0:T(8,128)(2,1)S(1)} %get-tuple-element.26), channel_id=1, source_target_pairs={{0,2},{1,3},{2,0},{3,1},{32,160},{33,161},{34,162},{35,163},{64,66... | collective-permute-start | bytes 1572872 | tf_op jit(solution)/shard_map/ppermute | solution.py:336
  27.4 17.3 %collective-permute-start.7 = (bf16[128,2048]{1,0:T(8,128)(2,1)S(1)}, bf16[128,2048]{1,0:T(8,128)(2,1)S(1)}, u32[]{:S(2)}, u32[]{:S(2)}) collective-permute-start(bf16[128,2048]{1,0:T(8,128)(2,1)S(1)} %get-tuple-element.27), channel_id=1, source_target_pairs={{0,1},{1,2},{2,3},{3,0},{32,96},{33,97},{34,98},{35,99},{64,65},{6... | collective-permute-start | bytes 1572872 | tf_op jit(solution)/shard_map/ppermute | solution.py:336
  27.9 16.8 %collective-permute-start.8 = (bf16[128,2048]{1,0:T(8,128)(2,1)S(1)}, bf16[128,2048]{1,0:T(8,128)(2,1)S(1)}, u32[]{:S(2)}, u32[]{:S(2)}) collective-permute-start(bf16[128,2048]{1,0:T(8,128)(2,1)S(1)} %get-tuple-element.28), channel_id=1, source_target_pairs={{0,3},{1,0},{2,1},{3,2},{32,224},{33,225},{34,226},{35,227},{64,67... | collective-permute-start | bytes 1572872 | tf_op jit(solution)/shard_map/ppermute | solution.py:336
  45.8 7.0 %collective-permute-start.10 = (bf16[8,8,2048]{2,1,0:T(8,128)(2,1)S(1)}, bf16[8,8,2048]{2,1,0:T(8,128)(2,1)S(1)}, u32[]{:S(2)}, u32[]{:S(2)}) collective-permute-start(bf16[8,8,2048]{2,1,0:T(8,128)(2,1)S(1)} %get-tuple-element.31), channel_id=1, source_target_pairs={{0,64},{1,65},{2,66},{3,67},{32,33},{33,34},{34,35},{35,32},{64,12... | collective-permute-start | bytes 786440 | tf_op jit(solution)/shard_map/ppermute | solution.py:336
  46.0 8.8 %collective-permute-start.11 = (bf16[8,8,2048]{2,1,0:T(8,128)(2,1)S(1)}, bf16[8,8,2048]{2,1,0:T(8,128)(2,1)S(1)}, u32[]{:S(2)}, u32[]{:S(2)}) collective-permute-start(bf16[8,8,2048]{2,1,0:T(8,128)(2,1)S(1)} %get-tuple-element.32), channel_id=1, source_target_pairs={{0,192},{1,193},{2,194},{3,195},{32,35},{33,32},{34,33},{35,34},{6... | collective-permute-start | bytes 786440 | tf_op jit(solution)/shard_map/ppermute | solution.py:336
  48.7 7.0 %collective-permute-start.9 = (bf16[8,8,2048]{2,1,0:T(8,128)(2,1)S(1)}, bf16[8,8,2048]{2,1,0:T(8,128)(2,1)S(1)}, u32[]{:S(2)}, u32[]{:S(2)}) collective-permute-start(bf16[8,8,2048]{2,1,0:T(8,128)(2,1)S(1)} %get-tuple-element.30), channel_id=1, source_target_pairs={{0,128},{1,129},{2,130},{3,131},{32,34},{33,35},{34,32},{35,33},{6... | collective-permute-start | bytes 786440 | tf_op jit(solution)/shard_map/ppermute | solution.py:336
  56.6 16.9 %all-to-all-start = ((bf16[8,8,2048]{2,1,0:T(8,128)(2,1)}), bf16[8,8,2048]{2,1,0:T(8,128)(2,1)S(1)}, u32[]{:S(2)}, u32[]{:S(2)}) async-start(bf16[8,8,2048]{2,1,0:T(8,128)(2,1)} %shard_map.142), calls=%async_computation | async-start | bytes 524288 | tf_op jit(solution)/shard_map/all_to_all | solution.py:377
  90.2 6.9 %collective-permute-start.12 = (bf16[32,4096]{1,0:T(8,128)(2,1)S(1)}, bf16[32,4096]{1,0:T(8,128)(2,1)S(1)}, u32[]{:S(2)}, u32[]{:S(2)}) collective-permute-start(bf16[32,4096]{1,0:T(8,128)(2,1)S(1)} %reshape.44.refs_0_), channel_id=1, source_target_pairs={{0,128},{1,129},{2,130},{3,131},{32,34},{33,35},{34,32},{35,33},{6... | collective-permute-start | bytes 786440 | tf_op jit(solution)/shard_map/ppermute | solution.py:336
  90.9 9.2 %collective-permute-start.13 = (bf16[32,4096]{1,0:T(8,128)(2,1)S(1)}, bf16[32,4096]{1,0:T(8,128)(2,1)S(1)}, u32[]{:S(2)}, u32[]{:S(2)}) collective-permute-start(bf16[32,4096]{1,0:T(8,128)(2,1)S(1)} %reshape.44.refs_0_), channel_id=1, source_target_pairs={{0,64},{1,65},{2,66},{3,67},{32,33},{33,34},{34,35},{35,32},{64,12... | collective-permute-start | bytes 786440 | tf_op jit(solution)/shard_map/ppermute | solution.py:336
  92.8 7.4 %collective-permute-start.14 = (bf16[32,4096]{1,0:T(8,128)(2,1)S(1)}, bf16[32,4096]{1,0:T(8,128)(2,1)S(1)}, u32[]{:S(2)}, u32[]{:S(2)}) collective-permute-start(bf16[32,4096]{1,0:T(8,128)(2,1)S(1)} %reshape.44.refs_0_), channel_id=1, source_target_pairs={{0,192},{1,193},{2,194},{3,195},{32,35},{33,32},{34,33},{35,34},{6... | collective-permute-start | bytes 786440 | tf_op jit(solution)/shard_map/ppermute | solution.py:336
  100.2 16.3 %collective-permute-start.15 = (bf16[128,4096]{1,0:T(8,128)(2,1)S(1)}, bf16[128,4096]{1,0:T(8,128)(2,1)S(1)}, u32[]{:S(2)}, u32[]{:S(2)}) collective-permute-start(bf16[128,4096]{1,0:T(8,128)(2,1)S(1)} %shard_map.143.refs_4_), channel_id=1, source_target_pairs={{0,2},{1,3},{2,0},{3,1},{32,160},{33,161},{34,162},{35,163},{64,66... | collective-permute-start | bytes 3145736 | tf_op jit(solution)/shard_map/ppermute | solution.py:336
  101.8 25.9 %collective-permute-start.16 = (bf16[128,4096]{1,0:T(8,128)(2,1)S(1)}, bf16[128,4096]{1,0:T(8,128)(2,1)S(1)}, u32[]{:S(2)}, u32[]{:S(2)}) collective-permute-start(bf16[128,4096]{1,0:T(8,128)(2,1)S(1)} %shard_map.143.refs_4_), channel_id=1, source_target_pairs={{0,1},{1,2},{2,3},{3,0},{32,96},{33,97},{34,98},{35,99},{64,65},{6... | collective-permute-start | bytes 3145736 | tf_op jit(solution)/shard_map/ppermute | solution.py:336
  103.9 23.8 %collective-permute-start.17 = (bf16[128,4096]{1,0:T(8,128)(2,1)S(1)}, bf16[128,4096]{1,0:T(8,128)(2,1)S(1)}, u32[]{:S(2)}, u32[]{:S(2)}) collective-permute-start(bf16[128,4096]{1,0:T(8,128)(2,1)S(1)} %shard_map.143.refs_4_), channel_id=1, source_target_pairs={{0,3},{1,0},{2,1},{3,2},{32,224},{33,225},{34,226},{35,227},{64,67... | collective-permute-start | bytes 3145736 | tf_op jit(solution)/shard_map/ppermute | solution.py:336
  104.5 1.9 %copy-start = (bf16[384,4096]{1,0:T(8,128)(2,1)S(1)}, bf16[384,4096]{1,0:T(8,128)(2,1)}, u32[]{:S(2)}) copy-start(bf16[384,4096]{1,0:T(8,128)(2,1)} %refs_3_.5) | copy-start | bytes 9437188
  129.8 18.8 %collective-permute-start.18 = (bf16[384,512]{1,0:T(8,128)(2,1)S(1)}, bf16[384,512]{1,0:T(8,128)(2,1)S(1)}, u32[]{:S(2)}, u32[]{:S(2)}) collective-permute-start(bf16[384,512]{1,0:T(8,128)(2,1)S(1)} %shard_map.147), channel_id=1, source_target_pairs={{0,32},{32,0},{1,33},{33,1},{2,34},{34,2},{3,35},{35,3},{4,36},{36... | collective-permute-start | bytes 1179656 | tf_op jit(solution)/shard_map/ppermute | solution.py:325

commit v10 on v9

--- a/solution.py
+++ b/solution.py
@@ -239,9 +239,11 @@
 
 
 def pack_kernel(*refs):
-    rows = refs[0].shape[0]
-    for at, ref in enumerate(refs[:-1]):
-        refs[-1][at * rows : (at + 1) * rows, :] = ref[...]
+    *piece_refs, out_ref, flag_ref = refs
+    rows = piece_refs[0].shape[0]
+    for at, ref in enumerate(piece_refs):
+        out_ref[at * rows : (at + 1) * rows, :] = ref[...]
+    flag_ref[...] = piece_refs[-1][: flag_ref.shape[0], : flag_ref.shape[1]]
 
 
 def packed(pieces):
@@ -250,14 +252,18 @@
     return pl.pallas_call(
         pack_kernel,
         in_specs=[whole] * len(pieces),
-        out_specs=whole,
-        out_shape=jax.ShapeDtypeStruct((len(pieces) * rows, model_width), jnp.bfloat16),
+        out_specs=[whole, whole],
+        out_shape=[
+            jax.ShapeDtypeStruct((len(pieces) * rows, model_width), jnp.bfloat16),
+            jax.ShapeDtypeStruct((16, 128), jnp.bfloat16),
+        ],
         compiler_params=pltpu.CompilerParams(vmem_limit_bytes=8 << 20),
     )(*pieces)
 
 
-def product_kernel(offsets, added, core_ref, x_ref, y_ref, tok_ref, *refs):
-    early_refs, weight_refs, (out_ref, spread_ref) = refs[:added], refs[added:-2], refs[-2:]
+def product_kernel(offsets, added, flags, core_ref, x_ref, y_ref, tok_ref, *refs):
+    early_refs, weight_refs = refs[:added], refs[added : -2 - flags]
+    out_ref, spread_ref = refs[-2:]
     core, at_x, at_y = core_ref[0], x_ref[0], y_ref[0]
     piece, columns = spread_ref.shape[0] // len(offsets), spread_ref.shape[1]
     row_at = lax.broadcasted_iota(jnp.int32, (piece, columns), 0)
@@ -282,20 +288,20 @@
     out_ref[...] = out.astype(jnp.bfloat16)
 
 
-def spread_product(place, offsets, tokens, weights, early=()):
+def spread_product(place, offsets, tokens, weights, early=(), flag=()):
     whole = pl.BlockSpec(memory_space=pltpu.VMEM)
     scalar = pl.BlockSpec(memory_space=pltpu.SMEM)
     rows = sum(value.shape[0] for value in weights)
     columns = 16 * (rows // len(offsets))
-    body = lambda *refs: product_kernel(offsets, len(early), *refs)
+    body = lambda *refs: product_kernel(offsets, len(early), len(flag), *refs)
     return pl.pallas_call(
         body,
-        in_specs=[scalar] * 3 + [whole] * (1 + len(early) + len(weights)),
+        in_specs=[scalar] * 3 + [whole] * (1 + len(early) + len(weights) + len(flag)),
         out_specs=whole,
         out_shape=jax.ShapeDtypeStruct((tokens.shape[0], columns), jnp.bfloat16),
         scratch_shapes=[pltpu.VMEM((rows, columns), jnp.bfloat16)],
         compiler_params=pltpu.CompilerParams(vmem_limit_bytes=12 << 20),
-    )(*place, tokens, *early, *weights)
+    )(*place, tokens, *early, *weights, *flag)
 
 
 def interleave_kernel(core_ref, own_ref, peer_ref, out_ref):
@@ -390,11 +396,14 @@
     stacked = lax.all_to_all(
         jnp.broadcast_to(effective[None], (count_z, *effective.shape)), "z", 0, 0, tiled=True
     ).reshape(count_z * rows_dev, model_width)
-    face = packed([stacked, *(shifted(stacked, 1, far) for far in order_far[1:])])
+    face, flag = packed([stacked, *(shifted(stacked, 1, far) for far in order_far[1:])])
+    face, flag = lax.optimization_barrier((face, swapped(flag)))
     arrived = [shifted(face, 0, far) for far in order_far[1:]]
     near = [(0, second) for second in order_far]
     beyond = [(first, second) for first in order_far[1:] for second in order_far]
-    early = [spread_product(place, near, rows, [face]) for rows in (peer_tokens, tokens)]
+    early = [
+        spread_product(place, near, rows, [face], flag=[flag]) for rows in (peer_tokens, tokens)
+    ]
     early, arrived = lax.optimization_barrier((early, arrived))
     peer_part = swapped(spread_product(place, beyond, peer_tokens, arrived, early[:1]))
     own_part = spread_product(place, beyond, tokens, arrived, early[1:])

time: 150 us -> 140 us (0.933)
  starting transfers between devices: 46.1 us -> 36.1 us
    ppermute x4 -> x5, starting transfers between devices: 20.6 us -> 10.7 us  [swapped(): return lax.ppermute(value, 'c', [(0, 1), (1, 0)])]
  transfers between devices with their start and end apart: 20 -> 21, of which waited for: 12 -> 13; matrix products, arithmetic and copies ran while one was open for 0% -> 1% of each run, Pallas kernels for 12% -> 13%
where the time goes in v10:
time: 140 us
  waiting for transfers between devices  55.7 us (40%)
  starting transfers between devices  36.1 us (26%)
  Pallas kernels  27.9 us (20%)
  blocking collectives  12.5 us (9%)
  local copies, waits for them, and re-layouts  3.25 us (2%)
  other arithmetic  2.42 us (2%)
    ppermute x15, waiting for transfers between devices, shifted(): return lax.ppermute(value, FACE, pairs)  46.4 us
    pallas_call x3, Pallas kernels, coded_gradient(): pl.pallas_call(body, grid_spec=pltpu.PrefetchScalarGridSpec(num_scalar_pr...  18.1 us
    ppermute x15, starting transfers between devices, shifted(): return lax.ppermute(value, FACE, pairs)  17.6 us
    all_to_all x1, blocking collectives, shards(): lax.all_to_all(jnp.broadcast_to(effective[None], (count_z, *effective.sha...  12.5 us
    ppermute x5, starting transfers between devices, swapped(): return lax.ppermute(value, 'c', [(0, 1), (1, 0)])  10.7 us
    all_to_all x1, waiting for transfers between devices, shards(): parts = lax.all_to_all(face, 'z', 0, 0, tiled=True)  8.45 us
    all_to_all x1, starting transfers between devices, shards(): parts = lax.all_to_all(face, 'z', 0, 0, tiled=True)  7.71 us
    pallas_call x4, Pallas kernels, spread_product(): pl.pallas_call(body, in_specs=[scalar] * 3 + [whole] * (1 + len(early) +...  6.74 us
  transfers between devices with their start and end apart: 21, of which 13 were waited for; matrix products, arithmetic and copies ran while one was open for 1% of the time, Pallas kernels for 13%

profile of v10, /device:TPU:1, one launch (start us, length us, event | category | flops | bytes accessed | tf_op | source)
XLA Modules:
  0.0 139.7 jit_solution(10678467606366315136)
XLA Ops:
  0.6 3.3 %collective-permute-start = (bf16[384,4096]{1,0:T(8,128)(2,1)}, bf16[384,4096]{1,0:T(8,128)(2,1)S(1)}, u32[]{:S(2)}, u32[]{:S(2)}) collective-permute-start(bf16[384,4096]{1,0:T(8,128)(2,1)} %refs_3_.5), channel_id=1, source_target_pairs={{0,32},{32,0},{1,33},{33,1},{2,34},{34,2},{3,35},{35,3},{4,36},{36... | collective-permute-start | bytes 9437192 | tf_op jit(solution)/shard_map/ppermute | solution.py:331
  4.1 0.4 collective-permute-start.2
  4.5 8.4 %shard_map.138.refs_12_ = bf16[512,4096]{1,0:T(8,128)(2,1)} custom-call(s32[1]{0:T(128)} %bitcast.refs_0_.core_ref, s32[1]{0:T(128)} %bitcast.1.refs_1_, s32[1]{0:T(128)} %bitcast.2.refs_2_, bf16[384,4096]{1,0:T(8,128)(2,1)} %refs_3_.5, bf16[384,1024]{1,0:T(8,128)(2,1)} %refs_7_.1, bf16[384,1024]{1,0:T(8,128)(2,1)} %refs_7_.1, bf16[384,1024]{1,0:T(8,128)(2,1)} %refs_7_.1, ...), custom_call_target="tpu_custom_call" | custom-call | tf_op jit(solution)/shard_map/pallas_call | solution.py:166
  13.0 4.9 %shard_map.139 = (bf16[128,2048]{1,0:T(8,128)(2,1)S(1)}, bf16[128,2048]{1,0:T(8,128)(2,1)S(1)}, bf16[128,2048]{1,0:T(8,128)(2,1)S(1)}, bf16[128,2048]{1,0:T(8,128)(2,1)S(1)}) custom-call(s32[1]{0:T(128)} %bitcast.refs_0_.core_ref, s32[1]{0:T(128)} %bitcast.1.refs_1_, s32[1]{0:T(128)} %bitcast.2.refs_2_, bf16[384,4096]{1,0:T(8,128)(2,1)S(1)} %collective-permute-done.refs_3_, ...), custom_call_target="tpu_custom_call" | custom-call | tf_op jit(solution)/shard_map/pallas_call | solution.py:166
  17.8 1.3 collective-permute-start.3
  19.1 0.4 collective-permute-start.4
  19.5 2.3 %collective-permute-start.5 = (bf16[128,2048]{1,0:T(8,128)(2,1)S(1)}, bf16[128,2048]{1,0:T(8,128)(2,1)S(1)}, u32[]{:S(2)}, u32[]{:S(2)}) collective-permute-start(bf16[128,2048]{1,0:T(8,128)(2,1)S(1)} %get-tuple-element.28), channel_id=1, source_target_pairs={{0,3},{1,0},{2,1},{3,2},{32,224},{33,225},{34,226},{35,227},{64,67... | collective-permute-start | bytes 1572872 | tf_op jit(solution)/shard_map/ppermute | solution.py:342
  21.8 4.8 %shard_map.140 = (bf16[128,2048]{1,0:T(8,128)(2,1)S(1)}, bf16[128,2048]{1,0:T(8,128)(2,1)S(1)}, bf16[128,2048]{1,0:T(8,128)(2,1)S(1)}, bf16[128,2048]{1,0:T(8,128)(2,1)S(1)}) custom-call(s32[1]{0:T(128)} %bitcast.refs_0_.core_ref, s32[1]{0:T(128)} %bitcast.1.refs_1_, s32[1]{0:T(128)} %bitcast.2.refs_2_, bf16[384,4096]{1,0:T(8,128)(2,1)S(1)} %collective-permute-done.refs_3_, ...), custom_call_target="tpu_custom_call" | custom-call | tf_op jit(solution)/shard_map/pallas_call | solution.py:166
  26.6 0.7 collective-permute-start.6
  27.3 0.5 collective-permute-done.3.refs_1_
  27.8 2.2 %collective-permute-start.8 = (bf16[128,2048]{1,0:T(8,128)(2,1)S(1)}, bf16[128,2048]{1,0:T(8,128)(2,1)S(1)}, u32[]{:S(2)}, u32[]{:S(2)}) collective-permute-start(bf16[128,2048]{1,0:T(8,128)(2,1)S(1)} %get-tuple-element.32), channel_id=1, source_target_pairs={{0,3},{1,0},{2,1},{3,2},{32,224},{33,225},{34,226},{35,227},{64,67... | collective-permute-start | bytes 1572872 | tf_op jit(solution)/shard_map/ppermute | solution.py:342
  29.9 3.4 %collective-permute-done.4.refs_2_ = bf16[128,2048]{1,0:T(8,128)(2,1)S(1)} collective-permute-done((bf16[128,2048]{1,0:T(8,128)(2,1)S(1)}, bf16[128,2048]{1,0:T(8,128)(2,1)S(1)}, u32[]{:S(2)}, u32[]{:S(2)}) %collective-permute-start.4) | collective-permute-done | bytes 524320 | tf_op jit(solution)/shard_map/ppermute | solution.py:342
  33.4 5.7 %collective-permute-done.6.refs_5_ = bf16[128,2048]{1,0:T(8,128)(2,1)S(1)} collective-permute-done((bf16[128,2048]{1,0:T(8,128)(2,1)S(1)}, bf16[128,2048]{1,0:T(8,128)(2,1)S(1)}, u32[]{:S(2)}, u32[]{:S(2)}) %collective-permute-start.6) | collective-permute-done | bytes 524320 | tf_op jit(solution)/shard_map/ppermute | solution.py:342
  39.1 5.5 %collective-permute-done.7.refs_6_ = bf16[128,2048]{1,0:T(8,128)(2,1)S(1)} collective-permute-done((bf16[128,2048]{1,0:T(8,128)(2,1)S(1)}, bf16[128,2048]{1,0:T(8,128)(2,1)S(1)}, u32[]{:S(2)}, u32[]{:S(2)}) %collective-permute-start.7) | collective-permute-done | bytes 524320 | tf_op jit(solution)/shard_map/ppermute | solution.py:342
  44.6 1.1 shard_map.141
  45.7 0.3 collective-permute-start.10
  45.9 2.7 %collective-permute-start.11 = (bf16[8,8,2048]{2,1,0:T(8,128)(2,1)S(1)}, bf16[8,8,2048]{2,1,0:T(8,128)(2,1)S(1)}, u32[]{:S(2)}, u32[]{:S(2)}) collective-permute-start(bf16[8,8,2048]{2,1,0:T(8,128)(2,1)S(1)} %get-tuple-element.36), channel_id=1, source_target_pairs={{0,192},{1,193},{2,194},{3,195},{32,35},{33,32},{34,33},{35,34},{6... | collective-permute-start | bytes 786440 | tf_op jit(solution)/shard_map/ppermute | solution.py:342
  48.6 0.2 collective-permute-start.9
  48.8 3.8 %collective-permute-done.10.refs_2_ = bf16[8,8,2048]{2,1,0:T(8,128)(2,1)S(1)} collective-permute-done((bf16[8,8,2048]{2,1,0:T(8,128)(2,1)S(1)}, bf16[8,8,2048]{2,1,0:T(8,128)(2,1)S(1)}, u32[]{:S(2)}, u32[]{:S(2)}) %collective-permute-start.10) | collective-permute-done | bytes 262176 | tf_op jit(solution)/shard_map/ppermute | solution.py:342
  52.6 2.1 %collective-permute-done.11.refs_3_ = bf16[8,8,2048]{2,1,0:T(8,128)(2,1)S(1)} collective-permute-done((bf16[8,8,2048]{2,1,0:T(8,128)(2,1)S(1)}, bf16[8,8,2048]{2,1,0:T(8,128)(2,1)S(1)}, u32[]{:S(2)}, u32[]{:S(2)}) %collective-permute-start.11) | collective-permute-done | bytes 262176 | tf_op jit(solution)/shard_map/ppermute | solution.py:342
  54.7 0.9 collective-permute-done.9.refs_1_
  55.6 0.9 shard_map.142
  56.5 7.7 %all-to-all-start = ((bf16[8,8,2048]{2,1,0:T(8,128)(2,1)}), bf16[8,8,2048]{2,1,0:T(8,128)(2,1)S(1)}, u32[]{:S(2)}, u32[]{:S(2)}) async-start(bf16[8,8,2048]{2,1,0:T(8,128)(2,1)} %shard_map.142), calls=%async_computation | async-start | bytes 524288 | tf_op jit(solution)/shard_map/all_to_all | solution.py:383
  64.3 0.6 convert_bitcast_fusion
  65.0 8.4 %all-to-all-done = bf16[8,8,2048]{2,1,0:T(8,128)(2,1)S(1)} async-done(((bf16[8,8,2048]{2,1,0:T(8,128)(2,1)}), bf16[8,8,2048]{2,1,0:T(8,128)(2,1)S(1)}, u32[]{:S(2)}, u32[]{:S(2)}) %all-to-all-start) | async-done | bytes 262176 | tf_op jit(solution)/shard_map/all_to_all | solution.py:383
  73.6 1.0 convolution_multiply_fusion
  74.7 1.8 %fusion.3 = (bf16[4,4096]{1,0:T(4,128)(2,1)S(1)}, f32[4,4096]{1,0:T(4,128)}, f32[4,4096]{1,0:T(4,128)}, f32[4,4096]{1,0:T(4,128)}) fusion(bf16[1,4,32,128]{3,2,1,0:T(8,128)(2,1)S(1)} %get-tuple-element.52, bf16[1,4,32,128]{3,2,1,0:T(8,128)(2,1)S(1)} %get-tuple-element.53, bf16[1024,4096]{1,0:T(8,128)(2,1)} %param.14, s32[]{:T(128)S(6)} %select_n.3, ...), kind=kLoop, calls=%fused_computation.8 | loop fusion | flops 409600 | bytes 606212 | tf_op jit(solution)/shard_map/convert_element_type | solution.py:394
  76.5 12.5 %all_to_all.10 = bf16[8,4,4096]{2,1,0:T(4,128)(2,1)} all-to-all(bf16[8,4,4096]{2,1,0:T(4,128)(2,1)S(1)} %broadcast_in_dim.2), channel_id=1, replica_groups=mesh['y'=4,'c'=2,'z'=8,'x'=4] {'z'}, dimensions={0} | all-to-all | bytes 524288 | tf_op jit(solution)/shard_map/all_to_all | solution.py:396
  89.1 1.0 reshape.44.refs_0_
  90.1 0.7 collective-permute-start.12
  90.8 1.9 %collective-permute-start.13 = (bf16[32,4096]{1,0:T(8,128)(2,1)S(1)}, bf16[32,4096]{1,0:T(8,128)(2,1)S(1)}, u32[]{:S(2)}, u32[]{:S(2)}) collective-permute-start(bf16[32,4096]{1,0:T(8,128)(2,1)S(1)} %reshape.44.refs_0_), channel_id=1, source_target_pairs={{0,64},{1,65},{2,66},{3,67},{32,33},{33,34},{34,35},{35,32},{64,12... | collective-permute-start | bytes 786440 | tf_op jit(solution)/shard_map/ppermute | solution.py:342
  92.7 1.0 collective-permute-start.14
  93.7 3.4 %collective-permute-done.12.refs_1_ = bf16[32,4096]{1,0:T(8,128)(2,1)S(1)} collective-permute-done((bf16[32,4096]{1,0:T(8,128)(2,1)S(1)}, bf16[32,4096]{1,0:T(8,128)(2,1)S(1)}, u32[]{:S(2)}, u32[]{:S(2)}) %collective-permute-start.12) | collective-permute-done | bytes 262176 | tf_op jit(solution)/shard_map/ppermute | solution.py:342
  97.0 3.0 %collective-permute-done.13.refs_2_ = bf16[32,4096]{1,0:T(8,128)(2,1)S(1)} collective-permute-done((bf16[32,4096]{1,0:T(8,128)(2,1)S(1)}, bf16[32,4096]{1,0:T(8,128)(2,1)S(1)}, u32[]{:S(2)}, u32[]{:S(2)}) %collective-permute-start.13) | collective-permute-done | bytes 262176 | tf_op jit(solution)/shard_map/ppermute | solution.py:342
  100.1 5.6 %collective-permute-start.15 = (bf16[16,128]{1,0:T(8,128)(2,1)S(1)}, bf16[16,128]{1,0:T(8,128)(2,1)S(1)}, u32[]{:S(2)}, u32[]{:S(2)}) collective-permute-start(bf16[16,128]{1,0:T(8,128)(2,1)S(1)} %get-tuple-element.38), channel_id=1, source_target_pairs={{0,32},{32,0},{1,33},{33,1},{2,34},{34,2},{3,35},{35,3},{4,36},{36... | collective-permute-start | bytes 12296 | tf_op jit(solution)/shard_map/ppermute | solution.py:331
  105.7 0.8 collective-permute-done.15.refs_5_
  106.5 1.4 %collective-permute-start.16 = (bf16[128,4096]{1,0:T(8,128)(2,1)S(1)}, bf16[128,4096]{1,0:T(8,128)(2,1)S(1)}, u32[]{:S(2)}, u32[]{:S(2)}) collective-permute-start(bf16[128,4096]{1,0:T(8,128)(2,1)S(1)} %get-tuple-element.39.refs_4_), channel_id=1, source_target_pairs={{0,2},{1,3},{2,0},{3,1},{32,160},{33,161},{34,162},{35,163},{64,66... | collective-permute-start | bytes 3145736 | tf_op jit(solution)/shard_map/ppermute | solution.py:342
  108.0 1.4 %collective-permute-start.17 = (bf16[128,4096]{1,0:T(8,128)(2,1)S(1)}, bf16[128,4096]{1,0:T(8,128)(2,1)S(1)}, u32[]{:S(2)}, u32[]{:S(2)}) collective-permute-start(bf16[128,4096]{1,0:T(8,128)(2,1)S(1)} %get-tuple-element.39.refs_4_), channel_id=1, source_target_pairs={{0,1},{1,2},{2,3},{3,0},{32,96},{33,97},{34,98},{35,99},{64,65},{6... | collective-permute-start | bytes 3145736 | tf_op jit(solution)/shard_map/ppermute | solution.py:342
  109.4 1.3 collective-permute-start.18
  110.7 1.9 %copy-done = bf16[384,4096]{1,0:T(8,128)(2,1)S(1)} copy-done((bf16[384,4096]{1,0:T(8,128)(2,1)S(1)}, bf16[384,4096]{1,0:T(8,128)(2,1)}, u32[]{:S(2)}) %copy-start) | copy-done | bytes 3145752
  112.5 1.3 shard_map.145.refs_4_
  113.8 1.3 shard_map.144.refs_4_
  115.2 6.9 %collective-permute-done.16.refs_5_ = bf16[128,4096]{1,0:T(8,128)(2,1)S(1)} collective-permute-done((bf16[128,4096]{1,0:T(8,128)(2,1)S(1)}, bf16[128,4096]{1,0:T(8,128)(2,1)S(1)}, u32[]{:S(2)}, u32[]{:S(2)}) %collective-permute-start.16) | collective-permute-done | bytes 1048608 | tf_op jit(solution)/shard_map/ppermute | solution.py:342
  122.0 11.2 %collective-permute-done.17.refs_6_ = bf16[128,4096]{1,0:T(8,128)(2,1)S(1)} collective-permute-done((bf16[128,4096]{1,0:T(8,128)(2,1)S(1)}, bf16[128,4096]{1,0:T(8,128)(2,1)S(1)}, u32[]{:S(2)}, u32[]{:S(2)}) %collective-permute-start.17) | collective-permute-done | bytes 1048608 | tf_op jit(solution)/shard_map/ppermute | solution.py:342
  133.2 2.1 %shard_map.147 = bf16[384,512]{1,0:T(8,128)(2,1)S(1)} custom-call(s32[1]{0:T(128)} %bitcast.refs_0_.core_ref, s32[1]{0:T(128)} %bitcast.1.refs_1_, s32[1]{0:T(128)} %bitcast.2.refs_2_, bf16[384,4096]{1,0:T(8,128)(2,1)S(1)} %collective-permute-done.refs_3_, bf16[384,512]{1,0:T(8,128)(2,1)S(1)} %shard_map.144.refs_4_, ...), custom_call_target="tpu_custom_call" | custom-call | tf_op jit(solution)/shard_map/pallas_call | solution.py:297
  135.3 1.3 collective-permute-start.19
  136.6 2.1 %shard_map.146.own_ref = bf16[384,512]{1,0:T(8,128)(2,1)S(1)} custom-call(s32[1]{0:T(128)} %bitcast.refs_0_.core_ref, s32[1]{0:T(128)} %bitcast.1.refs_1_, s32[1]{0:T(128)} %bitcast.2.refs_2_, bf16[384,4096]{1,0:T(8,128)(2,1)S(1)} %copy-done, bf16[384,512]{1,0:T(8,128)(2,1)S(1)} %shard_map.145.refs_4_, ...), custom_call_target="tpu_custom_call" | custom-call | tf_op jit(solution)/shard_map/pallas_call | solution.py:297
  138.7 1.0 shard_map.148
  (28 shorter events, 0.6 us)
Async XLA Ops:
  0.6 12.3 %collective-permute-start = (bf16[384,4096]{1,0:T(8,128)(2,1)}, bf16[384,4096]{1,0:T(8,128)(2,1)S(1)}, u32[]{:S(2)}, u32[]{:S(2)}) collective-permute-start(bf16[384,4096]{1,0:T(8,128)(2,1)} %refs_3_.5), channel_id=1, source_target_pairs={{0,32},{32,0},{1,33},{33,1},{2,34},{34,2},{3,35},{35,3},{4,36},{36... | collective-permute-start | bytes 9437192 | tf_op jit(solution)/shard_map/ppermute | solution.py:331
  4.0 9.0 %collective-permute-start.1 = (bf16[384,1024]{1,0:T(8,128)(2,1)}, bf16[384,1024]{1,0:T(8,128)(2,1)}, u32[]{:S(2)}, u32[]{:S(2)}) collective-permute-start(bf16[384,1024]{1,0:T(8,128)(2,1)} %refs_7_.1), channel_id=1, source_target_pairs={{0,32},{32,0},{1,33},{33,1},{2,34},{34,2},{3,35},{35,3},{4,36},{36... | collective-permute-start | bytes 2359304 | tf_op jit(solution)/shard_map/ppermute | solution.py:331
  4.1 8.8 %collective-permute-start.2 = (s32[8,32]{1,0:T(8,128)}, s32[8,32]{1,0:T(8,128)S(1)}, u32[]{:S(2)}, u32[]{:S(2)}) collective-permute-start(s32[8,32]{1,0:T(8,128)} %bitcast.22), channel_id=1, source_target_pairs={{0,32},{32,0},{1,33},{33,1},{2,34},{34,2},{3,35},{35,3},{4,36},{36... | collective-permute-start | bytes 3080 | tf_op jit(solution)/shard_map/ppermute | solution.py:331
  4.5 8.5 %copy-start.1 = (bf16[128,128]{1,0:T(8,128)(2,1)S(1)}, bf16[128,128]{1,0:T(8,128)(2,1)}, u32[]{:S(2)}) copy-start(bf16[128,128]{1,0:T(8,128)(2,1)} %constant.74.refs_10_) | copy-start | bytes 98308
  4.5 8.5 %copy-start.2 = (bf16[128,128]{1,0:T(8,128)(2,1)S(1)}, bf16[128,128]{1,0:T(8,128)(2,1)}, u32[]{:S(2)}) copy-start(bf16[128,128]{1,0:T(8,128)(2,1)} %constant.75.refs_11_) | copy-start | bytes 98308
  4.5 8.5 %copy-start.3 = (s32[32,128]{1,0:T(8,128)S(1)}, s32[32,128]{1,0:T(8,128)}, u32[]{:S(2)}) copy-start(s32[32,128]{1,0:T(8,128)} %refs_8_.5) | copy-start | bytes 49156
  17.8 10.0 %collective-permute-start.3 = (bf16[128,2048]{1,0:T(8,128)(2,1)S(1)}, bf16[128,2048]{1,0:T(8,128)(2,1)S(1)}, u32[]{:S(2)}, u32[]{:S(2)}) collective-permute-start(bf16[128,2048]{1,0:T(8,128)(2,1)S(1)} %get-tuple-element.26), channel_id=1, source_target_pairs={{0,2},{1,3},{2,0},{3,1},{32,160},{33,161},{34,162},{35,163},{64,66... | collective-permute-start | bytes 1572872 | tf_op jit(solution)/shard_map/ppermute | solution.py:342
  19.1 14.3 %collective-permute-start.4 = (bf16[128,2048]{1,0:T(8,128)(2,1)S(1)}, bf16[128,2048]{1,0:T(8,128)(2,1)S(1)}, u32[]{:S(2)}, u32[]{:S(2)}) collective-permute-start(bf16[128,2048]{1,0:T(8,128)(2,1)S(1)} %get-tuple-element.27), channel_id=1, source_target_pairs={{0,1},{1,2},{2,3},{3,0},{32,96},{33,97},{34,98},{35,99},{64,65},{6... | collective-permute-start | bytes 1572872 | tf_op jit(solution)/shard_map/ppermute | solution.py:342
  19.5 13.9 %collective-permute-start.5 = (bf16[128,2048]{1,0:T(8,128)(2,1)S(1)}, bf16[128,2048]{1,0:T(8,128)(2,1)S(1)}, u32[]{:S(2)}, u32[]{:S(2)}) collective-permute-start(bf16[128,2048]{1,0:T(8,128)(2,1)S(1)} %get-tuple-element.28), channel_id=1, source_target_pairs={{0,3},{1,0},{2,1},{3,2},{32,224},{33,225},{34,226},{35,227},{64,67... | collective-permute-start | bytes 1572872 | tf_op jit(solution)/shard_map/ppermute | solution.py:342
  26.6 37.7 %copy-start.4 = (s32[4,32]{1,0:T(4,128)S(1)}, s32[4,32]{1,0:T(4,128)}, u32[]{:S(2)}) copy-start(s32[4,32]{1,0:T(4,128)} %param.18) | copy-start | bytes 1540
  26.6 12.5 %collective-permute-start.6 = (bf16[128,2048]{1,0:T(8,128)(2,1)S(1)}, bf16[128,2048]{1,0:T(8,128)(2,1)S(1)}, u32[]{:S(2)}, u32[]{:S(2)}) collective-permute-start(bf16[128,2048]{1,0:T(8,128)(2,1)S(1)} %get-tuple-element.30), channel_id=1, source_target_pairs={{0,2},{1,3},{2,0},{3,1},{32,160},{33,161},{34,162},{35,163},{64,66... | collective-permute-start | bytes 1572872 | tf_op jit(solution)/shard_map/ppermute | solution.py:342
  27.3 17.3 %collective-permute-start.7 = (bf16[128,2048]{1,0:T(8,128)(2,1)S(1)}, bf16[128,2048]{1,0:T(8,128)(2,1)S(1)}, u32[]{:S(2)}, u32[]{:S(2)}) collective-permute-start(bf16[128,2048]{1,0:T(8,128)(2,1)S(1)} %get-tuple-element.31), channel_id=1, source_target_pairs={{0,1},{1,2},{2,3},{3,0},{32,96},{33,97},{34,98},{35,99},{64,65},{6... | collective-permute-start | bytes 1572872 | tf_op jit(solution)/shard_map/ppermute | solution.py:342
  27.8 16.8 %collective-permute-start.8 = (bf16[128,2048]{1,0:T(8,128)(2,1)S(1)}, bf16[128,2048]{1,0:T(8,128)(2,1)S(1)}, u32[]{:S(2)}, u32[]{:S(2)}) collective-permute-start(bf16[128,2048]{1,0:T(8,128)(2,1)S(1)} %get-tuple-element.32), channel_id=1, source_target_pairs={{0,3},{1,0},{2,1},{3,2},{32,224},{33,225},{34,226},{35,227},{64,67... | collective-permute-start | bytes 1572872 | tf_op jit(solution)/shard_map/ppermute | solution.py:342
  45.7 7.0 %collective-permute-start.10 = (bf16[8,8,2048]{2,1,0:T(8,128)(2,1)S(1)}, bf16[8,8,2048]{2,1,0:T(8,128)(2,1)S(1)}, u32[]{:S(2)}, u32[]{:S(2)}) collective-permute-start(bf16[8,8,2048]{2,1,0:T(8,128)(2,1)S(1)} %get-tuple-element.35), channel_id=1, source_target_pairs={{0,64},{1,65},{2,66},{3,67},{32,33},{33,34},{34,35},{35,32},{64,12... | collective-permute-start | bytes 786440 | tf_op jit(solution)/shard_map/ppermute | solution.py:342
  45.9 8.8 %collective-permute-start.11 = (bf16[8,8,2048]{2,1,0:T(8,128)(2,1)S(1)}, bf16[8,8,2048]{2,1,0:T(8,128)(2,1)S(1)}, u32[]{:S(2)}, u32[]{:S(2)}) collective-permute-start(bf16[8,8,2048]{2,1,0:T(8,128)(2,1)S(1)} %get-tuple-element.36), channel_id=1, source_target_pairs={{0,192},{1,193},{2,194},{3,195},{32,35},{33,32},{34,33},{35,34},{6... | collective-permute-start | bytes 786440 | tf_op jit(solution)/shard_map/ppermute | solution.py:342
  48.6 7.0 %collective-permute-start.9 = (bf16[8,8,2048]{2,1,0:T(8,128)(2,1)S(1)}, bf16[8,8,2048]{2,1,0:T(8,128)(2,1)S(1)}, u32[]{:S(2)}, u32[]{:S(2)}) collective-permute-start(bf16[8,8,2048]{2,1,0:T(8,128)(2,1)S(1)} %get-tuple-element.34), channel_id=1, source_target_pairs={{0,128},{1,129},{2,130},{3,131},{32,34},{33,35},{34,32},{35,33},{6... | collective-permute-start | bytes 786440 | tf_op jit(solution)/shard_map/ppermute | solution.py:342
  56.5 16.9 %all-to-all-start = ((bf16[8,8,2048]{2,1,0:T(8,128)(2,1)}), bf16[8,8,2048]{2,1,0:T(8,128)(2,1)S(1)}, u32[]{:S(2)}, u32[]{:S(2)}) async-start(bf16[8,8,2048]{2,1,0:T(8,128)(2,1)} %shard_map.142), calls=%async_computation | async-start | bytes 524288 | tf_op jit(solution)/shard_map/all_to_all | solution.py:383
  90.1 6.9 %collective-permute-start.12 = (bf16[32,4096]{1,0:T(8,128)(2,1)S(1)}, bf16[32,4096]{1,0:T(8,128)(2,1)S(1)}, u32[]{:S(2)}, u32[]{:S(2)}) collective-permute-start(bf16[32,4096]{1,0:T(8,128)(2,1)S(1)} %reshape.44.refs_0_), channel_id=1, source_target_pairs={{0,128},{1,129},{2,130},{3,131},{32,34},{33,35},{34,32},{35,33},{6... | collective-permute-start | bytes 786440 | tf_op jit(solution)/shard_map/ppermute | solution.py:342
  90.8 9.2 %collective-permute-start.13 = (bf16[32,4096]{1,0:T(8,128)(2,1)S(1)}, bf16[32,4096]{1,0:T(8,128)(2,1)S(1)}, u32[]{:S(2)}, u32[]{:S(2)}) collective-permute-start(bf16[32,4096]{1,0:T(8,128)(2,1)S(1)} %reshape.44.refs_0_), channel_id=1, source_target_pairs={{0,64},{1,65},{2,66},{3,67},{32,33},{33,34},{34,35},{35,32},{64,12... | collective-permute-start | bytes 786440 | tf_op jit(solution)/shard_map/ppermute | solution.py:342
  92.7 7.4 %collective-permute-start.14 = (bf16[32,4096]{1,0:T(8,128)(2,1)S(1)}, bf16[32,4096]{1,0:T(8,128)(2,1)S(1)}, u32[]{:S(2)}, u32[]{:S(2)}) collective-permute-start(bf16[32,4096]{1,0:T(8,128)(2,1)S(1)} %reshape.44.refs_0_), channel_id=1, source_target_pairs={{0,192},{1,193},{2,194},{3,195},{32,35},{33,32},{34,33},{35,34},{6... | collective-permute-start | bytes 786440 | tf_op jit(solution)/shard_map/ppermute | solution.py:342
  100.1 6.4 %collective-permute-start.15 = (bf16[16,128]{1,0:T(8,128)(2,1)S(1)}, bf16[16,128]{1,0:T(8,128)(2,1)S(1)}, u32[]{:S(2)}, u32[]{:S(2)}) collective-permute-start(bf16[16,128]{1,0:T(8,128)(2,1)S(1)} %get-tuple-element.38), channel_id=1, source_target_pairs={{0,32},{32,0},{1,33},{33,1},{2,34},{34,2},{3,35},{35,3},{4,36},{36... | collective-permute-start | bytes 12296 | tf_op jit(solution)/shard_map/ppermute | solution.py:331
  106.5 15.5 %collective-permute-start.16 = (bf16[128,4096]{1,0:T(8,128)(2,1)S(1)}, bf16[128,4096]{1,0:T(8,128)(2,1)S(1)}, u32[]{:S(2)}, u32[]{:S(2)}) collective-permute-start(bf16[128,4096]{1,0:T(8,128)(2,1)S(1)} %get-tuple-element.39.refs_4_), channel_id=1, source_target_pairs={{0,2},{1,3},{2,0},{3,1},{32,160},{33,161},{34,162},{35,163},{64,66... | collective-permute-start | bytes 3145736 | tf_op jit(solution)/shard_map/ppermute | solution.py:342
  108.0 25.2 %collective-permute-start.17 = (bf16[128,4096]{1,0:T(8,128)(2,1)S(1)}, bf16[128,4096]{1,0:T(8,128)(2,1)S(1)}, u32[]{:S(2)}, u32[]{:S(2)}) collective-permute-start(bf16[128,4096]{1,0:T(8,128)(2,1)S(1)} %get-tuple-element.39.refs_4_), channel_id=1, source_target_pairs={{0,1},{1,2},{2,3},{3,0},{32,96},{33,97},{34,98},{35,99},{64,65},{6... | collective-permute-start | bytes 3145736 | tf_op jit(solution)/shard_map/ppermute | solution.py:342
  109.4 23.8 %collective-permute-start.18 = (bf16[128,4096]{1,0:T(8,128)(2,1)S(1)}, bf16[128,4096]{1,0:T(8,128)(2,1)S(1)}, u32[]{:S(2)}, u32[]{:S(2)}) collective-permute-start(bf16[128,4096]{1,0:T(8,128)(2,1)S(1)} %get-tuple-element.39.refs_4_), channel_id=1, source_target_pairs={{0,3},{1,0},{2,1},{3,2},{32,224},{33,225},{34,226},{35,227},{64,67... | collective-permute-start | bytes 3145736 | tf_op jit(solution)/shard_map/ppermute | solution.py:342
  110.7 1.9 %copy-start = (bf16[384,4096]{1,0:T(8,128)(2,1)S(1)}, bf16[384,4096]{1,0:T(8,128)(2,1)}, u32[]{:S(2)}) copy-start(bf16[384,4096]{1,0:T(8,128)(2,1)} %refs_3_.5) | copy-start | bytes 9437188
  135.3 3.4 %collective-permute-start.19 = (bf16[384,512]{1,0:T(8,128)(2,1)S(1)}, bf16[384,512]{1,0:T(8,128)(2,1)S(1)}, u32[]{:S(2)}, u32[]{:S(2)}) collective-permute-start(bf16[384,512]{1,0:T(8,128)(2,1)S(1)} %shard_map.147), channel_id=1, source_target_pairs={{0,32},{32,0},{1,33},{33,1},{2,34},{34,2},{3,35},{35,3},{4,36},{36... | collective-permute-start | bytes 1179656 | tf_op jit(solution)/shard_map/ppermute | solution.py:331

commit v11 on v10

--- a/solution.py
+++ b/solution.py
@@ -31,31 +31,58 @@
     return (1 - 2 * (parity % 2)).astype(np.float32)
 
 
-def unrotate_rows(row_block, sign_rows, matrix):
-    row_count = row_block.shape[0]
+def update_kernel(parts_ref, sign_ref, mat_ref, master_ref, base_ref, first_ref, second_ref, exps_ref, *refs):
+    out_master_ref, out_first_ref, out_second_ref, out_ref, grad_ref, bound_ref = refs
+    block_len = mat_ref.shape[0]
+    rows, half = master_ref.shape[0], parts_ref.shape[2]
+    blocks = half // block_len
+    total = parts_ref[0].astype(jnp.float32)
+    for at in range(1, parts_ref.shape[0]):
+        total = total + parts_ref[at].astype(jnp.float32)
+    stacked = jnp.concatenate(
+        [total[:, at * block_len : (at + 1) * block_len] for at in range(blocks)], axis=0
+    )
     turned = jnp.dot(
-        row_block.reshape(-1, sign_rows.shape[1]), matrix, precision=highest
-    ) / math.sqrt(sign_rows.shape[1])
-    return (turned.reshape(row_count, sign_rows.shape[0], sign_rows.shape[1]) * sign_rows).reshape(
-        row_block.shape
-    )
-
-
-def clip_rows(row_block, bound_rows):
-    row_count = row_block.shape[0]
-    shaped = row_block.reshape(row_count, bound_rows.shape[1], -1)
-    limits = bound_rows[:, :, None]
-    return jnp.clip(shaped, -limits, limits).reshape(row_block.shape)
-
-
-def adam_update(gradient, master, first, second):
-    new_first = beta_one * first + (1.0 - beta_one) * gradient
-    new_second = beta_two * second + (1.0 - beta_two) * gradient * gradient
+        stacked, mat_ref[...], precision=highest, preferred_element_type=jnp.float32
+    ) / math.sqrt(block_len)
+    signs = (2 * sign_ref[...] - 1).astype(jnp.float32)
+    levels = clip_level * jnp.exp2(exps_ref[...].astype(jnp.float32))
+    for at in range(blocks):
+        piece = turned[2 * rows * at : 2 * rows * (at + 1)]
+        for side in range(2):
+            block = side * blocks + at
+            cols = slice(block * block_len, (block + 1) * block_len)
+            grad_ref[:, cols] = piece[side * rows : (side + 1) * rows] * signs[block : block + 1]
+            bound_ref[:, cols] = jnp.broadcast_to(levels[:, block : block + 1], (rows, block_len))
+    gradient, master = grad_ref[...], master_ref[...]
+    new_first = beta_one * first_ref[...] + (1.0 - beta_one) * gradient
+    new_second = beta_two * second_ref[...] + (1.0 - beta_two) * gradient * gradient
     fix_one = 1.0 - beta_one**ADAM_STEP
     fix_two = 1.0 - beta_two**ADAM_STEP
     step_dir = new_first / fix_one / (jnp.sqrt(new_second / fix_two) + adam_eps)
     new_master = master - learn_rate * (step_dir + decay_rate * master)
-    return (new_master, new_first, new_second)
+    base, bound = base_ref[...].astype(jnp.float32), bound_ref[...]
+    coded = jnp.clip(new_master - base, -bound, bound).astype(jnp.bfloat16)
+    effective = (base + coded.astype(jnp.float32)).astype(jnp.bfloat16)
+    out_master_ref[...] = new_master
+    out_first_ref[...] = new_first
+    out_second_ref[...] = new_second
+    for at in range(out_ref.shape[0]):
+        out_ref[at] = effective
+
+
+def updated(parts, signs, matrix, master, base, first, second, exps):
+    whole = pl.BlockSpec(memory_space=pltpu.VMEM)
+    shape = jax.ShapeDtypeStruct(master.shape, jnp.float32)
+    copies = jax.ShapeDtypeStruct((parts.shape[0], *master.shape), jnp.bfloat16)
+    return pl.pallas_call(
+        update_kernel,
+        in_specs=[whole] * 8,
+        out_specs=[whole] * 4,
+        out_shape=[shape, shape, shape, copies],
+        scratch_shapes=[pltpu.VMEM(master.shape, jnp.float32)] * 2,
+        compiler_params=pltpu.CompilerParams(vmem_limit_bytes=8 << 20),
+    )(parts, signs, matrix, master, base, first, second, exps)
 
 
 def row_order(count_z, count_x, rows_dev):
@@ -355,8 +382,7 @@
 ):
     count_z = lax.axis_size("z")
     rows_dev, model_width = master_weights.shape
-    sign_rows = (2 * hadamard_signs - 1).astype(jnp.float32)
-    block_len = sign_rows.shape[1]
+    block_len = hadamard_signs.shape[1]
     matrix = jnp.asarray(hadamard(block_len))
     order = jnp.asarray(row_order(count_z, 4, rows_dev))
     place = [lax.axis_index(axis).reshape(1).astype(jnp.int32) for axis in ("c", "x", "y")]
@@ -381,32 +407,36 @@
     lines = line_sums(*halves)
     face = face_sum([lines[0], *(shifted(lines[far], 1, far) for far in (2, 1, 3))])
     parts = lax.all_to_all(face, "z", 0, 0, tiled=True)
-    summed = jnp.sum(parts.astype(jnp.float32), axis=0)
-    summed = jnp.swapaxes(summed.reshape(2, rows_dev, -1), 0, 1).reshape(rows_dev, model_width)
-    gradient = unrotate_rows(summed, sign_rows, matrix)
-    new_master, new_first, new_second = adam_update(gradient, master_weights, adam_m, adam_v)
     owner = lax.axis_index(AXES)
-    base_own = lax.dynamic_slice_in_dim(base_weights, owner * rows_dev, rows_dev, 0).astype(
-        jnp.float32
-    )
-    diff_bound = clip_level * jnp.exp2(diff_exps.astype(jnp.float32))
-    diff_coded = clip_rows(new_master - base_own, diff_bound).astype(jnp.bfloat16)
-    effective = (base_own + diff_coded.astype(jnp.float32)).astype(jnp.bfloat16)
+    base_own = lax.dynamic_slice_in_dim(base_weights, owner * rows_dev, rows_dev, 0)
+    new_master, new_first, new_second, effective = updated(
+        parts,
+        hadamard_signs,
+        matrix,
+        master_weights,
+        base_own,
+        adam_m,
+        adam_v,
+        diff_exps,
+    )
     order_far = (0, 2, 1, 3)
-    stacked = lax.all_to_all(
-        jnp.broadcast_to(effective[None], (count_z, *effective.shape)), "z", 0, 0, tiled=True
-    ).reshape(count_z * rows_dev, model_width)
+    stacked = lax.all_to_all(effective, "z", 0, 0, tiled=True).reshape(-1, model_width)
     face, flag = packed([stacked, *(shifted(stacked, 1, far) for far in order_far[1:])])
     face, flag = lax.optimization_barrier((face, swapped(flag)))
     arrived = [shifted(face, 0, far) for far in order_far[1:]]
     near = [(0, second) for second in order_far]
-    beyond = [(first, second) for first in order_far[1:] for second in order_far]
+    beyond = [[(first, second) for second in order_far] for first in order_far[1:]]
     early = [
         spread_product(place, near, rows, [face], flag=[flag]) for rows in (peer_tokens, tokens)
     ]
-    early, arrived = lax.optimization_barrier((early, arrived))
-    peer_part = swapped(spread_product(place, beyond, peer_tokens, arrived, early[:1]))
-    own_part = spread_product(place, beyond, tokens, arrived, early[1:])
+    early = [
+        spread_product(place, beyond[0], rows, arrived[:1], [done])
+        for rows, done in zip((peer_tokens, tokens), early)
+    ]
+    early, last = lax.optimization_barrier((early, arrived[1:]))
+    beyond = beyond[1] + beyond[2]
+    peer_part = swapped(spread_product(place, beyond, peer_tokens, last, early[:1]))
+    own_part = spread_product(place, beyond, tokens, last, early[1:])
     projected = interleaved(place[0], own_part, peer_part)
     return (projected, new_master, new_first, new_second)
 

time: 140 us -> 138 us (0.986)
  waiting for transfers between devices: 55.7 us -> 50.4 us
  local copies, waits for them, and re-layouts: 3.25 us -> 6.3 us
  other arithmetic: 2.42 us -> 0 us
  Pallas kernels: 27.9 us -> 30 us
  starting transfers between devices: 36.1 us -> 37.8 us
    ppermute x15, waiting for transfers between devices: 46.4 us -> 41.3 us  [shifted(): return lax.ppermute(value, FACE, pairs)]
    ppermute x15, starting transfers between devices: 17.6 us -> 20.1 us  [shifted(): return lax.ppermute(value, FACE, pairs)]
    unnamed x11 -> x18, local copies, waits for them, and re-layouts: 2 us -> 4.43 us
    convert_element_type x1 -> x0, other arithmetic: 1.77 us -> none  [shards(): effective = (base_own + diff_coded.astype(jnp.float32)).astype(jnp.bfloat16)]
    pallas_call x4 -> x6, Pallas kernels: 6.74 us -> 7.84 us  [spread_product(): pl.pallas_call(body, in_specs=[scalar] * 3 + [whole] * (1 + len(early) +...]
  transfers between devices with their start and end apart: 21 -> 21, of which waited for: 13 -> 12; matrix products, arithmetic and copies ran while one was open for 1% -> 1% of each run, Pallas kernels for 13% -> 14%
where the time goes in v11:
time: 138 us
  waiting for transfers between devices  50.4 us (37%)
  starting transfers between devices  37.8 us (27%)
  Pallas kernels  30 us (22%)
  blocking collectives  12.5 us (9%)
  local copies, waits for them, and re-layouts  6.3 us (5%)
    ppermute x15, waiting for transfers between devices, shifted(): return lax.ppermute(value, FACE, pairs)  41.3 us
    ppermute x15, starting transfers between devices, shifted(): return lax.ppermute(value, FACE, pairs)  20.1 us
    pallas_call x3, Pallas kernels, coded_gradient(): pl.pallas_call(body, grid_spec=pltpu.PrefetchScalarGridSpec(num_scalar_pr...  18.1 us
    all_to_all x1, blocking collectives, shards(): lax.all_to_all(effective, 'z', 0, 0, tiled=True).reshape(-1, model_width)  12.5 us
    ppermute x5, starting transfers between devices, swapped(): return lax.ppermute(value, 'c', [(0, 1), (1, 0)])  10.7 us
    all_to_all x1, waiting for transfers between devices, shards(): parts = lax.all_to_all(face, 'z', 0, 0, tiled=True)  8.32 us
    pallas_call x6, Pallas kernels, spread_product(): pl.pallas_call(body, in_specs=[scalar] * 3 + [whole] * (1 + len(early) +...  7.84 us
    all_to_all x1, starting transfers between devices, shards(): parts = lax.all_to_all(face, 'z', 0, 0, tiled=True)  6.96 us
  transfers between devices with their start and end apart: 21, of which 12 were waited for; matrix products, arithmetic and copies ran while one was open for 1% of the time, Pallas kernels for 14%

profile of v11, /device:TPU:1, one launch (start us, length us, event | category | flops | bytes accessed | tf_op | source)
XLA Modules:
  0.0 137.9 jit_solution(9889697531878489608)
XLA Ops:
  0.6 3.3 %collective-permute-start = (bf16[384,4096]{1,0:T(8,128)(2,1)}, bf16[384,4096]{1,0:T(8,128)(2,1)S(1)}, u32[]{:S(2)}, u32[]{:S(2)}) collective-permute-start(bf16[384,4096]{1,0:T(8,128)(2,1)} %refs_3_.7), channel_id=1, source_target_pairs={{0,32},{32,0},{1,33},{33,1},{2,34},{34,2},{3,35},{35,3},{4,36},{36... | collective-permute-start | bytes 9437192 | tf_op jit(solution)/shard_map/ppermute | solution.py:358
  4.5 8.5 %shard_map.138.refs_12_ = bf16[512,4096]{1,0:T(8,128)(2,1)} custom-call(s32[1]{0:T(128)} %bitcast.refs_0_.core_ref, s32[1]{0:T(128)} %bitcast.1.refs_1_, s32[1]{0:T(128)} %bitcast.2.refs_2_, bf16[384,4096]{1,0:T(8,128)(2,1)} %refs_3_.7, bf16[384,1024]{1,0:T(8,128)(2,1)} %refs_7_.1, bf16[384,1024]{1,0:T(8,128)(2,1)} %refs_7_.1, bf16[384,1024]{1,0:T(8,128)(2,1)} %refs_7_.1, ...), custom_call_target="tpu_custom_call" | custom-call | tf_op jit(solution)/shard_map/pallas_call | solution.py:193
  13.0 4.9 %shard_map.139 = (bf16[128,2048]{1,0:T(8,128)(2,1)S(1)}, bf16[128,2048]{1,0:T(8,128)(2,1)S(1)}, bf16[128,2048]{1,0:T(8,128)(2,1)S(1)}, bf16[128,2048]{1,0:T(8,128)(2,1)S(1)}) custom-call(s32[1]{0:T(128)} %bitcast.refs_0_.core_ref, s32[1]{0:T(128)} %bitcast.1.refs_1_, s32[1]{0:T(128)} %bitcast.2.refs_2_, bf16[384,4096]{1,0:T(8,128)(2,1)S(1)} %collective-permute-done.refs_3_, ...), custom_call_target="tpu_custom_call" | custom-call | tf_op jit(solution)/shard_map/pallas_call | solution.py:193
  17.9 1.3 collective-permute-start.3
  19.5 2.3 %collective-permute-start.5 = (bf16[128,2048]{1,0:T(8,128)(2,1)S(1)}, bf16[128,2048]{1,0:T(8,128)(2,1)S(1)}, u32[]{:S(2)}, u32[]{:S(2)}) collective-permute-start(bf16[128,2048]{1,0:T(8,128)(2,1)S(1)} %get-tuple-element.31), channel_id=1, source_target_pairs={{0,3},{1,0},{2,1},{3,2},{32,224},{33,225},{34,226},{35,227},{64,67... | collective-permute-start | bytes 1572872 | tf_op jit(solution)/shard_map/ppermute | solution.py:369
  21.8 4.8 %shard_map.140 = (bf16[128,2048]{1,0:T(8,128)(2,1)S(1)}, bf16[128,2048]{1,0:T(8,128)(2,1)S(1)}, bf16[128,2048]{1,0:T(8,128)(2,1)S(1)}, bf16[128,2048]{1,0:T(8,128)(2,1)S(1)}) custom-call(s32[1]{0:T(128)} %bitcast.refs_0_.core_ref, s32[1]{0:T(128)} %bitcast.1.refs_1_, s32[1]{0:T(128)} %bitcast.2.refs_2_, bf16[384,4096]{1,0:T(8,128)(2,1)S(1)} %collective-permute-done.refs_3_, ...), custom_call_target="tpu_custom_call" | custom-call | tf_op jit(solution)/shard_map/pallas_call | solution.py:193
  26.7 0.7 collective-permute-start.6
  27.3 0.5 collective-permute-done.3.refs_1_
  27.8 2.2 %collective-permute-start.8 = (bf16[128,2048]{1,0:T(8,128)(2,1)S(1)}, bf16[128,2048]{1,0:T(8,128)(2,1)S(1)}, u32[]{:S(2)}, u32[]{:S(2)}) collective-permute-start(bf16[128,2048]{1,0:T(8,128)(2,1)S(1)} %get-tuple-element.35), channel_id=1, source_target_pairs={{0,3},{1,0},{2,1},{3,2},{32,224},{33,225},{34,226},{35,227},{64,67... | collective-permute-start | bytes 1572872 | tf_op jit(solution)/shard_map/ppermute | solution.py:369
  30.0 3.4 %collective-permute-done.4.refs_2_ = bf16[128,2048]{1,0:T(8,128)(2,1)S(1)} collective-permute-done((bf16[128,2048]{1,0:T(8,128)(2,1)S(1)}, bf16[128,2048]{1,0:T(8,128)(2,1)S(1)}, u32[]{:S(2)}, u32[]{:S(2)}) %collective-permute-start.4) | collective-permute-done | bytes 524320 | tf_op jit(solution)/shard_map/ppermute | solution.py:369
  33.4 5.7 %collective-permute-done.6.refs_5_ = bf16[128,2048]{1,0:T(8,128)(2,1)S(1)} collective-permute-done((bf16[128,2048]{1,0:T(8,128)(2,1)S(1)}, bf16[128,2048]{1,0:T(8,128)(2,1)S(1)}, u32[]{:S(2)}, u32[]{:S(2)}) %collective-permute-start.6) | collective-permute-done | bytes 524320 | tf_op jit(solution)/shard_map/ppermute | solution.py:369
  39.1 5.5 %collective-permute-done.7.refs_6_ = bf16[128,2048]{1,0:T(8,128)(2,1)S(1)} collective-permute-done((bf16[128,2048]{1,0:T(8,128)(2,1)S(1)}, bf16[128,2048]{1,0:T(8,128)(2,1)S(1)}, u32[]{:S(2)}, u32[]{:S(2)}) %collective-permute-start.7) | collective-permute-done | bytes 524320 | tf_op jit(solution)/shard_map/ppermute | solution.py:369
  44.6 1.1 shard_map.141
  45.7 1.5 %collective-permute-start.9 = (bf16[8,8,2048]{2,1,0:T(8,128)(2,1)S(1)}, bf16[8,8,2048]{2,1,0:T(8,128)(2,1)S(1)}, u32[]{:S(2)}, u32[]{:S(2)}) collective-permute-start(bf16[8,8,2048]{2,1,0:T(8,128)(2,1)S(1)} %get-tuple-element.37), channel_id=1, source_target_pairs={{0,128},{1,129},{2,130},{3,131},{32,34},{33,35},{34,32},{35,33},{6... | collective-permute-start | bytes 786440 | tf_op jit(solution)/shard_map/ppermute | solution.py:369
  47.6 2.4 %collective-permute-start.11 = (bf16[8,8,2048]{2,1,0:T(8,128)(2,1)S(1)}, bf16[8,8,2048]{2,1,0:T(8,128)(2,1)S(1)}, u32[]{:S(2)}, u32[]{:S(2)}) collective-permute-start(bf16[8,8,2048]{2,1,0:T(8,128)(2,1)S(1)} %get-tuple-element.39), channel_id=1, source_target_pairs={{0,192},{1,193},{2,194},{3,195},{32,35},{33,32},{34,33},{35,34},{6... | collective-permute-start | bytes 786440 | tf_op jit(solution)/shard_map/ppermute | solution.py:369
  49.9 2.9 %collective-permute-done.9.refs_1_ = bf16[8,8,2048]{2,1,0:T(8,128)(2,1)S(1)} collective-permute-done((bf16[8,8,2048]{2,1,0:T(8,128)(2,1)S(1)}, bf16[8,8,2048]{2,1,0:T(8,128)(2,1)S(1)}, u32[]{:S(2)}, u32[]{:S(2)}) %collective-permute-start.9) | collective-permute-done | bytes 262176 | tf_op jit(solution)/shard_map/ppermute | solution.py:369
  52.8 2.8 %collective-permute-done.10.refs_2_ = bf16[8,8,2048]{2,1,0:T(8,128)(2,1)S(1)} collective-permute-done((bf16[8,8,2048]{2,1,0:T(8,128)(2,1)S(1)}, bf16[8,8,2048]{2,1,0:T(8,128)(2,1)S(1)}, u32[]{:S(2)}, u32[]{:S(2)}) %collective-permute-start.10) | collective-permute-done | bytes 262176 | tf_op jit(solution)/shard_map/ppermute | solution.py:369
  55.6 0.9 shard_map.142
  56.5 7.0 %all-to-all-start = ((bf16[8,8,2048]{2,1,0:T(8,128)(2,1)}), bf16[8,8,2048]{2,1,0:T(8,128)(2,1)S(1)}, u32[]{:S(2)}, u32[]{:S(2)}) async-start(bf16[8,8,2048]{2,1,0:T(8,128)(2,1)} %shard_map.142), calls=%async_computation | async-start | bytes 524288 | tf_op jit(solution)/shard_map/all_to_all | solution.py:409
  63.5 0.9 constant_dynamic-slice_fusion.base_ref
  64.4 8.3 %all-to-all-done.parts_ref = bf16[8,8,2048]{2,1,0:T(8,128)(2,1)S(1)} async-done(((bf16[8,8,2048]{2,1,0:T(8,128)(2,1)}), bf16[8,8,2048]{2,1,0:T(8,128)(2,1)S(1)}, u32[]{:S(2)}, u32[]{:S(2)}) %all-to-all-start) | async-done | bytes 262176 | tf_op jit(solution)/shard_map/all_to_all | solution.py:409
  72.7 0.8 copy-done.5
  73.5 0.8 copy-done.6
  74.4 0.8 copy-done.7
  75.2 1.0 shard_map.143
  76.2 12.5 %all_to_all.10 = bf16[8,4,4096]{2,1,0:T(4,128)(2,1)} all-to-all(bf16[8,4,4096]{2,1,0:T(4,128)(2,1)S(1)} %get-tuple-element.40), channel_id=1, replica_groups=mesh['y'=4,'c'=2,'z'=8,'x'=4] {'z'}, dimensions={0} | all-to-all | bytes 524288 | tf_op jit(solution)/shard_map/all_to_all | solution.py:423
  88.7 1.0 reshape.23.refs_0_
  89.7 2.0 %collective-permute-start.12 = (bf16[32,4096]{1,0:T(8,128)(2,1)S(1)}, bf16[32,4096]{1,0:T(8,128)(2,1)S(1)}, u32[]{:S(2)}, u32[]{:S(2)}) collective-permute-start(bf16[32,4096]{1,0:T(8,128)(2,1)S(1)} %reshape.23.refs_0_), channel_id=1, source_target_pairs={{0,128},{1,129},{2,130},{3,131},{32,34},{33,35},{34,32},{35,33},{6... | collective-permute-start | bytes 786440 | tf_op jit(solution)/shard_map/ppermute | solution.py:369
  91.7 1.1 collective-permute-start.13
  92.8 1.6 %collective-permute-start.14 = (bf16[32,4096]{1,0:T(8,128)(2,1)S(1)}, bf16[32,4096]{1,0:T(8,128)(2,1)S(1)}, u32[]{:S(2)}, u32[]{:S(2)}) collective-permute-start(bf16[32,4096]{1,0:T(8,128)(2,1)S(1)} %reshape.23.refs_0_), channel_id=1, source_target_pairs={{0,192},{1,193},{2,194},{3,195},{32,35},{33,32},{34,33},{35,34},{6... | collective-permute-start | bytes 786440 | tf_op jit(solution)/shard_map/ppermute | solution.py:369
  94.4 2.2 %collective-permute-done.12.refs_1_ = bf16[32,4096]{1,0:T(8,128)(2,1)S(1)} collective-permute-done((bf16[32,4096]{1,0:T(8,128)(2,1)S(1)}, bf16[32,4096]{1,0:T(8,128)(2,1)S(1)}, u32[]{:S(2)}, u32[]{:S(2)}) %collective-permute-start.12) | collective-permute-done | bytes 262176 | tf_op jit(solution)/shard_map/ppermute | solution.py:369
  96.7 3.0 %collective-permute-done.13.refs_2_ = bf16[32,4096]{1,0:T(8,128)(2,1)S(1)} collective-permute-done((bf16[32,4096]{1,0:T(8,128)(2,1)S(1)}, bf16[32,4096]{1,0:T(8,128)(2,1)S(1)}, u32[]{:S(2)}, u32[]{:S(2)}) %collective-permute-start.13) | collective-permute-done | bytes 262176 | tf_op jit(solution)/shard_map/ppermute | solution.py:369
  99.7 5.6 %collective-permute-start.15 = (bf16[16,128]{1,0:T(8,128)(2,1)S(1)}, bf16[16,128]{1,0:T(8,128)(2,1)S(1)}, u32[]{:S(2)}, u32[]{:S(2)}) collective-permute-start(bf16[16,128]{1,0:T(8,128)(2,1)S(1)} %get-tuple-element.42), channel_id=1, source_target_pairs={{0,32},{32,0},{1,33},{33,1},{2,34},{34,2},{3,35},{35,3},{4,36},{36... | collective-permute-start | bytes 12296 | tf_op jit(solution)/shard_map/ppermute | solution.py:358
  105.3 0.8 collective-permute-done.15.refs_5_
  106.1 1.8 %collective-permute-start.16 = (bf16[128,4096]{1,0:T(8,128)(2,1)S(1)}, bf16[128,4096]{1,0:T(8,128)(2,1)S(1)}, u32[]{:S(2)}, u32[]{:S(2)}) collective-permute-start(bf16[128,4096]{1,0:T(8,128)(2,1)S(1)} %get-tuple-element.43.refs_4_), channel_id=1, source_target_pairs={{0,2},{1,3},{2,0},{3,1},{32,160},{33,161},{34,162},{35,163},{64,66... | collective-permute-start | bytes 3145736 | tf_op jit(solution)/shard_map/ppermute | solution.py:369
  107.9 1.2 collective-permute-start.17
  109.1 1.5 %collective-permute-start.18 = (bf16[128,4096]{1,0:T(8,128)(2,1)S(1)}, bf16[128,4096]{1,0:T(8,128)(2,1)S(1)}, u32[]{:S(2)}, u32[]{:S(2)}) collective-permute-start(bf16[128,4096]{1,0:T(8,128)(2,1)S(1)} %get-tuple-element.43.refs_4_), channel_id=1, source_target_pairs={{0,3},{1,0},{2,1},{3,2},{32,224},{33,225},{34,226},{35,227},{64,67... | collective-permute-start | bytes 3145736 | tf_op jit(solution)/shard_map/ppermute | solution.py:369
  110.6 1.9 %copy-done = bf16[384,4096]{1,0:T(8,128)(2,1)S(1)} copy-done((bf16[384,4096]{1,0:T(8,128)(2,1)S(1)}, bf16[384,4096]{1,0:T(8,128)(2,1)}, u32[]{:S(2)}) %copy-start) | copy-done | bytes 3145752
  112.5 1.3 shard_map.147.refs_4_
  113.8 1.3 shard_map.145.refs_4_
  115.1 6.6 %collective-permute-done.16.refs_5_ = bf16[128,4096]{1,0:T(8,128)(2,1)S(1)} collective-permute-done((bf16[128,4096]{1,0:T(8,128)(2,1)S(1)}, bf16[128,4096]{1,0:T(8,128)(2,1)S(1)}, u32[]{:S(2)}, u32[]{:S(2)}) %collective-permute-start.16) | collective-permute-done | bytes 1048608 | tf_op jit(solution)/shard_map/ppermute | solution.py:369
  121.6 1.3 shard_map.146.refs_4_
  122.9 1.3 shard_map.148.refs_4_
  124.2 8.6 %collective-permute-done.17.refs_5_ = bf16[128,4096]{1,0:T(8,128)(2,1)S(1)} collective-permute-done((bf16[128,4096]{1,0:T(8,128)(2,1)S(1)}, bf16[128,4096]{1,0:T(8,128)(2,1)S(1)}, u32[]{:S(2)}, u32[]{:S(2)}) %collective-permute-start.17) | collective-permute-done | bytes 1048608 | tf_op jit(solution)/shard_map/ppermute | solution.py:369
  132.8 1.3 shard_map.150
  134.2 1.3 collective-permute-start.19
  135.5 1.3 shard_map.149.own_ref
  136.8 1.0 shard_map.151
  (29 shorter events, 1.4 us)
Async XLA Ops:
  0.6 12.3 %collective-permute-start = (bf16[384,4096]{1,0:T(8,128)(2,1)}, bf16[384,4096]{1,0:T(8,128)(2,1)S(1)}, u32[]{:S(2)}, u32[]{:S(2)}) collective-permute-start(bf16[384,4096]{1,0:T(8,128)(2,1)} %refs_3_.7), channel_id=1, source_target_pairs={{0,32},{32,0},{1,33},{33,1},{2,34},{34,2},{3,35},{35,3},{4,36},{36... | collective-permute-start | bytes 9437192 | tf_op jit(solution)/shard_map/ppermute | solution.py:358
  4.0 9.0 %collective-permute-start.1 = (bf16[384,1024]{1,0:T(8,128)(2,1)}, bf16[384,1024]{1,0:T(8,128)(2,1)}, u32[]{:S(2)}, u32[]{:S(2)}) collective-permute-start(bf16[384,1024]{1,0:T(8,128)(2,1)} %refs_7_.1), channel_id=1, source_target_pairs={{0,32},{32,0},{1,33},{33,1},{2,34},{34,2},{3,35},{35,3},{4,36},{36... | collective-permute-start | bytes 2359304 | tf_op jit(solution)/shard_map/ppermute | solution.py:358
  4.1 8.9 %collective-permute-start.2 = (s32[8,32]{1,0:T(8,128)}, s32[8,32]{1,0:T(8,128)S(1)}, u32[]{:S(2)}, u32[]{:S(2)}) collective-permute-start(s32[8,32]{1,0:T(8,128)} %bitcast.4), channel_id=1, source_target_pairs={{0,32},{32,0},{1,33},{33,1},{2,34},{34,2},{3,35},{35,3},{4,36},{36... | collective-permute-start | bytes 3080 | tf_op jit(solution)/shard_map/ppermute | solution.py:358
  4.5 8.5 %copy-start.1 = (bf16[128,128]{1,0:T(8,128)(2,1)S(1)}, bf16[128,128]{1,0:T(8,128)(2,1)}, u32[]{:S(2)}) copy-start(bf16[128,128]{1,0:T(8,128)(2,1)} %constant.42.refs_10_) | copy-start | bytes 98308
  4.5 8.5 %copy-start.2 = (bf16[128,128]{1,0:T(8,128)(2,1)S(1)}, bf16[128,128]{1,0:T(8,128)(2,1)}, u32[]{:S(2)}) copy-start(bf16[128,128]{1,0:T(8,128)(2,1)} %constant.43.refs_11_) | copy-start | bytes 98308
  4.5 8.5 %copy-start.3 = (s32[32,128]{1,0:T(8,128)S(1)}, s32[32,128]{1,0:T(8,128)}, u32[]{:S(2)}) copy-start(s32[32,128]{1,0:T(8,128)} %sign_ref.1) | copy-start | bytes 49156
  17.9 10.0 %collective-permute-start.3 = (bf16[128,2048]{1,0:T(8,128)(2,1)S(1)}, bf16[128,2048]{1,0:T(8,128)(2,1)S(1)}, u32[]{:S(2)}, u32[]{:S(2)}) collective-permute-start(bf16[128,2048]{1,0:T(8,128)(2,1)S(1)} %get-tuple-element.29), channel_id=1, source_target_pairs={{0,2},{1,3},{2,0},{3,1},{32,160},{33,161},{34,162},{35,163},{64,66... | collective-permute-start | bytes 1572872 | tf_op jit(solution)/shard_map/ppermute | solution.py:369
  19.1 14.3 %collective-permute-start.4 = (bf16[128,2048]{1,0:T(8,128)(2,1)S(1)}, bf16[128,2048]{1,0:T(8,128)(2,1)S(1)}, u32[]{:S(2)}, u32[]{:S(2)}) collective-permute-start(bf16[128,2048]{1,0:T(8,128)(2,1)S(1)} %get-tuple-element.30), channel_id=1, source_target_pairs={{0,1},{1,2},{2,3},{3,0},{32,96},{33,97},{34,98},{35,99},{64,65},{6... | collective-permute-start | bytes 1572872 | tf_op jit(solution)/shard_map/ppermute | solution.py:369
  19.5 13.9 %collective-permute-start.5 = (bf16[128,2048]{1,0:T(8,128)(2,1)S(1)}, bf16[128,2048]{1,0:T(8,128)(2,1)S(1)}, u32[]{:S(2)}, u32[]{:S(2)}) collective-permute-start(bf16[128,2048]{1,0:T(8,128)(2,1)S(1)} %get-tuple-element.31), channel_id=1, source_target_pairs={{0,3},{1,0},{2,1},{3,2},{32,224},{33,225},{34,226},{35,227},{64,67... | collective-permute-start | bytes 1572872 | tf_op jit(solution)/shard_map/ppermute | solution.py:369
  26.6 46.1 %copy-start.4 = (f32[4,4096]{1,0:T(4,128)S(1)}, f32[4,4096]{1,0:T(4,128)}, u32[]{:S(2)}) copy-start(f32[4,4096]{1,0:T(4,128)} %master_ref.1) | copy-start | bytes 196612
  26.7 46.0 %copy-start.8 = (s32[4,32]{1,0:T(4,128)S(1)}, s32[4,32]{1,0:T(4,128)}, u32[]{:S(2)}) copy-start(s32[4,32]{1,0:T(4,128)} %exps_ref.1) | copy-start | bytes 1540
  26.7 12.4 %collective-permute-start.6 = (bf16[128,2048]{1,0:T(8,128)(2,1)S(1)}, bf16[128,2048]{1,0:T(8,128)(2,1)S(1)}, u32[]{:S(2)}, u32[]{:S(2)}) collective-permute-start(bf16[128,2048]{1,0:T(8,128)(2,1)S(1)} %get-tuple-element.33), channel_id=1, source_target_pairs={{0,2},{1,3},{2,0},{3,1},{32,160},{33,161},{34,162},{35,163},{64,66... | collective-permute-start | bytes 1572872 | tf_op jit(solution)/shard_map/ppermute | solution.py:369
  27.3 17.3 %collective-permute-start.7 = (bf16[128,2048]{1,0:T(8,128)(2,1)S(1)}, bf16[128,2048]{1,0:T(8,128)(2,1)S(1)}, u32[]{:S(2)}, u32[]{:S(2)}) collective-permute-start(bf16[128,2048]{1,0:T(8,128)(2,1)S(1)} %get-tuple-element.34), channel_id=1, source_target_pairs={{0,1},{1,2},{2,3},{3,0},{32,96},{33,97},{34,98},{35,99},{64,65},{6... | collective-permute-start | bytes 1572872 | tf_op jit(solution)/shard_map/ppermute | solution.py:369
  27.8 16.8 %collective-permute-start.8 = (bf16[128,2048]{1,0:T(8,128)(2,1)S(1)}, bf16[128,2048]{1,0:T(8,128)(2,1)S(1)}, u32[]{:S(2)}, u32[]{:S(2)}) collective-permute-start(bf16[128,2048]{1,0:T(8,128)(2,1)S(1)} %get-tuple-element.35), channel_id=1, source_target_pairs={{0,3},{1,0},{2,1},{3,2},{32,224},{33,225},{34,226},{35,227},{64,67... | collective-permute-start | bytes 1572872 | tf_op jit(solution)/shard_map/ppermute | solution.py:369
  45.7 7.1 %collective-permute-start.9 = (bf16[8,8,2048]{2,1,0:T(8,128)(2,1)S(1)}, bf16[8,8,2048]{2,1,0:T(8,128)(2,1)S(1)}, u32[]{:S(2)}, u32[]{:S(2)}) collective-permute-start(bf16[8,8,2048]{2,1,0:T(8,128)(2,1)S(1)} %get-tuple-element.37), channel_id=1, source_target_pairs={{0,128},{1,129},{2,130},{3,131},{32,34},{33,35},{34,32},{35,33},{6... | collective-permute-start | bytes 786440 | tf_op jit(solution)/shard_map/ppermute | solution.py:369
  47.2 8.4 %collective-permute-start.10 = (bf16[8,8,2048]{2,1,0:T(8,128)(2,1)S(1)}, bf16[8,8,2048]{2,1,0:T(8,128)(2,1)S(1)}, u32[]{:S(2)}, u32[]{:S(2)}) collective-permute-start(bf16[8,8,2048]{2,1,0:T(8,128)(2,1)S(1)} %get-tuple-element.38), channel_id=1, source_target_pairs={{0,64},{1,65},{2,66},{3,67},{32,33},{33,34},{34,35},{35,32},{64,12... | collective-permute-start | bytes 786440 | tf_op jit(solution)/shard_map/ppermute | solution.py:369
  47.6 8.1 %collective-permute-start.11 = (bf16[8,8,2048]{2,1,0:T(8,128)(2,1)S(1)}, bf16[8,8,2048]{2,1,0:T(8,128)(2,1)S(1)}, u32[]{:S(2)}, u32[]{:S(2)}) collective-permute-start(bf16[8,8,2048]{2,1,0:T(8,128)(2,1)S(1)} %get-tuple-element.39), channel_id=1, source_target_pairs={{0,192},{1,193},{2,194},{3,195},{32,35},{33,32},{34,33},{35,34},{6... | collective-permute-start | bytes 786440 | tf_op jit(solution)/shard_map/ppermute | solution.py:369
  56.5 16.2 %all-to-all-start = ((bf16[8,8,2048]{2,1,0:T(8,128)(2,1)}), bf16[8,8,2048]{2,1,0:T(8,128)(2,1)S(1)}, u32[]{:S(2)}, u32[]{:S(2)}) async-start(bf16[8,8,2048]{2,1,0:T(8,128)(2,1)} %shard_map.142), calls=%async_computation | async-start | bytes 524288 | tf_op jit(solution)/shard_map/all_to_all | solution.py:409
  72.7 0.8 copy-start.5
  73.5 0.8 copy-start.6
  74.4 0.8 copy-start.7
  89.7 6.9 %collective-permute-start.12 = (bf16[32,4096]{1,0:T(8,128)(2,1)S(1)}, bf16[32,4096]{1,0:T(8,128)(2,1)S(1)}, u32[]{:S(2)}, u32[]{:S(2)}) collective-permute-start(bf16[32,4096]{1,0:T(8,128)(2,1)S(1)} %reshape.23.refs_0_), channel_id=1, source_target_pairs={{0,128},{1,129},{2,130},{3,131},{32,34},{33,35},{34,32},{35,33},{6... | collective-permute-start | bytes 786440 | tf_op jit(solution)/shard_map/ppermute | solution.py:369
  91.7 7.9 %collective-permute-start.13 = (bf16[32,4096]{1,0:T(8,128)(2,1)S(1)}, bf16[32,4096]{1,0:T(8,128)(2,1)S(1)}, u32[]{:S(2)}, u32[]{:S(2)}) collective-permute-start(bf16[32,4096]{1,0:T(8,128)(2,1)S(1)} %reshape.23.refs_0_), channel_id=1, source_target_pairs={{0,64},{1,65},{2,66},{3,67},{32,33},{33,34},{34,35},{35,32},{64,12... | collective-permute-start | bytes 786440 | tf_op jit(solution)/shard_map/ppermute | solution.py:369
  92.8 6.9 %collective-permute-start.14 = (bf16[32,4096]{1,0:T(8,128)(2,1)S(1)}, bf16[32,4096]{1,0:T(8,128)(2,1)S(1)}, u32[]{:S(2)}, u32[]{:S(2)}) collective-permute-start(bf16[32,4096]{1,0:T(8,128)(2,1)S(1)} %reshape.23.refs_0_), channel_id=1, source_target_pairs={{0,192},{1,193},{2,194},{3,195},{32,35},{33,32},{34,33},{35,34},{6... | collective-permute-start | bytes 786440 | tf_op jit(solution)/shard_map/ppermute | solution.py:369
  99.7 6.4 %collective-permute-start.15 = (bf16[16,128]{1,0:T(8,128)(2,1)S(1)}, bf16[16,128]{1,0:T(8,128)(2,1)S(1)}, u32[]{:S(2)}, u32[]{:S(2)}) collective-permute-start(bf16[16,128]{1,0:T(8,128)(2,1)S(1)} %get-tuple-element.42), channel_id=1, source_target_pairs={{0,32},{32,0},{1,33},{33,1},{2,34},{34,2},{3,35},{35,3},{4,36},{36... | collective-permute-start | bytes 12296 | tf_op jit(solution)/shard_map/ppermute | solution.py:358
  106.1 15.5 %collective-permute-start.16 = (bf16[128,4096]{1,0:T(8,128)(2,1)S(1)}, bf16[128,4096]{1,0:T(8,128)(2,1)S(1)}, u32[]{:S(2)}, u32[]{:S(2)}) collective-permute-start(bf16[128,4096]{1,0:T(8,128)(2,1)S(1)} %get-tuple-element.43.refs_4_), channel_id=1, source_target_pairs={{0,2},{1,3},{2,0},{3,1},{32,160},{33,161},{34,162},{35,163},{64,66... | collective-permute-start | bytes 3145736 | tf_op jit(solution)/shard_map/ppermute | solution.py:369
  107.9 24.9 %collective-permute-start.17 = (bf16[128,4096]{1,0:T(8,128)(2,1)S(1)}, bf16[128,4096]{1,0:T(8,128)(2,1)S(1)}, u32[]{:S(2)}, u32[]{:S(2)}) collective-permute-start(bf16[128,4096]{1,0:T(8,128)(2,1)S(1)} %get-tuple-element.43.refs_4_), channel_id=1, source_target_pairs={{0,1},{1,2},{2,3},{3,0},{32,96},{33,97},{34,98},{35,99},{64,65},{6... | collective-permute-start | bytes 3145736 | tf_op jit(solution)/shard_map/ppermute | solution.py:369
  109.1 23.8 %collective-permute-start.18 = (bf16[128,4096]{1,0:T(8,128)(2,1)S(1)}, bf16[128,4096]{1,0:T(8,128)(2,1)S(1)}, u32[]{:S(2)}, u32[]{:S(2)}) collective-permute-start(bf16[128,4096]{1,0:T(8,128)(2,1)S(1)} %get-tuple-element.43.refs_4_), channel_id=1, source_target_pairs={{0,3},{1,0},{2,1},{3,2},{32,224},{33,225},{34,226},{35,227},{64,67... | collective-permute-start | bytes 3145736 | tf_op jit(solution)/shard_map/ppermute | solution.py:369
  110.6 1.9 %copy-start = (bf16[384,4096]{1,0:T(8,128)(2,1)S(1)}, bf16[384,4096]{1,0:T(8,128)(2,1)}, u32[]{:S(2)}) copy-start(bf16[384,4096]{1,0:T(8,128)(2,1)} %refs_3_.7) | copy-start | bytes 9437188
  134.2 2.7 %collective-permute-start.19 = (bf16[384,512]{1,0:T(8,128)(2,1)S(1)}, bf16[384,512]{1,0:T(8,128)(2,1)S(1)}, u32[]{:S(2)}, u32[]{:S(2)}) collective-permute-start(bf16[384,512]{1,0:T(8,128)(2,1)S(1)} %shard_map.150), channel_id=1, source_target_pairs={{0,32},{32,0},{1,33},{33,1},{2,34},{34,2},{3,35},{35,3},{4,36},{36... | collective-permute-start | bytes 1179656 | tf_op jit(solution)/shard_map/ppermute | solution.py:358
